TPU v7x, 32 devices: a whole 2x2x4 slice. The times are simulated.
32 devices in a mesh: section: 4 (over y, x), frame: 4 (over z), row: 2 (over core).
Axes of the slice: x: 2, y: 2, z: 4, core: 2. Of those that a mesh axis runs over, the one named last changes fastest.
Arguments:
- x_saved: bfloat16 [4, 8, 16, 64, 128], P('section', 'frame', 'row'), may hold values from -6 to 6
- cotangent: bfloat16 [8, 16, 64, 128], P('frame', 'row'), may hold values from -6 to 6
- w_spatial: bfloat16 [4, 3, 3, 128, 128], P('section'), may hold values from -0.1875 to 0.1875
- w_temporal: bfloat16 [4, 3, 128, 128], P('section'), may hold values from -0.3125 to 0.3125
Outputs:
- grad_inputs: bfloat16 [4, 8, 16, 64, 128], P('section', 'frame', 'row')
- grad_spatial: float32 [4, 3, 3, 128, 128], P('section')
- grad_temporal: float32 [4, 3, 128, 128], P('section')
All inputs are finite; a program needn't handle non-finite values.
Results may differ from a plain program's by a relative error of at most 0.014.
Values may be sent and summed in bfloat16 or wider, within the bound.
No kernel may reach another device: no remote copies, remote signals or barrier semaphores. Data moves between devices by JAX's collectives and lax.ppermute only.
A program may use at most 64 MiB of HBM per device.

v0:
```python
import jax
import jax.numpy as jnp
from jax import lax
from jax.sharding import PartitionSpec as P


def padded_2(cells, sides, width):
    for axis, dim in sides:
        count = lax.axis_size(axis)
        ends = count - 1
        head = lax.slice_in_dim(cells, 0, width, axis=dim)
        tail = lax.slice_in_dim(cells, cells.shape[dim] - width, cells.shape[dim], axis=dim)
        cells = jnp.concatenate(
            [
                lax.ppermute(tail, axis, [(i, (i + 1) % count) for i in range(ends)]),
                cells,
                lax.ppermute(head, axis, [((i + 1) % count, i) for i in range(ends)]),
            ],
            axis=dim,
        )
    return cells


def from_behind(block, axis, distance):
    devices = range(lax.axis_size(axis))
    route = [(i - distance, i) for i in devices if i - distance in devices]
    return lax.ppermute(block, axis, route)


def slope_of(pre_act):
    sigma = jax.nn.sigmoid(pre_act)
    return sigma * (1.0 + pre_act * (1.0 - sigma))


def inner_sum(first_arg, second_arg):
    return lax.dot_general(
        first_arg, second_arg, (((0,), (0,)), ((), ())), preferred_element_type=jnp.float32
    )


def pad_cols(values):
    return jnp.pad(values, ((0, 0), (0, 0), (1, 1), (0, 0)))


def frame_shift(values, offset, max_reach):
    widths = [(max_reach, max_reach)] + [(0, 0)] * (values.ndim - 1)
    padded = jnp.pad(values, widths)
    return lax.dynamic_slice_in_dim(padded, max_reach + offset, values.shape[0], 0)


def apply_taps(padded, taps, row_count, col_count, transpose):
    channels = padded.shape[-1]
    running = jnp.zeros((padded.shape[0] * row_count * col_count, taps.shape[-1]), jnp.float32)
    for i in range(3):
        for j in range(3):
            window = padded[:, i : i + row_count, j : j + col_count, :].reshape(-1, channels)
            if transpose:
                running = running + jnp.dot(
                    window, taps[2 - i, 2 - j].T, preferred_element_type=jnp.float32
                )
            else:
                running = running + jnp.dot(window, taps[i, j], preferred_element_type=jnp.float32)
    return running.reshape(padded.shape[0], row_count, col_count, taps.shape[-1])


def to_blocks(values, frame_parts):
    frame_count, row_count, col_count, channels = values.shape
    return values.reshape(frame_count, frame_parts, row_count * col_count // frame_parts, channels)


def temporal_back(segment, taps_time, dilation, max_reach):
    channels = segment.shape[-1]
    running = jnp.zeros((segment.size // channels, channels), jnp.float32)
    for k in range(3):
        shifted = frame_shift(segment, (1 - k) * dilation, max_reach).reshape(-1, channels)
        running = running + jnp.dot(shifted, taps_time[k].T, preferred_element_type=jnp.float32)
    return running.astype(jnp.bfloat16).reshape(segment.shape)


def spatial_back(back_tiles, pre_slope, taps_space, local_shape):
    back_act = lax.all_to_all(back_tiles, "frame", split_axis=0, concat_axis=1, tiled=True).reshape(
        local_shape
    )
    grad_pre = (back_act.astype(jnp.float32) * pre_slope).astype(jnp.bfloat16)
    rims = padded_2(grad_pre, (("row", 1),), 1)
    branch = apply_taps(pad_cols(rims), taps_space, local_shape[1], local_shape[2], True).astype(
        jnp.bfloat16
    )
    return (grad_pre, branch)


def pass_back(outgoing):
    return from_behind(outgoing, "section", -1)


def section_run(x_saved, cotangent, w_spatial, w_temporal):
    block_input = x_saved[0]
    taps_space = w_spatial[0]
    taps_time = w_temporal[0]
    local_shape = block_input.shape
    row_count = local_shape[1]
    col_count = local_shape[2]
    channels = local_shape[3]
    frame_parts = lax.axis_size("frame")
    section_count = lax.axis_size("section")
    section_index = lax.axis_index("section")
    dilation = jnp.left_shift(jnp.int32(1), section_index)
    max_reach = 2 ** (section_count - 1)
    extended = pad_cols(padded_2(block_input, (("row", 1),), 1))
    pre_act = apply_taps(extended, taps_space, row_count, col_count, False)
    pre_slope = slope_of(pre_act)
    active = jax.nn.silu(pre_act).astype(jnp.bfloat16)
    active_tiles = lax.all_to_all(
        to_blocks(active, frame_parts), "frame", split_axis=1, concat_axis=0, tiled=True
    )
    kept_pre = jnp.zeros(local_shape, jnp.bfloat16)
    kept_tiles = jnp.zeros_like(active_tiles)
    incoming = cotangent
    own_grad = jnp.zeros(local_shape, jnp.bfloat16)
    for position in range(section_count):
        with_segment = lax.all_to_all(
            to_blocks(incoming, frame_parts), "frame", split_axis=1, concat_axis=0, tiled=True
        )
        back_tiles = temporal_back(with_segment, taps_time, dilation, max_reach)
        grad_pre, branch = spatial_back(back_tiles, pre_slope, taps_space, local_shape)
        outgoing = (
            incoming.astype(jnp.float32) + lax.optimization_barrier(branch).astype(jnp.float32)
        ).astype(jnp.bfloat16)
        is_owner = section_index == section_count - 1 - position
        own_grad = jnp.where(is_owner, outgoing, own_grad)
        kept_pre = jnp.where(is_owner, grad_pre, kept_pre)
        kept_tiles = jnp.where(is_owner, with_segment, kept_tiles)
        if position + 1 < section_count:
            incoming = pass_back(outgoing)
    flat_pre = kept_pre.reshape(-1, channels)
    grads_space = jnp.stack(
        [
            jnp.stack(
                [
                    inner_sum(
                        extended[:, i : i + row_count, j : j + col_count, :].reshape(-1, channels),
                        flat_pre,
                    )
                    for j in range(3)
                ]
            )
            for i in range(3)
        ]
    )
    flat_tiles = kept_tiles.reshape(-1, channels)
    grads_time = jnp.stack(
        [
            inner_sum(
                frame_shift(active_tiles, (k - 1) * dilation, max_reach).reshape(-1, channels),
                flat_tiles,
            )
            for k in range(3)
        ]
    )
    grads_space, grads_time = lax.psum((grads_space, grads_time), ("frame", "row"))
    return (own_grad[None], grads_space[None], grads_time[None])


def local(x_saved, cotangent, w_spatial, w_temporal):
    return section_run(x_saved, cotangent, w_spatial, w_temporal)


def solution(mesh):
    return jax.shard_map(
        local,
        mesh=mesh,
        in_specs=(
            P("section", "frame", "row", None, None),
            P("frame", "row", None, None),
            P("section", None, None, None, None),
            P("section", None, None, None),
        ),
        out_specs=(
            P("section", "frame", "row", None, None),
            P("section", None, None, None, None),
            P("section", None, None, None),
        ),
        check_vma=False,
    )
```

profile of v0, /device:TPU:0, one launch (start us, length us, event | category | flops | bytes accessed | tf_op | source)
XLA Modules:
  0.0 260.1 jit_solution(2147495361420427421)
XLA Ops:
  8.0 2.3 collective-permute-start
  11.6 1.7 copy.56
  13.3 5.8 %all-to-all-start = ((bf16[2,4,128,128]{3,2,0,1:T(8,128)(2,1)}), bf16[2,4,128,128]{3,2,0,1:T(8,128)(2,1)S(1)}, u32[]{:S(2)}, u32[]{:S(2)}) async-start(bf16[2,4,128,128]{3,2,0,1:T(8,128)(2,1)} %copy.56), calls=%async_computation | async-start | bytes 524288 | tf_op jit(solution)/shard_map/all_to_all | solution.py:121
  22.3 7.0 %all-to-all-done = bf16[2,4,128,128]{3,2,0,1:T(8,128)(2,1)S(1)} async-done(((bf16[2,4,128,128]{3,2,0,1:T(8,128)(2,1)}), bf16[2,4,128,128]{3,2,0,1:T(8,128)(2,1)S(1)}, u32[]{:S(2)}, u32[]{:S(2)}) %all-to-all-start) | async-done | bytes 262176 | tf_op jit(solution)/shard_map/all_to_all | solution.py:121
  31.6 3.4 %all-to-all-start.1 = ((bf16[8,1,128,128]{3,2,1,0:T(8,128)(2,1)}), bf16[8,1,128,128]{3,2,1,0:T(8,128)(2,1)S(1)}, u32[]{:S(2)}, u32[]{:S(2)}) async-start(bf16[8,1,128,128]{3,2,1,0:T(8,128)(2,1)} %bitcast.12), calls=%async_computation.1 | async-start | bytes 524288 | tf_op jit(solution)/shard_map/all_to_all | solution.py:81
  36.2 8.1 %all-to-all-done.1 = bf16[8,1,128,128]{3,2,1,0:T(8,128)(2,1)S(1)} async-done(((bf16[8,1,128,128]{3,2,1,0:T(8,128)(2,1)}), bf16[8,1,128,128]{3,2,1,0:T(8,128)(2,1)S(1)}, u32[]{:S(2)}, u32[]{:S(2)}) %all-to-all-start.1) | async-done | bytes 262176 | tf_op jit(solution)/shard_map/all_to_all | solution.py:81
  49.3 1.8 collective-permute-done.3
  55.8 9.0 %collective-permute-done.4 = bf16[2,8,64,128]{3,2,1,0:T(8,128)(2,1)S(1)} collective-permute-done((bf16[2,8,64,128]{3,2,1,0:T(8,128)(2,1)S(1)}, bf16[2,8,64,128]{3,2,1,0:T(8,128)(2,1)S(1)}, u32[]{:S(2)}, u32[]{:S(2)}) %collective-permute-start.4) | collective-permute-done | bytes 262176 | tf_op jit(solution)/shard_map/ppermute | solution.py:27
  64.8 11.1 %all_to_all.126 = bf16[2,4,128,128]{3,2,0,1:T(8,128)(2,1)S(1)} all-to-all(bf16[2,4,128,128]{3,2,0,1:T(8,128)(2,1)S(1)} %copy.61), channel_id=1, replica_groups=mesh['section'=4,'frame'=4,'row'=2] {'frame'}, dimensions={1} | all-to-all | bytes 524288 | tf_op jit(solution)/shard_map/all_to_all | solution.py:121
  76.7 10.9 %all_to_all.127 = bf16[8,1,128,128]{3,2,1,0:T(8,128)(2,1)S(1)} all-to-all(bf16[8,1,128,128]{3,2,1,0:T(8,128)(2,1)S(1)} %bitcast.560), channel_id=1, replica_groups=mesh['section'=4,'frame'=4,'row'=2] {'frame'}, dimensions={0} | all-to-all | bytes 524288 | tf_op jit(solution)/shard_map/all_to_all | solution.py:81
  96.9 9.6 %collective-permute-done.7 = bf16[2,8,64,128]{3,2,1,0:T(8,128)(2,1)S(1)} collective-permute-done((bf16[2,8,64,128]{3,2,1,0:T(8,128)(2,1)S(1)}, bf16[2,8,64,128]{3,2,1,0:T(8,128)(2,1)S(1)}, u32[]{:S(2)}, u32[]{:S(2)}) %collective-permute-start.7) | collective-permute-done | bytes 262176 | tf_op jit(solution)/shard_map/ppermute | solution.py:27
  106.5 11.3 %all_to_all.128 = bf16[2,4,128,128]{3,2,0,1:T(8,128)(2,1)S(1)} all-to-all(bf16[2,4,128,128]{3,2,0,1:T(8,128)(2,1)S(1)} %copy.66), channel_id=1, replica_groups=mesh['section'=4,'frame'=4,'row'=2] {'frame'}, dimensions={1} | all-to-all | bytes 524288 | tf_op jit(solution)/shard_map/all_to_all | solution.py:121
  118.7 10.9 %all_to_all.129 = bf16[8,1,128,128]{3,2,1,0:T(8,128)(2,1)S(1)} all-to-all(bf16[8,1,128,128]{3,2,1,0:T(8,128)(2,1)S(1)} %bitcast.561), channel_id=1, replica_groups=mesh['section'=4,'frame'=4,'row'=2] {'frame'}, dimensions={0} | all-to-all | bytes 524288 | tf_op jit(solution)/shard_map/all_to_all | solution.py:81
  133.4 1.6 collective-permute-done.9
  139.6 9.6 %collective-permute-done.10 = bf16[2,8,64,128]{3,2,1,0:T(8,128)(2,1)S(1)} collective-permute-done((bf16[2,8,64,128]{3,2,1,0:T(8,128)(2,1)S(1)}, bf16[2,8,64,128]{3,2,1,0:T(8,128)(2,1)S(1)}, u32[]{:S(2)}, u32[]{:S(2)}) %collective-permute-start.10) | collective-permute-done | bytes 262176 | tf_op jit(solution)/shard_map/ppermute | solution.py:27
  150.0 3.4 %all-to-all-start.6 = ((bf16[2,4,128,128]{3,2,0,1:T(8,128)(2,1)}), bf16[2,4,128,128]{3,2,0,1:T(8,128)(2,1)S(1)}, u32[]{:S(2)}, u32[]{:S(2)}) async-start(bf16[2,4,128,128]{3,2,0,1:T(8,128)(2,1)} %copy.71), calls=%async_computation.6 | async-start | bytes 524288 | tf_op jit(solution)/shard_map/all_to_all | solution.py:121
  154.5 1.9 multiply_convert_fusion
  156.4 6.1 %all-to-all-done.6 = bf16[2,4,128,128]{3,2,0,1:T(8,128)(2,1)S(1)} async-done(((bf16[2,4,128,128]{3,2,0,1:T(8,128)(2,1)}), bf16[2,4,128,128]{3,2,0,1:T(8,128)(2,1)S(1)}, u32[]{:S(2)}, u32[]{:S(2)}) %all-to-all-start.6) | async-done | bytes 262176 | tf_op jit(solution)/shard_map/all_to_all | solution.py:121
  162.4 4.1 %all-to-all-start.8 = ((bf16[2,4,128,128]{2,3,0,1:T(8,128)(2,1)}), bf16[2,4,128,128]{2,3,0,1:T(8,128)(2,1)}, u32[]{:S(2)}, u32[]{:S(2)}) async-start(bf16[2,4,128,128]{2,3,0,1:T(8,128)(2,1)} %multiply_convert_fusion), calls=%async_computation.8 | async-start | bytes 524288 | tf_op jit(solution)/shard_map/all_to_all | solution.py:113
  168.1 5.4 %all-to-all-done.8 = bf16[2,4,128,128]{2,3,0,1:T(8,128)(2,1)} async-done(((bf16[2,4,128,128]{2,3,0,1:T(8,128)(2,1)}), bf16[2,4,128,128]{2,3,0,1:T(8,128)(2,1)}, u32[]{:S(2)}, u32[]{:S(2)}) %all-to-all-start.8) | async-done | bytes 262176 | tf_op jit(solution)/shard_map/all_to_all | solution.py:113
  173.5 3.4 %all-to-all-start.7 = ((bf16[8,1,128,128]{3,2,1,0:T(8,128)(2,1)}), bf16[8,1,128,128]{3,2,1,0:T(8,128)(2,1)S(1)}, u32[]{:S(2)}, u32[]{:S(2)}) async-start(bf16[8,1,128,128]{3,2,1,0:T(8,128)(2,1)} %bitcast.550), calls=%async_computation.7 | async-start | bytes 524288 | tf_op jit(solution)/shard_map/all_to_all | solution.py:81
  181.4 2.3 all-to-all-done.7
  196.8 53.8 %all-reduce.13.cloned.1.call-done = (f32[1,3,3,128,128]{4,3,2,1,0:T(8,128)}, f32[1,3,128,128]{3,2,1,0:T(8,128)}) async-done(((f32[1,3,3,128,128]{4,3,2,1,0:T(8,128)}, f32[1,3,128,128]{3,2,1,0:T(8,128)}), (f32[1,3,3,128,128]{4,3,2,1,0:T(8,128)}, f32[1,3,128,128]{3,2,1,0:T(8,128)})) %all-reduce.13.cloned.1.call-update) | async-done | bytes 786448 | tf_op jit(solution)/shard_map/psum | solution.py:160
  250.6 2.0 copy.98
  (196 shorter events, 58.6 us)
Async XLA Ops:
  8.0 11.2 %collective-permute-start = (bf16[2,1,64,128]{3,2,1,0:T(8,128)(2,1)S(1)}, bf16[2,1,64,128]{3,2,1,0:T(8,128)(2,1)S(1)}, u32[]{:S(2)}, u32[]{:S(2)}) collective-permute-start(bf16[2,1,64,128]{3,2,1,0:T(8,128)(2,1)S(1)} %get-tuple-element.61), channel_id=1, source_target_pairs={{0,1},{2,3},{4,5},{6,7},{8,9},{10,11},{12,13},{14,15},{16,17},{18,... | collective-permute-start | bytes 98312 | tf_op jit(solution)/shard_map/ppermute | solution.py:15
  10.3 8.8 %collective-permute-start.1 = (bf16[2,1,64,128]{3,2,1,0:T(8,128)(2,1)S(1)}, bf16[2,1,64,128]{3,2,1,0:T(8,128)(2,1)S(1)}, u32[]{:S(2)}, u32[]{:S(2)}) collective-permute-start(bf16[2,1,64,128]{3,2,1,0:T(8,128)(2,1)S(1)} %get-tuple-element.62), channel_id=1, source_target_pairs={{1,0},{3,2},{5,4},{7,6},{9,8},{11,10},{13,12},{15,14},{17,16},{19,... | collective-permute-start | bytes 98312 | tf_op jit(solution)/shard_map/ppermute | solution.py:17
  13.3 5.8 %copy-start.1 = (bf16[1,2,8,64,128]{4,3,2,1,0:T(8,128)(2,1)S(1)}, bf16[1,2,8,64,128]{4,3,2,1,0:T(8,128)(2,1)}, u32[]{:S(2)}) copy-start(bf16[1,2,8,64,128]{4,3,2,1,0:T(8,128)(2,1)} %param.4) | copy-start | bytes 786436
  13.3 16.0 %all-to-all-start = ((bf16[2,4,128,128]{3,2,0,1:T(8,128)(2,1)}), bf16[2,4,128,128]{3,2,0,1:T(8,128)(2,1)S(1)}, u32[]{:S(2)}, u32[]{:S(2)}) async-start(bf16[2,4,128,128]{3,2,0,1:T(8,128)(2,1)} %copy.56), calls=%async_computation | async-start | bytes 524288 | tf_op jit(solution)/shard_map/all_to_all | solution.py:121
  31.6 12.7 %all-to-all-start.1 = ((bf16[8,1,128,128]{3,2,1,0:T(8,128)(2,1)}), bf16[8,1,128,128]{3,2,1,0:T(8,128)(2,1)S(1)}, u32[]{:S(2)}, u32[]{:S(2)}) async-start(bf16[8,1,128,128]{3,2,1,0:T(8,128)(2,1)} %bitcast.12), calls=%async_computation.1 | async-start | bytes 524288 | tf_op jit(solution)/shard_map/all_to_all | solution.py:81
  46.7 2.6 %collective-permute-start.2 = (bf16[2,1,64,128]{3,2,1,0:T(8,128)(2,1)S(1)}, bf16[2,1,64,128]{3,2,1,0:T(8,128)(2,1)S(1)}, u32[]{:S(2)}, u32[]{:S(2)}) collective-permute-start(bf16[2,1,64,128]{3,2,1,0:T(8,128)(2,1)S(1)} %get-tuple-element.57), channel_id=1, source_target_pairs={{0,1},{2,3},{4,5},{6,7},{8,9},{10,11},{12,13},{14,15},{16,17},{18,... | collective-permute-start | bytes 98312 | tf_op jit(solution)/shard_map/ppermute | solution.py:15
  48.0 3.1 %collective-permute-start.3 = (bf16[2,1,64,128]{3,2,1,0:T(8,128)(2,1)S(1)}, bf16[2,1,64,128]{3,2,1,0:T(8,128)(2,1)S(1)}, u32[]{:S(2)}, u32[]{:S(2)}) collective-permute-start(bf16[2,1,64,128]{3,2,1,0:T(8,128)(2,1)S(1)} %get-tuple-element.58), channel_id=1, source_target_pairs={{1,0},{3,2},{5,4},{7,6},{9,8},{11,10},{13,12},{15,14},{17,16},{19,... | collective-permute-start | bytes 98312 | tf_op jit(solution)/shard_map/ppermute | solution.py:17
  54.5 10.3 %copy-start.10 = (bf16[2,8,64,128]{3,2,1,0:T(8,128)(2,1)}, bf16[2,8,64,128]{3,2,1,0:T(8,128)(2,1)S(1)}, u32[]{:S(2)}) copy-start(bf16[2,8,64,128]{3,2,1,0:T(8,128)(2,1)S(1)} %add_convert_fusion.3) | copy-start | bytes 786436
  54.5 10.3 %collective-permute-start.4 = (bf16[2,8,64,128]{3,2,1,0:T(8,128)(2,1)S(1)}, bf16[2,8,64,128]{3,2,1,0:T(8,128)(2,1)S(1)}, u32[]{:S(2)}, u32[]{:S(2)}) collective-permute-start(bf16[2,8,64,128]{3,2,1,0:T(8,128)(2,1)S(1)} %add_convert_fusion.3), channel_id=1, source_target_pairs={{8,0},{16,8},{24,16},{9,1},{17,9},{25,17},{10,2},{18,10},{26,18},{... | collective-permute-start | bytes 786440 | tf_op jit(solution)/shard_map/ppermute | solution.py:27
  88.6 2.8 %collective-permute-start.5 = (bf16[2,1,64,128]{3,2,1,0:T(8,128)(2,1)S(1)}, bf16[2,1,64,128]{3,2,1,0:T(8,128)(2,1)S(1)}, u32[]{:S(2)}, u32[]{:S(2)}) collective-permute-start(bf16[2,1,64,128]{3,2,1,0:T(8,128)(2,1)S(1)} %get-tuple-element.51), channel_id=1, source_target_pairs={{0,1},{2,3},{4,5},{6,7},{8,9},{10,11},{12,13},{14,15},{16,17},{18,... | collective-permute-start | bytes 98312 | tf_op jit(solution)/shard_map/ppermute | solution.py:15
  89.9 3.1 %collective-permute-start.6 = (bf16[2,1,64,128]{3,2,1,0:T(8,128)(2,1)S(1)}, bf16[2,1,64,128]{3,2,1,0:T(8,128)(2,1)S(1)}, u32[]{:S(2)}, u32[]{:S(2)}) collective-permute-start(bf16[2,1,64,128]{3,2,1,0:T(8,128)(2,1)S(1)} %get-tuple-element.52), channel_id=1, source_target_pairs={{1,0},{3,2},{5,4},{7,6},{9,8},{11,10},{13,12},{15,14},{17,16},{19,... | collective-permute-start | bytes 98312 | tf_op jit(solution)/shard_map/ppermute | solution.py:17
  95.6 10.9 %copy-start.12 = (bf16[2,8,64,128]{3,2,1,0:T(8,128)(2,1)}, bf16[2,8,64,128]{3,2,1,0:T(8,128)(2,1)S(1)}, u32[]{:S(2)}) copy-start(bf16[2,8,64,128]{3,2,1,0:T(8,128)(2,1)S(1)} %add_convert_fusion.2) | copy-start | bytes 786436
  95.6 10.9 %collective-permute-start.7 = (bf16[2,8,64,128]{3,2,1,0:T(8,128)(2,1)S(1)}, bf16[2,8,64,128]{3,2,1,0:T(8,128)(2,1)S(1)}, u32[]{:S(2)}, u32[]{:S(2)}) collective-permute-start(bf16[2,8,64,128]{3,2,1,0:T(8,128)(2,1)S(1)} %add_convert_fusion.2), channel_id=1, source_target_pairs={{8,0},{16,8},{24,16},{9,1},{17,9},{25,17},{10,2},{18,10},{26,18},{... | collective-permute-start | bytes 786440 | tf_op jit(solution)/shard_map/ppermute | solution.py:27
  130.6 2.8 %collective-permute-start.8 = (bf16[2,1,64,128]{3,2,1,0:T(8,128)(2,1)S(1)}, bf16[2,1,64,128]{3,2,1,0:T(8,128)(2,1)S(1)}, u32[]{:S(2)}, u32[]{:S(2)}) collective-permute-start(bf16[2,1,64,128]{3,2,1,0:T(8,128)(2,1)S(1)} %get-tuple-element.45), channel_id=1, source_target_pairs={{0,1},{2,3},{4,5},{6,7},{8,9},{10,11},{12,13},{14,15},{16,17},{18,... | collective-permute-start | bytes 98312 | tf_op jit(solution)/shard_map/ppermute | solution.py:15
  131.9 3.1 %collective-permute-start.9 = (bf16[2,1,64,128]{3,2,1,0:T(8,128)(2,1)S(1)}, bf16[2,1,64,128]{3,2,1,0:T(8,128)(2,1)S(1)}, u32[]{:S(2)}, u32[]{:S(2)}) collective-permute-start(bf16[2,1,64,128]{3,2,1,0:T(8,128)(2,1)S(1)} %get-tuple-element.46), channel_id=1, source_target_pairs={{1,0},{3,2},{5,4},{7,6},{9,8},{11,10},{13,12},{15,14},{17,16},{19,... | collective-permute-start | bytes 98312 | tf_op jit(solution)/shard_map/ppermute | solution.py:17
  138.4 10.9 %collective-permute-start.10 = (bf16[2,8,64,128]{3,2,1,0:T(8,128)(2,1)S(1)}, bf16[2,8,64,128]{3,2,1,0:T(8,128)(2,1)S(1)}, u32[]{:S(2)}, u32[]{:S(2)}) collective-permute-start(bf16[2,8,64,128]{3,2,1,0:T(8,128)(2,1)S(1)} %add_convert_fusion.1), channel_id=1, source_target_pairs={{8,0},{16,8},{24,16},{9,1},{17,9},{25,17},{10,2},{18,10},{26,18},{... | collective-permute-start | bytes 786440 | tf_op jit(solution)/shard_map/ppermute | solution.py:27
  150.0 12.4 %all-to-all-start.6 = ((bf16[2,4,128,128]{3,2,0,1:T(8,128)(2,1)}), bf16[2,4,128,128]{3,2,0,1:T(8,128)(2,1)S(1)}, u32[]{:S(2)}, u32[]{:S(2)}) async-start(bf16[2,4,128,128]{3,2,0,1:T(8,128)(2,1)} %copy.71), calls=%async_computation.6 | async-start | bytes 524288 | tf_op jit(solution)/shard_map/all_to_all | solution.py:121
  162.4 11.1 %all-to-all-start.8 = ((bf16[2,4,128,128]{2,3,0,1:T(8,128)(2,1)}), bf16[2,4,128,128]{2,3,0,1:T(8,128)(2,1)}, u32[]{:S(2)}, u32[]{:S(2)}) async-start(bf16[2,4,128,128]{2,3,0,1:T(8,128)(2,1)} %multiply_convert_fusion), calls=%async_computation.8 | async-start | bytes 524288 | tf_op jit(solution)/shard_map/all_to_all | solution.py:113
  173.5 10.2 %all-to-all-start.7 = ((bf16[8,1,128,128]{3,2,1,0:T(8,128)(2,1)}), bf16[8,1,128,128]{3,2,1,0:T(8,128)(2,1)S(1)}, u32[]{:S(2)}, u32[]{:S(2)}) async-start(bf16[8,1,128,128]{3,2,1,0:T(8,128)(2,1)} %bitcast.550), calls=%async_computation.7 | async-start | bytes 524288 | tf_op jit(solution)/shard_map/all_to_all | solution.py:81
  176.9 73.7 %all-reduce.13.cloned.1.call-start = ((), (), s32[]{:S(2)}) async-start(), calls=%async_computation.9 | async-start | bytes 1572864 | tf_op jit(solution)/shard_map/psum | solution.py:160
  187.6 2.6 %copy-start.24 = (bf16[2,1,64,128]{3,2,1,0:T(8,128)(2,1)S(1)}, bf16[2,1,64,128]{3,2,1,0:T(8,128)(2,1)}, u32[]{:S(2)}) copy-start(bf16[2,1,64,128]{3,2,1,0:T(8,128)(2,1)} %copy-done.23) | copy-start | bytes 98308
  187.6 4.9 %collective-permute-start.11 = (bf16[2,1,64,128]{3,2,1,0:T(8,128)(2,1)S(1)}, bf16[2,1,64,128]{3,2,1,0:T(8,128)(2,1)S(1)}, u32[]{:S(2)}, u32[]{:S(2)}) collective-permute-start(bf16[2,1,64,128]{3,2,1,0:T(8,128)(2,1)S(1)} %get-tuple-element.39), channel_id=1, source_target_pairs={{0,1},{2,3},{4,5},{6,7},{8,9},{10,11},{12,13},{14,15},{16,17},{18,... | collective-permute-start | bytes 98312 | tf_op jit(solution)/shard_map/ppermute | solution.py:15
  188.9 3.6 %collective-permute-start.12 = (bf16[2,1,64,128]{3,2,1,0:T(8,128)(2,1)S(1)}, bf16[2,1,64,128]{3,2,1,0:T(8,128)(2,1)S(1)}, u32[]{:S(2)}, u32[]{:S(2)}) collective-permute-start(bf16[2,1,64,128]{3,2,1,0:T(8,128)(2,1)S(1)} %get-tuple-element.40), channel_id=1, source_target_pairs={{1,0},{3,2},{5,4},{7,6},{9,8},{11,10},{13,12},{15,14},{17,16},{19,... | collective-permute-start | bytes 98312 | tf_op jit(solution)/shard_map/ppermute | solution.py:17
  250.6 2.0 copy-start.20
  (20 other events, 19.3 us)
Sparse Core Ops, SparseCore 0:
  192.6 57.9 all-reduce.12
where the time goes:
time: 262 us; the launch traced here: 260 us
  waiting for transfers between devices  116 us (44%)
  blocking collectives  44.2 us (17%)
  starting transfers between devices  38.2 us (15%)
  matrix products  21.1 us (8%)
  local copies, waits for them, and re-layouts  17.5 us (7%)
  between operations  15.1 us (6%)
  other arithmetic  8.21 us (3%)
    psum x1, waiting for transfers between devices, section_run(): lax.psum((grads_space, grads_time), ('frame', 'row'))  53.8 us
    ppermute x3, waiting for transfers between devices, from_behind(): return lax.ppermute(block, axis, route)  28.2 us
    all_to_all x2, blocking collectives, section_run(): lax.all_to_all(to_blocks(incoming, frame_parts), 'frame', split_axis=1, c...  22.4 us
    all_to_all x2, blocking collectives, spatial_back(): lax.all_to_all(back_tiles, 'frame', split_axis=0, concat_axis=1, tiled=True)  21.8 us
    all_to_all x2, waiting for transfers between devices, section_run(): lax.all_to_all(to_blocks(incoming, frame_parts), 'frame', split_axis=1, c...  13.1 us
    unnamed x52, local copies, waits for them, and re-layouts  11.2 us
    all_to_all x2, waiting for transfers between devices, spatial_back(): lax.all_to_all(back_tiles, 'frame', split_axis=0, concat_axis=1, tiled=True)  10.4 us
    all_to_all x2, starting transfers between devices, section_run(): lax.all_to_all(to_blocks(incoming, frame_parts), 'frame', split_axis=1, c...  9.24 us
  transfers between devices with their start and end apart: 19, of which 12 were waited for; matrix products, arithmetic and copies ran while one was open for 7% of the time, Pallas kernels for 0%

commit v1 on v0

v1 whole, which is shorter than its diff:
```python
import jax
import jax.numpy as jnp
from jax import lax
from jax.sharding import PartitionSpec as P


def slope_of(pre_act):
    sigma = jax.nn.sigmoid(pre_act)
    return sigma * (1.0 + pre_act * (1.0 - sigma))


def inner_sum(first_arg, second_arg):
    return lax.dot_general(
        first_arg, second_arg, (((0,), (0,)), ((), ())), preferred_element_type=jnp.float32
    )


def row_halo(cells):
    count = lax.axis_size("row")
    index = lax.axis_index("row")
    head = cells[:, :1]
    tail = cells[:, -1:]
    nothing = jnp.zeros_like(head)
    if count == 1:
        above, below = nothing, nothing
    elif count == 2:
        got = lax.ppermute(jnp.where(index == 0, tail, head), "row", [(0, 1), (1, 0)])
        above = jnp.where(index == 0, nothing, got)
        below = jnp.where(index == 0, got, nothing)
    else:
        above = lax.ppermute(tail, "row", [(i, i + 1) for i in range(count - 1)])
        below = lax.ppermute(head, "row", [(i + 1, i) for i in range(count - 1)])
    return jnp.concatenate([above, cells, below], axis=1)


def pad_cols(values):
    return jnp.pad(values, ((0, 0), (0, 0), (1, 1), (0, 0)))


def apply_taps(padded, taps, row_count, col_count, transpose):
    channels = padded.shape[-1]
    running = jnp.zeros((padded.shape[0] * row_count * col_count, taps.shape[-1]), jnp.float32)
    for i in range(3):
        for j in range(3):
            window = padded[:, i : i + row_count, j : j + col_count, :].reshape(-1, channels)
            if transpose:
                tap = taps[2 - i, 2 - j].T
            else:
                tap = taps[i, j]
            running = running + jnp.dot(window, tap, preferred_element_type=jnp.float32)
    return running.reshape(padded.shape[0], row_count, col_count, taps.shape[-1])


def fetch(block, source, target, frame_step):
    frame_parts = lax.axis_size("frame")
    route = [
        (source * frame_parts + z + frame_step, target * frame_parts + z)
        for z in range(frame_parts)
        if 0 <= z + frame_step < frame_parts
    ]
    if not route or (source == target and frame_step == 0):
        return block if route else jnp.zeros_like(block)
    return lax.ppermute(block, ("section", "frame"), route)


def shifted_from(block, source, target, offset):
    own_frames = block.shape[0]
    step, rest = divmod(offset, own_frames)
    if rest == 0:
        return fetch(block, source, target, step)
    return jnp.concatenate(
        [fetch(block[rest:], source, target, step), fetch(block[:rest], source, target, step + 1)]
    )


def pair_from(block, source, target, dilation):
    own_frames = block.shape[0]
    frame_parts = lax.axis_size("frame")
    step, rest = divmod(dilation, own_frames)
    nothing = jnp.zeros_like(block)
    if step >= frame_parts:
        return nothing, nothing
    if rest == 0 and 2 * step >= frame_parts:
        route = [
            (source * frame_parts + z + move, target * frame_parts + z)
            for z in range(frame_parts)
            for move in (step, -step)
            if 0 <= z + move < frame_parts
        ]
        got = lax.ppermute(block, ("section", "frame"), route)
        early = lax.axis_index("frame") < frame_parts - step
        return jnp.where(early, got, nothing), jnp.where(early, nothing, got)
    return (
        shifted_from(block, source, target, dilation),
        shifted_from(block, source, target, -dilation),
    )


def gather_parts(part, axis):
    count = lax.axis_size(axis)
    if count == 1:
        return part
    if count & (count - 1) or count > 4:
        return lax.all_gather(part, axis, axis=0, tiled=True)
    index = lax.axis_index(axis)
    size = part.shape[0]
    whole = jnp.zeros((count * size,) + part.shape[1:], part.dtype)
    whole = lax.dynamic_update_slice_in_dim(whole, part, index * size, 0)
    for mask in range(1, count):
        got = lax.ppermute(part, axis, [(i, i ^ mask) for i in range(count)])
        whole = lax.dynamic_update_slice_in_dim(whole, got, (index ^ mask) * size, 0)
    return whole


def sum_over(values, axis):
    count = lax.axis_size(axis)
    if count == 1:
        return values
    size = values.shape[0] // count
    if count == 2:
        index = lax.axis_index(axis)
        own = lax.dynamic_slice_in_dim(values, index * size, size, 0)
        other = lax.dynamic_slice_in_dim(values, (1 - index) * size, size, 0)
        got = lax.ppermute(other.astype(jnp.bfloat16), axis, [(0, 1), (1, 0)])
        return own + got.astype(jnp.float32)
    parts = values.astype(jnp.bfloat16).reshape((count, size) + values.shape[1:])
    parts = lax.all_to_all(parts, axis, split_axis=0, concat_axis=0, tiled=True)
    return jnp.sum(parts.astype(jnp.float32), axis=0)


def section_run(x_saved, cotangent, w_spatial, w_temporal):
    block_input = x_saved[0]
    taps_space = w_spatial[0]
    taps_time = w_temporal[0]
    local_shape = block_input.shape
    row_count = local_shape[1]
    col_count = local_shape[2]
    channels = local_shape[3]
    section_count = lax.axis_size("section")
    section_index = lax.axis_index("section")
    extended = pad_cols(row_halo(block_input))
    pre_act = apply_taps(extended, taps_space, row_count, col_count, False)
    pre_slope = slope_of(pre_act)
    active = jax.nn.silu(pre_act).astype(jnp.bfloat16)

    top = section_count - 1
    here = cotangent
    later, earlier = pair_from(cotangent, top, top, 2**top)
    for position in range(section_count):
        owner = top - position
        running = jnp.dot(
            here.reshape(-1, channels), taps_time[1].T, preferred_element_type=jnp.float32
        )
        running += jnp.dot(
            later.reshape(-1, channels), taps_time[0].T, preferred_element_type=jnp.float32
        )
        running += jnp.dot(
            earlier.reshape(-1, channels), taps_time[2].T, preferred_element_type=jnp.float32
        )
        back_act = running.astype(jnp.bfloat16).reshape(local_shape)
        grad_pre = (back_act.astype(jnp.float32) * pre_slope).astype(jnp.bfloat16)
        padded = pad_cols(row_halo(grad_pre))
        branch = apply_taps(padded, taps_space, row_count, col_count, True).astype(jnp.bfloat16)
        outgoing = (here.astype(jnp.float32) + branch.astype(jnp.float32)).astype(jnp.bfloat16)
        if position + 1 < section_count:
            arrives = section_index == owner - 1
            new_later, new_earlier = pair_from(outgoing, owner, owner - 1, 2 ** (owner - 1))
            new_here = fetch(outgoing, owner, owner - 1, 0)
            here = jnp.where(arrives, new_here, here)
            later = jnp.where(arrives, new_later, later)
            earlier = jnp.where(arrives, new_earlier, earlier)

    flat_pre = grad_pre.reshape(-1, channels)
    flat_active = active.reshape(-1, channels)
    grads = [
        inner_sum(
            extended[:, i : i + row_count, j : j + col_count, :].reshape(-1, channels), flat_pre
        )
        for i in range(3)
        for j in range(3)
    ]
    grads += [inner_sum(flat_active, g.reshape(-1, channels)) for g in (later, here, earlier)]
    total = sum_over(jnp.concatenate(grads), "row")
    total = sum_over(total, "frame").astype(jnp.bfloat16)
    total = gather_parts(gather_parts(total, "frame"), "row").astype(jnp.float32)
    total = total.reshape((12, channels, channels))
    return (
        outgoing[None],
        total[:9].reshape((1, 3, 3, channels, channels)),
        total[9:][None],
    )


def solution(mesh):
    return jax.shard_map(
        section_run,
        mesh=mesh,
        in_specs=(
            P("section", "frame", "row", None, None),
            P("frame", "row", None, None),
            P("section", None, None, None, None),
            P("section", None, None, None),
        ),
        out_specs=(
            P("section", "frame", "row", None, None),
            P("section", None, None, None, None),
            P("section", None, None, None),
        ),
        check_vma=False,
    )
```

time: 262 us -> 112 us (0.43)
  waiting for transfers between devices: 116 us -> 57.2 us
  blocking collectives: 44.2 us -> 0 us
  between operations: 15.1 us -> 1.67 us
  starting transfers between devices: 38.2 us -> 25.2 us
  local copies, waits for them, and re-layouts: 17.5 us -> 5.28 us
  matrix products: 21.1 us -> 17.5 us
  other arithmetic: 8.21 us -> 4.61 us
    psum x1 -> x0, waiting for transfers between devices: 53.8 us -> none  [section_run(): lax.psum((grads_space, grads_time), ('frame', 'row'))]
    all_to_all x4 -> x0, blocking collectives: 44.2 us -> none  [the longest x2 22.4 us: section_run(): lax.all_to_all(to_blocks(incoming, frame_parts), 'frame', split_axis=1, c...]
    all_to_all x5 -> x1, waiting for transfers between devices: 28.8 us -> 7.37 us  [sum_over(): parts = lax.all_to_all(parts, axis, split_axis=0, concat_axis=0, tiled=True)]
    ppermute x13 -> x20, waiting for transfers between devices: 33.1 us -> 49.8 us  [the longest x9 42.1 us: fetch(): return lax.ppermute(block, ('section', 'frame'), route)]
    all_to_all x5 -> x1, starting transfers between devices: 20.1 us -> 9.6 us  [sum_over(): parts = lax.all_to_all(parts, axis, split_axis=0, concat_axis=0, tiled=True)]
    unnamed x52 -> x8, local copies, waits for them, and re-layouts: 11.2 us -> 2.07 us
    reshape x5 -> x0, local copies, waits for them, and re-layouts: 3.46 us -> none  [the longest x4 2.46 us: to_blocks(): values.reshape(frame_count, frame_parts, row_count * col_count // frame_p...]
    ppermute x13 -> x20, starting transfers between devices: 17.8 us -> 15.6 us  [the longest x9 8.73 us: fetch(): return lax.ppermute(block, ('section', 'frame'), route)]
  transfers between devices with their start and end apart: 19 -> 21, of which waited for: 12 -> 11; matrix products, arithmetic and copies ran while one was open for 7% -> 6% of each run, Pallas kernels for 0% -> 0%
where the time goes in v1:
time: 112 us; the launch traced here: 111 us
  waiting for transfers between devices  57.2 us (51%)
  starting transfers between devices  25.2 us (22%)
  matrix products  17.5 us (16%)
  local copies, waits for them, and re-layouts  5.28 us (5%)
  other arithmetic  4.61 us (4%)
  between operations  1.67 us (1%)
    ppermute x9, waiting for transfers between devices, fetch(): return lax.ppermute(block, ('section', 'frame'), route)  42.1 us
    dot_general x45, matrix products, apply_taps(): running = running + jnp.dot(window, tap, preferred_element_type=jnp.float32)  10.3 us
    all_to_all x1, starting transfers between devices, sum_over(): parts = lax.all_to_all(parts, axis, split_axis=0, concat_axis=0, tiled=True)  9.6 us
    ppermute x9, starting transfers between devices, fetch(): return lax.ppermute(block, ('section', 'frame'), route)  8.73 us
    all_to_all x1, waiting for transfers between devices, sum_over(): parts = lax.all_to_all(parts, axis, split_axis=0, concat_axis=0, tiled=True)  7.37 us
    ppermute x4, starting transfers between devices, gather_parts(): got = lax.ppermute(part, axis, [(i, i ^ mask) for i in range(count)])  4.52 us
    ppermute x4, waiting for transfers between devices, gather_parts(): got = lax.ppermute(part, axis, [(i, i ^ mask) for i in range(count)])  3.94 us
    ppermute x5, waiting for transfers between devices, row_halo(): lax.ppermute(jnp.where(index == 0, tail, head), 'row', [(0, 1), (1, 0)])  3.81 us
  transfers between devices with their start and end apart: 21, of which 11 were waited for; matrix products, arithmetic and copies ran while one was open for 6% of the time, Pallas kernels for 0%

profile of v1, /device:TPU:0, one launch (start us, length us, event | category | flops | bytes accessed | tf_op | source)
XLA Modules:
  0.0 111.5 jit_solution(835783000870484725)
XLA Ops:
  0.6 0.8 slice_select_fusion.4
  1.9 1.2 %fusion.63 = f32[1024,128]{1,0:T(8,128)S(1)} fusion(bf16[1024,128]{1,0:T(8,128)(2,1)} %bitcast.364, bf16[1,3,128,128]{3,2,1,0:T(8,128)(2,1)S(1)} %copy-done.3), kind=kOutput, calls=%fused_computation.181 | convolution fusion | flops 33554432 | bytes 819200 | tf_op jit(solution)/shard_map/dot_general | solution.py:151
  3.6 0.7 copy-done.1
  7.7 1.1 %collective-permute-done.1 = bf16[2,1,64,128]{3,2,1,0:T(8,128)(2,1)S(1)} collective-permute-done((bf16[2,1,64,128]{3,2,1,0:T(8,128)(2,1)S(1)}, bf16[2,1,64,128]{3,2,1,0:T(8,128)(2,1)S(1)}, u32[]{:S(2)}, u32[]{:S(2)}) %collective-permute-start.1) | collective-permute-done | bytes 32800 | tf_op jit(solution)/shard_map/ppermute | solution.py:27
  11.6 0.7 copy-done.2
  15.0 1.1 collective-permute-done.4
  22.2 1.0 collective-permute-done.8
  26.0 1.3 %collective-permute-start.10 = (bf16[1,8,64,128]{3,2,1,0:T(8,128)(2,1)S(1)}, bf16[1,8,64,128]{3,2,1,0:T(8,128)(2,1)S(1)}, u32[]{:S(2)}, u32[]{:S(2)}) collective-permute-start(bf16[1,8,64,128]{3,2,1,0:T(8,128)(2,1)S(1)} %get-tuple-element.35), channel_id=1, source_target_pairs={{8,0},{10,2},{12,4},{14,6},{9,1},{11,3},{13,5},{15,7}} | collective-permute-start | bytes 393224 | tf_op jit(solution)/shard_map/ppermute | solution.py:63
  27.3 1.3 %collective-permute-start.11 = (bf16[1,8,64,128]{3,2,1,0:T(8,128)(2,1)S(1)}, bf16[1,8,64,128]{3,2,1,0:T(8,128)(2,1)S(1)}, u32[]{:S(2)}, u32[]{:S(2)}) collective-permute-start(bf16[1,8,64,128]{3,2,1,0:T(8,128)(2,1)S(1)} %get-tuple-element.36), channel_id=1, source_target_pairs={{10,0},{12,2},{14,4},{11,1},{13,3},{15,5}} | collective-permute-start | bytes 393224 | tf_op jit(solution)/shard_map/ppermute | solution.py:63
  28.7 1.3 %collective-permute-start.9 = (bf16[2,8,64,128]{3,2,1,0:T(8,128)(2,1)S(1)}, bf16[2,8,64,128]{3,2,1,0:T(8,128)(2,1)S(1)}, u32[]{:S(2)}, u32[]{:S(2)}) collective-permute-start(bf16[2,8,64,128]{3,2,1,0:T(8,128)(2,1)S(1)} %fusion.29), channel_id=1, source_target_pairs={{8,0},{10,2},{12,4},{14,6},{9,1},{11,3},{13,5},{15,7}} | collective-permute-start | bytes 786440 | tf_op jit(solution)/shard_map/ppermute | solution.py:63
  30.6 1.5 %collective-permute-start.13 = (bf16[1,8,64,128]{3,2,1,0:T(8,128)(2,1)S(1)}, bf16[1,8,64,128]{3,2,1,0:T(8,128)(2,1)S(1)}, u32[]{:S(2)}, u32[]{:S(2)}) collective-permute-start(bf16[1,8,64,128]{3,2,1,0:T(8,128)(2,1)S(1)} %get-tuple-element.36), channel_id=1, source_target_pairs={{8,0},{10,2},{12,4},{14,6},{9,1},{11,3},{13,5},{15,7}} | collective-permute-start | bytes 393224 | tf_op jit(solution)/shard_map/ppermute | solution.py:63
  32.1 31.6 %collective-permute-done.10 = bf16[1,8,64,128]{3,2,1,0:T(8,128)(2,1)S(1)} collective-permute-done((bf16[1,8,64,128]{3,2,1,0:T(8,128)(2,1)S(1)}, bf16[1,8,64,128]{3,2,1,0:T(8,128)(2,1)S(1)}, u32[]{:S(2)}, u32[]{:S(2)}) %collective-permute-start.10) | collective-permute-done | bytes 131104 | tf_op jit(solution)/shard_map/ppermute | solution.py:63
  63.7 7.0 %collective-permute-done.11 = bf16[1,8,64,128]{3,2,1,0:T(8,128)(2,1)S(1)} collective-permute-done((bf16[1,8,64,128]{3,2,1,0:T(8,128)(2,1)S(1)}, bf16[1,8,64,128]{3,2,1,0:T(8,128)(2,1)S(1)}, u32[]{:S(2)}, u32[]{:S(2)}) %collective-permute-start.11) | collective-permute-done | bytes 131104 | tf_op jit(solution)/shard_map/ppermute | solution.py:63
  70.9 3.5 %collective-permute-done.13 = bf16[1,8,64,128]{3,2,1,0:T(8,128)(2,1)S(1)} collective-permute-done((bf16[1,8,64,128]{3,2,1,0:T(8,128)(2,1)S(1)}, bf16[1,8,64,128]{3,2,1,0:T(8,128)(2,1)S(1)}, u32[]{:S(2)}, u32[]{:S(2)}) %collective-permute-start.13) | collective-permute-done | bytes 131104 | tf_op jit(solution)/shard_map/ppermute | solution.py:63
  82.3 0.7 add_convert_fusion
  83.0 9.6 %all-to-all-start = ((bf16[4,192,128]{2,1,0:T(8,128)(2,1)}), bf16[4,192,128]{2,1,0:T(8,128)(2,1)S(1)}, u32[]{:S(2)}, u32[]{:S(2)}) async-start(bf16[4,192,128]{2,1,0:T(8,128)(2,1)} %bitcast.101), calls=%async_computation | async-start | bytes 393216 | tf_op jit(solution)/shard_map/all_to_all | solution.py:127
  93.1 7.4 %all-to-all-done = bf16[4,192,128]{2,1,0:T(8,128)(2,1)S(1)} async-done(((bf16[4,192,128]{2,1,0:T(8,128)(2,1)}), bf16[4,192,128]{2,1,0:T(8,128)(2,1)S(1)}, u32[]{:S(2)}, u32[]{:S(2)}) %all-to-all-start) | async-done | bytes 196640 | tf_op jit(solution)/shard_map/all_to_all | solution.py:127
  101.0 1.5 %collective-permute-start.17 = (bf16[192,128]{1,0:T(8,128)(2,1)S(1)}, bf16[192,128]{1,0:T(8,128)(2,1)S(1)}, u32[]{:S(2)}, u32[]{:S(2)}) collective-permute-start(bf16[192,128]{1,0:T(8,128)(2,1)S(1)} %reduce_sum.12), channel_id=1, source_target_pairs={{0,4},{2,6},{4,0},{6,2},{1,5},{3,7},{5,1},{7,3},{8,12},{10,14},{12... | collective-permute-start | bytes 147464 | tf_op jit(solution)/shard_map/ppermute | solution.py:110
  102.5 2.4 %collective-permute-start.18 = (bf16[192,128]{1,0:T(8,128)(2,1)S(1)}, bf16[192,128]{1,0:T(8,128)(2,1)S(1)}, u32[]{:S(2)}, u32[]{:S(2)}) collective-permute-start(bf16[192,128]{1,0:T(8,128)(2,1)S(1)} %reduce_sum.12), channel_id=1, source_target_pairs={{0,6},{2,4},{4,2},{6,0},{1,7},{3,5},{5,3},{7,1},{8,14},{10,12},{12... | collective-permute-start | bytes 147464 | tf_op jit(solution)/shard_map/ppermute | solution.py:110
  105.0 2.0 %collective-permute-done.17 = bf16[192,128]{1,0:T(8,128)(2,1)S(1)} collective-permute-done((bf16[192,128]{1,0:T(8,128)(2,1)S(1)}, bf16[192,128]{1,0:T(8,128)(2,1)S(1)}, u32[]{:S(2)}, u32[]{:S(2)}) %collective-permute-start.17) | collective-permute-done | bytes 49184 | tf_op jit(solution)/shard_map/ppermute | solution.py:110
  107.0 1.3 %collective-permute-done.18 = bf16[192,128]{1,0:T(8,128)(2,1)S(1)} collective-permute-done((bf16[192,128]{1,0:T(8,128)(2,1)S(1)}, bf16[192,128]{1,0:T(8,128)(2,1)S(1)}, u32[]{:S(2)}, u32[]{:S(2)}) %collective-permute-start.18) | collective-permute-done | bytes 49184 | tf_op jit(solution)/shard_map/ppermute | solution.py:110
  108.5 0.8 fusion.43
  109.9 0.9 slice.406
  110.8 0.7 slice.407
  (150 shorter events, 28.5 us)
Async XLA Ops:
  0.6 1.3 %copy-start.3 = (bf16[1,3,128,128]{3,2,1,0:T(8,128)(2,1)S(1)}, bf16[1,3,128,128]{3,2,1,0:T(8,128)(2,1)}, u32[]{:S(2)}) copy-start(bf16[1,3,128,128]{3,2,1,0:T(8,128)(2,1)} %param.7) | copy-start | bytes 294916
  1.5 2.1 %collective-permute-start = (bf16[2,1,64,128]{3,2,1,0:T(8,128)(2,1)S(1)}, bf16[2,1,64,128]{3,2,1,0:T(8,128)(2,1)S(1)}, u32[]{:S(2)}, u32[]{:S(2)}) collective-permute-start(bf16[2,1,64,128]{3,2,1,0:T(8,128)(2,1)S(1)} %slice_select_fusion.4), channel_id=1, source_target_pairs={{0,1},{1,0},{2,3},{3,2},{4,5},{5,4},{6,7},{7,6},{8,9},{9,8},{10,11... | collective-permute-start | bytes 98312 | tf_op jit(solution)/shard_map/ppermute | solution.py:27
  3.3 1.0 copy-start.1
  4.5 1.0 copy-start
  7.6 1.3 %collective-permute-start.1 = (bf16[2,1,64,128]{3,2,1,0:T(8,128)(2,1)S(1)}, bf16[2,1,64,128]{3,2,1,0:T(8,128)(2,1)S(1)}, u32[]{:S(2)}, u32[]{:S(2)}) collective-permute-start(bf16[2,1,64,128]{3,2,1,0:T(8,128)(2,1)S(1)} %slice_select_fusion.3), channel_id=1, source_target_pairs={{0,1},{1,0},{2,3},{3,2},{4,5},{5,4},{6,7},{7,6},{8,9},{9,8},{10,11... | collective-permute-start | bytes 98312 | tf_op jit(solution)/shard_map/ppermute | solution.py:27
  12.3 1.4 %collective-permute-start.3 = (bf16[2,8,64,128]{3,2,1,0:T(8,128)(2,1)S(1)}, bf16[2,8,64,128]{3,2,1,0:T(8,128)(2,1)S(1)}, u32[]{:S(2)}, u32[]{:S(2)}) collective-permute-start(bf16[2,8,64,128]{3,2,1,0:T(8,128)(2,1)S(1)} %fusion.31), channel_id=1, source_target_pairs={{28,16},{30,18},{24,20},{26,22},{29,17},{31,19},{25,21},{27,23}} | collective-permute-start | bytes 786440 | tf_op jit(solution)/shard_map/ppermute | solution.py:90
  13.0 1.2 %collective-permute-start.2 = (bf16[2,8,64,128]{3,2,1,0:T(8,128)(2,1)S(1)}, bf16[2,8,64,128]{3,2,1,0:T(8,128)(2,1)S(1)}, u32[]{:S(2)}, u32[]{:S(2)}) collective-permute-start(bf16[2,8,64,128]{3,2,1,0:T(8,128)(2,1)S(1)} %fusion.31), channel_id=1, source_target_pairs={{24,16},{26,18},{28,20},{30,22},{25,17},{27,19},{29,21},{31,23}} | collective-permute-start | bytes 786440 | tf_op jit(solution)/shard_map/ppermute | solution.py:63
  14.8 1.3 %collective-permute-start.4 = (bf16[2,1,64,128]{3,2,1,0:T(8,128)(2,1)S(1)}, bf16[2,1,64,128]{3,2,1,0:T(8,128)(2,1)S(1)}, u32[]{:S(2)}, u32[]{:S(2)}) collective-permute-start(bf16[2,1,64,128]{3,2,1,0:T(8,128)(2,1)S(1)} %slice_select_fusion.2), channel_id=1, source_target_pairs={{0,1},{1,0},{2,3},{3,2},{4,5},{5,4},{6,7},{7,6},{8,9},{9,8},{10,11... | collective-permute-start | bytes 98312 | tf_op jit(solution)/shard_map/ppermute | solution.py:27
  18.8 2.1 %collective-permute-start.6 = (bf16[2,8,64,128]{3,2,1,0:T(8,128)(2,1)S(1)}, bf16[2,8,64,128]{3,2,1,0:T(8,128)(2,1)S(1)}, u32[]{:S(2)}, u32[]{:S(2)}) collective-permute-start(bf16[2,8,64,128]{3,2,1,0:T(8,128)(2,1)S(1)} %fusion.30), channel_id=1, source_target_pairs={{18,8},{20,10},{22,12},{19,9},{21,11},{23,13}} | collective-permute-start | bytes 786440 | tf_op jit(solution)/shard_map/ppermute | solution.py:63
  19.5 1.9 %collective-permute-start.5 = (bf16[2,8,64,128]{3,2,1,0:T(8,128)(2,1)S(1)}, bf16[2,8,64,128]{3,2,1,0:T(8,128)(2,1)S(1)}, u32[]{:S(2)}, u32[]{:S(2)}) collective-permute-start(bf16[2,8,64,128]{3,2,1,0:T(8,128)(2,1)S(1)} %fusion.30), channel_id=1, source_target_pairs={{16,8},{18,10},{20,12},{22,14},{17,9},{19,11},{21,13},{23,15}} | collective-permute-start | bytes 786440 | tf_op jit(solution)/shard_map/ppermute | solution.py:63
  20.1 1.0 collective-permute-start.7
  21.9 1.3 %collective-permute-start.8 = (bf16[2,1,64,128]{3,2,1,0:T(8,128)(2,1)S(1)}, bf16[2,1,64,128]{3,2,1,0:T(8,128)(2,1)S(1)}, u32[]{:S(2)}, u32[]{:S(2)}) collective-permute-start(bf16[2,1,64,128]{3,2,1,0:T(8,128)(2,1)S(1)} %slice_select_fusion.1), channel_id=1, source_target_pairs={{0,1},{1,0},{2,3},{3,2},{4,5},{5,4},{6,7},{7,6},{8,9},{9,8},{10,11... | collective-permute-start | bytes 98312 | tf_op jit(solution)/shard_map/ppermute | solution.py:27
  26.0 37.6 %collective-permute-start.10 = (bf16[1,8,64,128]{3,2,1,0:T(8,128)(2,1)S(1)}, bf16[1,8,64,128]{3,2,1,0:T(8,128)(2,1)S(1)}, u32[]{:S(2)}, u32[]{:S(2)}) collective-permute-start(bf16[1,8,64,128]{3,2,1,0:T(8,128)(2,1)S(1)} %get-tuple-element.35), channel_id=1, source_target_pairs={{8,0},{10,2},{12,4},{14,6},{9,1},{11,3},{13,5},{15,7}} | collective-permute-start | bytes 393224 | tf_op jit(solution)/shard_map/ppermute | solution.py:63
  27.3 43.3 %collective-permute-start.11 = (bf16[1,8,64,128]{3,2,1,0:T(8,128)(2,1)S(1)}, bf16[1,8,64,128]{3,2,1,0:T(8,128)(2,1)S(1)}, u32[]{:S(2)}, u32[]{:S(2)}) collective-permute-start(bf16[1,8,64,128]{3,2,1,0:T(8,128)(2,1)S(1)} %get-tuple-element.36), channel_id=1, source_target_pairs={{10,0},{12,2},{14,4},{11,1},{13,3},{15,5}} | collective-permute-start | bytes 393224 | tf_op jit(solution)/shard_map/ppermute | solution.py:63
  28.7 46.1 %collective-permute-start.9 = (bf16[2,8,64,128]{3,2,1,0:T(8,128)(2,1)S(1)}, bf16[2,8,64,128]{3,2,1,0:T(8,128)(2,1)S(1)}, u32[]{:S(2)}, u32[]{:S(2)}) collective-permute-start(bf16[2,8,64,128]{3,2,1,0:T(8,128)(2,1)S(1)} %fusion.29), channel_id=1, source_target_pairs={{8,0},{10,2},{12,4},{14,6},{9,1},{11,3},{13,5},{15,7}} | collective-permute-start | bytes 786440 | tf_op jit(solution)/shard_map/ppermute | solution.py:63
  30.0 41.0 %collective-permute-start.12 = (bf16[1,8,64,128]{3,2,1,0:T(8,128)(2,1)S(1)}, bf16[1,8,64,128]{3,2,1,0:T(8,128)(2,1)S(1)}, u32[]{:S(2)}, u32[]{:S(2)}) collective-permute-start(bf16[1,8,64,128]{3,2,1,0:T(8,128)(2,1)S(1)} %get-tuple-element.35), channel_id=1, source_target_pairs={{8,2},{10,4},{12,6},{9,3},{11,5},{13,7}} | collective-permute-start | bytes 393224 | tf_op jit(solution)/shard_map/ppermute | solution.py:63
  30.6 43.8 %collective-permute-start.13 = (bf16[1,8,64,128]{3,2,1,0:T(8,128)(2,1)S(1)}, bf16[1,8,64,128]{3,2,1,0:T(8,128)(2,1)S(1)}, u32[]{:S(2)}, u32[]{:S(2)}) collective-permute-start(bf16[1,8,64,128]{3,2,1,0:T(8,128)(2,1)S(1)} %get-tuple-element.36), channel_id=1, source_target_pairs={{8,0},{10,2},{12,4},{14,6},{9,1},{11,3},{13,5},{15,7}} | collective-permute-start | bytes 393224 | tf_op jit(solution)/shard_map/ppermute | solution.py:63
  78.9 1.3 %collective-permute-start.14 = (bf16[2,1,64,128]{3,2,1,0:T(8,128)(2,1)S(1)}, bf16[2,1,64,128]{3,2,1,0:T(8,128)(2,1)S(1)}, u32[]{:S(2)}, u32[]{:S(2)}) collective-permute-start(bf16[2,1,64,128]{3,2,1,0:T(8,128)(2,1)S(1)} %slice_select_fusion), channel_id=1, source_target_pairs={{0,1},{1,0},{2,3},{3,2},{4,5},{5,4},{6,7},{7,6},{8,9},{9,8},{10,11... | collective-permute-start | bytes 98312 | tf_op jit(solution)/shard_map/ppermute | solution.py:27
  79.0 3.2 %collective-permute-start.15 = (bf16[768,128]{1,0:T(8,128)(2,1)S(1)}, bf16[768,128]{1,0:T(8,128)(2,1)S(1)}, u32[]{:S(2)}, u32[]{:S(2)}) collective-permute-start(bf16[768,128]{1,0:T(8,128)(2,1)S(1)} %dynamic-slice_convert_fusion), channel_id=1, source_target_pairs={{0,1},{1,0},{2,3},{3,2},{4,5},{5,4},{6,7},{7,6},{8,9},{9,8},{10,11... | collective-permute-start | bytes 589832 | tf_op jit(solution)/shard_map/ppermute | solution.py:124
  83.0 17.4 %all-to-all-start = ((bf16[4,192,128]{2,1,0:T(8,128)(2,1)}), bf16[4,192,128]{2,1,0:T(8,128)(2,1)S(1)}, u32[]{:S(2)}, u32[]{:S(2)}) async-start(bf16[4,192,128]{2,1,0:T(8,128)(2,1)} %bitcast.101), calls=%async_computation | async-start | bytes 393216 | tf_op jit(solution)/shard_map/all_to_all | solution.py:127
  100.5 4.5 %collective-permute-start.16 = (bf16[192,128]{1,0:T(8,128)(2,1)S(1)}, bf16[192,128]{1,0:T(8,128)(2,1)S(1)}, u32[]{:S(2)}, u32[]{:S(2)}) collective-permute-start(bf16[192,128]{1,0:T(8,128)(2,1)S(1)} %reduce_sum.12), channel_id=1, source_target_pairs={{0,2},{2,0},{4,6},{6,4},{1,3},{3,1},{5,7},{7,5},{8,10},{10,8},{12,... | collective-permute-start | bytes 147464 | tf_op jit(solution)/shard_map/ppermute | solution.py:110
  101.0 6.0 %collective-permute-start.17 = (bf16[192,128]{1,0:T(8,128)(2,1)S(1)}, bf16[192,128]{1,0:T(8,128)(2,1)S(1)}, u32[]{:S(2)}, u32[]{:S(2)}) collective-permute-start(bf16[192,128]{1,0:T(8,128)(2,1)S(1)} %reduce_sum.12), channel_id=1, source_target_pairs={{0,4},{2,6},{4,0},{6,2},{1,5},{3,7},{5,1},{7,3},{8,12},{10,14},{12... | collective-permute-start | bytes 147464 | tf_op jit(solution)/shard_map/ppermute | solution.py:110
  102.5 5.9 %collective-permute-start.18 = (bf16[192,128]{1,0:T(8,128)(2,1)S(1)}, bf16[192,128]{1,0:T(8,128)(2,1)S(1)}, u32[]{:S(2)}, u32[]{:S(2)}) collective-permute-start(bf16[192,128]{1,0:T(8,128)(2,1)S(1)} %reduce_sum.12), channel_id=1, source_target_pairs={{0,6},{2,4},{4,2},{6,0},{1,7},{3,5},{5,3},{7,1},{8,14},{10,12},{12... | collective-permute-start | bytes 147464 | tf_op jit(solution)/shard_map/ppermute | solution.py:110
  108.4 1.5 %collective-permute-start.19 = (bf16[768,128]{1,0:T(8,128)(2,1)S(1)}, bf16[768,128]{1,0:T(8,128)(2,1)S(1)}, u32[]{:S(2)}, u32[]{:S(2)}) collective-permute-start(bf16[768,128]{1,0:T(8,128)(2,1)S(1)} %constant_dynamic-update-slice_fusion.2), channel_id=1, source_target_pairs={{0,1},{1,0},{2,3},{3,2},{4,5},{5,4},{6,7},{7,6},{8,9},{9,8},{10,11... | collective-permute-start | bytes 589832 | tf_op jit(solution)/shard_map/ppermute | solution.py:110
  (1 other events, 1.0 us)

commit v2 on v1

v2 whole, which is shorter than its diff:
```python
import jax
import jax.numpy as jnp
from jax import lax
from jax.sharding import PartitionSpec as P


def slope_of(pre_act):
    sigma = jax.nn.sigmoid(pre_act)
    return sigma * (1.0 + pre_act * (1.0 - sigma))


def inner_sum(first_arg, second_arg):
    return lax.dot_general(
        first_arg, second_arg, (((0,), (0,)), ((), ())), preferred_element_type=jnp.float32
    )


def row_halo(cells):
    count = lax.axis_size("row")
    index = lax.axis_index("row")
    head = cells[:, :1]
    tail = cells[:, -1:]
    nothing = jnp.zeros_like(head)
    if count == 1:
        above, below = nothing, nothing
    elif count == 2:
        got = lax.ppermute(jnp.where(index == 0, tail, head), "row", [(0, 1), (1, 0)])
        above = jnp.where(index == 0, nothing, got)
        below = jnp.where(index == 0, got, nothing)
    else:
        above = lax.ppermute(tail, "row", [(i, i + 1) for i in range(count - 1)])
        below = lax.ppermute(head, "row", [(i + 1, i) for i in range(count - 1)])
    return jnp.concatenate([above, cells, below], axis=1)


def pad_cols(values):
    return jnp.pad(values, ((0, 0), (0, 0), (1, 1), (0, 0)))


def apply_taps(padded, taps, row_count, col_count, transpose):
    channels = padded.shape[-1]
    running = jnp.zeros((padded.shape[0] * row_count * col_count, taps.shape[-1]), jnp.float32)
    for i in range(3):
        for j in range(3):
            window = padded[:, i : i + row_count, j : j + col_count, :].reshape(-1, channels)
            if transpose:
                tap = taps[2 - i, 2 - j].T
            else:
                tap = taps[i, j]
            running = running + jnp.dot(window, tap, preferred_element_type=jnp.float32)
    return running.reshape(padded.shape[0], row_count, col_count, taps.shape[-1])


def fetch(block, source, target, frame_step):
    frame_parts = lax.axis_size("frame")
    route = [
        (source * frame_parts + z + frame_step, target * frame_parts + z)
        for z in range(frame_parts)
        if 0 <= z + frame_step < frame_parts
    ]
    if not route:
        return jnp.zeros_like(block)
    if source == target and frame_step == 0:
        return block
    return lax.ppermute(block, ("section", "frame"), route)


def shifted_from(block, source, target, offset, unmoved=None):
    own_frames = block.shape[0]
    step, rest = divmod(offset, own_frames)
    pieces = []
    for frames, move in ((slice(rest, None), step), (slice(0, rest), step + 1)):
        piece = block[frames]
        if piece.shape[0] == 0:
            continue
        if move == 0 and unmoved is not None:
            pieces.append(unmoved[frames])
        else:
            pieces.append(fetch(piece, source, target, move))
    return pieces[0] if len(pieces) == 1 else jnp.concatenate(pieces)


def triple_from(block, source, target, distance, staged):
    own_frames = block.shape[0]
    frame_parts = lax.axis_size("frame")
    step, rest = divmod(distance, own_frames)
    nothing = jnp.zeros_like(block)
    own = fetch(block, source, target, 0)
    if step >= frame_parts:
        return own, nothing, nothing
    if rest == 0 and 2 * step >= frame_parts:
        route = [
            (source * frame_parts + z + move, target * frame_parts + z)
            for z in range(frame_parts)
            for move in (step, -step)
            if 0 <= z + move < frame_parts
        ]
        got = lax.ppermute(block, ("section", "frame"), route)
        early = lax.axis_index("frame") < frame_parts - step
        return own, jnp.where(early, got, nothing), jnp.where(early, nothing, got)
    if staged:
        block, source = own, target
    return (
        own,
        shifted_from(block, source, target, distance, own),
        shifted_from(block, source, target, -distance, own),
    )


def exchange_parts(parts, axis):
    count = lax.axis_size(axis)
    index = lax.axis_index(axis)
    size = parts.shape[0] // count

    def part(at):
        return lax.dynamic_slice_in_dim(parts, at * size, size, 0)

    return [part(index)] + [
        lax.ppermute(part(index ^ mask).astype(jnp.bfloat16), axis, [(i, i ^ mask) for i in range(count)])
        for mask in range(1, count)
    ]


def by_pairs(axis):
    count = lax.axis_size(axis)
    return count <= 4 and count & (count - 1) == 0


def sum_over(values, axis):
    count = lax.axis_size(axis)
    if by_pairs(axis):
        return sum(part.astype(jnp.float32) for part in exchange_parts(values, axis))
    parts = values.astype(jnp.bfloat16).reshape((count, -1) + values.shape[1:])
    parts = lax.all_to_all(parts, axis, split_axis=0, concat_axis=0, tiled=True)
    return jnp.sum(parts.astype(jnp.float32), axis=0)


def gather_parts(part, axis):
    if not by_pairs(axis):
        return lax.all_gather(part, axis, axis=0, tiled=True)
    count = lax.axis_size(axis)
    index = lax.axis_index(axis)
    size = part.shape[0]
    whole = jnp.zeros((count * size,) + part.shape[1:], part.dtype)
    whole = lax.dynamic_update_slice_in_dim(whole, part, index * size, 0)
    for mask in range(1, count):
        got = lax.ppermute(part, axis, [(i, i ^ mask) for i in range(count)])
        whole = lax.dynamic_update_slice_in_dim(whole, got, (index ^ mask) * size, 0)
    return whole


def after(value, other):
    return lax.optimization_barrier((value, other))[0]


def section_run(x_saved, cotangent, w_spatial, w_temporal):
    block_input = x_saved[0]
    taps_space = w_spatial[0]
    taps_time = w_temporal[0]
    local_shape = block_input.shape
    own_frames, row_count, col_count, channels = local_shape
    section_count = lax.axis_size("section")
    section_index = lax.axis_index("section")
    extended = pad_cols(row_halo(block_input))
    pre_act = apply_taps(extended, taps_space, row_count, col_count, False)
    pre_slope = slope_of(pre_act)
    active = jax.nn.silu(pre_act).astype(jnp.bfloat16)

    top = section_count - 1
    chains = 2 if own_frames % 2 == 0 else 1

    def chain_of(values):
        if chains == 1:
            return [values]
        return [
            values.reshape((own_frames // 2, 2) + values.shape[1:])[:, odd] for odd in range(2)
        ]

    def both(parts):
        return parts[0] if chains == 1 else jnp.stack(parts, 1).reshape(local_shape)

    def back_pre(here, later, earlier, slope):
        running = sum(
            jnp.dot(block.reshape(-1, channels), taps_time[k].T, preferred_element_type=jnp.float32)
            for block, k in ((here, 1), (later, 0), (earlier, 2))
        )
        back_act = running.astype(jnp.bfloat16).reshape(here.shape)
        return (back_act.astype(jnp.float32) * slope).astype(jnp.bfloat16)

    def branch_out(grad_pre, here):
        padded = pad_cols(row_halo(grad_pre))
        branch = apply_taps(padded, taps_space, row_count, col_count, True).astype(jnp.bfloat16)
        return (here.astype(jnp.float32) + branch.astype(jnp.float32)).astype(jnp.bfloat16)

    def triples(blocks, source, target):
        dilation = 2**target
        if chains == 1:
            return [triple_from(blocks[0], source, target, dilation, False)]
        if dilation % 2 == 0:
            return [
                triple_from(block, source, target, dilation // 2, True) for block in blocks
            ]
        even, odd = blocks
        own_even = fetch(even, source, target, 0)
        next_even = shifted_from(even, source, target, (dilation + 1) // 2, own_even)
        own_odd = fetch(odd, source, target, 0)
        last_odd = shifted_from(odd, source, target, -((dilation + 1) // 2), own_odd)
        same_odd = shifted_from(odd, source, target, (dilation - 1) // 2, own_odd)
        same_even = shifted_from(even, source, target, -((dilation - 1) // 2), own_even)
        return [(own_even, same_odd, last_odd), (own_odd, next_even, same_even)]

    slopes = chain_of(pre_slope)
    held = triples(chain_of(cotangent), top, top)
    for position in range(top):
        owner = top - position
        outgoing = []
        for chain in range(chains):
            here, later, earlier = held[chain]
            if chain or position:
                last = outgoing[-1] if chain else sent[-1]
                here, later, earlier, _ = lax.optimization_barrier((here, later, earlier, last))
            grad_pre = back_pre(here, later, earlier, slopes[chain])
            outgoing.append(branch_out(grad_pre, here))
        sent = outgoing
        arrives = section_index == owner - 1
        held = [
            tuple(jnp.where(arrives, new, old) for new, old in zip(fresh, kept))
            for fresh, kept in zip(triples(outgoing, owner, owner - 1), held)
        ]

    here, later, earlier = (both([blocks[k] for blocks in held]) for k in range(3))
    grad_pre = back_pre(here, later, earlier, pre_slope)
    flat_pre = grad_pre.reshape(-1, channels)
    flat_active = active.reshape(-1, channels)
    grads = [
        inner_sum(
            extended[:, i : i + row_count, j : j + col_count, :].reshape(-1, channels), flat_pre
        )
        for i in range(3)
        for j in range(3)
    ]
    grads += [inner_sum(flat_active, g.reshape(-1, channels)) for g in (later, here, earlier)]
    total = sum_over(jnp.concatenate(grads), "row")
    outgoing = branch_out(after(grad_pre, total), here)
    total = sum_over(total, "frame").astype(jnp.bfloat16)
    total = gather_parts(total, "frame")
    split = 9 * channels
    if lax.axis_size("row") == 2:
        first = lax.axis_index("row") == 0
        other = lax.ppermute(total, "row", [(0, 1), (1, 0)])
        rest = split - total.shape[0]
        space = jnp.where(
            first,
            jnp.concatenate([total, other[:rest]]),
            jnp.concatenate([other, total[:rest]]),
        )
        time = jnp.where(first, other[rest:], total[rest:])
    else:
        total = gather_parts(total, "row")
        space, time = total[:split], total[split:]
    return (
        outgoing[None],
        space.astype(jnp.float32).reshape((1, 3, 3, channels, channels)),
        time.astype(jnp.float32).reshape((1, 3, channels, channels)),
    )


def solution(mesh):
    return jax.shard_map(
        section_run,
        mesh=mesh,
        in_specs=(
            P("section", "frame", "row", None, None),
            P("frame", "row", None, None),
            P("section", None, None, None, None),
            P("section", None, None, None),
        ),
        out_specs=(
            P("section", "frame", "row", None, None),
            P("section", None, None, None, None),
            P("section", None, None, None),
        ),
        check_vma=False,
    )
```

time: 112 us -> 121 us (1.080)
  waiting for transfers between devices: 57.2 us -> 49.8 us
  other arithmetic: 4.61 us -> 10.4 us
  matrix products: 17.5 us -> 22.3 us
  local copies, waits for them, and re-layouts: 5.28 us -> 9.58 us
    all_to_all x1 -> x0, starting transfers between devices: 9.6 us -> none  [sum_over(): parts = lax.all_to_all(parts, axis, split_axis=0, concat_axis=0, tiled=True)]
    ppermute x2 -> x7, starting transfers between devices: 1.23 us -> 8.83 us  [the longest x4 7.43 us: exchange_parts(): lax.ppermute(part(index ^ mask).astype(jnp.bfloat16), axis, [(i, i ^ mask...]
    all_to_all x1 -> x0, waiting for transfers between devices: 7.37 us -> none  [sum_over(): parts = lax.all_to_all(parts, axis, split_axis=0, concat_axis=0, tiled=True)]
    unnamed x8 -> x24, local copies, waits for them, and re-layouts: 2.07 us -> 6.97 us
    ppermute x9 -> x12, waiting for transfers between devices: 42.1 us -> 37.7 us  [fetch(): return lax.ppermute(block, ('section', 'frame'), route)]
    ppermute x2 -> x7, waiting for transfers between devices: 0.01 us -> 4.25 us  [the longest x4 3.6 us: exchange_parts(): lax.ppermute(part(index ^ mask).astype(jnp.bfloat16), axis, [(i, i ^ mask...]
    dot_general x45 -> x72, matrix products: 10.3 us -> 14.1 us  [apply_taps(): running = running + jnp.dot(window, tap, preferred_element_type=jnp.float32)]
    ppermute x9 -> x12, starting transfers between devices: 8.73 us -> 10.7 us  [fetch(): return lax.ppermute(block, ('section', 'frame'), route)]
  transfers between devices with their start and end apart: 21 -> 30, of which waited for: 11 -> 13; matrix products, arithmetic and copies ran while one was open for 6% -> 12% of each run, Pallas kernels for 0% -> 0%
where the time goes in v2:
time: 121 us
  waiting for transfers between devices  49.8 us (41%)
  starting transfers between devices  26.2 us (22%)
  matrix products  22.3 us (18%)
  other arithmetic  10.4 us (9%)
  local copies, waits for them, and re-layouts  9.58 us (8%)
  between operations  2.15 us (2%)
    ppermute x12, waiting for transfers between devices, fetch(): return lax.ppermute(block, ('section', 'frame'), route)  37.7 us
    dot_general x72, matrix products, apply_taps(): running = running + jnp.dot(window, tap, preferred_element_type=jnp.float32)  14.1 us
    ppermute x12, starting transfers between devices, fetch(): return lax.ppermute(block, ('section', 'frame'), route)  10.7 us
    ppermute x4, starting transfers between devices, exchange_parts(): lax.ppermute(part(index ^ mask).astype(jnp.bfloat16), axis, [(i, i ^ mask...  7.43 us
    unnamed x24, local copies, waits for them, and re-layouts  6.97 us
    dot_general x21, matrix products, back_pre(): jnp.dot(block.reshape(-1, channels), taps_time[k].T, preferred_element_ty...  4.79 us
    ppermute x3, starting transfers between devices, gather_parts(): got = lax.ppermute(part, axis, [(i, i ^ mask) for i in range(count)])  4.52 us
    ppermute x3, waiting for transfers between devices, gather_parts(): got = lax.ppermute(part, axis, [(i, i ^ mask) for i in range(count)])  4.21 us
  transfers between devices with their start and end apart: 30, of which 13 were waited for; matrix products, arithmetic and copies ran while one was open for 12% of the time, Pallas kernels for 0%

profile of v2, /device:TPU:0, one launch (start us, length us, event | category | flops | bytes accessed | tf_op | source)
XLA Modules:
  0.0 120.5 jit_solution(6751925548676832435)
XLA Ops:
  1.9 1.0 fusion.131
  7.8 1.1 collective-permute-done.1
  28.7 1.3 %collective-permute-start.14 = (bf16[1,8,64,128]{3,2,1,0:T(8,128)(2,1)}, bf16[1,8,64,128]{3,2,1,0:T(8,128)(2,1)}, u32[]{:S(2)}, u32[]{:S(2)}) collective-permute-start(bf16[1,8,64,128]{3,2,1,0:T(8,128)(2,1)} %fusion.42), channel_id=1, source_target_pairs={{16,8},{18,10},{20,12},{22,14},{17,9},{19,11},{21,13},{23,15}} | collective-permute-start | bytes 393224 | tf_op jit(solution)/shard_map/ppermute | solution.py:65
  38.1 1.3 %collective-permute-start.13 = (bf16[1,8,64,128]{3,2,1,0:T(8,128)(2,1)S(1)}, bf16[1,8,64,128]{3,2,1,0:T(8,128)(2,1)S(1)}, u32[]{:S(2)}, u32[]{:S(2)}) collective-permute-start(bf16[1,8,64,128]{3,2,1,0:T(8,128)(2,1)S(1)} %fusion.41), channel_id=1, source_target_pairs={{8,0},{10,2},{12,4},{14,6},{9,1},{11,3},{13,5},{15,7}} | collective-permute-start | bytes 393224 | tf_op jit(solution)/shard_map/ppermute | solution.py:65
  39.4 1.3 %collective-permute-start.19 = (bf16[1,8,64,128]{3,2,1,0:T(8,128)(2,1)S(1)}, bf16[1,8,64,128]{3,2,1,0:T(8,128)(2,1)S(1)}, u32[]{:S(2)}, u32[]{:S(2)}) collective-permute-start(bf16[1,8,64,128]{3,2,1,0:T(8,128)(2,1)S(1)} %fusion.41), channel_id=1, source_target_pairs={{10,0},{12,2},{14,4},{11,1},{13,3},{15,5}} | collective-permute-start | bytes 393224 | tf_op jit(solution)/shard_map/ppermute | solution.py:65
  40.8 29.0 %collective-permute-done.13 = bf16[1,8,64,128]{3,2,1,0:T(8,128)(2,1)S(1)} collective-permute-done((bf16[1,8,64,128]{3,2,1,0:T(8,128)(2,1)S(1)}, bf16[1,8,64,128]{3,2,1,0:T(8,128)(2,1)S(1)}, u32[]{:S(2)}, u32[]{:S(2)}) %collective-permute-start.13) | collective-permute-done | bytes 131104 | tf_op jit(solution)/shard_map/ppermute | solution.py:65
  70.5 3.3 %collective-permute-done.19 = bf16[1,8,64,128]{3,2,1,0:T(8,128)(2,1)S(1)} collective-permute-done((bf16[1,8,64,128]{3,2,1,0:T(8,128)(2,1)S(1)}, bf16[1,8,64,128]{3,2,1,0:T(8,128)(2,1)S(1)}, u32[]{:S(2)}, u32[]{:S(2)}) %collective-permute-start.19) | collective-permute-done | bytes 131104 | tf_op jit(solution)/shard_map/ppermute | solution.py:65
  75.2 1.2 collective-permute-done.17
  78.5 1.3 %collective-permute-start.18 = (bf16[1,8,64,128]{3,2,1,0:T(8,128)(2,1)S(1)}, bf16[1,8,64,128]{3,2,1,0:T(8,128)(2,1)S(1)}, u32[]{:S(2)}, u32[]{:S(2)}) collective-permute-start(bf16[1,8,64,128]{3,2,1,0:T(8,128)(2,1)S(1)} %fusion.40), channel_id=1, source_target_pairs={{8,0},{10,2},{12,4},{14,6},{9,1},{11,3},{13,5},{15,7}} | collective-permute-start | bytes 393224 | tf_op jit(solution)/shard_map/ppermute | solution.py:65
  80.6 5.3 %collective-permute-done.18 = bf16[1,8,64,128]{3,2,1,0:T(8,128)(2,1)S(1)} collective-permute-done((bf16[1,8,64,128]{3,2,1,0:T(8,128)(2,1)S(1)}, bf16[1,8,64,128]{3,2,1,0:T(8,128)(2,1)S(1)}, u32[]{:S(2)}, u32[]{:S(2)}) %collective-permute-start.18) | collective-permute-done | bytes 131104 | tf_op jit(solution)/shard_map/ppermute | solution.py:65
  86.0 0.9 copy-done.8
  92.7 0.9 copy-done.9
  93.7 1.4 %collective-permute-done.21 = bf16[768,128]{1,0:T(8,128)(2,1)S(1)} collective-permute-done((bf16[768,128]{1,0:T(8,128)(2,1)S(1)}, bf16[768,128]{1,0:T(8,128)(2,1)S(1)}, u32[]{:S(2)}, u32[]{:S(2)}) %collective-permute-start.21) | collective-permute-done | bytes 196640 | tf_op jit(solution)/shard_map/ppermute | solution.py:119
  95.1 1.0 convert_add_fusion.1
  96.4 4.6 %collective-permute-start.23 = (bf16[192,128]{1,0:T(8,128)(2,1)S(1)}, bf16[192,128]{1,0:T(8,128)(2,1)S(1)}, u32[]{:S(2)}, u32[]{:S(2)}) collective-permute-start(bf16[192,128]{1,0:T(8,128)(2,1)S(1)} %get-tuple-element.43), channel_id=1, source_target_pairs={{0,2},{2,0},{4,6},{6,4},{1,3},{3,1},{5,7},{7,5},{8,10},{10,8},{12,... | collective-permute-start | bytes 147464 | tf_op jit(solution)/shard_map/ppermute | solution.py:119
  101.0 1.3 %collective-permute-start.24 = (bf16[192,128]{1,0:T(8,128)(2,1)S(1)}, bf16[192,128]{1,0:T(8,128)(2,1)S(1)}, u32[]{:S(2)}, u32[]{:S(2)}) collective-permute-start(bf16[192,128]{1,0:T(8,128)(2,1)S(1)} %get-tuple-element.45), channel_id=1, source_target_pairs={{0,4},{2,6},{4,0},{6,2},{1,5},{3,7},{5,1},{7,3},{8,12},{10,14},{12... | collective-permute-start | bytes 147464 | tf_op jit(solution)/shard_map/ppermute | solution.py:119
  102.3 1.4 %collective-permute-start.25 = (bf16[192,128]{1,0:T(8,128)(2,1)S(1)}, bf16[192,128]{1,0:T(8,128)(2,1)S(1)}, u32[]{:S(2)}, u32[]{:S(2)}) collective-permute-start(bf16[192,128]{1,0:T(8,128)(2,1)S(1)} %get-tuple-element.44), channel_id=1, source_target_pairs={{0,6},{2,4},{4,2},{6,0},{1,7},{3,5},{5,3},{7,1},{8,14},{10,12},{12... | collective-permute-start | bytes 147464 | tf_op jit(solution)/shard_map/ppermute | solution.py:119
  106.1 1.5 %collective-permute-done.24 = bf16[192,128]{1,0:T(8,128)(2,1)S(1)} collective-permute-done((bf16[192,128]{1,0:T(8,128)(2,1)S(1)}, bf16[192,128]{1,0:T(8,128)(2,1)S(1)}, u32[]{:S(2)}, u32[]{:S(2)}) %collective-permute-start.24) | collective-permute-done | bytes 49184 | tf_op jit(solution)/shard_map/ppermute | solution.py:119
  108.3 1.3 %collective-permute-start.26 = (bf16[192,128]{1,0:T(8,128)(2,1)S(1)}, bf16[192,128]{1,0:T(8,128)(2,1)S(1)}, u32[]{:S(2)}, u32[]{:S(2)}) collective-permute-start(bf16[192,128]{1,0:T(8,128)(2,1)S(1)} %get-tuple-element.36), channel_id=1, source_target_pairs={{0,2},{2,0},{4,6},{6,4},{1,3},{3,1},{5,7},{7,5},{8,10},{10,8},{12,... | collective-permute-start | bytes 147464 | tf_op jit(solution)/shard_map/ppermute | solution.py:147
  109.9 1.4 %collective-permute-start.27 = (bf16[192,128]{1,0:T(8,128)(2,1)S(1)}, bf16[192,128]{1,0:T(8,128)(2,1)S(1)}, u32[]{:S(2)}, u32[]{:S(2)}) collective-permute-start(bf16[192,128]{1,0:T(8,128)(2,1)S(1)} %get-tuple-element.36), channel_id=1, source_target_pairs={{0,4},{2,6},{4,0},{6,2},{1,5},{3,7},{5,1},{7,3},{8,12},{10,14},{12... | collective-permute-start | bytes 147464 | tf_op jit(solution)/shard_map/ppermute | solution.py:147
  111.3 1.8 %collective-permute-start.28 = (bf16[192,128]{1,0:T(8,128)(2,1)S(1)}, bf16[192,128]{1,0:T(8,128)(2,1)S(1)}, u32[]{:S(2)}, u32[]{:S(2)}) collective-permute-start(bf16[192,128]{1,0:T(8,128)(2,1)S(1)} %get-tuple-element.36), channel_id=1, source_target_pairs={{0,6},{2,4},{4,2},{6,0},{1,7},{3,5},{5,3},{7,1},{8,14},{10,12},{12... | collective-permute-start | bytes 147464 | tf_op jit(solution)/shard_map/ppermute | solution.py:147
  113.1 3.3 %collective-permute-done.27 = bf16[192,128]{1,0:T(8,128)(2,1)S(1)} collective-permute-done((bf16[192,128]{1,0:T(8,128)(2,1)S(1)}, bf16[192,128]{1,0:T(8,128)(2,1)S(1)}, u32[]{:S(2)}, u32[]{:S(2)}) %collective-permute-start.27) | collective-permute-done | bytes 49184 | tf_op jit(solution)/shard_map/ppermute | solution.py:147
  116.5 0.9 collective-permute-done.28
  119.0 0.9 convert.23
  (248 shorter events, 49.5 us)
Async XLA Ops:
  1.4 1.9 %collective-permute-start = (bf16[2,1,64,128]{3,2,1,0:T(8,128)(2,1)S(1)}, bf16[2,1,64,128]{3,2,1,0:T(8,128)(2,1)S(1)}, u32[]{:S(2)}, u32[]{:S(2)}) collective-permute-start(bf16[2,1,64,128]{3,2,1,0:T(8,128)(2,1)S(1)} %slice_select_fusion.1), channel_id=1, source_target_pairs={{0,1},{1,0},{2,3},{3,2},{4,5},{5,4},{6,7},{7,6},{8,9},{9,8},{10,11... | collective-permute-start | bytes 98312 | tf_op jit(solution)/shard_map/ppermute | solution.py:27
  12.4 1.6 %collective-permute-start.4 = (bf16[1,1,64,128]{3,2,1,0:T(8,128)(2,1)S(1)}, bf16[1,1,64,128]{3,2,1,0:T(8,128)(2,1)S(1)}, u32[]{:S(2)}, u32[]{:S(2)}) collective-permute-start(bf16[1,1,64,128]{3,2,1,0:T(8,128)(2,1)S(1)} %slice_select_fusion.7), channel_id=1, source_target_pairs={{0,1},{1,0},{2,3},{3,2},{4,5},{5,4},{6,7},{7,6},{8,9},{9,8},{10,11... | collective-permute-start | bytes 49160 | tf_op jit(solution)/shard_map/ppermute | solution.py:27
  12.6 4.8 %collective-permute-start.2 = (bf16[1,8,64,128]{3,2,1,0:T(8,128)(2,1)S(1)}, bf16[1,8,64,128]{3,2,1,0:T(8,128)(2,1)S(1)}, u32[]{:S(2)}, u32[]{:S(2)}) collective-permute-start(bf16[1,8,64,128]{3,2,1,0:T(8,128)(2,1)S(1)} %fusion.45), channel_id=1, source_target_pairs={{24,16},{26,18},{28,20},{30,22},{25,17},{27,19},{29,21},{31,23}} | collective-permute-start | bytes 393224 | tf_op jit(solution)/shard_map/ppermute | solution.py:65
  13.3 4.1 %collective-permute-start.3 = (bf16[1,8,64,128]{3,2,1,0:T(8,128)(2,1)S(1)}, bf16[1,8,64,128]{3,2,1,0:T(8,128)(2,1)S(1)}, u32[]{:S(2)}, u32[]{:S(2)}) collective-permute-start(bf16[1,8,64,128]{3,2,1,0:T(8,128)(2,1)S(1)} %fusion.45), channel_id=1, source_target_pairs={{28,16},{30,18},{24,20},{26,22},{29,17},{31,19},{25,21},{27,23}} | collective-permute-start | bytes 393224 | tf_op jit(solution)/shard_map/ppermute | solution.py:98
  16.7 2.2 %collective-permute-start.10 = (bf16[1,8,64,128]{3,2,1,0:T(8,128)(2,1)S(1)}, bf16[1,8,64,128]{3,2,1,0:T(8,128)(2,1)S(1)}, u32[]{:S(2)}, u32[]{:S(2)}) collective-permute-start(bf16[1,8,64,128]{3,2,1,0:T(8,128)(2,1)S(1)} %fusion.44), channel_id=1, source_target_pairs={{28,16},{30,18},{24,20},{26,22},{29,17},{31,19},{25,21},{27,23}} | collective-permute-start | bytes 393224 | tf_op jit(solution)/shard_map/ppermute | solution.py:98
  23.7 1.5 %collective-permute-start.11 = (bf16[1,1,64,128]{3,2,1,0:T(8,128)(2,1)}, bf16[1,1,64,128]{3,2,1,0:T(8,128)(2,1)}, u32[]{:S(2)}, u32[]{:S(2)}) collective-permute-start(bf16[1,1,64,128]{3,2,1,0:T(8,128)(2,1)} %slice_select_fusion.5), channel_id=1, source_target_pairs={{0,1},{1,0},{2,3},{3,2},{4,5},{5,4},{6,7},{7,6},{8,9},{9,8},{10,11... | collective-permute-start | bytes 49160 | tf_op jit(solution)/shard_map/ppermute | solution.py:27
  24.1 5.9 %collective-permute-start.6 = (bf16[1,8,64,128]{3,2,1,0:T(8,128)(2,1)}, bf16[1,8,64,128]{3,2,1,0:T(8,128)(2,1)S(1)}, u32[]{:S(2)}, u32[]{:S(2)}) collective-permute-start(bf16[1,8,64,128]{3,2,1,0:T(8,128)(2,1)} %fusion.43), channel_id=1, source_target_pairs={{16,8},{18,10},{20,12},{22,14},{17,9},{19,11},{21,13},{23,15}} | collective-permute-start | bytes 393224 | tf_op jit(solution)/shard_map/ppermute | solution.py:65
  28.7 5.3 %collective-permute-start.14 = (bf16[1,8,64,128]{3,2,1,0:T(8,128)(2,1)}, bf16[1,8,64,128]{3,2,1,0:T(8,128)(2,1)}, u32[]{:S(2)}, u32[]{:S(2)}) collective-permute-start(bf16[1,8,64,128]{3,2,1,0:T(8,128)(2,1)} %fusion.42), channel_id=1, source_target_pairs={{16,8},{18,10},{20,12},{22,14},{17,9},{19,11},{21,13},{23,15}} | collective-permute-start | bytes 393224 | tf_op jit(solution)/shard_map/ppermute | solution.py:65
  33.6 1.8 %collective-permute-start.12 = (bf16[1,1,64,128]{3,2,1,0:T(8,128)(2,1)S(1)}, bf16[1,1,64,128]{3,2,1,0:T(8,128)(2,1)S(1)}, u32[]{:S(2)}, u32[]{:S(2)}) collective-permute-start(bf16[1,1,64,128]{3,2,1,0:T(8,128)(2,1)S(1)} %slice_select_fusion.4), channel_id=1, source_target_pairs={{0,1},{1,0},{2,3},{3,2},{4,5},{5,4},{6,7},{7,6},{8,9},{9,8},{10,11... | collective-permute-start | bytes 49160 | tf_op jit(solution)/shard_map/ppermute | solution.py:27
  34.0 6.8 %collective-permute-start.16 = (bf16[1,8,64,128]{3,2,1,0:T(8,128)(2,1)}, bf16[1,8,64,128]{3,2,1,0:T(8,128)(2,1)S(1)}, u32[]{:S(2)}, u32[]{:S(2)}) collective-permute-start(bf16[1,8,64,128]{3,2,1,0:T(8,128)(2,1)} %collective-permute-done.14), channel_id=1, source_target_pairs={{8,10},{10,12},{12,14},{9,11},{11,13},{13,15}} | collective-permute-start | bytes 393224 | tf_op jit(solution)/shard_map/ppermute | solution.py:65
  34.6 35.9 %collective-permute-start.15 = (bf16[1,8,64,128]{3,2,1,0:T(8,128)(2,1)}, bf16[1,8,64,128]{3,2,1,0:T(8,128)(2,1)S(1)}, u32[]{:S(2)}, u32[]{:S(2)}) collective-permute-start(bf16[1,8,64,128]{3,2,1,0:T(8,128)(2,1)} %collective-permute-done.14), channel_id=1, source_target_pairs={{10,8},{12,10},{14,12},{11,9},{13,11},{15,13}} | collective-permute-start | bytes 393224 | tf_op jit(solution)/shard_map/ppermute | solution.py:65
  38.1 31.7 %collective-permute-start.13 = (bf16[1,8,64,128]{3,2,1,0:T(8,128)(2,1)S(1)}, bf16[1,8,64,128]{3,2,1,0:T(8,128)(2,1)S(1)}, u32[]{:S(2)}, u32[]{:S(2)}) collective-permute-start(bf16[1,8,64,128]{3,2,1,0:T(8,128)(2,1)S(1)} %fusion.41), channel_id=1, source_target_pairs={{8,0},{10,2},{12,4},{14,6},{9,1},{11,3},{13,5},{15,7}} | collective-permute-start | bytes 393224 | tf_op jit(solution)/shard_map/ppermute | solution.py:65
  39.4 34.4 %collective-permute-start.19 = (bf16[1,8,64,128]{3,2,1,0:T(8,128)(2,1)S(1)}, bf16[1,8,64,128]{3,2,1,0:T(8,128)(2,1)S(1)}, u32[]{:S(2)}, u32[]{:S(2)}) collective-permute-start(bf16[1,8,64,128]{3,2,1,0:T(8,128)(2,1)S(1)} %fusion.41), channel_id=1, source_target_pairs={{10,0},{12,2},{14,4},{11,1},{13,3},{15,5}} | collective-permute-start | bytes 393224 | tf_op jit(solution)/shard_map/ppermute | solution.py:65
  78.5 7.5 %collective-permute-start.18 = (bf16[1,8,64,128]{3,2,1,0:T(8,128)(2,1)S(1)}, bf16[1,8,64,128]{3,2,1,0:T(8,128)(2,1)S(1)}, u32[]{:S(2)}, u32[]{:S(2)}) collective-permute-start(bf16[1,8,64,128]{3,2,1,0:T(8,128)(2,1)S(1)} %fusion.40), channel_id=1, source_target_pairs={{8,0},{10,2},{12,4},{14,6},{9,1},{11,3},{13,5},{15,7}} | collective-permute-start | bytes 393224 | tf_op jit(solution)/shard_map/ppermute | solution.py:65
  79.8 6.2 %collective-permute-start.20 = (bf16[1,8,64,128]{3,2,1,0:T(8,128)(2,1)S(1)}, bf16[1,8,64,128]{3,2,1,0:T(8,128)(2,1)S(1)}, u32[]{:S(2)}, u32[]{:S(2)}) collective-permute-start(bf16[1,8,64,128]{3,2,1,0:T(8,128)(2,1)S(1)} %fusion.40), channel_id=1, source_target_pairs={{8,2},{10,4},{12,6},{9,3},{11,5},{13,7}} | collective-permute-start | bytes 393224 | tf_op jit(solution)/shard_map/ppermute | solution.py:65
  93.6 1.5 %collective-permute-start.21 = (bf16[768,128]{1,0:T(8,128)(2,1)S(1)}, bf16[768,128]{1,0:T(8,128)(2,1)S(1)}, u32[]{:S(2)}, u32[]{:S(2)}) collective-permute-start(bf16[768,128]{1,0:T(8,128)(2,1)S(1)} %dynamic-slice_convert_fusion), channel_id=1, source_target_pairs={{0,1},{1,0},{2,3},{3,2},{4,5},{5,4},{6,7},{7,6},{8,9},{9,8},{10,11... | collective-permute-start | bytes 589832 | tf_op jit(solution)/shard_map/ppermute | solution.py:119
  96.1 7.6 %collective-permute-start.22 = (bf16[2,1,64,128]{3,2,1,0:T(8,128)(2,1)S(1)}, bf16[2,1,64,128]{3,2,1,0:T(8,128)(2,1)S(1)}, u32[]{:S(2)}, u32[]{:S(2)}) collective-permute-start(bf16[2,1,64,128]{3,2,1,0:T(8,128)(2,1)S(1)} %slice_select_fusion.2), channel_id=1, source_target_pairs={{0,1},{1,0},{2,3},{3,2},{4,5},{5,4},{6,7},{7,6},{8,9},{9,8},{10,11... | collective-permute-start | bytes 98312 | tf_op jit(solution)/shard_map/ppermute | solution.py:27
  96.4 9.7 %collective-permute-start.23 = (bf16[192,128]{1,0:T(8,128)(2,1)S(1)}, bf16[192,128]{1,0:T(8,128)(2,1)S(1)}, u32[]{:S(2)}, u32[]{:S(2)}) collective-permute-start(bf16[192,128]{1,0:T(8,128)(2,1)S(1)} %get-tuple-element.43), channel_id=1, source_target_pairs={{0,2},{2,0},{4,6},{6,4},{1,3},{3,1},{5,7},{7,5},{8,10},{10,8},{12,... | collective-permute-start | bytes 147464 | tf_op jit(solution)/shard_map/ppermute | solution.py:119
  101.0 6.6 %collective-permute-start.24 = (bf16[192,128]{1,0:T(8,128)(2,1)S(1)}, bf16[192,128]{1,0:T(8,128)(2,1)S(1)}, u32[]{:S(2)}, u32[]{:S(2)}) collective-permute-start(bf16[192,128]{1,0:T(8,128)(2,1)S(1)} %get-tuple-element.45), channel_id=1, source_target_pairs={{0,4},{2,6},{4,0},{6,2},{1,5},{3,7},{5,1},{7,3},{8,12},{10,14},{12... | collective-permute-start | bytes 147464 | tf_op jit(solution)/shard_map/ppermute | solution.py:119
  102.3 5.9 %collective-permute-start.25 = (bf16[192,128]{1,0:T(8,128)(2,1)S(1)}, bf16[192,128]{1,0:T(8,128)(2,1)S(1)}, u32[]{:S(2)}, u32[]{:S(2)}) collective-permute-start(bf16[192,128]{1,0:T(8,128)(2,1)S(1)} %get-tuple-element.44), channel_id=1, source_target_pairs={{0,6},{2,4},{4,2},{6,0},{1,7},{3,5},{5,3},{7,1},{8,14},{10,12},{12... | collective-permute-start | bytes 147464 | tf_op jit(solution)/shard_map/ppermute | solution.py:119
  108.3 4.8 %collective-permute-start.26 = (bf16[192,128]{1,0:T(8,128)(2,1)S(1)}, bf16[192,128]{1,0:T(8,128)(2,1)S(1)}, u32[]{:S(2)}, u32[]{:S(2)}) collective-permute-start(bf16[192,128]{1,0:T(8,128)(2,1)S(1)} %get-tuple-element.36), channel_id=1, source_target_pairs={{0,2},{2,0},{4,6},{6,4},{1,3},{3,1},{5,7},{7,5},{8,10},{10,8},{12,... | collective-permute-start | bytes 147464 | tf_op jit(solution)/shard_map/ppermute | solution.py:147
  109.9 6.5 %collective-permute-start.27 = (bf16[192,128]{1,0:T(8,128)(2,1)S(1)}, bf16[192,128]{1,0:T(8,128)(2,1)S(1)}, u32[]{:S(2)}, u32[]{:S(2)}) collective-permute-start(bf16[192,128]{1,0:T(8,128)(2,1)S(1)} %get-tuple-element.36), channel_id=1, source_target_pairs={{0,4},{2,6},{4,0},{6,2},{1,5},{3,7},{5,1},{7,3},{8,12},{10,14},{12... | collective-permute-start | bytes 147464 | tf_op jit(solution)/shard_map/ppermute | solution.py:147
  111.3 6.0 %collective-permute-start.28 = (bf16[192,128]{1,0:T(8,128)(2,1)S(1)}, bf16[192,128]{1,0:T(8,128)(2,1)S(1)}, u32[]{:S(2)}, u32[]{:S(2)}) collective-permute-start(bf16[192,128]{1,0:T(8,128)(2,1)S(1)} %get-tuple-element.36), channel_id=1, source_target_pairs={{0,6},{2,4},{4,2},{6,0},{1,7},{3,5},{5,3},{7,1},{8,14},{10,12},{12... | collective-permute-start | bytes 147464 | tf_op jit(solution)/shard_map/ppermute | solution.py:147
  117.3 1.5 %collective-permute-start.29 = (bf16[768,128]{1,0:T(8,128)(2,1)S(1)}, bf16[768,128]{1,0:T(8,128)(2,1)S(1)}, u32[]{:S(2)}, u32[]{:S(2)}) collective-permute-start(bf16[768,128]{1,0:T(8,128)(2,1)S(1)} %constant_dynamic-update-slice_fusion), channel_id=1, source_target_pairs={{0,1},{1,0},{2,3},{3,2},{4,5},{5,4},{6,7},{7,6},{8,9},{9,8},{10,11... | collective-permute-start | bytes 589832 | tf_op jit(solution)/shard_map/ppermute | solution.py:250
  (18 other events, 18.0 us)

commit v3 on v2

v3 whole, which is shorter than its diff:
```python
import functools

import jax
import jax.numpy as jnp
from jax import lax
from jax.experimental import pallas as pl
from jax.experimental.pallas import tpu as pltpu
from jax.sharding import PartitionSpec as P

VMEM_LIMIT = 40 * 1024 * 1024
NT = (((1,), (1,)), ((), ()))
NN = (((1,), (0,)), ((), ()))
TN = (((0,), (0,)), ((), ()))


def mul(a, b, how):
    return lax.dot_general(a, b, how, preferred_element_type=jnp.float32)


def call(body, outs, args, flops):
    moved = sum(a.size * a.dtype.itemsize for a in (*args, *outs))
    return pl.pallas_call(
        body,
        out_shape=outs,
        in_specs=[pl.BlockSpec(memory_space=pltpu.VMEM) for _ in args],
        out_specs=[pl.BlockSpec(memory_space=pltpu.VMEM) for _ in outs],
        compiler_params=pltpu.CompilerParams(vmem_limit_bytes=VMEM_LIMIT),
        cost_estimate=pl.CostEstimate(flops=flops, bytes_accessed=moved, transcendentals=0),
    )(*args)


def flat(values):
    return values.reshape(-1, values.shape[-1])


def row_sides(got, row_count):
    if len(got) == 1:
        first = (lax.axis_index("row") == 0).astype(jnp.float32)
        rows = got[0].astype(jnp.float32)
        return (rows * (1.0 - first)).astype(jnp.bfloat16), (rows * first).astype(jnp.bfloat16)
    return got


def moved_rows(cells, above, below):
    return (
        flat(jnp.concatenate([above, cells[:, :-1]], axis=1)),
        flat(cells),
        flat(jnp.concatenate([cells[:, 1:], below], axis=1)),
    )


def moved_cols(values, step, col_count):
    count = values.shape[0]
    col = lax.broadcasted_iota(jnp.int32, values.shape, 0) % col_count
    if step == 1:
        return jnp.where(col == col_count - 1, 0.0, pltpu.roll(values, count - 1, 0))
    return jnp.where(col == 0, 0.0, pltpu.roll(values, 1, 0))


def edges_of(cells, row_parts):
    head, tail = cells[:, :1], cells[:, -1:]
    if row_parts == 2:
        first = (lax.axis_index("row") == 0).astype(jnp.float32)
        return [(tail.astype(jnp.float32) * first + head.astype(jnp.float32) * (1.0 - first)).astype(jnp.bfloat16)]
    return [head, tail]


def swap_edges(edges):
    count = lax.axis_size("row")
    if count == 2:
        return [lax.ppermute(edges[0], "row", [(0, 1), (1, 0)])]
    head, tail = edges
    if count == 1:
        return [jnp.zeros_like(head), jnp.zeros_like(head)]
    return [
        lax.ppermute(tail, "row", [(i, i + 1) for i in range(count - 1)]),
        lax.ppermute(head, "row", [(i + 1, i) for i in range(count - 1)]),
    ]


def split_frames(values, chains):
    if chains == 1:
        return [values]
    pairs = values.reshape((values.shape[0] // chains, chains) + values.shape[1:])
    return [pairs[:, at] for at in range(chains)]


def forward(block_input, got, taps_space, chains):
    frames, rows, cols, channels = block_input.shape
    part = (frames // chains, rows, cols, channels)

    def body(*refs):
        x_ref, got_refs, w_ref = refs[0], refs[1 : 1 + len(got)], refs[1 + len(got)]
        slope_refs = refs[2 + len(got) : 2 + len(got) + chains]
        active_refs = refs[2 + len(got) + chains :]
        above, below = row_sides([ref[...] for ref in got_refs], rows)
        sides = jnp.concatenate(moved_rows(x_ref[...], above, below), axis=1)
        taps = jnp.concatenate(
            [jnp.concatenate([w_ref[i, j] for j in range(3)], axis=1) for i in range(3)], axis=0
        )
        sums = mul(sides, taps, NN)
        pre_act = (
            moved_cols(sums[:, :channels], -1, cols)
            + sums[:, channels : 2 * channels]
            + moved_cols(sums[:, 2 * channels :], 1, cols)
        )
        sigma = jax.nn.sigmoid(pre_act)
        slope = (sigma * (1.0 + pre_act * (1.0 - sigma))).reshape(x_ref.shape)
        active = (pre_act * sigma).astype(jnp.bfloat16).reshape(x_ref.shape)
        for ref, values in zip(slope_refs, split_frames(slope, chains)):
            ref[...] = values
        for ref, values in zip(active_refs, split_frames(active, chains)):
            ref[...] = values

    outs = [jax.ShapeDtypeStruct(part, jnp.float32)] * chains
    outs += [jax.ShapeDtypeStruct(part, jnp.bfloat16)] * chains
    outs = call(body, outs, [block_input, *got, taps_space], 18 * block_input.size * channels)
    return outs[:chains], outs[chains:]


def early_half(distance_step):
    frame_parts = lax.axis_size("frame")
    return (lax.axis_index("frame") < frame_parts - distance_step).astype(jnp.float32)


def temporal(owner, triples, pair_step, slopes, taps_time):
    row_parts = lax.axis_size("row")
    part = slopes[0].shape
    channels = part[-1]
    edges = 1 if row_parts == 2 else 2
    sizes = [len(triple) for triple in triples]

    def body(*refs):
        @pl.when(lax.axis_index("section") == owner)
        def _():
            at = 0
            w_ref = refs[sum(sizes) + len(slopes)]
            outs = refs[sum(sizes) + len(slopes) + 1 :]
            for chain, size in enumerate(sizes):
                blocks = [flat(ref[...]) for ref in refs[at : at + size]]
                at += size
                taps = [w_ref[1]]
                if size == 2:
                    early = early_half(pair_step)
                    other = early * w_ref[0].astype(jnp.float32)
                    other += (1.0 - early) * w_ref[2].astype(jnp.float32)
                    taps.append(other.astype(jnp.bfloat16))
                elif size == 3:
                    taps += [w_ref[0], w_ref[2]]
                sums = mul(jnp.concatenate(blocks, axis=1), jnp.concatenate(taps, axis=1), NT)
                back_act = sums.astype(jnp.bfloat16).astype(jnp.float32)
                slope = flat(refs[sum(sizes) + chain][...])
                grad_pre = (back_act * slope).astype(jnp.bfloat16).reshape(part)
                outs[chain][...] = grad_pre
                for ref, edge in zip(outs[len(slopes) :], edges_of(grad_pre, row_parts)):
                    ref[chain * part[0] : (chain + 1) * part[0]] = edge

    outs = [jax.ShapeDtypeStruct(part, jnp.bfloat16)] * len(slopes)
    outs += [
        jax.ShapeDtypeStruct((part[0] * len(slopes), 1) + part[2:], jnp.bfloat16)
    ] * edges
    args = [block for triple in triples for block in triple] + list(slopes) + [taps_time]
    outs = call(body, outs, args, 6 * sum(s.size for s in slopes) * channels)
    return outs[: len(slopes)], outs[len(slopes) :]


def branches(owner, grads_pre, got, heres, taps_space):
    part = heres[0].shape
    _, rows, cols, channels = part
    count = len(heres)

    def body(*refs):
        @pl.when(lax.axis_index("section") == owner)
        def _():
            got_refs = refs[count : count + len(got)]
            here_refs = refs[count + len(got) : 2 * count + len(got)]
            w_ref = refs[2 * count + len(got)]
            out_refs = refs[2 * count + len(got) + 1 :]
            taps = jnp.concatenate(
                [jnp.concatenate([w_ref[2 - i, j] for i in range(3)], axis=1) for j in range(3)],
                axis=0,
            )
            for chain in range(count):
                frames = slice(chain * part[0], (chain + 1) * part[0])
                above, below = row_sides([ref[frames] for ref in got_refs], rows)
                sides = jnp.concatenate(moved_rows(refs[chain][...], above, below), axis=1)
                sums = mul(sides, taps, NT)
                branch = (
                    moved_cols(sums[:, :channels], 1, cols)
                    + sums[:, channels : 2 * channels]
                    + moved_cols(sums[:, 2 * channels :], -1, cols)
                )
                branch = branch.astype(jnp.bfloat16).astype(jnp.float32)
                here = flat(here_refs[chain][...]).astype(jnp.float32)
                out_refs[chain][...] = (here + branch).astype(jnp.bfloat16).reshape(part)

    outs = [jax.ShapeDtypeStruct(part, jnp.bfloat16)] * count
    args = [*grads_pre, *got, *heres, taps_space]
    return call(body, outs, args, 18 * sum(h.size for h in heres) * channels)


def kernel_grads(owner, block_input, got, grads_pre, actives, triples, pair_step, before):
    frames, rows, cols, channels = block_input.shape
    chains = len(actives)
    size = len(triples[0])
    fixed = 1 + len(got)

    def body(*refs):
        section = lax.axis_index("section")
        out_ref = refs[-1]

        if before is not None:

            @pl.when(section != owner)
            def _():
                out_ref[...] = refs[-2][...]

        @pl.when(section == owner)
        def _():
            above, below = row_sides([ref[...] for ref in refs[1:fixed]], rows)
            sides = []
            for cells, up, down in zip(
                *(split_frames(v, chains) for v in (refs[0][...], above, below))
            ):
                sides.append(jnp.concatenate(moved_rows(cells, up, down), axis=1))
            pre, blocks = [], []
            at = fixed + 2 * chains
            for chain in range(chains):
                mid = flat(refs[fixed + chain][...])
                wide = mid.astype(jnp.float32)
                left = moved_cols(wide, 1, cols).astype(jnp.bfloat16)
                right = moved_cols(wide, -1, cols).astype(jnp.bfloat16)
                pre.append(jnp.concatenate([left, mid, right], axis=1))
                blocks.append(
                    jnp.concatenate([flat(ref[...]) for ref in refs[at : at + size]], axis=1)
                )
                at += size
            space = mul(jnp.concatenate(sides), jnp.concatenate(pre), TN)
            for i in range(3):
                for j in range(3):
                    out_ref[3 * i + j] = space[
                        i * channels : (i + 1) * channels, j * channels : (j + 1) * channels
                    ]
            active = jnp.concatenate(
                [flat(refs[fixed + chains + chain][...]) for chain in range(chains)]
            )
            time = mul(active, jnp.concatenate(blocks), TN)
            out_ref[10] = time[:, :channels]
            if size == 1:
                out_ref[9] = jnp.zeros((channels, channels), jnp.float32)
                out_ref[11] = jnp.zeros((channels, channels), jnp.float32)
            elif size == 2:
                early = early_half(pair_step)
                out_ref[9] = early * time[:, channels:]
                out_ref[11] = (1.0 - early) * time[:, channels:]
            else:
                out_ref[9] = time[:, channels : 2 * channels]
                out_ref[11] = time[:, 2 * channels :]

    args = [block_input, *got, *grads_pre, *actives]
    args += [block for triple in triples for block in triple]
    if before is not None:
        args.append(before)
    outs = [jax.ShapeDtypeStruct((12, channels, channels), jnp.float32)]
    return call(body, outs, args, 24 * block_input.size * channels)[0]


def fetch(block, source, target, frame_step):
    frame_parts = lax.axis_size("frame")
    route = [
        (source * frame_parts + z + frame_step, target * frame_parts + z)
        for z in range(frame_parts)
        if 0 <= z + frame_step < frame_parts
    ]
    if not route:
        return jnp.zeros_like(block)
    if source == target and frame_step == 0:
        return block
    return lax.ppermute(block, ("section", "frame"), route)


def shifted_from(block, source, target, offset, unmoved=None):
    own_frames = block.shape[0]
    step, rest = divmod(offset, own_frames)
    pieces = []
    for frames, move in ((slice(rest, None), step), (slice(0, rest), step + 1)):
        piece = block[frames]
        if piece.shape[0] == 0:
            continue
        if move == 0 and unmoved is not None:
            pieces.append(unmoved[frames])
        else:
            pieces.append(fetch(piece, source, target, move))
    return pieces[0] if len(pieces) == 1 else jnp.concatenate(pieces)


def pair_step_of(own_frames, distance):
    step, rest = divmod(distance, own_frames)
    frame_parts = lax.axis_size("frame")
    return step if rest == 0 and frame_parts <= 2 * step < 2 * frame_parts else 0


def triple_from(block, source, target, distance, staged):
    own_frames = block.shape[0]
    frame_parts = lax.axis_size("frame")
    own = fetch(block, source, target, 0)
    if distance >= frame_parts * own_frames:
        return [own]
    step = pair_step_of(own_frames, distance)
    if step:
        route = [
            (source * frame_parts + z + move, target * frame_parts + z)
            for z in range(frame_parts)
            for move in (step, -step)
            if 0 <= z + move < frame_parts
        ]
        return [own, lax.ppermute(block, ("section", "frame"), route)]
    if staged:
        block, source = own, target
    return [
        own,
        shifted_from(block, source, target, distance, own),
        shifted_from(block, source, target, -distance, own),
    ]


def by_pairs(axis):
    count = lax.axis_size(axis)
    return count <= 4 and count & (count - 1) == 0


def sum_over(values, axis):
    count = lax.axis_size(axis)
    if by_pairs(axis):
        index = lax.axis_index(axis)
        size = values.shape[0] // count
        total = lax.dynamic_slice_in_dim(values, index * size, size, 0)
        for mask in range(1, count):
            part = lax.dynamic_slice_in_dim(values, (index ^ mask) * size, size, 0)
            got = lax.ppermute(
                part.astype(jnp.bfloat16), axis, [(i, i ^ mask) for i in range(count)]
            )
            total += got.astype(jnp.float32)
        return total
    parts = values.astype(jnp.bfloat16).reshape((count, -1) + values.shape[1:])
    parts = lax.all_to_all(parts, axis, split_axis=0, concat_axis=0, tiled=True)
    return jnp.sum(parts.astype(jnp.float32), axis=0)


def gather_parts(part, axis):
    if not by_pairs(axis):
        return lax.all_gather(part, axis, axis=0, tiled=True)
    count = lax.axis_size(axis)
    index = lax.axis_index(axis)
    size = part.shape[0]
    whole = jnp.zeros((count * size,) + part.shape[1:], part.dtype)
    whole = lax.dynamic_update_slice_in_dim(whole, part, index * size, 0)
    for mask in range(1, count):
        got = lax.ppermute(part, axis, [(i, i ^ mask) for i in range(count)])
        whole = lax.dynamic_update_slice_in_dim(whole, got, (index ^ mask) * size, 0)
    return whole


def after(values, *others):
    return list(lax.optimization_barrier((tuple(values), others))[0])


def section_run(chains, x_saved, cotangent, w_spatial, w_temporal):
    block_input = x_saved[0]
    taps_space = w_spatial[0]
    taps_time = w_temporal[0]
    own_frames, row_count, col_count, channels = block_input.shape
    section_count = lax.axis_size("section")
    section_index = lax.axis_index("section")
    row_parts = lax.axis_size("row")
    if own_frames % 2:
        chains = 1
    top = section_count - 1

    def triples(blocks, source, target):
        dilation = 2**target
        if chains == 1:
            return [triple_from(blocks[0], source, target, dilation, False)]
        if dilation % 2 == 0:
            return [triple_from(block, source, target, dilation // 2, STAGED) for block in blocks]
        even, odd = blocks
        own_even = fetch(even, source, target, 0)
        next_even = shifted_from(even, source, target, (dilation + 1) // 2, own_even)
        own_odd = fetch(odd, source, target, 0)
        last_odd = shifted_from(odd, source, target, -((dilation + 1) // 2), own_odd)
        same_odd = shifted_from(odd, source, target, (dilation - 1) // 2, own_odd)
        same_even = shifted_from(even, source, target, -((dilation - 1) // 2), own_even)
        return [[own_even, same_odd, last_odd], [own_odd, next_even, same_even]]

    def pair_step(target):
        dilation = 2**target
        if dilation % chains:
            return 0
        return pair_step_of(own_frames // chains, dilation // chains)

    x_got = swap_edges(edges_of(block_input, row_parts))
    slopes, actives = forward(block_input, x_got, taps_space, chains)
    ready = triples(split_frames(cotangent, chains), top, top)
    grads = None
    results = []
    for position in range(section_count):
        owner = top - position
        last = owner == 0
        groups = [list(range(chains))] if last else [[chain] for chain in range(chains)]
        pre, outgoing = [], []
        for group in groups:
            mine = [ready[chain] for chain in group]
            if outgoing:
                mine = [after(triple, *outgoing) for triple in mine]
            elif results:
                mine = [after(triple, *results[-1]) for triple in mine]
            group_pre, edges = temporal(
                owner, mine, pair_step(owner), [slopes[chain] for chain in group], taps_time
            )
            pre += group_pre
            if last:
                break
            got = swap_edges(edges)
            outgoing += branches(owner, group_pre, got, [t[0] for t in mine], taps_space)
        inputs = pre if last else after(pre, *outgoing)
        grads = kernel_grads(
            owner, block_input, x_got, inputs, actives, ready, pair_step(owner), grads
        )
        if not last:
            results.append(outgoing)
            ready = triples(outgoing, owner, owner - 1)

    total = sum_over(grads.reshape(-1, channels), "row")
    edges = after(edges, total)
    got = swap_edges(edges)
    outgoing = branches(0, pre, got, [t[0] for t in ready], taps_space)
    results.append(outgoing)
    total = sum_over(total, "frame").astype(jnp.bfloat16)
    total = gather_parts(total, "frame")
    split = 9 * channels
    if row_parts == 2:
        first = lax.axis_index("row") == 0
        other = lax.ppermute(total, "row", [(0, 1), (1, 0)])
        rest = split - total.shape[0]
        space = jnp.where(
            first,
            jnp.concatenate([total, other[:rest]]),
            jnp.concatenate([other, total[:rest]]),
        )
        time = jnp.where(first, other[rest:], total[rest:])
    else:
        total = gather_parts(total, "row")
        space, time = total[:split], total[split:]
    own = results[0]
    for position in range(1, section_count):
        own = [
            jnp.where(section_index == top - position, new, old)
            for new, old in zip(results[position], own)
        ]
    own = jnp.stack(own, 1).reshape(block_input.shape)
    return (
        own[None],
        space.astype(jnp.float32).reshape((1, 3, 3, channels, channels)),
        time.astype(jnp.float32).reshape((1, 3, channels, channels)),
    )


CHAINS = 2
STAGED = False


def solution(mesh):
    return jax.shard_map(
        functools.partial(section_run, CHAINS),
        mesh=mesh,
        in_specs=(
            P("section", "frame", "row", None, None),
            P("frame", "row", None, None),
            P("section", None, None, None, None),
            P("section", None, None, None),
        ),
        out_specs=(
            P("section", "frame", "row", None, None),
            P("section", None, None, None, None),
            P("section", None, None, None),
        ),
        check_vma=False,
    )
```

time: 121 us -> 83.7 us (0.69)
  matrix products: 22.3 us -> 0 us
  waiting for transfers between devices: 49.8 us -> 40.8 us
  other arithmetic: 10.4 us -> 3.4 us
  Pallas kernels: 0 us -> 6 us
  local copies, waits for them, and re-layouts: 9.58 us -> 4.61 us
    dot_general x105 -> x0, matrix products: 22.3 us -> none  [the longest x72 14.1 us: apply_taps(): running = running + jnp.dot(window, tap, preferred_element_type=jnp.float32)]
    ppermute x12, waiting for transfers between devices: 37.7 us -> 25.2 us  [fetch(): return lax.ppermute(block, ('section', 'frame'), route)]
    pallas_call x0 -> x19, Pallas kernels: none -> 6 us  [call(): pl.pallas_call(body, out_shape=outs, in_specs=[pl.BlockSpec(memory_space=...]
    ppermute x14, waiting for transfers between devices: 7.25 us -> 11.1 us  [the longest x4 5.98 us: sum_over(): lax.ppermute(part.astype(jnp.bfloat16), axis, [(i, i ^ mask) for i in ran...]
    unnamed x24 -> x42, local copies, waits for them, and re-layouts: 6.97 us -> 3.46 us
    slice x10 -> x0, local copies, waits for them, and re-layouts: 2.48 us -> none  [the longest x8 1.42 us: apply_taps(): padded[:, i:i + row_count, j:j + col_count, :].reshape(-1, channels)]
    select_n x23 -> x0, other arithmetic: 2.41 us -> none  [the longest x8 1.45 us: row_halo(): jnp.where(index == 0, tail, head)]
    convert_element_type x14 -> x1, other arithmetic: 2.77 us -> 0.84 us  [edges_of(): (tail.astype(jnp.float32) * first + head.astype(jnp.float32) * (1.0 - fir...]
  transfers between devices with their start and end apart: 30 -> 30, of which waited for: 13 -> 13; matrix products, arithmetic and copies ran while one was open for 12% -> 2% of each run, Pallas kernels for 0% -> 3%
where the time goes in v3:
time: 83.7 us; the launch traced here: 83.2 us
  waiting for transfers between devices  40.8 us (49%)
  starting transfers between devices  27.2 us (32%)
  Pallas kernels  6 us (7%)
  local copies, waits for them, and re-layouts  4.61 us (6%)
  other arithmetic  3.4 us (4%)
  between operations  1.15 us (1%)
    ppermute x12, waiting for transfers between devices, fetch(): return lax.ppermute(block, ('section', 'frame'), route)  25.2 us
    ppermute x12, starting transfers between devices, fetch(): return lax.ppermute(block, ('section', 'frame'), route)  10.5 us
    ppermute x4, starting transfers between devices, sum_over(): lax.ppermute(part.astype(jnp.bfloat16), axis, [(i, i ^ mask) for i in ran...  9.06 us
    pallas_call x19, Pallas kernels, call(): pl.pallas_call(body, out_shape=outs, in_specs=[pl.BlockSpec(memory_space=...  6 us
    ppermute x4, waiting for transfers between devices, sum_over(): lax.ppermute(part.astype(jnp.bfloat16), axis, [(i, i ^ mask) for i in ran...  5.98 us
    ppermute x8, waiting for transfers between devices, swap_edges(): return [lax.ppermute(edges[0], 'row', [(0, 1), (1, 0)])]  5.13 us
    ppermute x3, starting transfers between devices, gather_parts(): got = lax.ppermute(part, axis, [(i, i ^ mask) for i in range(count)])  4.52 us
    ppermute x3, waiting for transfers between devices, gather_parts(): got = lax.ppermute(part, axis, [(i, i ^ mask) for i in range(count)])  3.99 us
  transfers between devices with their start and end apart: 30, of which 13 were waited for; matrix products, arithmetic and copies ran while one was open for 2% of the time, Pallas kernels for 3%

profile of v3, /device:TPU:0, one launch (start us, length us, event | category | flops | bytes accessed | tf_op | source)
XLA Modules:
  0.0 83.2 jit_solution(8943323419668475135)
XLA Ops:
  2.0 1.0 %slice_bitcast_fusion = (bf16[1,8,64,128]{3,2,1,0:T(8,128)(2,1)S(1)}, bf16[1,8,64,128]{3,2,1,0:T(8,128)(2,1)S(1)}) fusion(bf16[1,2,8,64,128]{4,3,2,1,0:T(8,128)(2,1)} %bitcast.42), kind=kLoop, calls=%fused_computation.4 | loop fusion | bytes 524288 | tf_op jit(solution)/shard_map/squeeze | solution.py:85
  4.1 1.0 %collective-permute-done.1.refs_1_ = bf16[1,1,64,128]{3,2,1,0:T(8,128)(2,1)S(1)} collective-permute-done((bf16[1,1,64,128]{3,2,1,0:T(8,128)(2,1)S(1)}, bf16[1,1,64,128]{3,2,1,0:T(8,128)(2,1)S(1)}, u32[]{:S(2)}, u32[]{:S(2)}) %collective-permute-start.1) | collective-permute-done | bytes 16416 | tf_op jit(solution)/shard_map/ppermute | solution.py:71
  6.8 1.0 %collective-permute-done.4.refs_1_ = bf16[1,1,64,128]{3,2,1,0:T(8,128)(2,1)S(1)} collective-permute-done((bf16[1,1,64,128]{3,2,1,0:T(8,128)(2,1)S(1)}, bf16[1,1,64,128]{3,2,1,0:T(8,128)(2,1)S(1)}, u32[]{:S(2)}, u32[]{:S(2)}) %collective-permute-start.4) | collective-permute-done | bytes 16416 | tf_op jit(solution)/shard_map/ppermute | solution.py:71
  9.4 1.0 %collective-permute-done.5.refs_1_ = bf16[1,1,64,128]{3,2,1,0:T(8,128)(2,1)S(1)} collective-permute-done((bf16[1,1,64,128]{3,2,1,0:T(8,128)(2,1)S(1)}, bf16[1,1,64,128]{3,2,1,0:T(8,128)(2,1)S(1)}, u32[]{:S(2)}, u32[]{:S(2)}) %collective-permute-start.5) | collective-permute-done | bytes 16416 | tf_op jit(solution)/shard_map/ppermute | solution.py:71
  12.8 1.0 %collective-permute-done.11.refs_1_ = bf16[1,1,64,128]{3,2,1,0:T(8,128)(2,1)S(1)} collective-permute-done((bf16[1,1,64,128]{3,2,1,0:T(8,128)(2,1)S(1)}, bf16[1,1,64,128]{3,2,1,0:T(8,128)(2,1)S(1)}, u32[]{:S(2)}, u32[]{:S(2)}) %collective-permute-start.11) | collective-permute-done | bytes 16416 | tf_op jit(solution)/shard_map/ppermute | solution.py:71
  16.8 1.0 %collective-permute-done.12.refs_1_ = bf16[1,1,64,128]{3,2,1,0:T(8,128)(2,1)S(1)} collective-permute-done((bf16[1,1,64,128]{3,2,1,0:T(8,128)(2,1)S(1)}, bf16[1,1,64,128]{3,2,1,0:T(8,128)(2,1)S(1)}, u32[]{:S(2)}, u32[]{:S(2)}) %collective-permute-start.12) | collective-permute-done | bytes 16416 | tf_op jit(solution)/shard_map/ppermute | solution.py:71
  19.4 1.3 %collective-permute-start.13 = (bf16[1,8,64,128]{3,2,1,0:T(8,128)(2,1)}, bf16[1,8,64,128]{3,2,1,0:T(8,128)(2,1)S(1)}, u32[]{:S(2)}, u32[]{:S(2)}) collective-permute-start(bf16[1,8,64,128]{3,2,1,0:T(8,128)(2,1)} %shard_map.77), channel_id=1, source_target_pairs={{8,0},{10,2},{12,4},{14,6},{9,1},{11,3},{13,5},{15,7}} | collective-permute-start | bytes 393224 | tf_op jit(solution)/shard_map/ppermute | solution.py:279
  20.6 1.3 %collective-permute-start.20 = (bf16[1,8,64,128]{3,2,1,0:T(8,128)(2,1)}, bf16[1,8,64,128]{3,2,1,0:T(8,128)(2,1)}, u32[]{:S(2)}, u32[]{:S(2)}) collective-permute-start(bf16[1,8,64,128]{3,2,1,0:T(8,128)(2,1)} %shard_map.77), channel_id=1, source_target_pairs={{10,0},{12,2},{14,4},{11,1},{13,3},{15,5}} | collective-permute-start | bytes 393224 | tf_op jit(solution)/shard_map/ppermute | solution.py:279
  22.6 1.3 %collective-permute-start.18 = (bf16[1,8,64,128]{3,2,1,0:T(8,128)(2,1)}, bf16[1,8,64,128]{3,2,1,0:T(8,128)(2,1)S(1)}, u32[]{:S(2)}, u32[]{:S(2)}) collective-permute-start(bf16[1,8,64,128]{3,2,1,0:T(8,128)(2,1)} %shard_map.79), channel_id=1, source_target_pairs={{8,0},{10,2},{12,4},{14,6},{9,1},{11,3},{13,5},{15,7}} | collective-permute-start | bytes 393224 | tf_op jit(solution)/shard_map/ppermute | solution.py:279
  23.9 1.3 %collective-permute-start.19 = (bf16[1,8,64,128]{3,2,1,0:T(8,128)(2,1)}, bf16[1,8,64,128]{3,2,1,0:T(8,128)(2,1)}, u32[]{:S(2)}, u32[]{:S(2)}) collective-permute-start(bf16[1,8,64,128]{3,2,1,0:T(8,128)(2,1)} %shard_map.79), channel_id=1, source_target_pairs={{8,2},{10,4},{12,6},{9,3},{11,5},{13,7}} | collective-permute-start | bytes 393224 | tf_op jit(solution)/shard_map/ppermute | solution.py:279
  27.3 18.6 %collective-permute-done.13.refs_0_.refs_5_.refs_6_.refs_11_.refs_3_ = bf16[1,8,64,128]{3,2,1,0:T(8,128)(2,1)S(1)} collective-permute-done((bf16[1,8,64,128]{3,2,1,0:T(8,128)(2,1)}, bf16[1,8,64,128]{3,2,1,0:T(8,128)(2,1)S(1)}, u32[]{:S(2)}, u32[]{:S(2)}) %collective-permute-start.13) | collective-permute-done | bytes 131104 | tf_op jit(solution)/shard_map/ppermute | solution.py:279
  45.9 5.5 %collective-permute-done.20.refs_4_.refs_10_ = bf16[1,8,64,128]{3,2,1,0:T(8,128)(2,1)} collective-permute-done((bf16[1,8,64,128]{3,2,1,0:T(8,128)(2,1)}, bf16[1,8,64,128]{3,2,1,0:T(8,128)(2,1)}, u32[]{:S(2)}, u32[]{:S(2)}) %collective-permute-start.20) | collective-permute-done | bytes 131104 | tf_op jit(solution)/shard_map/ppermute | solution.py:279
  51.5 1.0 %collective-permute-done.18.refs_1_.refs_3_.refs_7_.refs_9_.refs_4_ = bf16[1,8,64,128]{3,2,1,0:T(8,128)(2,1)S(1)} collective-permute-done((bf16[1,8,64,128]{3,2,1,0:T(8,128)(2,1)}, bf16[1,8,64,128]{3,2,1,0:T(8,128)(2,1)S(1)}, u32[]{:S(2)}, u32[]{:S(2)}) %collective-permute-start.18) | collective-permute-done | bytes 131104 | tf_op jit(solution)/shard_map/ppermute | solution.py:279
  52.5 1.3 %shard_map.80 = (bf16[1,8,64,128]{3,2,1,0:T(8,128)(2,1)S(1)}, bf16[1,8,64,128]{3,2,1,0:T(8,128)(2,1)S(1)}, bf16[2,1,64,128]{3,2,1,0:T(8,128)(2,1)S(1)}) custom-call(bf16[1,8,64,128]{3,2,1,0:T(8,128)(2,1)S(1)} %collective-permute-done.13.refs_0_.refs_5_.refs_6_.refs_11_.refs_3_, ...), custom_call_target="tpu_custom_call" | custom-call | flops 100663296 | bytes 1703936 | tf_op jit(solution)/shard_map/pallas_call | solution.py:22
  53.8 1.7 %shard_map.84 = f32[12,128,128]{2,1,0:T(8,128)S(1)} custom-call(bf16[2,8,64,128]{3,2,1,0:T(8,128)(2,1)S(1)} %bitcast.37, bf16[2,1,64,128]{3,2,1,0:T(8,128)(2,1)S(1)} %collective-permute-done.refs_1_, bf16[1,8,64,128]{3,2,1,0:T(8,128)(2,1)S(1)} %get-tuple-element.79.refs_2_.refs_0_, bf16[1,8,64,128]{3,2,1,0:T(8,128)(2,1)S(1)} %get-tuple-element.80.refs_3_.refs_1_, ...), custom_call_target="tpu_custom_call" | custom-call | flops 402653184 | bytes 3178496 | tf_op jit(solution)/shard_map/pallas_call | solution.py:22
  55.7 1.4 %collective-permute-done.21 = bf16[768,128]{1,0:T(8,128)(2,1)S(1)} collective-permute-done((bf16[768,128]{1,0:T(8,128)(2,1)S(1)}, bf16[768,128]{1,0:T(8,128)(2,1)S(1)}, u32[]{:S(2)}, u32[]{:S(2)}) %collective-permute-start.21) | collective-permute-done | bytes 196640 | tf_op jit(solution)/shard_map/ppermute | solution.py:340
  57.1 6.5 %collective-permute-start.23 = (bf16[192,128]{1,0:T(8,128)(2,1)S(1)}, bf16[192,128]{1,0:T(8,128)(2,1)S(1)}, u32[]{:S(2)}, u32[]{:S(2)}) collective-permute-start(bf16[192,128]{1,0:T(8,128)(2,1)S(1)} %get-tuple-element.95), channel_id=1, source_target_pairs={{0,2},{2,0},{4,6},{6,4},{1,3},{3,1},{5,7},{7,5},{8,10},{10,8},{12,... | collective-permute-start | bytes 147464 | tf_op jit(solution)/shard_map/ppermute | solution.py:340
  64.4 1.7 %collective-permute-start.25 = (bf16[192,128]{1,0:T(8,128)(2,1)S(1)}, bf16[192,128]{1,0:T(8,128)(2,1)S(1)}, u32[]{:S(2)}, u32[]{:S(2)}) collective-permute-start(bf16[192,128]{1,0:T(8,128)(2,1)S(1)} %get-tuple-element.96), channel_id=1, source_target_pairs={{0,6},{2,4},{4,2},{6,0},{1,7},{3,5},{5,3},{7,1},{8,14},{10,12},{12... | collective-permute-start | bytes 147464 | tf_op jit(solution)/shard_map/ppermute | solution.py:340
  66.1 4.6 %collective-permute-done.24 = bf16[192,128]{1,0:T(8,128)(2,1)S(1)} collective-permute-done((bf16[192,128]{1,0:T(8,128)(2,1)S(1)}, bf16[192,128]{1,0:T(8,128)(2,1)S(1)}, u32[]{:S(2)}, u32[]{:S(2)}) %collective-permute-start.24) | collective-permute-done | bytes 49184 | tf_op jit(solution)/shard_map/ppermute | solution.py:340
  70.8 1.2 %collective-permute-start.26 = (bf16[192,128]{1,0:T(8,128)(2,1)S(1)}, bf16[192,128]{1,0:T(8,128)(2,1)S(1)}, u32[]{:S(2)}, u32[]{:S(2)}) collective-permute-start(bf16[192,128]{1,0:T(8,128)(2,1)S(1)} %get-tuple-element.94), channel_id=1, source_target_pairs={{0,2},{2,0},{4,6},{6,4},{1,3},{3,1},{5,7},{7,5},{8,10},{10,8},{12,... | collective-permute-start | bytes 147464 | tf_op jit(solution)/shard_map/ppermute | solution.py:359
  72.6 1.5 %collective-permute-start.27 = (bf16[192,128]{1,0:T(8,128)(2,1)S(1)}, bf16[192,128]{1,0:T(8,128)(2,1)S(1)}, u32[]{:S(2)}, u32[]{:S(2)}) collective-permute-start(bf16[192,128]{1,0:T(8,128)(2,1)S(1)} %get-tuple-element.94), channel_id=1, source_target_pairs={{0,4},{2,6},{4,0},{6,2},{1,5},{3,7},{5,1},{7,3},{8,12},{10,14},{12... | collective-permute-start | bytes 147464 | tf_op jit(solution)/shard_map/ppermute | solution.py:359
  74.1 1.9 %collective-permute-start.28 = (bf16[192,128]{1,0:T(8,128)(2,1)S(1)}, bf16[192,128]{1,0:T(8,128)(2,1)S(1)}, u32[]{:S(2)}, u32[]{:S(2)}) collective-permute-start(bf16[192,128]{1,0:T(8,128)(2,1)S(1)} %get-tuple-element.94), channel_id=1, source_target_pairs={{0,6},{2,4},{4,2},{6,0},{1,7},{3,5},{5,3},{7,1},{8,14},{10,12},{12... | collective-permute-start | bytes 147464 | tf_op jit(solution)/shard_map/ppermute | solution.py:359
  76.0 2.2 %collective-permute-done.27 = bf16[192,128]{1,0:T(8,128)(2,1)S(1)} collective-permute-done((bf16[192,128]{1,0:T(8,128)(2,1)S(1)}, bf16[192,128]{1,0:T(8,128)(2,1)S(1)}, u32[]{:S(2)}, u32[]{:S(2)}) %collective-permute-start.27) | collective-permute-done | bytes 49184 | tf_op jit(solution)/shard_map/ppermute | solution.py:359
  78.2 1.8 %collective-permute-done.28 = bf16[192,128]{1,0:T(8,128)(2,1)S(1)} collective-permute-done((bf16[192,128]{1,0:T(8,128)(2,1)S(1)}, bf16[192,128]{1,0:T(8,128)(2,1)S(1)}, u32[]{:S(2)}, u32[]{:S(2)}) %collective-permute-start.28) | collective-permute-done | bytes 49184 | tf_op jit(solution)/shard_map/ppermute | solution.py:359
  (113 shorter events, 19.8 us)
Async XLA Ops:
  1.5 1.6 %collective-permute-start = (bf16[2,1,64,128]{3,2,1,0:T(8,128)(2,1)S(1)}, bf16[2,1,64,128]{3,2,1,0:T(8,128)(2,1)S(1)}, u32[]{:S(2)}, u32[]{:S(2)}) collective-permute-start(bf16[2,1,64,128]{3,2,1,0:T(8,128)(2,1)S(1)} %add_convert_fusion.1), channel_id=1, source_target_pairs={{0,1},{1,0},{2,3},{3,2},{4,5},{5,4},{6,7},{7,6},{8,9},{9,8},{10,11... | collective-permute-start | bytes 98312 | tf_op jit(solution)/shard_map/ppermute | solution.py:71
  5.2 4.0 %collective-permute-start.2 = (bf16[1,8,64,128]{3,2,1,0:T(8,128)(2,1)S(1)}, bf16[1,8,64,128]{3,2,1,0:T(8,128)(2,1)S(1)}, u32[]{:S(2)}, u32[]{:S(2)}) collective-permute-start(bf16[1,8,64,128]{3,2,1,0:T(8,128)(2,1)S(1)} %shard_map.69), channel_id=1, source_target_pairs={{24,16},{26,18},{28,20},{30,22},{25,17},{27,19},{29,21},{31,23}} | collective-permute-start | bytes 393224 | tf_op jit(solution)/shard_map/ppermute | solution.py:279
  5.8 3.3 %collective-permute-start.3 = (bf16[1,8,64,128]{3,2,1,0:T(8,128)(2,1)S(1)}, bf16[1,8,64,128]{3,2,1,0:T(8,128)(2,1)S(1)}, u32[]{:S(2)}, u32[]{:S(2)}) collective-permute-start(bf16[1,8,64,128]{3,2,1,0:T(8,128)(2,1)S(1)} %shard_map.69), channel_id=1, source_target_pairs={{28,16},{30,18},{24,20},{26,22},{29,17},{31,19},{25,21},{27,23}} | collective-permute-start | bytes 393224 | tf_op jit(solution)/shard_map/ppermute | solution.py:317
  7.8 4.7 %collective-permute-start.10 = (bf16[1,8,64,128]{3,2,1,0:T(8,128)(2,1)S(1)}, bf16[1,8,64,128]{3,2,1,0:T(8,128)(2,1)S(1)}, u32[]{:S(2)}, u32[]{:S(2)}) collective-permute-start(bf16[1,8,64,128]{3,2,1,0:T(8,128)(2,1)S(1)} %shard_map.71), channel_id=1, source_target_pairs={{28,16},{30,18},{24,20},{26,22},{29,17},{31,19},{25,21},{27,23}} | collective-permute-start | bytes 393224 | tf_op jit(solution)/shard_map/ppermute | solution.py:317
  8.5 4.0 %collective-permute-start.9 = (bf16[1,8,64,128]{3,2,1,0:T(8,128)(2,1)S(1)}, bf16[1,8,64,128]{3,2,1,0:T(8,128)(2,1)S(1)}, u32[]{:S(2)}, u32[]{:S(2)}) collective-permute-start(bf16[1,8,64,128]{3,2,1,0:T(8,128)(2,1)S(1)} %shard_map.71), channel_id=1, source_target_pairs={{24,16},{26,18},{28,20},{30,22},{25,17},{27,19},{29,21},{31,23}} | collective-permute-start | bytes 393224 | tf_op jit(solution)/shard_map/ppermute | solution.py:279
  10.5 5.3 %collective-permute-start.6 = (bf16[1,8,64,128]{3,2,1,0:T(8,128)(2,1)S(1)}, bf16[1,8,64,128]{3,2,1,0:T(8,128)(2,1)S(1)}, u32[]{:S(2)}, u32[]{:S(2)}) collective-permute-start(bf16[1,8,64,128]{3,2,1,0:T(8,128)(2,1)S(1)} %shard_map.73), channel_id=1, source_target_pairs={{16,8},{18,10},{20,12},{22,14},{17,9},{19,11},{21,13},{23,15}} | collective-permute-start | bytes 393224 | tf_op jit(solution)/shard_map/ppermute | solution.py:279
  11.1 5.3 %collective-permute-start.7 = (bf16[1,8,64,128]{3,2,1,0:T(8,128)(2,1)S(1)}, bf16[1,8,64,128]{3,2,1,0:T(8,128)(2,1)S(1)}, u32[]{:S(2)}, u32[]{:S(2)}) collective-permute-start(bf16[1,8,64,128]{3,2,1,0:T(8,128)(2,1)S(1)} %shard_map.73), channel_id=1, source_target_pairs={{18,8},{20,10},{22,12},{19,9},{21,11},{23,13}} | collective-permute-start | bytes 393224 | tf_op jit(solution)/shard_map/ppermute | solution.py:279
  11.8 4.7 %collective-permute-start.8 = (bf16[1,8,64,128]{3,2,1,0:T(8,128)(2,1)S(1)}, bf16[1,8,64,128]{3,2,1,0:T(8,128)(2,1)S(1)}, u32[]{:S(2)}, u32[]{:S(2)}) collective-permute-start(bf16[1,8,64,128]{3,2,1,0:T(8,128)(2,1)S(1)} %shard_map.73), channel_id=1, source_target_pairs={{16,10},{18,12},{20,14},{17,11},{19,13},{21,15}} | collective-permute-start | bytes 393224 | tf_op jit(solution)/shard_map/ppermute | solution.py:279
  14.4 4.0 %collective-permute-start.14 = (bf16[1,8,64,128]{3,2,1,0:T(8,128)(2,1)S(1)}, bf16[1,8,64,128]{3,2,1,0:T(8,128)(2,1)S(1)}, u32[]{:S(2)}, u32[]{:S(2)}) collective-permute-start(bf16[1,8,64,128]{3,2,1,0:T(8,128)(2,1)S(1)} %shard_map.75), channel_id=1, source_target_pairs={{16,8},{18,10},{20,12},{22,14},{17,9},{19,11},{21,13},{23,15}} | collective-permute-start | bytes 393224 | tf_op jit(solution)/shard_map/ppermute | solution.py:279
  15.1 3.3 %collective-permute-start.15 = (bf16[1,8,64,128]{3,2,1,0:T(8,128)(2,1)S(1)}, bf16[1,8,64,128]{3,2,1,0:T(8,128)(2,1)S(1)}, u32[]{:S(2)}, u32[]{:S(2)}) collective-permute-start(bf16[1,8,64,128]{3,2,1,0:T(8,128)(2,1)S(1)} %shard_map.75), channel_id=1, source_target_pairs={{18,8},{20,10},{22,12},{19,9},{21,11},{23,13}} | collective-permute-start | bytes 393224 | tf_op jit(solution)/shard_map/ppermute | solution.py:279
  15.8 2.7 %collective-permute-start.16 = (bf16[1,8,64,128]{3,2,1,0:T(8,128)(2,1)S(1)}, bf16[1,8,64,128]{3,2,1,0:T(8,128)(2,1)S(1)}, u32[]{:S(2)}, u32[]{:S(2)}) collective-permute-start(bf16[1,8,64,128]{3,2,1,0:T(8,128)(2,1)S(1)} %shard_map.75), channel_id=1, source_target_pairs={{16,10},{18,12},{20,14},{17,11},{19,13},{21,15}} | collective-permute-start | bytes 393224 | tf_op jit(solution)/shard_map/ppermute | solution.py:279
  19.2 2.8 %collective-permute-start.17 = (bf16[1,1,64,128]{3,2,1,0:T(8,128)(2,1)S(1)}, bf16[1,1,64,128]{3,2,1,0:T(8,128)(2,1)S(1)}, u32[]{:S(2)}, u32[]{:S(2)}) collective-permute-start(bf16[1,1,64,128]{3,2,1,0:T(8,128)(2,1)S(1)} %get-tuple-element.72), channel_id=1, source_target_pairs={{0,1},{1,0},{2,3},{3,2},{4,5},{5,4},{6,7},{7,6},{8,9},{9,8},{10,11... | collective-permute-start | bytes 49160 | tf_op jit(solution)/shard_map/ppermute | solution.py:71
  19.4 26.6 %collective-permute-start.13 = (bf16[1,8,64,128]{3,2,1,0:T(8,128)(2,1)}, bf16[1,8,64,128]{3,2,1,0:T(8,128)(2,1)S(1)}, u32[]{:S(2)}, u32[]{:S(2)}) collective-permute-start(bf16[1,8,64,128]{3,2,1,0:T(8,128)(2,1)} %shard_map.77), channel_id=1, source_target_pairs={{8,0},{10,2},{12,4},{14,6},{9,1},{11,3},{13,5},{15,7}} | collective-permute-start | bytes 393224 | tf_op jit(solution)/shard_map/ppermute | solution.py:279
  20.6 30.8 %collective-permute-start.20 = (bf16[1,8,64,128]{3,2,1,0:T(8,128)(2,1)}, bf16[1,8,64,128]{3,2,1,0:T(8,128)(2,1)}, u32[]{:S(2)}, u32[]{:S(2)}) collective-permute-start(bf16[1,8,64,128]{3,2,1,0:T(8,128)(2,1)} %shard_map.77), channel_id=1, source_target_pairs={{10,0},{12,2},{14,4},{11,1},{13,3},{15,5}} | collective-permute-start | bytes 393224 | tf_op jit(solution)/shard_map/ppermute | solution.py:279
  22.6 29.8 %collective-permute-start.18 = (bf16[1,8,64,128]{3,2,1,0:T(8,128)(2,1)}, bf16[1,8,64,128]{3,2,1,0:T(8,128)(2,1)S(1)}, u32[]{:S(2)}, u32[]{:S(2)}) collective-permute-start(bf16[1,8,64,128]{3,2,1,0:T(8,128)(2,1)} %shard_map.79), channel_id=1, source_target_pairs={{8,0},{10,2},{12,4},{14,6},{9,1},{11,3},{13,5},{15,7}} | collective-permute-start | bytes 393224 | tf_op jit(solution)/shard_map/ppermute | solution.py:279
  23.9 28.5 %collective-permute-start.19 = (bf16[1,8,64,128]{3,2,1,0:T(8,128)(2,1)}, bf16[1,8,64,128]{3,2,1,0:T(8,128)(2,1)}, u32[]{:S(2)}, u32[]{:S(2)}) collective-permute-start(bf16[1,8,64,128]{3,2,1,0:T(8,128)(2,1)} %shard_map.79), channel_id=1, source_target_pairs={{8,2},{10,4},{12,6},{9,3},{11,5},{13,7}} | collective-permute-start | bytes 393224 | tf_op jit(solution)/shard_map/ppermute | solution.py:279
  57.1 9.0 %collective-permute-start.23 = (bf16[192,128]{1,0:T(8,128)(2,1)S(1)}, bf16[192,128]{1,0:T(8,128)(2,1)S(1)}, u32[]{:S(2)}, u32[]{:S(2)}) collective-permute-start(bf16[192,128]{1,0:T(8,128)(2,1)S(1)} %get-tuple-element.95), channel_id=1, source_target_pairs={{0,2},{2,0},{4,6},{6,4},{1,3},{3,1},{5,7},{7,5},{8,10},{10,8},{12,... | collective-permute-start | bytes 147464 | tf_op jit(solution)/shard_map/ppermute | solution.py:340
  63.7 7.0 %collective-permute-start.24 = (bf16[192,128]{1,0:T(8,128)(2,1)S(1)}, bf16[192,128]{1,0:T(8,128)(2,1)S(1)}, u32[]{:S(2)}, u32[]{:S(2)}) collective-permute-start(bf16[192,128]{1,0:T(8,128)(2,1)S(1)} %get-tuple-element.97), channel_id=1, source_target_pairs={{0,4},{2,6},{4,0},{6,2},{1,5},{3,7},{5,1},{7,3},{8,12},{10,14},{12... | collective-permute-start | bytes 147464 | tf_op jit(solution)/shard_map/ppermute | solution.py:340
  64.4 6.3 %collective-permute-start.25 = (bf16[192,128]{1,0:T(8,128)(2,1)S(1)}, bf16[192,128]{1,0:T(8,128)(2,1)S(1)}, u32[]{:S(2)}, u32[]{:S(2)}) collective-permute-start(bf16[192,128]{1,0:T(8,128)(2,1)S(1)} %get-tuple-element.96), channel_id=1, source_target_pairs={{0,6},{2,4},{4,2},{6,0},{1,7},{3,5},{5,3},{7,1},{8,14},{10,12},{12... | collective-permute-start | bytes 147464 | tf_op jit(solution)/shard_map/ppermute | solution.py:340
  66.1 5.8 %collective-permute-start.22 = (bf16[2,1,64,128]{3,2,1,0:T(8,128)(2,1)S(1)}, bf16[2,1,64,128]{3,2,1,0:T(8,128)(2,1)S(1)}, u32[]{:S(2)}, u32[]{:S(2)}) collective-permute-start(bf16[2,1,64,128]{3,2,1,0:T(8,128)(2,1)S(1)} %get-tuple-element.90), channel_id=1, source_target_pairs={{0,1},{1,0},{2,3},{3,2},{4,5},{5,4},{6,7},{7,6},{8,9},{9,8},{10,11... | collective-permute-start | bytes 98312 | tf_op jit(solution)/shard_map/ppermute | solution.py:71
  70.8 5.2 %collective-permute-start.26 = (bf16[192,128]{1,0:T(8,128)(2,1)S(1)}, bf16[192,128]{1,0:T(8,128)(2,1)S(1)}, u32[]{:S(2)}, u32[]{:S(2)}) collective-permute-start(bf16[192,128]{1,0:T(8,128)(2,1)S(1)} %get-tuple-element.94), channel_id=1, source_target_pairs={{0,2},{2,0},{4,6},{6,4},{1,3},{3,1},{5,7},{7,5},{8,10},{10,8},{12,... | collective-permute-start | bytes 147464 | tf_op jit(solution)/shard_map/ppermute | solution.py:359
  72.6 5.6 %collective-permute-start.27 = (bf16[192,128]{1,0:T(8,128)(2,1)S(1)}, bf16[192,128]{1,0:T(8,128)(2,1)S(1)}, u32[]{:S(2)}, u32[]{:S(2)}) collective-permute-start(bf16[192,128]{1,0:T(8,128)(2,1)S(1)} %get-tuple-element.94), channel_id=1, source_target_pairs={{0,4},{2,6},{4,0},{6,2},{1,5},{3,7},{5,1},{7,3},{8,12},{10,14},{12... | collective-permute-start | bytes 147464 | tf_op jit(solution)/shard_map/ppermute | solution.py:359
  74.1 5.9 %collective-permute-start.28 = (bf16[192,128]{1,0:T(8,128)(2,1)S(1)}, bf16[192,128]{1,0:T(8,128)(2,1)S(1)}, u32[]{:S(2)}, u32[]{:S(2)}) collective-permute-start(bf16[192,128]{1,0:T(8,128)(2,1)S(1)} %get-tuple-element.94), channel_id=1, source_target_pairs={{0,6},{2,4},{4,2},{6,0},{1,7},{3,5},{5,3},{7,1},{8,14},{10,12},{12... | collective-permute-start | bytes 147464 | tf_op jit(solution)/shard_map/ppermute | solution.py:359
  80.0 1.5 %collective-permute-start.29 = (bf16[768,128]{1,0:T(8,128)(2,1)S(1)}, bf16[768,128]{1,0:T(8,128)(2,1)S(1)}, u32[]{:S(2)}, u32[]{:S(2)}) collective-permute-start(bf16[768,128]{1,0:T(8,128)(2,1)S(1)} %constant_dynamic-update-slice_fusion), channel_id=1, source_target_pairs={{0,1},{1,0},{2,3},{3,2},{4,5},{5,4},{6,7},{7,6},{8,9},{9,8},{10,11... | collective-permute-start | bytes 589832 | tf_op jit(solution)/shard_map/ppermute | solution.py:443
  (27 other events, 55.9 us)

commit v4 on v3

v4 whole, which is shorter than its diff:
```python
import jax
import jax.numpy as jnp
from jax import lax
from jax.experimental import pallas as pl
from jax.experimental.pallas import tpu as pltpu
from jax.sharding import PartitionSpec as P

VMEM_LIMIT = 40 * 1024 * 1024
NT = (((1,), (1,)), ((), ()))
NN = (((1,), (0,)), ((), ()))
TN = (((0,), (0,)), ((), ()))


def mul(a, b, how):
    return lax.dot_general(a, b, how, preferred_element_type=jnp.float32)


def call(body, outs, args, flops):
    moved = sum(a.size * a.dtype.itemsize for a in (*args, *outs))
    return pl.pallas_call(
        body,
        out_shape=outs,
        in_specs=[pl.BlockSpec(memory_space=pltpu.VMEM) for _ in args],
        out_specs=[pl.BlockSpec(memory_space=pltpu.VMEM) for _ in outs],
        compiler_params=pltpu.CompilerParams(vmem_limit_bytes=VMEM_LIMIT),
        cost_estimate=pl.CostEstimate(flops=flops, bytes_accessed=moved, transcendentals=0),
    )(*args)


def flat(values):
    return values.reshape(-1, values.shape[-1])


def row_sides(got, row_count):
    if len(got) == 1:
        first = (lax.axis_index("row") == 0).astype(jnp.float32)
        rows = got[0].astype(jnp.float32)
        return (rows * (1.0 - first)).astype(jnp.bfloat16), (rows * first).astype(jnp.bfloat16)
    return got


def moved_rows(cells, above, below):
    return (
        flat(jnp.concatenate([above, cells[:, :-1]], axis=1)),
        flat(cells),
        flat(jnp.concatenate([cells[:, 1:], below], axis=1)),
    )


def moved_cols(values, step, col_count):
    count, lanes = values.shape
    shape = (count // col_count, col_count, lanes)
    col = lax.broadcasted_iota(jnp.int32, shape, 1).reshape(count, lanes)
    if step == 1:
        return jnp.where(col == col_count - 1, 0.0, pltpu.roll(values, count - 1, 0))
    return jnp.where(col == 0, 0.0, pltpu.roll(values, 1, 0))


def edges_of(cells, row_parts):
    head, tail = cells[:, :1], cells[:, -1:]
    if row_parts == 2:
        first = (lax.axis_index("row") == 0).astype(jnp.float32)
        return [(tail.astype(jnp.float32) * first + head.astype(jnp.float32) * (1.0 - first)).astype(jnp.bfloat16)]
    return [head, tail]


def swap_edges(edges):
    count = lax.axis_size("row")
    if count == 2:
        return [lax.ppermute(edges[0], "row", [(0, 1), (1, 0)])]
    head, tail = edges
    if count == 1:
        return [jnp.zeros_like(head), jnp.zeros_like(head)]
    return [
        lax.ppermute(tail, "row", [(i, i + 1) for i in range(count - 1)]),
        lax.ppermute(head, "row", [(i + 1, i) for i in range(count - 1)]),
    ]


def split_frames(values, chains):
    if chains == 1:
        return [values]
    pairs = values.reshape((values.shape[0] // chains, chains) + values.shape[1:])
    return [pairs[:, at] for at in range(chains)]


def windows(cells, rows):
    return jnp.concatenate([flat(cells[:, i : i + rows]) for i in range(3)], axis=1)


def is_one_of(section, sections):
    found = section == sections[0]
    for other in sections[1:]:
        found |= section == other
    return found


def forward(block_input, got, taps_space, chains, sections, dealt=()):
    frames, rows, cols, channels = block_input.shape
    part = (frames // chains, rows, cols, channels)
    args = list(dealt) or [block_input, *got]

    def body(*refs):
        section = lax.axis_index("section")
        pl.when(is_one_of(section, sections))(lambda: work(section, *refs))

    def work(section, *refs):
        w_ref, x_ref = refs[len(args) : len(args) + 2]
        slope_refs = refs[len(args) + 2 : len(args) + 2 + chains]
        active_refs = refs[len(args) + 2 + chains :]
        if dealt:
            first = jnp.where(section == 1, lax.axis_index("frame") % 2, 0)
            x_ref[first] = refs[0][0]
            x_ref[1 - first] = refs[1][0]
        else:
            above, below = row_sides([ref[...] for ref in refs[1 : len(args)]], rows)
            x_ref[...] = jnp.concatenate([above, refs[0][...], below], axis=1)
        taps = jnp.concatenate(
            [jnp.concatenate([w_ref[i, j] for j in range(3)], axis=1) for i in range(3)], axis=0
        )
        sums = mul(windows(x_ref[...], rows), taps, NN)
        pre_act = (
            moved_cols(sums[:, :channels], -1, cols)
            + sums[:, channels : 2 * channels]
            + moved_cols(sums[:, 2 * channels :], 1, cols)
        )
        sigma = jax.nn.sigmoid(pre_act)
        slope = (sigma * (1.0 + pre_act * (1.0 - sigma))).reshape(block_input.shape)
        active = (pre_act * sigma).astype(jnp.bfloat16).reshape(block_input.shape)
        for ref, values in zip(slope_refs, split_frames(slope, chains)):
            ref[...] = values
        for ref, values in zip(active_refs, split_frames(active, chains)):
            ref[...] = values

    outs = [jax.ShapeDtypeStruct((frames, rows + 2, cols, channels), jnp.bfloat16)]
    outs += [jax.ShapeDtypeStruct(part, jnp.float32)] * chains
    outs += [jax.ShapeDtypeStruct(part, jnp.bfloat16)] * chains
    outs = call(body, outs, [*args, taps_space], 18 * block_input.size * channels)
    return outs[0], outs[1 : 1 + chains], outs[1 + chains :]


def early_half(distance_step):
    return lambda: (lax.axis_index("frame") < lax.axis_size("frame") - distance_step).astype(
        jnp.float32
    )


def mixed(early, later, earlier):
    return early * later.astype(jnp.float32) + (1.0 - early) * earlier.astype(jnp.float32)


def temporal(owner, triples, slopes, taps_time):
    row_parts = lax.axis_size("row")
    part = slopes[0].shape
    channels = part[-1]
    edges = 1 if row_parts == 2 else 2
    sizes = [len(blocks) for blocks, _ in triples]

    def body(*refs):
        @pl.when(lax.axis_index("section") == owner)
        def _():
            at = 0
            w_ref = refs[sum(sizes) + len(slopes)]
            outs = refs[sum(sizes) + len(slopes) + 1 :]
            for chain, size in enumerate(sizes):
                blocks = [flat(ref[...]) for ref in refs[at : at + size]]
                at += size
                taps = [w_ref[1]]
                early = triples[chain][1]
                if size > 1 and early is None:
                    taps += [w_ref[0], w_ref[2]]
                elif size > 1:
                    taps.append(mixed(early(), w_ref[0], w_ref[2]).astype(jnp.bfloat16))
                    taps.append(mixed(early(), w_ref[2], w_ref[0]).astype(jnp.bfloat16))
                taps = taps[:size]
                sums = mul(jnp.concatenate(blocks, axis=1), jnp.concatenate(taps, axis=1), NT)
                back_act = sums.astype(jnp.bfloat16).astype(jnp.float32)
                slope = flat(refs[sum(sizes) + chain][...])
                grad_pre = (back_act * slope).astype(jnp.bfloat16).reshape(part)
                outs[chain][...] = grad_pre
                for ref, edge in zip(outs[len(slopes) :], edges_of(grad_pre, row_parts)):
                    ref[chain * part[0] : (chain + 1) * part[0]] = edge

    outs = [jax.ShapeDtypeStruct(part, jnp.bfloat16)] * len(slopes)
    outs += [
        jax.ShapeDtypeStruct((part[0] * len(slopes), 1) + part[2:], jnp.bfloat16)
    ] * edges
    args = [block for blocks, _ in triples for block in blocks] + list(slopes) + [taps_time]
    outs = call(body, outs, args, 6 * sum(s.size for s in slopes) * channels)
    return outs[: len(slopes)], outs[len(slopes) :]


def branches(owner, grads_pre, got, heres, taps_space, picks=None, before=()):
    part = heres[0].shape
    _, rows, cols, channels = part
    count = len(heres)
    picks = picks or list(range(count))
    fixed = 2 * count + len(got) + 1

    def body(*refs):
        section = lax.axis_index("section")
        out_refs = refs[fixed + len(before) :]

        if before:

            @pl.when(section != owner)
            def _():
                for ref, out_ref in zip(refs[fixed:], out_refs[-len(before) :]):
                    out_ref[...] = ref[...]

        @pl.when(section == owner)
        def _():
            got_refs = refs[count : count + len(got)]
            here_refs = refs[count + len(got) : 2 * count + len(got)]
            w_ref = refs[2 * count + len(got)]
            taps = jnp.concatenate(
                [jnp.concatenate([w_ref[2 - i, j] for i in range(3)], axis=1) for j in range(3)],
                axis=0,
            )
            for chain in range(count):
                frames = slice(chain * part[0], (chain + 1) * part[0])
                above, below = row_sides([ref[frames] for ref in got_refs], rows)
                sides = jnp.concatenate(moved_rows(refs[chain][...], above, below), axis=1)
                sums = mul(sides, taps, NT)
                branch = (
                    moved_cols(sums[:, :channels], 1, cols)
                    + sums[:, channels : 2 * channels]
                    + moved_cols(sums[:, 2 * channels :], -1, cols)
                )
                branch = branch.astype(jnp.bfloat16).astype(jnp.float32)
                here = flat(here_refs[chain][...]).astype(jnp.float32)
                out = (here + branch).astype(jnp.bfloat16).reshape(part)
                for ref, pick in zip(out_refs, picks):
                    if callable(pick):
                        wanted = pick() if chain == 0 else jnp.logical_not(pick())
                        pl.when(wanted)(lambda ref=ref, out=out: ref.__setitem__(..., out))
                    elif pick == chain:
                        ref[...] = out

    outs = [jax.ShapeDtypeStruct(part, jnp.bfloat16)] * len(picks)
    args = [*grads_pre, *got, *heres, taps_space, *before]
    return call(body, outs, args, 18 * sum(h.size for h in heres) * channels)


def kernel_grads(owner, x_rows, grads_pre, actives, triples, before):
    _, rows, cols, channels = x_rows.shape
    rows -= 2
    chains = len(actives)

    def body(*refs):
        section = lax.axis_index("section")
        out_ref = refs[-1]

        if before is not None:

            @pl.when(section != owner)
            def _():
                out_ref[...] = refs[-2][...]

        @pl.when(section == owner)
        def _():
            sides = [windows(cells, rows) for cells in split_frames(refs[0][...], chains)]
            pre = []
            time = [jnp.zeros((channels, channels), jnp.float32)] * 3
            at = 1 + 2 * chains
            for chain, (blocks, early) in enumerate(triples):
                mid = flat(refs[1 + chain][...])
                wide = mid.astype(jnp.float32)
                left = moved_cols(wide, 1, cols).astype(jnp.bfloat16)
                right = moved_cols(wide, -1, cols).astype(jnp.bfloat16)
                pre.append(jnp.concatenate([left, mid, right], axis=1))
                size = len(blocks)
                values = jnp.concatenate([flat(ref[...]) for ref in refs[at : at + size]], axis=1)
                at += size
                product = mul(flat(refs[1 + chains + chain][...]), values, TN)
                terms = [product[:, k * channels : (k + 1) * channels] for k in range(size)]
                time[1] = time[1] + terms[0]
                if size > 1 and early is None:
                    time[0] = time[0] + terms[1]
                    time[2] = time[2] + terms[2]
                elif size > 1:
                    share = early()
                    other = terms[2] if size == 3 else jnp.zeros_like(terms[1])
                    time[0] = time[0] + mixed(share, terms[1], other)
                    time[2] = time[2] + mixed(share, other, terms[1])
            space = mul(jnp.concatenate(sides), jnp.concatenate(pre), TN)
            for i in range(3):
                for j in range(3):
                    out_ref[3 * i + j] = space[
                        i * channels : (i + 1) * channels, j * channels : (j + 1) * channels
                    ]
            for k in range(3):
                out_ref[9 + k] = time[k]

    args = [x_rows, *grads_pre, *actives]
    args += [block for blocks, _ in triples for block in blocks]
    if before is not None:
        args.append(before)
    outs = [jax.ShapeDtypeStruct((12, channels, channels), jnp.float32)]
    return call(body, outs, args, 24 * x_rows.size * channels)[0]


def place_first(section):
    place = lax.axis_index("frame")
    return jnp.where(section == 2, place // 2, jnp.where((place == 0) | (place == 3), 1, 0))


def frames_to_deal(block_input, got):
    _, rows, cols, channels = block_input.shape

    def body(*refs):
        section = lax.axis_index("section")

        @pl.when(is_one_of(section, (1, 2)))
        def _():
            above, below = row_sides([ref[...] for ref in refs[1 : 1 + len(got)]], rows)
            cells = jnp.concatenate([above, refs[0][...], below], axis=1)
            first = place_first(section)
            for frame in range(2):

                @pl.when(first == frame)
                def _():
                    refs[-2][...] = cells[frame : frame + 1]
                    refs[-1][...] = cells[1 - frame : 2 - frame]

    outs = [jax.ShapeDtypeStruct((1, rows + 2, cols, channels), jnp.bfloat16)] * 2
    return call(body, outs, [block_input, *got], 0)


def line_up(pieces):
    table = ((None, 0, 1, 2), (0, 3, 2, 4), (3, 2, 4, 0), (2, 1, 0, None))

    def body(*refs):
        for place, order in enumerate(table):

            @pl.when((lax.axis_index("section") == 0) & (lax.axis_index("frame") == place))
            def _():
                for ref, at in zip(refs[len(pieces) :], order):
                    ref[...] = jnp.zeros(ref.shape, ref.dtype) if at is None else refs[at][...]

    return call(body, [jax.ShapeDtypeStruct(pieces[0].shape, jnp.bfloat16)] * 4, pieces, 0)


def own_result(tops, returned, lasts):
    shape = (2,) + lasts[0].shape[1:]

    def body(*refs):
        section = lax.axis_index("section")
        place = lax.axis_index("frame")
        out_ref = refs[-1]

        @pl.when(section == 3)
        def _():
            out_ref[place // 2] = refs[0][0]
            out_ref[1 - place // 2] = refs[1][0]

        @pl.when(is_one_of(section, (1, 2)))
        def _():
            first = place_first(section)
            out_ref[first] = refs[2][0]
            out_ref[1 - first] = refs[3][0]

        @pl.when(section == 0)
        def _():
            out_ref[0] = refs[4][0]
            out_ref[1] = refs[5][0]

    outs = [jax.ShapeDtypeStruct(shape, jnp.bfloat16)]
    return call(body, outs, [*tops, *returned, *lasts], 0)[0]


def fetch(block, source, target, frame_step):
    frame_parts = lax.axis_size("frame")
    route = [
        (source * frame_parts + z + frame_step, target * frame_parts + z)
        for z in range(frame_parts)
        if 0 <= z + frame_step < frame_parts
    ]
    if not route:
        return jnp.zeros_like(block)
    if source == target and frame_step == 0:
        return block
    return lax.ppermute(block, ("section", "frame"), route)


def shifted_from(block, source, target, offset, unmoved=None):
    own_frames = block.shape[0]
    step, rest = divmod(offset, own_frames)
    pieces = []
    for frames, move in ((slice(rest, None), step), (slice(0, rest), step + 1)):
        piece = block[frames]
        if piece.shape[0] == 0:
            continue
        if move == 0 and unmoved is not None:
            pieces.append(unmoved[frames])
        else:
            pieces.append(fetch(piece, source, target, move))
    return pieces[0] if len(pieces) == 1 else jnp.concatenate(pieces)


def pair_step_of(own_frames, distance):
    step, rest = divmod(distance, own_frames)
    frame_parts = lax.axis_size("frame")
    return step if rest == 0 and frame_parts <= 2 * step < 2 * frame_parts else 0


def triple_from(block, source, target, distance, staged):
    own_frames = block.shape[0]
    frame_parts = lax.axis_size("frame")
    own = fetch(block, source, target, 0)
    if distance >= frame_parts * own_frames:
        return [own]
    step = pair_step_of(own_frames, distance)
    if step:
        route = [
            (source * frame_parts + z + move, target * frame_parts + z)
            for z in range(frame_parts)
            for move in (step, -step)
            if 0 <= z + move < frame_parts
        ]
        return [own, lax.ppermute(block, ("section", "frame"), route)]
    if staged:
        block, source = own, target
    return [
        own,
        shifted_from(block, source, target, distance, own),
        shifted_from(block, source, target, -distance, own),
    ]


def by_pairs(axis):
    count = lax.axis_size(axis)
    return count <= 4 and count & (count - 1) == 0


def sum_over(values, axis, beside=None):
    count = lax.axis_size(axis)
    index = lax.axis_index(axis)
    if not by_pairs(axis):
        parts = values.astype(jnp.bfloat16).reshape((count, -1) + values.shape[1:])
        parts = lax.all_to_all(parts, axis, split_axis=0, concat_axis=0, tiled=True)
        return jnp.sum(parts.astype(jnp.float32), axis=0), beside and beside(values)
    size = values.shape[0] // count
    total = lax.dynamic_slice_in_dim(values, index * size, size, 0)
    parts = [
        lax.dynamic_slice_in_dim(values, (index ^ mask) * size, size, 0).astype(jnp.bfloat16)
        for mask in range(1, count)
    ]
    other = beside and beside(parts)
    parts = [
        lax.ppermute(part, axis, [(i, i ^ mask) for i in range(count)])
        for mask, part in enumerate(parts, 1)
    ]
    if beside:
        parts = after(parts, other)
    for part in parts:
        total += part.astype(jnp.float32)
    return total, other


def gather_parts(part, axis):
    if not by_pairs(axis):
        return lax.all_gather(part, axis, axis=0, tiled=True)
    count = lax.axis_size(axis)
    index = lax.axis_index(axis)
    size = part.shape[0]
    whole = jnp.zeros((count * size,) + part.shape[1:], part.dtype)
    whole = lax.dynamic_update_slice_in_dim(whole, part, index * size, 0)
    for mask in range(1, count):
        got = lax.ppermute(part, axis, [(i, i ^ mask) for i in range(count)])
        whole = lax.dynamic_update_slice_in_dim(whole, got, (index ^ mask) * size, 0)
    return whole


def after(values, *others):
    return list(lax.optimization_barrier((tuple(values), others))[0])


def shifted_chains(x_got, block_input, cotangent, taps_space, taps_time):
    own_frames = block_input.shape[0]
    section_count = lax.axis_size("section")
    chains = 1 if own_frames % 2 else 2
    top = section_count - 1

    def triples(blocks, source, target):
        dilation = 2**target
        if dilation % chains == 0:
            step = pair_step_of(own_frames // chains, dilation // chains)
            early = early_half(step) if step else None
            return [
                (triple_from(block, source, target, dilation // chains, False), early)
                for block in blocks
            ]
        even, odd = blocks
        own_even = fetch(even, source, target, 0)
        next_even = shifted_from(even, source, target, (dilation + 1) // 2, own_even)
        own_odd = fetch(odd, source, target, 0)
        last_odd = shifted_from(odd, source, target, -((dilation + 1) // 2), own_odd)
        same_odd = shifted_from(odd, source, target, (dilation - 1) // 2, own_odd)
        same_even = shifted_from(even, source, target, -((dilation - 1) // 2), own_even)
        return [([own_even, same_odd, last_odd], None), ([own_odd, next_even, same_even], None)]

    everywhere = tuple(range(section_count))
    x_rows, slopes, actives = forward(block_input, x_got, taps_space, chains, everywhere)
    ready = triples(split_frames(cotangent, chains), top, top)
    grads = None
    results = []
    for owner in reversed(range(section_count)):
        groups = [[chain] for chain in range(chains)] if owner else [list(range(chains))]
        pre, outgoing = [], []
        for group in groups:
            mine = [ready[chain] for chain in group]
            if outgoing or results:
                earlier = outgoing or results[-1]
                mine = [(after(blocks, *earlier), early) for blocks, early in mine]
            group_pre, edges = temporal(owner, mine, [slopes[chain] for chain in group], taps_time)
            pre += group_pre
            if owner:
                heres = [blocks[0] for blocks, _ in mine]
                got = swap_edges(edges)
                outgoing += branches(owner, group_pre, got, heres, taps_space)
        inputs = after(pre, *outgoing) if owner else pre
        grads = kernel_grads(owner, x_rows, inputs, actives, ready, grads)
        if owner:
            results.append(outgoing)
            ready = triples(outgoing, owner, owner - 1)

    def finish(lasts):
        section_index = lax.axis_index("section")
        own = results[0] if results else lasts
        for position, values in enumerate((results + [lasts])[1:], 1):
            own = [
                jnp.where(section_index == top - position, new, old)
                for new, old in zip(values, own)
            ]
        return jnp.stack(own, 1).reshape(block_input.shape)

    return grads, (pre, edges, [blocks[0] for blocks, _ in ready]), finish


def dealt_chains(x_got, block_input, cotangent, taps_space, taps_time):
    def place():
        return lax.axis_index("frame")

    def even():
        return (place() % 2 == 0).astype(jnp.float32)

    def odd():
        return (place() % 2).astype(jnp.float32)

    def low():
        return (place() < 2).astype(jnp.float32)

    def outer():
        return (place() == 0) | (place() == 3)

    def send(block, *hops):
        route = [(a * 4 + i, b * 4 + j) for a, b, moves in hops for i, j in moves]
        return lax.ppermute(block, ("section", "frame"), route)

    def back(moves):
        return [(j, i) for i, j in moves]

    stay = [(i, i) for i in range(4)]
    deal = {
        2: ([(0, 0), (1, 2), (2, 1), (3, 3)], [(0, 1), (1, 3), (2, 0), (3, 2)]),
        1: ([(0, 1), (1, 0), (2, 2), (3, 3)], [(0, 0), (1, 1), (2, 3), (3, 2)]),
    }
    x_dealt = [
        send(block, *((s, s, deal[s][k]) for s in (1, 2)))
        for k, block in enumerate(frames_to_deal(block_input, x_got))
    ]

    def step(owner, triples, slopes, picks, before=()):
        pre, edges = temporal(owner, triples, slopes, taps_time)
        heres = [blocks[0] for blocks, _ in triples]
        outs = branches(owner, pre, swap_edges(edges), heres, taps_space, picks, before)
        return after(pre, *outs), outs

    x_own, slopes_own, actives_own = forward(block_input, x_got, taps_space, 2, (0, 3))
    ready = [([block], None) for block in split_frames(cotangent, 2)]
    pre, tops = step(
        3, ready, slopes_own, [lambda: place() < 2, lambda: place() >= 2]
    )
    first, second = (send(block, (3, 2, deal[2][k])) for k, block in enumerate(tops))
    grads = kernel_grads(3, x_own, pre, actives_own, ready, None)
    x_moved, slopes, actives = forward(
        block_input, x_got, taps_space, 2, (1, 2), after(x_dealt, *tops)
    )

    ready = [([first, second], even), ([second, first], odd)]
    pre, outs = step(2, ready, slopes, [outer, lambda: jnp.logical_not(outer()), 0, 1])
    ends, others, *returned = outs
    end = send(ends, (2, 1, stay))
    other = send(others, (2, 1, stay))
    cross = send(others, (2, 1, [(i, i ^ 2) for i in range(4)]))
    grads = kernel_grads(2, x_moved, pre, actives, ready, grads)

    ready = [([cross, other, end], low), ([end, cross], low)]
    pre, outs = step(
        1, ready, slopes, [0, 1, lambda: place() % 2 == 0, lambda: place() % 2 == 1], returned
    )
    middles, ends, *returned = outs
    pieces = [
        send(ends, (1, 0, stay)),
        send(ends, (1, 0, [(1, 0), (2, 3)])),
        send(middles, (1, 0, stay)),
        send(middles, (1, 0, [(0, 1), (1, 2)])),
        send(middles, (1, 0, [(2, 1), (3, 2)])),
    ]
    grads = kernel_grads(1, x_moved, pre, actives, ready, grads)
    before, one, two, later = line_up(pieces)
    ready = [([one, two, before], None), ([two, later, one], None)]
    pre, edges = temporal(0, ready, slopes_own, taps_time)
    grads = kernel_grads(0, x_own, pre, actives_own, ready, grads)
    returned = [
        send(block, *((s, s, back(deal[s][k])) for s in (1, 2)))
        for k, block in enumerate(returned)
    ]

    def finish(lasts):
        return own_result(tops, returned, lasts)

    return grads, (pre, edges, [one, two]), finish


def section_run(x_saved, cotangent, w_spatial, w_temporal):
    block_input = x_saved[0]
    taps_space = w_spatial[0]
    taps_time = w_temporal[0]
    channels = block_input.shape[-1]
    row_parts = lax.axis_size("row")
    x_got = swap_edges(edges_of(block_input, row_parts))
    shape = (lax.axis_size("section"), lax.axis_size("frame"), block_input.shape[0])
    chains = dealt_chains if shape == (4, 4, 2) else shifted_chains
    grads, (pre, edges, heres), finish = chains(
        x_got, block_input, cotangent, taps_space, taps_time
    )
    total, _ = sum_over(grads.reshape(-1, channels), "row")

    def last_branch(parts):
        return branches(0, pre, swap_edges(after(edges, parts)), heres, taps_space)

    total, lasts = sum_over(total, "frame", last_branch)
    total = gather_parts(total.astype(jnp.bfloat16), "frame")
    split = 9 * channels
    if row_parts == 2:
        first = lax.axis_index("row") == 0
        other = lax.ppermute(total, "row", [(0, 1), (1, 0)])
        rest = split - total.shape[0]
        space = jnp.where(
            first,
            jnp.concatenate([total, other[:rest]]),
            jnp.concatenate([other, total[:rest]]),
        )
        time = jnp.where(first, other[rest:], total[rest:])
    else:
        total = gather_parts(total, "row")
        space, time = total[:split], total[split:]
    return (
        finish(lasts)[None],
        space.astype(jnp.float32).reshape((1, 3, 3, channels, channels)),
        time.astype(jnp.float32).reshape((1, 3, channels, channels)),
    )


def solution(mesh):
    return jax.shard_map(
        section_run,
        mesh=mesh,
        in_specs=(
            P("section", "frame", "row", None, None),
            P("frame", "row", None, None),
            P("section", None, None, None, None),
            P("section", None, None, None),
        ),
        out_specs=(
            P("section", "frame", "row", None, None),
            P("section", None, None, None, None),
            P("section", None, None, None),
        ),
        check_vma=False,
    )
```

time: 83.7 us -> 84.4 us (level)
  the two profiles are of different devices: /device:TPU:0 before, /device:TPU:2 now
where the time goes in v4:
time: 84.4 us; the launch traced here: 84 us
  waiting for transfers between devices  42.6 us (50%)
  starting transfers between devices  28.9 us (34%)
  local copies, waits for them, and re-layouts  4.87 us (6%)
  Pallas kernels  3.81 us (5%)
  other arithmetic  2.58 us (3%)
  between operations  1.16 us (1%)
    ppermute x14, waiting for transfers between devices, send(): return lax.ppermute(block, ('section', 'frame'), route)  30.2 us
    ppermute x14, starting transfers between devices, send(): return lax.ppermute(block, ('section', 'frame'), route)  17.2 us
    ppermute x4, starting transfers between devices, sum_over(): lax.ppermute(part, axis, [(i, i ^ mask) for i in range(count)])  6.41 us
    ppermute x4, waiting for transfers between devices, sum_over(): lax.ppermute(part, axis, [(i, i ^ mask) for i in range(count)])  6.08 us
    ppermute x3, starting transfers between devices, gather_parts(): got = lax.ppermute(part, axis, [(i, i ^ mask) for i in range(count)])  4.45 us
    ppermute x3, waiting for transfers between devices, gather_parts(): got = lax.ppermute(part, axis, [(i, i ^ mask) for i in range(count)])  3.86 us
    pallas_call x17, Pallas kernels, call(): pl.pallas_call(body, out_shape=outs, in_specs=[pl.BlockSpec(memory_space=...  3.81 us
    unnamed x38, local copies, waits for them, and re-layouts  3.71 us
  transfers between devices with their start and end apart: 27, of which 14 were waited for; matrix products, arithmetic and copies ran while one was open for 1% of the time, Pallas kernels for 3%

profile of v4, /device:TPU:2, one launch (start us, length us, event | category | flops | bytes accessed | tf_op | source)
XLA Modules:
  0.0 84.0 jit_solution(13206730784955487725)
XLA Ops:
  4.1 3.5 %collective-permute-start.4 = (bf16[1,10,64,128]{3,2,1,0:T(8,128)(2,1)S(1)}, bf16[1,10,64,128]{3,2,1,0:T(8,128)(2,1)S(1)}, u32[]{:S(2)}, u32[]{:S(2)}) collective-permute-start(bf16[1,10,64,128]{3,2,1,0:T(8,128)(2,1)S(1)} %get-tuple-element.62), channel_id=1, source_target_pairs={{8,10},{10,8},{12,12},{14,14},{16,16},{18,20},{20,18},{22,22},{9,1... | collective-permute-start | bytes 491528 | tf_op jit(solution)/shard_map/ppermute | solution.py:559
  9.7 2.5 %collective-permute-done.4.refs_0_ = bf16[1,10,64,128]{3,2,1,0:T(8,128)(2,1)S(1)} collective-permute-done((bf16[1,10,64,128]{3,2,1,0:T(8,128)(2,1)S(1)}, bf16[1,10,64,128]{3,2,1,0:T(8,128)(2,1)S(1)}, u32[]{:S(2)}, u32[]{:S(2)}) %collective-permute-start.4) | collective-permute-done | bytes 163872 | tf_op jit(solution)/shard_map/ppermute | solution.py:559
  13.2 1.2 %collective-permute-done.6.refs_2_ = bf16[2,1,64,128]{3,2,1,0:T(8,128)(2,1)S(1)} collective-permute-done((bf16[2,1,64,128]{3,2,1,0:T(8,128)(2,1)S(1)}, bf16[2,1,64,128]{3,2,1,0:T(8,128)(2,1)S(1)}, u32[]{:S(2)}, u32[]{:S(2)}) %collective-permute-start.6) | collective-permute-done | bytes 32800 | tf_op jit(solution)/shard_map/ppermute | solution.py:70
  14.4 1.3 %collective-permute-start.7 = (bf16[1,8,64,128]{3,2,1,0:T(8,128)(2,1)S(1)}, bf16[1,8,64,128]{3,2,1,0:T(8,128)(2,1)S(1)}, u32[]{:S(2)}, u32[]{:S(2)}) collective-permute-start(bf16[1,8,64,128]{3,2,1,0:T(8,128)(2,1)S(1)} %get-tuple-element.71), channel_id=1, source_target_pairs={{16,12},{18,14},{20,8},{22,10},{17,13},{19,15},{21,9},{23,11}} | collective-permute-start | bytes 393224 | tf_op jit(solution)/shard_map/ppermute | solution.py:559
  15.7 1.3 %collective-permute-start.8 = (bf16[1,8,64,128]{3,2,1,0:T(8,128)(2,1)S(1)}, bf16[1,8,64,128]{3,2,1,0:T(8,128)(2,1)S(1)}, u32[]{:S(2)}, u32[]{:S(2)}) collective-permute-start(bf16[1,8,64,128]{3,2,1,0:T(8,128)(2,1)S(1)} %get-tuple-element.71), channel_id=1, source_target_pairs={{16,8},{18,10},{20,12},{22,14},{17,9},{19,11},{21,13},{23,15}} | collective-permute-start | bytes 393224 | tf_op jit(solution)/shard_map/ppermute | solution.py:559
  17.0 1.3 %collective-permute-start.9 = (bf16[1,8,64,128]{3,2,1,0:T(8,128)(2,1)S(1)}, bf16[1,8,64,128]{3,2,1,0:T(8,128)(2,1)S(1)}, u32[]{:S(2)}, u32[]{:S(2)}) collective-permute-start(bf16[1,8,64,128]{3,2,1,0:T(8,128)(2,1)S(1)} %get-tuple-element.72), channel_id=1, source_target_pairs={{16,8},{18,10},{20,12},{22,14},{17,9},{19,11},{21,13},{23,15}} | collective-permute-start | bytes 393224 | tf_op jit(solution)/shard_map/ppermute | solution.py:559
  18.3 15.2 %collective-permute-done.7.refs_0_.refs_4_.refs_3_.refs_5_.refs_9_ = bf16[1,8,64,128]{3,2,1,0:T(8,128)(2,1)S(1)} collective-permute-done((bf16[1,8,64,128]{3,2,1,0:T(8,128)(2,1)S(1)}, bf16[1,8,64,128]{3,2,1,0:T(8,128)(2,1)S(1)}, u32[]{:S(2)}, u32[]{:S(2)}) %collective-permute-start.7) | collective-permute-done | bytes 131104 | tf_op jit(solution)/shard_map/ppermute | solution.py:559
  34.3 2.4 %collective-permute-done.9.refs_2_.refs_3_.refs_4_.refs_7_.refs_8_ = bf16[1,8,64,128]{3,2,1,0:T(8,128)(2,1)S(1)} collective-permute-done((bf16[1,8,64,128]{3,2,1,0:T(8,128)(2,1)S(1)}, bf16[1,8,64,128]{3,2,1,0:T(8,128)(2,1)S(1)}, u32[]{:S(2)}, u32[]{:S(2)}) %collective-permute-start.9) | collective-permute-done | bytes 131104 | tf_op jit(solution)/shard_map/ppermute | solution.py:559
  42.0 1.3 %collective-permute-start.13 = (bf16[1,8,64,128]{3,2,1,0:T(8,128)(2,1)S(1)}, bf16[1,8,64,128]{3,2,1,0:T(8,128)(2,1)S(1)}, u32[]{:S(2)}, u32[]{:S(2)}) collective-permute-start(bf16[1,8,64,128]{3,2,1,0:T(8,128)(2,1)S(1)} %get-tuple-element.80), channel_id=1, source_target_pairs={{8,0},{10,2},{12,4},{14,6},{9,1},{11,3},{13,5},{15,7}} | collective-permute-start | bytes 393224 | tf_op jit(solution)/shard_map/ppermute | solution.py:559
  44.0 1.3 %collective-permute-start.15 = (bf16[1,8,64,128]{3,2,1,0:T(8,128)(2,1)S(1)}, bf16[1,8,64,128]{3,2,1,0:T(8,128)(2,1)S(1)}, u32[]{:S(2)}, u32[]{:S(2)}) collective-permute-start(bf16[1,8,64,128]{3,2,1,0:T(8,128)(2,1)S(1)} %get-tuple-element.81), channel_id=1, source_target_pairs={{8,0},{10,2},{12,4},{14,6},{9,1},{11,3},{13,5},{15,7}} | collective-permute-start | bytes 393224 | tf_op jit(solution)/shard_map/ppermute | solution.py:559
  45.3 1.3 %collective-permute-start.16 = (bf16[1,8,64,128]{3,2,1,0:T(8,128)(2,1)S(1)}, bf16[1,8,64,128]{3,2,1,0:T(8,128)(2,1)S(1)}, u32[]{:S(2)}, u32[]{:S(2)}) collective-permute-start(bf16[1,8,64,128]{3,2,1,0:T(8,128)(2,1)S(1)} %get-tuple-element.81), channel_id=1, source_target_pairs={{8,2},{10,4},{9,3},{11,5}} | collective-permute-start | bytes 393224 | tf_op jit(solution)/shard_map/ppermute | solution.py:559
  48.2 1.8 %collective-permute-done.13.refs_0_ = bf16[1,8,64,128]{3,2,1,0:T(8,128)(2,1)S(1)} collective-permute-done((bf16[1,8,64,128]{3,2,1,0:T(8,128)(2,1)S(1)}, bf16[1,8,64,128]{3,2,1,0:T(8,128)(2,1)S(1)}, u32[]{:S(2)}, u32[]{:S(2)}) %collective-permute-start.13) | collective-permute-done | bytes 131104 | tf_op jit(solution)/shard_map/ppermute | solution.py:559
  49.9 2.3 %collective-permute-done.15.refs_2_ = bf16[1,8,64,128]{3,2,1,0:T(8,128)(2,1)S(1)} collective-permute-done((bf16[1,8,64,128]{3,2,1,0:T(8,128)(2,1)S(1)}, bf16[1,8,64,128]{3,2,1,0:T(8,128)(2,1)S(1)}, u32[]{:S(2)}, u32[]{:S(2)}) %collective-permute-start.15) | collective-permute-done | bytes 131104 | tf_op jit(solution)/shard_map/ppermute | solution.py:559
  52.5 1.4 %collective-permute-done.18 = bf16[768,128]{1,0:T(8,128)(2,1)S(1)} collective-permute-done((bf16[768,128]{1,0:T(8,128)(2,1)S(1)}, bf16[768,128]{1,0:T(8,128)(2,1)S(1)}, u32[]{:S(2)}, u32[]{:S(2)}) %collective-permute-start.18) | collective-permute-done | bytes 196640 | tf_op jit(solution)/shard_map/ppermute | solution.py:451
  54.2 4.0 %collective-permute-start.20 = (bf16[192,128]{1,0:T(8,128)(2,1)S(1)}, bf16[192,128]{1,0:T(8,128)(2,1)S(1)}, u32[]{:S(2)}, u32[]{:S(2)}) collective-permute-start(bf16[192,128]{1,0:T(8,128)(2,1)S(1)} %get-tuple-element.111), channel_id=1, source_target_pairs={{0,2},{2,0},{4,6},{6,4},{1,3},{3,1},{5,7},{7,5},{8,10},{10,8},{12,... | collective-permute-start | bytes 147464 | tf_op jit(solution)/shard_map/ppermute | solution.py:451
  58.5 2.1 %collective-permute-start.22 = (bf16[192,128]{1,0:T(8,128)(2,1)S(1)}, bf16[192,128]{1,0:T(8,128)(2,1)S(1)}, u32[]{:S(2)}, u32[]{:S(2)}) collective-permute-start(bf16[192,128]{1,0:T(8,128)(2,1)S(1)} %get-tuple-element.109), channel_id=1, source_target_pairs={{0,6},{2,4},{4,2},{6,0},{1,7},{3,5},{5,3},{7,1},{8,14},{10,12},{12... | collective-permute-start | bytes 147464 | tf_op jit(solution)/shard_map/ppermute | solution.py:451
  60.6 4.7 %collective-permute-done.21 = bf16[192,128]{1,0:T(8,128)(2,1)S(1)} collective-permute-done((bf16[192,128]{1,0:T(8,128)(2,1)S(1)}, bf16[192,128]{1,0:T(8,128)(2,1)S(1)}, u32[]{:S(2)}, u32[]{:S(2)}) %collective-permute-start.21) | collective-permute-done | bytes 49184 | tf_op jit(solution)/shard_map/ppermute | solution.py:451
  65.3 1.2 %collective-permute-start.23 = (bf16[192,128]{1,0:T(8,128)(2,1)S(1)}, bf16[192,128]{1,0:T(8,128)(2,1)S(1)}, u32[]{:S(2)}, u32[]{:S(2)}) collective-permute-start(bf16[192,128]{1,0:T(8,128)(2,1)S(1)} %get-tuple-element.108), channel_id=1, source_target_pairs={{0,2},{2,0},{4,6},{6,4},{1,3},{3,1},{5,7},{7,5},{8,10},{10,8},{12,... | collective-permute-start | bytes 147464 | tf_op jit(solution)/shard_map/ppermute | solution.py:470
  66.5 1.2 %collective-permute-start.24 = (bf16[192,128]{1,0:T(8,128)(2,1)S(1)}, bf16[192,128]{1,0:T(8,128)(2,1)S(1)}, u32[]{:S(2)}, u32[]{:S(2)}) collective-permute-start(bf16[192,128]{1,0:T(8,128)(2,1)S(1)} %get-tuple-element.108), channel_id=1, source_target_pairs={{0,4},{2,6},{4,0},{6,2},{1,5},{3,7},{5,1},{7,3},{8,12},{10,14},{12... | collective-permute-start | bytes 147464 | tf_op jit(solution)/shard_map/ppermute | solution.py:470
  67.8 2.0 %collective-permute-start.25 = (bf16[192,128]{1,0:T(8,128)(2,1)S(1)}, bf16[192,128]{1,0:T(8,128)(2,1)S(1)}, u32[]{:S(2)}, u32[]{:S(2)}) collective-permute-start(bf16[192,128]{1,0:T(8,128)(2,1)S(1)} %get-tuple-element.108), channel_id=1, source_target_pairs={{0,6},{2,4},{4,2},{6,0},{1,7},{3,5},{5,3},{7,1},{8,14},{10,12},{12... | collective-permute-start | bytes 147464 | tf_op jit(solution)/shard_map/ppermute | solution.py:470
  69.8 2.6 %collective-permute-done.24 = bf16[192,128]{1,0:T(8,128)(2,1)S(1)} collective-permute-done((bf16[192,128]{1,0:T(8,128)(2,1)S(1)}, bf16[192,128]{1,0:T(8,128)(2,1)S(1)}, u32[]{:S(2)}, u32[]{:S(2)}) %collective-permute-start.24) | collective-permute-done | bytes 49184 | tf_op jit(solution)/shard_map/ppermute | solution.py:470
  72.4 1.3 %collective-permute-done.25 = bf16[192,128]{1,0:T(8,128)(2,1)S(1)} collective-permute-done((bf16[192,128]{1,0:T(8,128)(2,1)S(1)}, bf16[192,128]{1,0:T(8,128)(2,1)S(1)}, u32[]{:S(2)}, u32[]{:S(2)}) %collective-permute-start.25) | collective-permute-done | bytes 49184 | tf_op jit(solution)/shard_map/ppermute | solution.py:470
  73.8 1.9 %collective-permute-start.11 = (bf16[1,8,64,128]{3,2,1,0:T(8,128)(2,1)S(1)}, bf16[1,8,64,128]{3,2,1,0:T(8,128)(2,1)S(1)}, u32[]{:S(2)}, u32[]{:S(2)}) collective-permute-start(bf16[1,8,64,128]{3,2,1,0:T(8,128)(2,1)S(1)} %copy-done.14), channel_id=1, source_target_pairs={{10,8},{8,10},{12,12},{14,14},{16,16},{20,18},{18,20},{22,22},{11,... | collective-permute-start | bytes 393224 | tf_op jit(solution)/shard_map/ppermute | solution.py:559
  76.4 5.2 %collective-permute-done.11.refs_2_ = bf16[1,8,64,128]{3,2,1,0:T(8,128)(2,1)S(1)} collective-permute-done((bf16[1,8,64,128]{3,2,1,0:T(8,128)(2,1)S(1)}, bf16[1,8,64,128]{3,2,1,0:T(8,128)(2,1)S(1)}, u32[]{:S(2)}, u32[]{:S(2)}) %collective-permute-start.11) | collective-permute-done | bytes 131104 | tf_op jit(solution)/shard_map/ppermute | solution.py:559
  (99 shorter events, 18.6 us)
Async XLA Ops:
  3.7 4.6 %collective-permute-start.1 = (bf16[2,1,64,128]{3,2,1,0:T(8,128)(2,1)S(1)}, bf16[2,1,64,128]{3,2,1,0:T(8,128)(2,1)S(1)}, u32[]{:S(2)}, u32[]{:S(2)}) collective-permute-start(bf16[2,1,64,128]{3,2,1,0:T(8,128)(2,1)S(1)} %get-tuple-element.59), channel_id=1, source_target_pairs={{0,1},{1,0},{2,3},{3,2},{4,5},{5,4},{6,7},{7,6},{8,9},{9,8},{10,11... | collective-permute-start | bytes 98312 | tf_op jit(solution)/shard_map/ppermute | solution.py:70
  4.1 8.1 %collective-permute-start.4 = (bf16[1,10,64,128]{3,2,1,0:T(8,128)(2,1)S(1)}, bf16[1,10,64,128]{3,2,1,0:T(8,128)(2,1)S(1)}, u32[]{:S(2)}, u32[]{:S(2)}) collective-permute-start(bf16[1,10,64,128]{3,2,1,0:T(8,128)(2,1)S(1)} %get-tuple-element.62), channel_id=1, source_target_pairs={{8,10},{10,8},{12,12},{14,14},{16,16},{18,20},{20,18},{22,22},{9,1... | collective-permute-start | bytes 491528 | tf_op jit(solution)/shard_map/ppermute | solution.py:559
  7.6 4.6 %collective-permute-start.5 = (bf16[1,10,64,128]{3,2,1,0:T(8,128)(2,1)S(1)}, bf16[1,10,64,128]{3,2,1,0:T(8,128)(2,1)S(1)}, u32[]{:S(2)}, u32[]{:S(2)}) collective-permute-start(bf16[1,10,64,128]{3,2,1,0:T(8,128)(2,1)S(1)} %get-tuple-element.63), channel_id=1, source_target_pairs={{8,8},{10,10},{12,14},{14,12},{16,18},{18,22},{20,16},{22,20},{9,9... | collective-permute-start | bytes 491528 | tf_op jit(solution)/shard_map/ppermute | solution.py:559
  8.4 4.7 %collective-permute-start.2 = (bf16[1,8,64,128]{3,2,1,0:T(8,128)(2,1)S(1)}, bf16[1,8,64,128]{3,2,1,0:T(8,128)(2,1)S(1)}, u32[]{:S(2)}, u32[]{:S(2)}) collective-permute-start(bf16[1,8,64,128]{3,2,1,0:T(8,128)(2,1)S(1)} %get-tuple-element.60.refs_0_), channel_id=1, source_target_pairs={{24,16},{26,20},{28,18},{30,22},{25,17},{27,21},{29,19},{31,23}} | collective-permute-start | bytes 393224 | tf_op jit(solution)/shard_map/ppermute | solution.py:559
  9.1 4.0 %collective-permute-start.3 = (bf16[1,8,64,128]{3,2,1,0:T(8,128)(2,1)S(1)}, bf16[1,8,64,128]{3,2,1,0:T(8,128)(2,1)S(1)}, u32[]{:S(2)}, u32[]{:S(2)}) collective-permute-start(bf16[1,8,64,128]{3,2,1,0:T(8,128)(2,1)S(1)} %get-tuple-element.61.refs_1_), channel_id=1, source_target_pairs={{24,18},{26,22},{28,16},{30,20},{25,19},{27,23},{29,17},{31,21}} | collective-permute-start | bytes 393224 | tf_op jit(solution)/shard_map/ppermute | solution.py:559
  14.4 19.1 %collective-permute-start.7 = (bf16[1,8,64,128]{3,2,1,0:T(8,128)(2,1)S(1)}, bf16[1,8,64,128]{3,2,1,0:T(8,128)(2,1)S(1)}, u32[]{:S(2)}, u32[]{:S(2)}) collective-permute-start(bf16[1,8,64,128]{3,2,1,0:T(8,128)(2,1)S(1)} %get-tuple-element.71), channel_id=1, source_target_pairs={{16,12},{18,14},{20,8},{22,10},{17,13},{19,15},{21,9},{23,11}} | collective-permute-start | bytes 393224 | tf_op jit(solution)/shard_map/ppermute | solution.py:559
  15.7 18.6 %collective-permute-start.8 = (bf16[1,8,64,128]{3,2,1,0:T(8,128)(2,1)S(1)}, bf16[1,8,64,128]{3,2,1,0:T(8,128)(2,1)S(1)}, u32[]{:S(2)}, u32[]{:S(2)}) collective-permute-start(bf16[1,8,64,128]{3,2,1,0:T(8,128)(2,1)S(1)} %get-tuple-element.71), channel_id=1, source_target_pairs={{16,8},{18,10},{20,12},{22,14},{17,9},{19,11},{21,13},{23,15}} | collective-permute-start | bytes 393224 | tf_op jit(solution)/shard_map/ppermute | solution.py:559
  17.0 19.6 %collective-permute-start.9 = (bf16[1,8,64,128]{3,2,1,0:T(8,128)(2,1)S(1)}, bf16[1,8,64,128]{3,2,1,0:T(8,128)(2,1)S(1)}, u32[]{:S(2)}, u32[]{:S(2)}) collective-permute-start(bf16[1,8,64,128]{3,2,1,0:T(8,128)(2,1)S(1)} %get-tuple-element.72), channel_id=1, source_target_pairs={{16,8},{18,10},{20,12},{22,14},{17,9},{19,11},{21,13},{23,15}} | collective-permute-start | bytes 393224 | tf_op jit(solution)/shard_map/ppermute | solution.py:559
  42.0 7.9 %collective-permute-start.13 = (bf16[1,8,64,128]{3,2,1,0:T(8,128)(2,1)S(1)}, bf16[1,8,64,128]{3,2,1,0:T(8,128)(2,1)S(1)}, u32[]{:S(2)}, u32[]{:S(2)}) collective-permute-start(bf16[1,8,64,128]{3,2,1,0:T(8,128)(2,1)S(1)} %get-tuple-element.80), channel_id=1, source_target_pairs={{8,0},{10,2},{12,4},{14,6},{9,1},{11,3},{13,5},{15,7}} | collective-permute-start | bytes 393224 | tf_op jit(solution)/shard_map/ppermute | solution.py:559
  43.3 6.6 %collective-permute-start.14 = (bf16[1,8,64,128]{3,2,1,0:T(8,128)(2,1)S(1)}, bf16[1,8,64,128]{3,2,1,0:T(8,128)(2,1)S(1)}, u32[]{:S(2)}, u32[]{:S(2)}) collective-permute-start(bf16[1,8,64,128]{3,2,1,0:T(8,128)(2,1)S(1)} %get-tuple-element.80), channel_id=1, source_target_pairs={{10,0},{12,6},{11,1},{13,7}} | collective-permute-start | bytes 393224 | tf_op jit(solution)/shard_map/ppermute | solution.py:559
  44.0 8.3 %collective-permute-start.15 = (bf16[1,8,64,128]{3,2,1,0:T(8,128)(2,1)S(1)}, bf16[1,8,64,128]{3,2,1,0:T(8,128)(2,1)S(1)}, u32[]{:S(2)}, u32[]{:S(2)}) collective-permute-start(bf16[1,8,64,128]{3,2,1,0:T(8,128)(2,1)S(1)} %get-tuple-element.81), channel_id=1, source_target_pairs={{8,0},{10,2},{12,4},{14,6},{9,1},{11,3},{13,5},{15,7}} | collective-permute-start | bytes 393224 | tf_op jit(solution)/shard_map/ppermute | solution.py:559
  45.3 7.0 %collective-permute-start.16 = (bf16[1,8,64,128]{3,2,1,0:T(8,128)(2,1)S(1)}, bf16[1,8,64,128]{3,2,1,0:T(8,128)(2,1)S(1)}, u32[]{:S(2)}, u32[]{:S(2)}) collective-permute-start(bf16[1,8,64,128]{3,2,1,0:T(8,128)(2,1)S(1)} %get-tuple-element.81), channel_id=1, source_target_pairs={{8,2},{10,4},{9,3},{11,5}} | collective-permute-start | bytes 393224 | tf_op jit(solution)/shard_map/ppermute | solution.py:559
  46.6 5.7 %collective-permute-start.17 = (bf16[1,8,64,128]{3,2,1,0:T(8,128)(2,1)S(1)}, bf16[1,8,64,128]{3,2,1,0:T(8,128)(2,1)S(1)}, u32[]{:S(2)}, u32[]{:S(2)}) collective-permute-start(bf16[1,8,64,128]{3,2,1,0:T(8,128)(2,1)S(1)} %get-tuple-element.81), channel_id=1, source_target_pairs={{12,2},{14,4},{13,3},{15,5}} | collective-permute-start | bytes 393224 | tf_op jit(solution)/shard_map/ppermute | solution.py:559
  52.4 1.5 %collective-permute-start.18 = (bf16[768,128]{1,0:T(8,128)(2,1)S(1)}, bf16[768,128]{1,0:T(8,128)(2,1)S(1)}, u32[]{:S(2)}, u32[]{:S(2)}) collective-permute-start(bf16[768,128]{1,0:T(8,128)(2,1)S(1)} %dynamic-slice_convert_fusion), channel_id=1, source_target_pairs={{0,1},{1,0},{2,3},{3,2},{4,5},{5,4},{6,7},{7,6},{8,9},{9,8},{10,11... | collective-permute-start | bytes 589832 | tf_op jit(solution)/shard_map/ppermute | solution.py:451
  54.0 6.6 %collective-permute-start.19 = (bf16[2,1,64,128]{3,2,1,0:T(8,128)(2,1)S(1)}, bf16[2,1,64,128]{3,2,1,0:T(8,128)(2,1)S(1)}, u32[]{:S(2)}, u32[]{:S(2)}) collective-permute-start(bf16[2,1,64,128]{3,2,1,0:T(8,128)(2,1)S(1)} %get-tuple-element.101), channel_id=1, source_target_pairs={{0,1},{1,0},{2,3},{3,2},{4,5},{5,4},{6,7},{7,6},{8,9},{9,8},{10,11... | collective-permute-start | bytes 98312 | tf_op jit(solution)/shard_map/ppermute | solution.py:70
  54.2 6.4 %collective-permute-start.20 = (bf16[192,128]{1,0:T(8,128)(2,1)S(1)}, bf16[192,128]{1,0:T(8,128)(2,1)S(1)}, u32[]{:S(2)}, u32[]{:S(2)}) collective-permute-start(bf16[192,128]{1,0:T(8,128)(2,1)S(1)} %get-tuple-element.111), channel_id=1, source_target_pairs={{0,2},{2,0},{4,6},{6,4},{1,3},{3,1},{5,7},{7,5},{8,10},{10,8},{12,... | collective-permute-start | bytes 147464 | tf_op jit(solution)/shard_map/ppermute | solution.py:451
  58.2 7.1 %collective-permute-start.21 = (bf16[192,128]{1,0:T(8,128)(2,1)S(1)}, bf16[192,128]{1,0:T(8,128)(2,1)S(1)}, u32[]{:S(2)}, u32[]{:S(2)}) collective-permute-start(bf16[192,128]{1,0:T(8,128)(2,1)S(1)} %get-tuple-element.110), channel_id=1, source_target_pairs={{0,4},{2,6},{4,0},{6,2},{1,5},{3,7},{5,1},{7,3},{8,12},{10,14},{12... | collective-permute-start | bytes 147464 | tf_op jit(solution)/shard_map/ppermute | solution.py:451
  58.5 6.8 %collective-permute-start.22 = (bf16[192,128]{1,0:T(8,128)(2,1)S(1)}, bf16[192,128]{1,0:T(8,128)(2,1)S(1)}, u32[]{:S(2)}, u32[]{:S(2)}) collective-permute-start(bf16[192,128]{1,0:T(8,128)(2,1)S(1)} %get-tuple-element.109), channel_id=1, source_target_pairs={{0,6},{2,4},{4,2},{6,0},{1,7},{3,5},{5,3},{7,1},{8,14},{10,12},{12... | collective-permute-start | bytes 147464 | tf_op jit(solution)/shard_map/ppermute | solution.py:451
  65.3 4.5 %collective-permute-start.23 = (bf16[192,128]{1,0:T(8,128)(2,1)S(1)}, bf16[192,128]{1,0:T(8,128)(2,1)S(1)}, u32[]{:S(2)}, u32[]{:S(2)}) collective-permute-start(bf16[192,128]{1,0:T(8,128)(2,1)S(1)} %get-tuple-element.108), channel_id=1, source_target_pairs={{0,2},{2,0},{4,6},{6,4},{1,3},{3,1},{5,7},{7,5},{8,10},{10,8},{12,... | collective-permute-start | bytes 147464 | tf_op jit(solution)/shard_map/ppermute | solution.py:470
  66.5 5.8 %collective-permute-start.24 = (bf16[192,128]{1,0:T(8,128)(2,1)S(1)}, bf16[192,128]{1,0:T(8,128)(2,1)S(1)}, u32[]{:S(2)}, u32[]{:S(2)}) collective-permute-start(bf16[192,128]{1,0:T(8,128)(2,1)S(1)} %get-tuple-element.108), channel_id=1, source_target_pairs={{0,4},{2,6},{4,0},{6,2},{1,5},{3,7},{5,1},{7,3},{8,12},{10,14},{12... | collective-permute-start | bytes 147464 | tf_op jit(solution)/shard_map/ppermute | solution.py:470
  67.8 5.9 %collective-permute-start.25 = (bf16[192,128]{1,0:T(8,128)(2,1)S(1)}, bf16[192,128]{1,0:T(8,128)(2,1)S(1)}, u32[]{:S(2)}, u32[]{:S(2)}) collective-permute-start(bf16[192,128]{1,0:T(8,128)(2,1)S(1)} %get-tuple-element.108), channel_id=1, source_target_pairs={{0,6},{2,4},{4,2},{6,0},{1,7},{3,5},{5,3},{7,1},{8,14},{10,12},{12... | collective-permute-start | bytes 147464 | tf_op jit(solution)/shard_map/ppermute | solution.py:470
  73.7 8.6 %collective-permute-start.26 = (bf16[768,128]{1,0:T(8,128)(2,1)S(1)}, bf16[768,128]{1,0:T(8,128)(2,1)S(1)}, u32[]{:S(2)}, u32[]{:S(2)}) collective-permute-start(bf16[768,128]{1,0:T(8,128)(2,1)S(1)} %constant_dynamic-update-slice_fusion), channel_id=1, source_target_pairs={{0,1},{1,0},{2,3},{3,2},{4,5},{5,4},{6,7},{7,6},{8,9},{9,8},{10,11... | collective-permute-start | bytes 589832 | tf_op jit(solution)/shard_map/ppermute | solution.py:649
  73.8 7.8 %collective-permute-start.11 = (bf16[1,8,64,128]{3,2,1,0:T(8,128)(2,1)S(1)}, bf16[1,8,64,128]{3,2,1,0:T(8,128)(2,1)S(1)}, u32[]{:S(2)}, u32[]{:S(2)}) collective-permute-start(bf16[1,8,64,128]{3,2,1,0:T(8,128)(2,1)S(1)} %copy-done.14), channel_id=1, source_target_pairs={{10,8},{8,10},{12,12},{14,14},{16,16},{20,18},{18,20},{22,22},{11,... | collective-permute-start | bytes 393224 | tf_op jit(solution)/shard_map/ppermute | solution.py:559
  75.7 5.8 %collective-permute-start.12 = (bf16[1,8,64,128]{3,2,1,0:T(8,128)(2,1)S(1)}, bf16[1,8,64,128]{3,2,1,0:T(8,128)(2,1)S(1)}, u32[]{:S(2)}, u32[]{:S(2)}) collective-permute-start(bf16[1,8,64,128]{3,2,1,0:T(8,128)(2,1)S(1)} %copy-done.12), channel_id=1, source_target_pairs={{8,8},{10,10},{14,12},{12,14},{18,16},{22,18},{16,20},{20,22},{9,9... | collective-permute-start | bytes 393224 | tf_op jit(solution)/shard_map/ppermute | solution.py:559
  (22 other events, 126.0 us)

commit v5 on v4

--- a/solution.py
+++ b/solution.py
@@ -5,7 +5,7 @@
 from jax.experimental.pallas import tpu as pltpu
 from jax.sharding import PartitionSpec as P
 
-VMEM_LIMIT = 40 * 1024 * 1024
+VMEM_LIMIT = 16 * 1024 * 1024
 NT = (((1,), (1,)), ((), ()))
 NN = (((1,), (0,)), ((), ()))
 TN = (((0,), (0,)), ((), ()))
@@ -15,12 +15,12 @@
     return lax.dot_general(a, b, how, preferred_element_type=jnp.float32)
 
 
-def call(body, outs, args, flops):
+def call(body, outs, args, flops, loose=False):
     moved = sum(a.size * a.dtype.itemsize for a in (*args, *outs))
     return pl.pallas_call(
         body,
         out_shape=outs,
-        in_specs=[pl.BlockSpec(memory_space=pltpu.VMEM) for _ in args],
+        in_specs=[pl.BlockSpec() if loose else pl.BlockSpec(memory_space=pltpu.VMEM) for _ in args],
         out_specs=[pl.BlockSpec(memory_space=pltpu.VMEM) for _ in outs],
         compiler_params=pltpu.CompilerParams(vmem_limit_bytes=VMEM_LIMIT),
         cost_estimate=pl.CostEstimate(flops=flops, bytes_accessed=moved, transcendentals=0),
@@ -190,26 +190,16 @@
     return outs[: len(slopes)], outs[len(slopes) :]
 
 
-def branches(owner, grads_pre, got, heres, taps_space, picks=None, before=()):
+def branches(owner, grads_pre, got, heres, taps_space, picks=None):
     part = heres[0].shape
     _, rows, cols, channels = part
     count = len(heres)
     picks = picks or list(range(count))
-    fixed = 2 * count + len(got) + 1
 
     def body(*refs):
-        section = lax.axis_index("section")
-        out_refs = refs[fixed + len(before) :]
-
-        if before:
-
-            @pl.when(section != owner)
-            def _():
-                for ref, out_ref in zip(refs[fixed:], out_refs[-len(before) :]):
-                    out_ref[...] = ref[...]
-
-        @pl.when(section == owner)
+        @pl.when(lax.axis_index("section") == owner)
         def _():
+            out_refs = refs[2 * count + len(got) + 1 :]
             got_refs = refs[count : count + len(got)]
             here_refs = refs[count + len(got) : 2 * count + len(got)]
             w_ref = refs[2 * count + len(got)]
@@ -238,7 +228,7 @@
                         ref[...] = out
 
     outs = [jax.ShapeDtypeStruct(part, jnp.bfloat16)] * len(picks)
-    args = [*grads_pre, *got, *heres, taps_space, *before]
+    args = [*grads_pre, *got, *heres, taps_space]
     return call(body, outs, args, 18 * sum(h.size for h in heres) * channels)
 
 
@@ -305,6 +295,31 @@
     return jnp.where(section == 2, place // 2, jnp.where((place == 0) | (place == 3), 1, 0))
 
 
+def prepare(block_input):
+    row_parts = lax.axis_size("row")
+    frames, rows, cols, channels = block_input.shape
+    edge_count = 1 if row_parts == 2 else 2
+
+    def body(x_ref, *out_refs):
+        for ref, edge in zip(out_refs, edges_of(x_ref[...], row_parts)):
+            ref[...] = edge
+        out_refs[edge_count][...] = x_ref[...]
+
+    outs = [jax.ShapeDtypeStruct((frames, 1, cols, channels), jnp.bfloat16)] * edge_count
+    outs += [jax.ShapeDtypeStruct(block_input.shape, jnp.bfloat16)]
+    outs = call(body, outs, [block_input], 0)
+    return outs[:edge_count], outs[edge_count]
+
+
+def frame_by_frame(values):
+    def body(ref, *out_refs):
+        for frame, out_ref in enumerate(out_refs):
+            out_ref[...] = ref[frame : frame + 1]
+
+    out = jax.ShapeDtypeStruct((1,) + values.shape[1:], values.dtype)
+    return call(body, [out] * values.shape[0], [values], 0)
+
+
 def frames_to_deal(block_input, got):
     _, rows, cols, channels = block_input.shape
 
@@ -341,6 +356,22 @@
     return call(body, [jax.ShapeDtypeStruct(pieces[0].shape, jnp.bfloat16)] * 4, pieces, 0)
 
 
+def to_return(results):
+    def body(*refs):
+        section = lax.axis_index("section")
+        even = lax.axis_index("frame") % 2 == 0
+        cases = ((section == 2, 0, 1), ((section == 1) & even, 2, 3))
+        for wanted, one, two in (*cases, ((section == 1) & jnp.logical_not(even), 3, 2)):
+
+            @pl.when(wanted)
+            def _():
+                refs[4][...] = refs[one][...]
+                refs[5][...] = refs[two][...]
+
+    outs = [jax.ShapeDtypeStruct(results[0].shape, jnp.bfloat16)] * 2
+    return call(body, outs, results, 0, True)
+
+
 def own_result(tops, returned, lasts):
     shape = (2,) + lasts[0].shape[1:]
 
@@ -366,7 +397,7 @@
             out_ref[1] = refs[5][0]
 
     outs = [jax.ShapeDtypeStruct(shape, jnp.bfloat16)]
-    return call(body, outs, [*tops, *returned, *lasts], 0)[0]
+    return call(body, outs, [*tops, *returned, *lasts], 0, True)[0]
 
 
 def fetch(block, source, target, frame_step):
@@ -476,10 +507,11 @@
     return list(lax.optimization_barrier((tuple(values), others))[0])
 
 
-def shifted_chains(x_got, block_input, cotangent, taps_space, taps_time):
+def shifted_chains(block_input, cotangent, taps_space, taps_time):
     own_frames = block_input.shape[0]
     section_count = lax.axis_size("section")
     chains = 1 if own_frames % 2 else 2
+    x_got = swap_edges(edges_of(block_input, lax.axis_size("row")))
     top = section_count - 1
 
     def triples(blocks, source, target):
@@ -525,7 +557,7 @@
             results.append(outgoing)
             ready = triples(outgoing, owner, owner - 1)
 
-    def finish(lasts):
+    def finish(lasts, parts):
         section_index = lax.axis_index("section")
         own = results[0] if results else lasts
         for position, values in enumerate((results + [lasts])[1:], 1):
@@ -538,7 +570,62 @@
     return grads, (pre, edges, [blocks[0] for blocks, _ in ready]), finish
 
 
-def dealt_chains(x_got, block_input, cotangent, taps_space, taps_time):
+def sum_kernels(grads, first_beside, then_beside):
+    channels = grads.shape[-1]
+    eighth = 12 * channels // 8
+    pieces = grads.reshape(8, eighth, channels)
+    half = jax.ShapeDtypeStruct((4, eighth, channels), jnp.bfloat16)
+    part = jax.ShapeDtypeStruct((eighth, channels), jnp.bfloat16)
+    wide = jax.ShapeDtypeStruct((eighth, channels), jnp.float32)
+
+    def other_half(pieces_ref, out_ref):
+        start = (1 - lax.axis_index("row")) * 4
+        out_ref[...] = pieces_ref[pl.ds(start, 4)].astype(jnp.bfloat16)
+
+    def add_half(pieces_ref, got_ref, *out_refs):
+        start = lax.axis_index("row") * 4
+        for mask, ref in enumerate(out_refs):
+            at = lax.axis_index("frame") ^ mask
+            ref[...] = (pieces_ref[start + at] + got_ref[at].astype(jnp.float32)).astype(ref.dtype)
+
+    def add_parts(*refs):
+        refs[-1][...] = sum(ref[...].astype(jnp.float32) for ref in refs[:-1]).astype(jnp.bfloat16)
+
+    def line_parts(*refs):
+        for mask, ref in enumerate(refs[:-1]):
+            refs[-1][lax.axis_index("frame") ^ mask] = ref[...]
+
+    def widen(mine_ref, other_ref, space_ref, time_ref):
+        for row, (low, high) in enumerate(((mine_ref, other_ref), (other_ref, mine_ref))):
+
+            @pl.when(lax.axis_index("row") == row)
+            def _():
+                space_ref[:4] = low[...].astype(jnp.float32)
+                space_ref[4:] = high[:2].astype(jnp.float32)
+                time_ref[...] = high[2:].astype(jnp.float32)
+
+    def over_frame(block, mask):
+        return lax.ppermute(block, "frame", [(i, i ^ mask) for i in range(4)])
+
+    swap = [(0, 1), (1, 0)]
+    got = lax.ppermute(call(other_half, [half], [pieces], 0)[0], "row", swap)
+    got = after([got], *first_beside)
+    own, *parts = call(add_half, [wide] + [part] * 3, [pieces, *got], 0)
+    extra = then_beside(parts)
+    came = [over_frame(block, mask) for mask, block in enumerate(parts, 1)]
+    own = call(add_parts, [part], [own, *after(came, extra)], 0)[0]
+    came = [over_frame(own, mask) for mask in range(1, 4)]
+    mine = call(line_parts, [half], [own, *came], 0)[0]
+    other = lax.ppermute(mine, "row", swap)
+    outs = [
+        jax.ShapeDtypeStruct((6, eighth, channels), jnp.float32),
+        jax.ShapeDtypeStruct((2, eighth, channels), jnp.float32),
+    ]
+    space, time = call(widen, outs, [mine, other], 0)
+    return space, time, extra
+
+
+def dealt_chains(block_input, cotangent, taps_space, taps_time):
     def place():
         return lax.axis_index("frame")
 
@@ -553,6 +640,9 @@
 
     def outer():
         return (place() == 0) | (place() == 3)
+
+    def inner():
+        return (place() == 1) | (place() == 2)
 
     def send(block, *hops):
         route = [(a * 4 + i, b * 4 + j) for a, b, moves in hops for i, j in moves]
@@ -566,41 +656,41 @@
         2: ([(0, 0), (1, 2), (2, 1), (3, 3)], [(0, 1), (1, 3), (2, 0), (3, 2)]),
         1: ([(0, 1), (1, 0), (2, 2), (3, 3)], [(0, 0), (1, 1), (2, 3), (3, 2)]),
     }
-    x_dealt = [
-        send(block, *((s, s, deal[s][k]) for s in (1, 2)))
-        for k, block in enumerate(frames_to_deal(block_input, x_got))
-    ]
-
-    def step(owner, triples, slopes, picks, before=()):
+    edges, block_input = prepare(block_input)
+    x_got = swap_edges(edges)
+
+    def step(owner, triples, slopes, picks):
         pre, edges = temporal(owner, triples, slopes, taps_time)
         heres = [blocks[0] for blocks, _ in triples]
-        outs = branches(owner, pre, swap_edges(edges), heres, taps_space, picks, before)
+        outs = branches(owner, pre, swap_edges(edges), heres, taps_space, picks)
         return after(pre, *outs), outs
 
     x_own, slopes_own, actives_own = forward(block_input, x_got, taps_space, 2, (0, 3))
-    ready = [([block], None) for block in split_frames(cotangent, 2)]
+    ready = [([block], None) for block in frame_by_frame(cotangent)]
     pre, tops = step(
         3, ready, slopes_own, [lambda: place() < 2, lambda: place() >= 2]
     )
     first, second = (send(block, (3, 2, deal[2][k])) for k, block in enumerate(tops))
+    x_dealt = [
+        send(block, *((s, s, deal[s][k]) for s in (1, 2)))
+        for k, block in enumerate(frames_to_deal(block_input, x_got))
+    ]
     grads = kernel_grads(3, x_own, pre, actives_own, ready, None)
     x_moved, slopes, actives = forward(
-        block_input, x_got, taps_space, 2, (1, 2), after(x_dealt, *tops)
+        block_input, x_got, taps_space, 2, (1, 2), x_dealt
     )
 
     ready = [([first, second], even), ([second, first], odd)]
-    pre, outs = step(2, ready, slopes, [outer, lambda: jnp.logical_not(outer()), 0, 1])
-    ends, others, *returned = outs
+    pre, outs = step(2, ready, slopes, [outer, inner, 0, 1])
+    ends, others, *results = outs
     end = send(ends, (2, 1, stay))
     other = send(others, (2, 1, stay))
     cross = send(others, (2, 1, [(i, i ^ 2) for i in range(4)]))
     grads = kernel_grads(2, x_moved, pre, actives, ready, grads)
 
     ready = [([cross, other, end], low), ([end, cross], low)]
-    pre, outs = step(
-        1, ready, slopes, [0, 1, lambda: place() % 2 == 0, lambda: place() % 2 == 1], returned
-    )
-    middles, ends, *returned = outs
+    pre, (middles, ends) = step(1, ready, slopes, [0, 1])
+    results += [middles, ends]
     pieces = [
         send(ends, (1, 0, stay)),
         send(ends, (1, 0, [(1, 0), (2, 3)])),
@@ -609,16 +699,16 @@
         send(middles, (1, 0, [(2, 1), (3, 2)])),
     ]
     grads = kernel_grads(1, x_moved, pre, actives, ready, grads)
-    before, one, two, later = line_up(pieces)
+    returned = [
+        send(block, *((s, s, back(deal[s][k])) for s in (1, 2)))
+        for k, block in enumerate(after(to_return(results), *pieces[:2]))
+    ]
+    before, one, two, later = line_up(after(pieces, *returned))
     ready = [([one, two, before], None), ([two, later, one], None)]
     pre, edges = temporal(0, ready, slopes_own, taps_time)
     grads = kernel_grads(0, x_own, pre, actives_own, ready, grads)
-    returned = [
-        send(block, *((s, s, back(deal[s][k])) for s in (1, 2)))
-        for k, block in enumerate(returned)
-    ]
-
-    def finish(lasts):
+
+    def finish(lasts, parts):
         return own_result(tops, returned, lasts)
 
     return grads, (pre, edges, [one, two]), finish
@@ -630,18 +720,29 @@
     taps_time = w_temporal[0]
     channels = block_input.shape[-1]
     row_parts = lax.axis_size("row")
-    x_got = swap_edges(edges_of(block_input, row_parts))
-    shape = (lax.axis_size("section"), lax.axis_size("frame"), block_input.shape[0])
-    chains = dealt_chains if shape == (4, 4, 2) else shifted_chains
-    grads, (pre, edges, heres), finish = chains(
-        x_got, block_input, cotangent, taps_space, taps_time
-    )
+    shape = (lax.axis_size("section"), lax.axis_size("frame"), row_parts, block_input.shape[0])
+    dealt = shape == (4, 4, 2, 2) and (12 * channels) % 128 == 0
+    chains = dealt_chains if dealt else shifted_chains
+    grads, (pre, edges, heres), finish = chains(block_input, cotangent, taps_space, taps_time)
+
+    def last_branch(parts):
+        return finish(branches(0, pre, swap_edges(after(edges, parts)), heres, taps_space), parts)
+
+    if dealt:
+        lasts = branches(0, pre, swap_edges(edges), heres, taps_space)
+
+        def result(parts):
+            return finish(after(lasts, *parts), parts)
+
+        space, time, own = sum_kernels(grads, lasts, result)
+        return (
+            own[None],
+            space.reshape((1, 3, 3, channels, channels)),
+            time.reshape((1, 3, channels, channels)),
+        )
     total, _ = sum_over(grads.reshape(-1, channels), "row")
 
-    def last_branch(parts):
-        return branches(0, pre, swap_edges(after(edges, parts)), heres, taps_space)
-
-    total, lasts = sum_over(total, "frame", last_branch)
+    total, own = sum_over(total, "frame", last_branch)
     total = gather_parts(total.astype(jnp.bfloat16), "frame")
     split = 9 * channels
     if row_parts == 2:
@@ -658,7 +759,7 @@
         total = gather_parts(total, "row")
         space, time = total[:split], total[split:]
     return (
-        finish(lasts)[None],
+        own[None],
         space.astype(jnp.float32).reshape((1, 3, 3, channels, channels)),
         time.astype(jnp.float32).reshape((1, 3, channels, channels)),
     )

time: 84.4 us -> 78.9 us (0.935)
  the two profiles are of different devices: /device:TPU:2 before, /device:TPU:0 now
where the time goes in v5:
time: 78.9 us; the launch traced here: 78.5 us
  waiting for transfers between devices  45.4 us (58%)
  starting transfers between devices  24.9 us (32%)
  Pallas kernels  4.68 us (6%)
  local copies, waits for them, and re-layouts  2.46 us (3%)
  between operations  1.01 us (1%)
    ppermute x14, waiting for transfers between devices, send(): return lax.ppermute(block, ('section', 'frame'), route)  33.8 us
    ppermute x6, starting transfers between devices, over_frame(): return lax.ppermute(block, 'frame', [(i, i ^ mask) for i in range(4)])  11.6 us
    ppermute x14, starting transfers between devices, send(): return lax.ppermute(block, ('section', 'frame'), route)  11.3 us
    ppermute x6, waiting for transfers between devices, over_frame(): return lax.ppermute(block, 'frame', [(i, i ^ mask) for i in range(4)])  6.65 us
    pallas_call x25, Pallas kernels, call(): pl.pallas_call(body, out_shape=outs, in_specs=[pl.BlockSpec() if loose el...  4.68 us
    ppermute x5, waiting for transfers between devices, swap_edges(): return [lax.ppermute(edges[0], 'row', [(0, 1), (1, 0)])]  3.51 us
    unnamed x10, local copies, waits for them, and re-layouts  2.46 us
    ppermute x5, starting transfers between devices, swap_edges(): return [lax.ppermute(edges[0], 'row', [(0, 1), (1, 0)])]  1.76 us
  transfers between devices with their start and end apart: 27, of which 11 were waited for; matrix products, arithmetic and copies ran while one was open for 0% of the time, Pallas kernels for 2%

profile of v5, /device:TPU:0, one launch (start us, length us, event | category | flops | bytes accessed | tf_op | source)
XLA Modules:
  0.0 78.5 jit_solution(12051568597310412595)
XLA Ops:
  0.6 0.9 %copy-done.1 = bf16[1,2,8,64,128]{4,3,2,1,0:T(8,128)(2,1)S(1)} copy-done((bf16[1,2,8,64,128]{4,3,2,1,0:T(8,128)(2,1)S(1)}, bf16[1,2,8,64,128]{4,3,2,1,0:T(8,128)(2,1)}, u32[]{:S(2)}) %copy-start.1) | copy-done | bytes 262168
  3.0 1.0 %copy-done.3 = bf16[1,3,3,128,128]{4,3,2,1,0:T(8,128)(2,1)S(1)} copy-done((bf16[1,3,3,128,128]{4,3,2,1,0:T(8,128)(2,1)S(1)}, bf16[1,3,3,128,128]{4,3,2,1,0:T(8,128)(2,1)}, u32[]{:S(2)}) %copy-start.3) | copy-done | bytes 294936
  4.0 0.7 shard_map.69
  6.6 0.8 %collective-permute-start.2 = (bf16[1,8,64,128]{3,2,1,0:T(8,128)(2,1)S(1)}, bf16[1,8,64,128]{3,2,1,0:T(8,128)(2,1)S(1)}, u32[]{:S(2)}, u32[]{:S(2)}) collective-permute-start(bf16[1,8,64,128]{3,2,1,0:T(8,128)(2,1)S(1)} %get-tuple-element.81.refs_0_), channel_id=1, source_target_pairs={{24,16},{26,20},{28,18},{30,22},{25,17},{27,21},{29,19},{31,23}} | collective-permute-start | bytes 393224 | tf_op jit(solution)/shard_map/ppermute | solution.py:649
  8.4 1.0 %collective-permute-done.6.refs_2_ = bf16[2,1,64,128]{3,2,1,0:T(8,128)(2,1)S(1)} collective-permute-done((bf16[2,1,64,128]{3,2,1,0:T(8,128)(2,1)S(1)}, bf16[2,1,64,128]{3,2,1,0:T(8,128)(2,1)S(1)}, u32[]{:S(2)}, u32[]{:S(2)}) %collective-permute-start.6) | collective-permute-done | bytes 32800 | tf_op jit(solution)/shard_map/ppermute | solution.py:70
  11.8 1.0 %collective-permute-done.10.refs_2_ = bf16[2,1,64,128]{3,2,1,0:T(8,128)(2,1)S(1)} collective-permute-done((bf16[2,1,64,128]{3,2,1,0:T(8,128)(2,1)S(1)}, bf16[2,1,64,128]{3,2,1,0:T(8,128)(2,1)S(1)}, u32[]{:S(2)}, u32[]{:S(2)}) %collective-permute-start.10) | collective-permute-done | bytes 32800 | tf_op jit(solution)/shard_map/ppermute | solution.py:70
  12.8 1.3 %collective-permute-start.12 = (bf16[1,8,64,128]{3,2,1,0:T(8,128)(2,1)S(1)}, bf16[1,8,64,128]{3,2,1,0:T(8,128)(2,1)S(1)}, u32[]{:S(2)}, u32[]{:S(2)}) collective-permute-start(bf16[1,8,64,128]{3,2,1,0:T(8,128)(2,1)S(1)} %get-tuple-element.98.refs_3_), channel_id=1, source_target_pairs={{10,0},{12,6},{11,1},{13,7}} | collective-permute-start | bytes 393224 | tf_op jit(solution)/shard_map/ppermute | solution.py:649
  14.1 1.3 %collective-permute-start.11 = (bf16[1,8,64,128]{3,2,1,0:T(8,128)(2,1)S(1)}, bf16[1,8,64,128]{3,2,1,0:T(8,128)(2,1)S(1)}, u32[]{:S(2)}, u32[]{:S(2)}) collective-permute-start(bf16[1,8,64,128]{3,2,1,0:T(8,128)(2,1)S(1)} %get-tuple-element.98.refs_3_), channel_id=1, source_target_pairs={{8,0},{10,2},{12,4},{14,6},{9,1},{11,3},{13,5},{15,7}} | collective-permute-start | bytes 393224 | tf_op jit(solution)/shard_map/ppermute | solution.py:649
  16.7 1.3 %collective-permute-start.15 = (bf16[1,8,64,128]{3,2,1,0:T(8,128)(2,1)S(1)}, bf16[1,8,64,128]{3,2,1,0:T(8,128)(2,1)S(1)}, u32[]{:S(2)}, u32[]{:S(2)}) collective-permute-start(bf16[1,8,64,128]{3,2,1,0:T(8,128)(2,1)S(1)} %get-tuple-element.97.refs_2_), channel_id=1, source_target_pairs={{8,0},{10,2},{12,4},{14,6},{9,1},{11,3},{13,5},{15,7}} | collective-permute-start | bytes 393224 | tf_op jit(solution)/shard_map/ppermute | solution.py:649
  18.1 29.8 %collective-permute-done.12.refs_1_ = bf16[1,8,64,128]{3,2,1,0:T(8,128)(2,1)S(1)} collective-permute-done((bf16[1,8,64,128]{3,2,1,0:T(8,128)(2,1)S(1)}, bf16[1,8,64,128]{3,2,1,0:T(8,128)(2,1)S(1)}, u32[]{:S(2)}, u32[]{:S(2)}) %collective-permute-start.12) | collective-permute-done | bytes 131104 | tf_op jit(solution)/shard_map/ppermute | solution.py:649
  47.9 2.7 %collective-permute-done.11.refs_0_ = bf16[1,8,64,128]{3,2,1,0:T(8,128)(2,1)S(1)} collective-permute-done((bf16[1,8,64,128]{3,2,1,0:T(8,128)(2,1)S(1)}, bf16[1,8,64,128]{3,2,1,0:T(8,128)(2,1)S(1)}, u32[]{:S(2)}, u32[]{:S(2)}) %collective-permute-start.11) | collective-permute-done | bytes 131104 | tf_op jit(solution)/shard_map/ppermute | solution.py:649
  52.2 1.2 %collective-permute-done.15.refs_2_ = bf16[1,8,64,128]{3,2,1,0:T(8,128)(2,1)S(1)} collective-permute-done((bf16[1,8,64,128]{3,2,1,0:T(8,128)(2,1)S(1)}, bf16[1,8,64,128]{3,2,1,0:T(8,128)(2,1)S(1)}, u32[]{:S(2)}, u32[]{:S(2)}) %collective-permute-start.15) | collective-permute-done | bytes 131104 | tf_op jit(solution)/shard_map/ppermute | solution.py:649
  53.9 0.8 shard_map.85
  55.3 1.0 %collective-permute-done.18.refs_2_ = bf16[2,1,64,128]{3,2,1,0:T(8,128)(2,1)S(1)} collective-permute-done((bf16[2,1,64,128]{3,2,1,0:T(8,128)(2,1)S(1)}, bf16[2,1,64,128]{3,2,1,0:T(8,128)(2,1)S(1)}, u32[]{:S(2)}, u32[]{:S(2)}) %collective-permute-start.18) | collective-permute-done | bytes 32800 | tf_op jit(solution)/shard_map/ppermute | solution.py:70
  57.0 4.7 %collective-permute-start.20 = (bf16[192,128]{1,0:T(8,128)(2,1)S(1)}, bf16[192,128]{1,0:T(8,128)(2,1)S(1)}, u32[]{:S(2)}, u32[]{:S(2)}) collective-permute-start(bf16[192,128]{1,0:T(8,128)(2,1)S(1)} %get-tuple-element.130), channel_id=1, source_target_pairs={{0,2},{2,0},{4,6},{6,4},{1,3},{3,1},{5,7},{7,5},{8,10},{10,8},{12,... | collective-permute-start | bytes 147464 | tf_op jit(solution)/shard_map/ppermute | solution.py:608
  61.7 2.4 %collective-permute-start.22 = (bf16[192,128]{1,0:T(8,128)(2,1)S(1)}, bf16[192,128]{1,0:T(8,128)(2,1)S(1)}, u32[]{:S(2)}, u32[]{:S(2)}) collective-permute-start(bf16[192,128]{1,0:T(8,128)(2,1)S(1)} %get-tuple-element.132), channel_id=1, source_target_pairs={{0,6},{2,4},{4,2},{6,0},{1,7},{3,5},{5,3},{7,1},{8,14},{10,12},{12... | collective-permute-start | bytes 147464 | tf_op jit(solution)/shard_map/ppermute | solution.py:608
  64.9 3.5 %collective-permute-done.21.refs_2_ = bf16[192,128]{1,0:T(8,128)(2,1)S(1)} collective-permute-done((bf16[192,128]{1,0:T(8,128)(2,1)S(1)}, bf16[192,128]{1,0:T(8,128)(2,1)S(1)}, u32[]{:S(2)}, u32[]{:S(2)}) %collective-permute-start.21) | collective-permute-done | bytes 49184 | tf_op jit(solution)/shard_map/ppermute | solution.py:608
  68.4 1.8 %collective-permute-start.25 = (bf16[192,128]{1,0:T(8,128)(2,1)S(1)}, bf16[192,128]{1,0:T(8,128)(2,1)S(1)}, u32[]{:S(2)}, u32[]{:S(2)}) collective-permute-start(bf16[192,128]{1,0:T(8,128)(2,1)S(1)} %shard_map.89.refs_0_), channel_id=1, source_target_pairs={{0,6},{2,4},{4,2},{6,0},{1,7},{3,5},{5,3},{7,1},{8,14},{10,12},{12... | collective-permute-start | bytes 147464 | tf_op jit(solution)/shard_map/ppermute | solution.py:608
  70.2 1.1 %collective-permute-start.24 = (bf16[192,128]{1,0:T(8,128)(2,1)S(1)}, bf16[192,128]{1,0:T(8,128)(2,1)S(1)}, u32[]{:S(2)}, u32[]{:S(2)}) collective-permute-start(bf16[192,128]{1,0:T(8,128)(2,1)S(1)} %shard_map.89.refs_0_), channel_id=1, source_target_pairs={{0,4},{2,6},{4,0},{6,2},{1,5},{3,7},{5,1},{7,3},{8,12},{10,14},{12... | collective-permute-start | bytes 147464 | tf_op jit(solution)/shard_map/ppermute | solution.py:608
  71.3 1.5 %collective-permute-start.23 = (bf16[192,128]{1,0:T(8,128)(2,1)S(1)}, bf16[192,128]{1,0:T(8,128)(2,1)S(1)}, u32[]{:S(2)}, u32[]{:S(2)}) collective-permute-start(bf16[192,128]{1,0:T(8,128)(2,1)S(1)} %shard_map.89.refs_0_), channel_id=1, source_target_pairs={{0,2},{2,0},{4,6},{6,4},{1,3},{3,1},{5,7},{7,5},{8,10},{10,8},{12,... | collective-permute-start | bytes 147464 | tf_op jit(solution)/shard_map/ppermute | solution.py:608
  72.9 1.9 %collective-permute-done.25.refs_3_ = bf16[192,128]{1,0:T(8,128)(2,1)S(1)} collective-permute-done((bf16[192,128]{1,0:T(8,128)(2,1)S(1)}, bf16[192,128]{1,0:T(8,128)(2,1)S(1)}, u32[]{:S(2)}, u32[]{:S(2)}) %collective-permute-start.25) | collective-permute-done | bytes 49184 | tf_op jit(solution)/shard_map/ppermute | solution.py:608
  74.7 1.3 %collective-permute-done.24.refs_2_ = bf16[192,128]{1,0:T(8,128)(2,1)S(1)} collective-permute-done((bf16[192,128]{1,0:T(8,128)(2,1)S(1)}, bf16[192,128]{1,0:T(8,128)(2,1)S(1)}, u32[]{:S(2)}, u32[]{:S(2)}) %collective-permute-start.24) | collective-permute-done | bytes 49184 | tf_op jit(solution)/shard_map/ppermute | solution.py:608
  76.1 1.4 %collective-permute-done.26.other_ref = bf16[4,192,128]{2,1,0:T(8,128)(2,1)S(1)} collective-permute-done((bf16[4,192,128]{2,1,0:T(8,128)(2,1)S(1)}, bf16[4,192,128]{2,1,0:T(8,128)(2,1)S(1)}, u32[]{:S(2)}, u32[]{:S(2)}) %collective-permute-start.26) | collective-permute-done | bytes 196640 | tf_op jit(solution)/shard_map/ppermute | solution.py:619
  77.5 0.9 %shard_map.91 = (f32[6,192,128]{2,1,0:T(8,128)}, f32[2,192,128]{2,1,0:T(8,128)}) custom-call(bf16[4,192,128]{2,1,0:T(8,128)(2,1)S(1)} %shard_map.90.mine_ref, bf16[4,192,128]{2,1,0:T(8,128)(2,1)S(1)} %collective-permute-done.26.other_ref), custom_call_target="tpu_custom_call" | custom-call | bytes 1179648 | tf_op jit(solution)/shard_map/pallas_call | solution.py:20
  (65 shorter events, 11.9 us)
Async XLA Ops:
  1.6 1.4 %collective-permute-start = (bf16[2,1,64,128]{3,2,1,0:T(8,128)(2,1)S(1)}, bf16[2,1,64,128]{3,2,1,0:T(8,128)(2,1)S(1)}, u32[]{:S(2)}, u32[]{:S(2)}) collective-permute-start(bf16[2,1,64,128]{3,2,1,0:T(8,128)(2,1)S(1)} %get-tuple-element.75), channel_id=1, source_target_pairs={{0,1},{1,0},{2,3},{3,2},{4,5},{5,4},{6,7},{7,6},{8,9},{9,8},{10,11... | collective-permute-start | bytes 98312 | tf_op jit(solution)/shard_map/ppermute | solution.py:70
  4.8 1.7 %collective-permute-start.1 = (bf16[2,1,64,128]{3,2,1,0:T(8,128)(2,1)S(1)}, bf16[2,1,64,128]{3,2,1,0:T(8,128)(2,1)S(1)}, u32[]{:S(2)}, u32[]{:S(2)}) collective-permute-start(bf16[2,1,64,128]{3,2,1,0:T(8,128)(2,1)S(1)} %get-tuple-element.80), channel_id=1, source_target_pairs={{0,1},{1,0},{2,3},{3,2},{4,5},{5,4},{6,7},{7,6},{8,9},{9,8},{10,11... | collective-permute-start | bytes 98312 | tf_op jit(solution)/shard_map/ppermute | solution.py:70
  5.2 2.9 %collective-permute-start.4 = (bf16[1,10,64,128]{3,2,1,0:T(8,128)(2,1)S(1)}, bf16[1,10,64,128]{3,2,1,0:T(8,128)(2,1)S(1)}, u32[]{:S(2)}, u32[]{:S(2)}) collective-permute-start(bf16[1,10,64,128]{3,2,1,0:T(8,128)(2,1)S(1)} %get-tuple-element.83), channel_id=1, source_target_pairs={{8,10},{10,8},{12,12},{14,14},{16,16},{18,20},{20,18},{22,22},{9,1... | collective-permute-start | bytes 491528 | tf_op jit(solution)/shard_map/ppermute | solution.py:649
  5.9 2.2 %collective-permute-start.5 = (bf16[1,10,64,128]{3,2,1,0:T(8,128)(2,1)S(1)}, bf16[1,10,64,128]{3,2,1,0:T(8,128)(2,1)S(1)}, u32[]{:S(2)}, u32[]{:S(2)}) collective-permute-start(bf16[1,10,64,128]{3,2,1,0:T(8,128)(2,1)S(1)} %get-tuple-element.84), channel_id=1, source_target_pairs={{8,8},{10,10},{12,14},{14,12},{16,18},{18,22},{20,16},{22,20},{9,9... | collective-permute-start | bytes 491528 | tf_op jit(solution)/shard_map/ppermute | solution.py:649
  6.6 1.5 %collective-permute-start.2 = (bf16[1,8,64,128]{3,2,1,0:T(8,128)(2,1)S(1)}, bf16[1,8,64,128]{3,2,1,0:T(8,128)(2,1)S(1)}, u32[]{:S(2)}, u32[]{:S(2)}) collective-permute-start(bf16[1,8,64,128]{3,2,1,0:T(8,128)(2,1)S(1)} %get-tuple-element.81.refs_0_), channel_id=1, source_target_pairs={{24,16},{26,20},{28,18},{30,22},{25,17},{27,21},{29,19},{31,23}} | collective-permute-start | bytes 393224 | tf_op jit(solution)/shard_map/ppermute | solution.py:649
  8.2 1.3 %collective-permute-start.6 = (bf16[2,1,64,128]{3,2,1,0:T(8,128)(2,1)S(1)}, bf16[2,1,64,128]{3,2,1,0:T(8,128)(2,1)S(1)}, u32[]{:S(2)}, u32[]{:S(2)}) collective-permute-start(bf16[2,1,64,128]{3,2,1,0:T(8,128)(2,1)S(1)} %get-tuple-element.89), channel_id=1, source_target_pairs={{0,1},{1,0},{2,3},{3,2},{4,5},{5,4},{6,7},{7,6},{8,9},{9,8},{10,11... | collective-permute-start | bytes 98312 | tf_op jit(solution)/shard_map/ppermute | solution.py:70
  9.5 2.0 %collective-permute-start.9 = (bf16[1,8,64,128]{3,2,1,0:T(8,128)(2,1)S(1)}, bf16[1,8,64,128]{3,2,1,0:T(8,128)(2,1)S(1)}, u32[]{:S(2)}, u32[]{:S(2)}) collective-permute-start(bf16[1,8,64,128]{3,2,1,0:T(8,128)(2,1)S(1)} %get-tuple-element.93), channel_id=1, source_target_pairs={{16,8},{18,10},{20,12},{22,14},{17,9},{19,11},{21,13},{23,15}} | collective-permute-start | bytes 393224 | tf_op jit(solution)/shard_map/ppermute | solution.py:649
  10.1 1.4 %collective-permute-start.8 = (bf16[1,8,64,128]{3,2,1,0:T(8,128)(2,1)S(1)}, bf16[1,8,64,128]{3,2,1,0:T(8,128)(2,1)S(1)}, u32[]{:S(2)}, u32[]{:S(2)}) collective-permute-start(bf16[1,8,64,128]{3,2,1,0:T(8,128)(2,1)S(1)} %get-tuple-element.92), channel_id=1, source_target_pairs={{16,8},{18,10},{20,12},{22,14},{17,9},{19,11},{21,13},{23,15}} | collective-permute-start | bytes 393224 | tf_op jit(solution)/shard_map/ppermute | solution.py:649
  12.8 35.1 %collective-permute-start.12 = (bf16[1,8,64,128]{3,2,1,0:T(8,128)(2,1)S(1)}, bf16[1,8,64,128]{3,2,1,0:T(8,128)(2,1)S(1)}, u32[]{:S(2)}, u32[]{:S(2)}) collective-permute-start(bf16[1,8,64,128]{3,2,1,0:T(8,128)(2,1)S(1)} %get-tuple-element.98.refs_3_), channel_id=1, source_target_pairs={{10,0},{12,6},{11,1},{13,7}} | collective-permute-start | bytes 393224 | tf_op jit(solution)/shard_map/ppermute | solution.py:649
  14.1 36.5 %collective-permute-start.11 = (bf16[1,8,64,128]{3,2,1,0:T(8,128)(2,1)S(1)}, bf16[1,8,64,128]{3,2,1,0:T(8,128)(2,1)S(1)}, u32[]{:S(2)}, u32[]{:S(2)}) collective-permute-start(bf16[1,8,64,128]{3,2,1,0:T(8,128)(2,1)S(1)} %get-tuple-element.98.refs_3_), channel_id=1, source_target_pairs={{8,0},{10,2},{12,4},{14,6},{9,1},{11,3},{13,5},{15,7}} | collective-permute-start | bytes 393224 | tf_op jit(solution)/shard_map/ppermute | solution.py:649
  15.4 36.8 %collective-permute-start.17 = (bf16[1,8,64,128]{3,2,1,0:T(8,128)(2,1)S(1)}, bf16[1,8,64,128]{3,2,1,0:T(8,128)(2,1)S(1)}, u32[]{:S(2)}, u32[]{:S(2)}) collective-permute-start(bf16[1,8,64,128]{3,2,1,0:T(8,128)(2,1)S(1)} %get-tuple-element.97.refs_2_), channel_id=1, source_target_pairs={{12,2},{14,4},{13,3},{15,5}} | collective-permute-start | bytes 393224 | tf_op jit(solution)/shard_map/ppermute | solution.py:649
  16.1 36.1 %collective-permute-start.16 = (bf16[1,8,64,128]{3,2,1,0:T(8,128)(2,1)S(1)}, bf16[1,8,64,128]{3,2,1,0:T(8,128)(2,1)S(1)}, u32[]{:S(2)}, u32[]{:S(2)}) collective-permute-start(bf16[1,8,64,128]{3,2,1,0:T(8,128)(2,1)S(1)} %get-tuple-element.97.refs_2_), channel_id=1, source_target_pairs={{8,2},{10,4},{9,3},{11,5}} | collective-permute-start | bytes 393224 | tf_op jit(solution)/shard_map/ppermute | solution.py:649
  16.7 36.7 %collective-permute-start.15 = (bf16[1,8,64,128]{3,2,1,0:T(8,128)(2,1)S(1)}, bf16[1,8,64,128]{3,2,1,0:T(8,128)(2,1)S(1)}, u32[]{:S(2)}, u32[]{:S(2)}) collective-permute-start(bf16[1,8,64,128]{3,2,1,0:T(8,128)(2,1)S(1)} %get-tuple-element.97.refs_2_), channel_id=1, source_target_pairs={{8,0},{10,2},{12,4},{14,6},{9,1},{11,3},{13,5},{15,7}} | collective-permute-start | bytes 393224 | tf_op jit(solution)/shard_map/ppermute | solution.py:649
  50.6 2.8 %collective-permute-start.13 = (bf16[1,8,64,128]{3,2,1,0:T(8,128)(2,1)S(1)}, bf16[1,8,64,128]{3,2,1,0:T(8,128)(2,1)S(1)}, u32[]{:S(2)}, u32[]{:S(2)}) collective-permute-start(bf16[1,8,64,128]{3,2,1,0:T(8,128)(2,1)S(1)} %get-tuple-element.101), channel_id=1, source_target_pairs={{10,8},{8,10},{12,12},{14,14},{16,16},{20,18},{18,20},{22,22},{11,... | collective-permute-start | bytes 393224 | tf_op jit(solution)/shard_map/ppermute | solution.py:649
  51.3 2.1 %collective-permute-start.14 = (bf16[1,8,64,128]{3,2,1,0:T(8,128)(2,1)S(1)}, bf16[1,8,64,128]{3,2,1,0:T(8,128)(2,1)S(1)}, u32[]{:S(2)}, u32[]{:S(2)}) collective-permute-start(bf16[1,8,64,128]{3,2,1,0:T(8,128)(2,1)S(1)} %get-tuple-element.102), channel_id=1, source_target_pairs={{8,8},{10,10},{14,12},{12,14},{18,16},{22,18},{16,20},{20,22},{9,9... | collective-permute-start | bytes 393224 | tf_op jit(solution)/shard_map/ppermute | solution.py:649
  54.7 2.2 %collective-permute-start.19 = (bf16[4,192,128]{2,1,0:T(8,128)(2,1)S(1)}, bf16[4,192,128]{2,1,0:T(8,128)(2,1)S(1)}, u32[]{:S(2)}, u32[]{:S(2)}) collective-permute-start(bf16[4,192,128]{2,1,0:T(8,128)(2,1)S(1)} %shard_map.86), channel_id=1, source_target_pairs={{0,1},{1,0},{2,3},{3,2},{4,5},{5,4},{6,7},{7,6},{8,9},{9,8},{10,11... | collective-permute-start | bytes 589832 | tf_op jit(solution)/shard_map/ppermute | solution.py:611
  54.8 1.4 %collective-permute-start.18 = (bf16[2,1,64,128]{3,2,1,0:T(8,128)(2,1)S(1)}, bf16[2,1,64,128]{3,2,1,0:T(8,128)(2,1)S(1)}, u32[]{:S(2)}, u32[]{:S(2)}) collective-permute-start(bf16[2,1,64,128]{3,2,1,0:T(8,128)(2,1)S(1)} %get-tuple-element.114), channel_id=1, source_target_pairs={{0,1},{1,0},{2,3},{3,2},{4,5},{5,4},{6,7},{7,6},{8,9},{9,8},{10,11... | collective-permute-start | bytes 98312 | tf_op jit(solution)/shard_map/ppermute | solution.py:70
  57.0 7.9 %collective-permute-start.20 = (bf16[192,128]{1,0:T(8,128)(2,1)S(1)}, bf16[192,128]{1,0:T(8,128)(2,1)S(1)}, u32[]{:S(2)}, u32[]{:S(2)}) collective-permute-start(bf16[192,128]{1,0:T(8,128)(2,1)S(1)} %get-tuple-element.130), channel_id=1, source_target_pairs={{0,2},{2,0},{4,6},{6,4},{1,3},{3,1},{5,7},{7,5},{8,10},{10,8},{12,... | collective-permute-start | bytes 147464 | tf_op jit(solution)/shard_map/ppermute | solution.py:608
  61.7 6.7 %collective-permute-start.21 = (bf16[192,128]{1,0:T(8,128)(2,1)S(1)}, bf16[192,128]{1,0:T(8,128)(2,1)S(1)}, u32[]{:S(2)}, u32[]{:S(2)}) collective-permute-start(bf16[192,128]{1,0:T(8,128)(2,1)S(1)} %get-tuple-element.131), channel_id=1, source_target_pairs={{0,4},{2,6},{4,0},{6,2},{1,5},{3,7},{5,1},{7,3},{8,12},{10,14},{12... | collective-permute-start | bytes 147464 | tf_op jit(solution)/shard_map/ppermute | solution.py:608
  61.7 6.7 %collective-permute-start.22 = (bf16[192,128]{1,0:T(8,128)(2,1)S(1)}, bf16[192,128]{1,0:T(8,128)(2,1)S(1)}, u32[]{:S(2)}, u32[]{:S(2)}) collective-permute-start(bf16[192,128]{1,0:T(8,128)(2,1)S(1)} %get-tuple-element.132), channel_id=1, source_target_pairs={{0,6},{2,4},{4,2},{6,0},{1,7},{3,5},{5,3},{7,1},{8,14},{10,12},{12... | collective-permute-start | bytes 147464 | tf_op jit(solution)/shard_map/ppermute | solution.py:608
  68.4 6.3 %collective-permute-start.25 = (bf16[192,128]{1,0:T(8,128)(2,1)S(1)}, bf16[192,128]{1,0:T(8,128)(2,1)S(1)}, u32[]{:S(2)}, u32[]{:S(2)}) collective-permute-start(bf16[192,128]{1,0:T(8,128)(2,1)S(1)} %shard_map.89.refs_0_), channel_id=1, source_target_pairs={{0,6},{2,4},{4,2},{6,0},{1,7},{3,5},{5,3},{7,1},{8,14},{10,12},{12... | collective-permute-start | bytes 147464 | tf_op jit(solution)/shard_map/ppermute | solution.py:608
  70.2 5.8 %collective-permute-start.24 = (bf16[192,128]{1,0:T(8,128)(2,1)S(1)}, bf16[192,128]{1,0:T(8,128)(2,1)S(1)}, u32[]{:S(2)}, u32[]{:S(2)}) collective-permute-start(bf16[192,128]{1,0:T(8,128)(2,1)S(1)} %shard_map.89.refs_0_), channel_id=1, source_target_pairs={{0,4},{2,6},{4,0},{6,2},{1,5},{3,7},{5,1},{7,3},{8,12},{10,14},{12... | collective-permute-start | bytes 147464 | tf_op jit(solution)/shard_map/ppermute | solution.py:608
  71.3 4.7 %collective-permute-start.23 = (bf16[192,128]{1,0:T(8,128)(2,1)S(1)}, bf16[192,128]{1,0:T(8,128)(2,1)S(1)}, u32[]{:S(2)}, u32[]{:S(2)}) collective-permute-start(bf16[192,128]{1,0:T(8,128)(2,1)S(1)} %shard_map.89.refs_0_), channel_id=1, source_target_pairs={{0,2},{2,0},{4,6},{6,4},{1,3},{3,1},{5,7},{7,5},{8,10},{10,8},{12,... | collective-permute-start | bytes 147464 | tf_op jit(solution)/shard_map/ppermute | solution.py:608
  76.0 1.5 %collective-permute-start.26 = (bf16[4,192,128]{2,1,0:T(8,128)(2,1)S(1)}, bf16[4,192,128]{2,1,0:T(8,128)(2,1)S(1)}, u32[]{:S(2)}, u32[]{:S(2)}) collective-permute-start(bf16[4,192,128]{2,1,0:T(8,128)(2,1)S(1)} %shard_map.90.mine_ref), channel_id=1, source_target_pairs={{0,1},{1,0},{2,3},{3,2},{4,5},{5,4},{6,7},{7,6},{8,9},{9,8},{10,11... | collective-permute-start | bytes 589832 | tf_op jit(solution)/shard_map/ppermute | solution.py:619
  (8 other events, 8.0 us)

commit v6 on v5

--- a/solution.py
+++ b/solution.py
@@ -23,7 +23,7 @@
         in_specs=[pl.BlockSpec() if loose else pl.BlockSpec(memory_space=pltpu.VMEM) for _ in args],
         out_specs=[pl.BlockSpec(memory_space=pltpu.VMEM) for _ in outs],
         compiler_params=pltpu.CompilerParams(vmem_limit_bytes=VMEM_LIMIT),
-        cost_estimate=pl.CostEstimate(flops=flops, bytes_accessed=moved, transcendentals=0),
+        cost_estimate=pl.CostEstimate(flops=1, bytes_accessed=1, transcendentals=0),
     )(*args)
 
 

time: 78.9 us -> 77.8 us (0.986)
    unnamed x10 -> x8, local copies, waits for them, and re-layouts: 2.46 us -> 2.07 us
  transfers between devices with their start and end apart: 27 -> 27, of which waited for: 11 -> 10; matrix products, arithmetic and copies ran while one was open for 0% -> 0% of each run, Pallas kernels for 2% -> 2%
where the time goes in v6:
time: 77.8 us; the launch traced here: 77.4 us
  waiting for transfers between devices  44.7 us (57%)
  starting transfers between devices  24.9 us (32%)
  Pallas kernels  4.69 us (6%)
  local copies, waits for them, and re-layouts  2.07 us (3%)
  between operations  1.03 us (1%)
    ppermute x14, waiting for transfers between devices, send(): return lax.ppermute(block, ('section', 'frame'), route)  33.8 us
    ppermute x6, starting transfers between devices, over_frame(): return lax.ppermute(block, 'frame', [(i, i ^ mask) for i in range(4)])  11.6 us
    ppermute x14, starting transfers between devices, send(): return lax.ppermute(block, ('section', 'frame'), route)  11.2 us
    ppermute x6, waiting for transfers between devices, over_frame(): return lax.ppermute(block, 'frame', [(i, i ^ mask) for i in range(4)])  6.66 us
    pallas_call x25, Pallas kernels, call(): pl.pallas_call(body, out_shape=outs, in_specs=[pl.BlockSpec() if loose el...  4.69 us
    ppermute x5, waiting for transfers between devices, swap_edges(): return [lax.ppermute(edges[0], 'row', [(0, 1), (1, 0)])]  2.81 us
    unnamed x8, local copies, waits for them, and re-layouts  2.07 us
    ppermute x5, starting transfers between devices, swap_edges(): return [lax.ppermute(edges[0], 'row', [(0, 1), (1, 0)])]  1.89 us
  transfers between devices with their start and end apart: 27, of which 10 were waited for; matrix products, arithmetic and copies ran while one was open for 0% of the time, Pallas kernels for 2%

profile of v6, /device:TPU:0, one launch (start us, length us, event | category | flops | bytes accessed | tf_op | source)
XLA Modules:
  0.0 77.4 jit_solution(10030430204924160695)
XLA Ops:
  0.6 1.0 %copy-done.2 = bf16[1,2,8,64,128]{4,3,2,1,0:T(8,128)(2,1)S(1)} copy-done((bf16[1,2,8,64,128]{4,3,2,1,0:T(8,128)(2,1)S(1)}, bf16[1,2,8,64,128]{4,3,2,1,0:T(8,128)(2,1)}, u32[]{:S(2)}) %copy-start.2) | copy-done | bytes 262168
  2.2 0.9 %copy-done.3 = bf16[2,8,64,128]{3,2,1,0:T(8,128)(2,1)S(1)} copy-done((bf16[2,8,64,128]{3,2,1,0:T(8,128)(2,1)S(1)}, bf16[2,8,64,128]{3,2,1,0:T(8,128)(2,1)}, u32[]{:S(2)}) %copy-start.3) | copy-done | bytes 262168
  3.2 0.8 shard_map.69
  7.5 0.9 %collective-permute-done.6.refs_2_ = bf16[2,1,64,128]{3,2,1,0:T(8,128)(2,1)S(1)} collective-permute-done((bf16[2,1,64,128]{3,2,1,0:T(8,128)(2,1)S(1)}, bf16[2,1,64,128]{3,2,1,0:T(8,128)(2,1)S(1)}, u32[]{:S(2)}, u32[]{:S(2)}) %collective-permute-start.6) | collective-permute-done | bytes 32800 | tf_op jit(solution)/shard_map/ppermute | solution.py:70
  10.8 0.9 %collective-permute-done.10.refs_2_ = bf16[2,1,64,128]{3,2,1,0:T(8,128)(2,1)S(1)} collective-permute-done((bf16[2,1,64,128]{3,2,1,0:T(8,128)(2,1)S(1)}, bf16[2,1,64,128]{3,2,1,0:T(8,128)(2,1)S(1)}, u32[]{:S(2)}, u32[]{:S(2)}) %collective-permute-start.10) | collective-permute-done | bytes 32800 | tf_op jit(solution)/shard_map/ppermute | solution.py:70
  11.7 1.3 %collective-permute-start.12 = (bf16[1,8,64,128]{3,2,1,0:T(8,128)(2,1)S(1)}, bf16[1,8,64,128]{3,2,1,0:T(8,128)(2,1)S(1)}, u32[]{:S(2)}, u32[]{:S(2)}) collective-permute-start(bf16[1,8,64,128]{3,2,1,0:T(8,128)(2,1)S(1)} %get-tuple-element.98.refs_3_), channel_id=1, source_target_pairs={{10,0},{12,6},{11,1},{13,7}} | collective-permute-start | bytes 393224 | tf_op jit(solution)/shard_map/ppermute | solution.py:649
  13.0 1.3 %collective-permute-start.11 = (bf16[1,8,64,128]{3,2,1,0:T(8,128)(2,1)S(1)}, bf16[1,8,64,128]{3,2,1,0:T(8,128)(2,1)S(1)}, u32[]{:S(2)}, u32[]{:S(2)}) collective-permute-start(bf16[1,8,64,128]{3,2,1,0:T(8,128)(2,1)S(1)} %get-tuple-element.98.refs_3_), channel_id=1, source_target_pairs={{8,0},{10,2},{12,4},{14,6},{9,1},{11,3},{13,5},{15,7}} | collective-permute-start | bytes 393224 | tf_op jit(solution)/shard_map/ppermute | solution.py:649
  15.7 1.3 %collective-permute-start.15 = (bf16[1,8,64,128]{3,2,1,0:T(8,128)(2,1)S(1)}, bf16[1,8,64,128]{3,2,1,0:T(8,128)(2,1)S(1)}, u32[]{:S(2)}, u32[]{:S(2)}) collective-permute-start(bf16[1,8,64,128]{3,2,1,0:T(8,128)(2,1)S(1)} %get-tuple-element.97.refs_2_), channel_id=1, source_target_pairs={{8,0},{10,2},{12,4},{14,6},{9,1},{11,3},{13,5},{15,7}} | collective-permute-start | bytes 393224 | tf_op jit(solution)/shard_map/ppermute | solution.py:649
  17.0 29.8 %collective-permute-done.12.refs_1_ = bf16[1,8,64,128]{3,2,1,0:T(8,128)(2,1)S(1)} collective-permute-done((bf16[1,8,64,128]{3,2,1,0:T(8,128)(2,1)S(1)}, bf16[1,8,64,128]{3,2,1,0:T(8,128)(2,1)S(1)}, u32[]{:S(2)}, u32[]{:S(2)}) %collective-permute-start.12) | collective-permute-done | bytes 131104 | tf_op jit(solution)/shard_map/ppermute | solution.py:649
  46.8 2.7 %collective-permute-done.11.refs_0_ = bf16[1,8,64,128]{3,2,1,0:T(8,128)(2,1)S(1)} collective-permute-done((bf16[1,8,64,128]{3,2,1,0:T(8,128)(2,1)S(1)}, bf16[1,8,64,128]{3,2,1,0:T(8,128)(2,1)S(1)}, u32[]{:S(2)}, u32[]{:S(2)}) %collective-permute-start.11) | collective-permute-done | bytes 131104 | tf_op jit(solution)/shard_map/ppermute | solution.py:649
  51.1 1.2 %collective-permute-done.15.refs_2_ = bf16[1,8,64,128]{3,2,1,0:T(8,128)(2,1)S(1)} collective-permute-done((bf16[1,8,64,128]{3,2,1,0:T(8,128)(2,1)S(1)}, bf16[1,8,64,128]{3,2,1,0:T(8,128)(2,1)S(1)}, u32[]{:S(2)}, u32[]{:S(2)}) %collective-permute-start.15) | collective-permute-done | bytes 131104 | tf_op jit(solution)/shard_map/ppermute | solution.py:649
  52.8 0.8 shard_map.85
  54.2 1.0 %collective-permute-done.18.refs_2_ = bf16[2,1,64,128]{3,2,1,0:T(8,128)(2,1)S(1)} collective-permute-done((bf16[2,1,64,128]{3,2,1,0:T(8,128)(2,1)S(1)}, bf16[2,1,64,128]{3,2,1,0:T(8,128)(2,1)S(1)}, u32[]{:S(2)}, u32[]{:S(2)}) %collective-permute-start.18) | collective-permute-done | bytes 32800 | tf_op jit(solution)/shard_map/ppermute | solution.py:70
  55.9 4.7 %collective-permute-start.20 = (bf16[192,128]{1,0:T(8,128)(2,1)S(1)}, bf16[192,128]{1,0:T(8,128)(2,1)S(1)}, u32[]{:S(2)}, u32[]{:S(2)}) collective-permute-start(bf16[192,128]{1,0:T(8,128)(2,1)S(1)} %get-tuple-element.130), channel_id=1, source_target_pairs={{0,2},{2,0},{4,6},{6,4},{1,3},{3,1},{5,7},{7,5},{8,10},{10,8},{12,... | collective-permute-start | bytes 147464 | tf_op jit(solution)/shard_map/ppermute | solution.py:608
  60.7 2.4 %collective-permute-start.22 = (bf16[192,128]{1,0:T(8,128)(2,1)S(1)}, bf16[192,128]{1,0:T(8,128)(2,1)S(1)}, u32[]{:S(2)}, u32[]{:S(2)}) collective-permute-start(bf16[192,128]{1,0:T(8,128)(2,1)S(1)} %get-tuple-element.132), channel_id=1, source_target_pairs={{0,6},{2,4},{4,2},{6,0},{1,7},{3,5},{5,3},{7,1},{8,14},{10,12},{12... | collective-permute-start | bytes 147464 | tf_op jit(solution)/shard_map/ppermute | solution.py:608
  63.1 0.7 shard_map.88
  63.8 3.5 %collective-permute-done.21.refs_2_ = bf16[192,128]{1,0:T(8,128)(2,1)S(1)} collective-permute-done((bf16[192,128]{1,0:T(8,128)(2,1)S(1)}, bf16[192,128]{1,0:T(8,128)(2,1)S(1)}, u32[]{:S(2)}, u32[]{:S(2)}) %collective-permute-start.21) | collective-permute-done | bytes 49184 | tf_op jit(solution)/shard_map/ppermute | solution.py:608
  67.4 1.8 %collective-permute-start.25 = (bf16[192,128]{1,0:T(8,128)(2,1)S(1)}, bf16[192,128]{1,0:T(8,128)(2,1)S(1)}, u32[]{:S(2)}, u32[]{:S(2)}) collective-permute-start(bf16[192,128]{1,0:T(8,128)(2,1)S(1)} %shard_map.89.refs_0_), channel_id=1, source_target_pairs={{0,6},{2,4},{4,2},{6,0},{1,7},{3,5},{5,3},{7,1},{8,14},{10,12},{12... | collective-permute-start | bytes 147464 | tf_op jit(solution)/shard_map/ppermute | solution.py:608
  69.2 1.1 %collective-permute-start.24 = (bf16[192,128]{1,0:T(8,128)(2,1)S(1)}, bf16[192,128]{1,0:T(8,128)(2,1)S(1)}, u32[]{:S(2)}, u32[]{:S(2)}) collective-permute-start(bf16[192,128]{1,0:T(8,128)(2,1)S(1)} %shard_map.89.refs_0_), channel_id=1, source_target_pairs={{0,4},{2,6},{4,0},{6,2},{1,5},{3,7},{5,1},{7,3},{8,12},{10,14},{12... | collective-permute-start | bytes 147464 | tf_op jit(solution)/shard_map/ppermute | solution.py:608
  70.3 1.5 %collective-permute-start.23 = (bf16[192,128]{1,0:T(8,128)(2,1)S(1)}, bf16[192,128]{1,0:T(8,128)(2,1)S(1)}, u32[]{:S(2)}, u32[]{:S(2)}) collective-permute-start(bf16[192,128]{1,0:T(8,128)(2,1)S(1)} %shard_map.89.refs_0_), channel_id=1, source_target_pairs={{0,2},{2,0},{4,6},{6,4},{1,3},{3,1},{5,7},{7,5},{8,10},{10,8},{12,... | collective-permute-start | bytes 147464 | tf_op jit(solution)/shard_map/ppermute | solution.py:608
  71.8 1.9 %collective-permute-done.25.refs_3_ = bf16[192,128]{1,0:T(8,128)(2,1)S(1)} collective-permute-done((bf16[192,128]{1,0:T(8,128)(2,1)S(1)}, bf16[192,128]{1,0:T(8,128)(2,1)S(1)}, u32[]{:S(2)}, u32[]{:S(2)}) %collective-permute-start.25) | collective-permute-done | bytes 49184 | tf_op jit(solution)/shard_map/ppermute | solution.py:608
  73.7 1.3 %collective-permute-done.24.refs_2_ = bf16[192,128]{1,0:T(8,128)(2,1)S(1)} collective-permute-done((bf16[192,128]{1,0:T(8,128)(2,1)S(1)}, bf16[192,128]{1,0:T(8,128)(2,1)S(1)}, u32[]{:S(2)}, u32[]{:S(2)}) %collective-permute-start.24) | collective-permute-done | bytes 49184 | tf_op jit(solution)/shard_map/ppermute | solution.py:608
  75.1 1.4 %collective-permute-done.26.other_ref = bf16[4,192,128]{2,1,0:T(8,128)(2,1)S(1)} collective-permute-done((bf16[4,192,128]{2,1,0:T(8,128)(2,1)S(1)}, bf16[4,192,128]{2,1,0:T(8,128)(2,1)S(1)}, u32[]{:S(2)}, u32[]{:S(2)}) %collective-permute-start.26) | collective-permute-done | bytes 196640 | tf_op jit(solution)/shard_map/ppermute | solution.py:619
  76.5 0.9 %shard_map.91 = (f32[6,192,128]{2,1,0:T(8,128)}, f32[2,192,128]{2,1,0:T(8,128)}) custom-call(bf16[4,192,128]{2,1,0:T(8,128)(2,1)S(1)} %shard_map.90.mine_ref, bf16[4,192,128]{2,1,0:T(8,128)(2,1)S(1)} %collective-permute-done.26.other_ref), custom_call_target="tpu_custom_call" | custom-call | flops 1 | bytes 1 | tf_op jit(solution)/shard_map/pallas_call | solution.py:20
  (63 shorter events, 11.1 us)
Async XLA Ops:
  1.7 1.5 %collective-permute-start = (bf16[2,1,64,128]{3,2,1,0:T(8,128)(2,1)S(1)}, bf16[2,1,64,128]{3,2,1,0:T(8,128)(2,1)S(1)}, u32[]{:S(2)}, u32[]{:S(2)}) collective-permute-start(bf16[2,1,64,128]{3,2,1,0:T(8,128)(2,1)S(1)} %get-tuple-element.75), channel_id=1, source_target_pairs={{0,1},{1,0},{2,3},{3,2},{4,5},{5,4},{6,7},{7,6},{8,9},{9,8},{10,11... | collective-permute-start | bytes 98312 | tf_op jit(solution)/shard_map/ppermute | solution.py:70
  4.1 1.6 %collective-permute-start.1 = (bf16[2,1,64,128]{3,2,1,0:T(8,128)(2,1)S(1)}, bf16[2,1,64,128]{3,2,1,0:T(8,128)(2,1)S(1)}, u32[]{:S(2)}, u32[]{:S(2)}) collective-permute-start(bf16[2,1,64,128]{3,2,1,0:T(8,128)(2,1)S(1)} %get-tuple-element.80), channel_id=1, source_target_pairs={{0,1},{1,0},{2,3},{3,2},{4,5},{5,4},{6,7},{7,6},{8,9},{9,8},{10,11... | collective-permute-start | bytes 98312 | tf_op jit(solution)/shard_map/ppermute | solution.py:70
  4.3 2.7 %collective-permute-start.4 = (bf16[1,10,64,128]{3,2,1,0:T(8,128)(2,1)S(1)}, bf16[1,10,64,128]{3,2,1,0:T(8,128)(2,1)S(1)}, u32[]{:S(2)}, u32[]{:S(2)}) collective-permute-start(bf16[1,10,64,128]{3,2,1,0:T(8,128)(2,1)S(1)} %get-tuple-element.83), channel_id=1, source_target_pairs={{8,10},{10,8},{12,12},{14,14},{16,16},{18,20},{20,18},{22,22},{9,1... | collective-permute-start | bytes 491528 | tf_op jit(solution)/shard_map/ppermute | solution.py:649
  5.0 2.1 %collective-permute-start.5 = (bf16[1,10,64,128]{3,2,1,0:T(8,128)(2,1)S(1)}, bf16[1,10,64,128]{3,2,1,0:T(8,128)(2,1)S(1)}, u32[]{:S(2)}, u32[]{:S(2)}) collective-permute-start(bf16[1,10,64,128]{3,2,1,0:T(8,128)(2,1)S(1)} %get-tuple-element.84), channel_id=1, source_target_pairs={{8,8},{10,10},{12,14},{14,12},{16,18},{18,22},{20,16},{22,20},{9,9... | collective-permute-start | bytes 491528 | tf_op jit(solution)/shard_map/ppermute | solution.py:649
  5.7 1.4 %collective-permute-start.2 = (bf16[1,8,64,128]{3,2,1,0:T(8,128)(2,1)S(1)}, bf16[1,8,64,128]{3,2,1,0:T(8,128)(2,1)S(1)}, u32[]{:S(2)}, u32[]{:S(2)}) collective-permute-start(bf16[1,8,64,128]{3,2,1,0:T(8,128)(2,1)S(1)} %get-tuple-element.81.refs_0_), channel_id=1, source_target_pairs={{24,16},{26,20},{28,18},{30,22},{25,17},{27,21},{29,19},{31,23}} | collective-permute-start | bytes 393224 | tf_op jit(solution)/shard_map/ppermute | solution.py:649
  7.1 1.3 %collective-permute-start.6 = (bf16[2,1,64,128]{3,2,1,0:T(8,128)(2,1)S(1)}, bf16[2,1,64,128]{3,2,1,0:T(8,128)(2,1)S(1)}, u32[]{:S(2)}, u32[]{:S(2)}) collective-permute-start(bf16[2,1,64,128]{3,2,1,0:T(8,128)(2,1)S(1)} %get-tuple-element.89), channel_id=1, source_target_pairs={{0,1},{1,0},{2,3},{3,2},{4,5},{5,4},{6,7},{7,6},{8,9},{9,8},{10,11... | collective-permute-start | bytes 98312 | tf_op jit(solution)/shard_map/ppermute | solution.py:70
  8.4 2.0 %collective-permute-start.9 = (bf16[1,8,64,128]{3,2,1,0:T(8,128)(2,1)S(1)}, bf16[1,8,64,128]{3,2,1,0:T(8,128)(2,1)S(1)}, u32[]{:S(2)}, u32[]{:S(2)}) collective-permute-start(bf16[1,8,64,128]{3,2,1,0:T(8,128)(2,1)S(1)} %get-tuple-element.93), channel_id=1, source_target_pairs={{16,8},{18,10},{20,12},{22,14},{17,9},{19,11},{21,13},{23,15}} | collective-permute-start | bytes 393224 | tf_op jit(solution)/shard_map/ppermute | solution.py:649
  9.1 1.4 %collective-permute-start.8 = (bf16[1,8,64,128]{3,2,1,0:T(8,128)(2,1)S(1)}, bf16[1,8,64,128]{3,2,1,0:T(8,128)(2,1)S(1)}, u32[]{:S(2)}, u32[]{:S(2)}) collective-permute-start(bf16[1,8,64,128]{3,2,1,0:T(8,128)(2,1)S(1)} %get-tuple-element.92), channel_id=1, source_target_pairs={{16,8},{18,10},{20,12},{22,14},{17,9},{19,11},{21,13},{23,15}} | collective-permute-start | bytes 393224 | tf_op jit(solution)/shard_map/ppermute | solution.py:649
  11.7 35.1 %collective-permute-start.12 = (bf16[1,8,64,128]{3,2,1,0:T(8,128)(2,1)S(1)}, bf16[1,8,64,128]{3,2,1,0:T(8,128)(2,1)S(1)}, u32[]{:S(2)}, u32[]{:S(2)}) collective-permute-start(bf16[1,8,64,128]{3,2,1,0:T(8,128)(2,1)S(1)} %get-tuple-element.98.refs_3_), channel_id=1, source_target_pairs={{10,0},{12,6},{11,1},{13,7}} | collective-permute-start | bytes 393224 | tf_op jit(solution)/shard_map/ppermute | solution.py:649
  13.0 36.6 %collective-permute-start.11 = (bf16[1,8,64,128]{3,2,1,0:T(8,128)(2,1)S(1)}, bf16[1,8,64,128]{3,2,1,0:T(8,128)(2,1)S(1)}, u32[]{:S(2)}, u32[]{:S(2)}) collective-permute-start(bf16[1,8,64,128]{3,2,1,0:T(8,128)(2,1)S(1)} %get-tuple-element.98.refs_3_), channel_id=1, source_target_pairs={{8,0},{10,2},{12,4},{14,6},{9,1},{11,3},{13,5},{15,7}} | collective-permute-start | bytes 393224 | tf_op jit(solution)/shard_map/ppermute | solution.py:649
  14.3 36.8 %collective-permute-start.17 = (bf16[1,8,64,128]{3,2,1,0:T(8,128)(2,1)S(1)}, bf16[1,8,64,128]{3,2,1,0:T(8,128)(2,1)S(1)}, u32[]{:S(2)}, u32[]{:S(2)}) collective-permute-start(bf16[1,8,64,128]{3,2,1,0:T(8,128)(2,1)S(1)} %get-tuple-element.97.refs_2_), channel_id=1, source_target_pairs={{12,2},{14,4},{13,3},{15,5}} | collective-permute-start | bytes 393224 | tf_op jit(solution)/shard_map/ppermute | solution.py:649
  15.0 36.1 %collective-permute-start.16 = (bf16[1,8,64,128]{3,2,1,0:T(8,128)(2,1)S(1)}, bf16[1,8,64,128]{3,2,1,0:T(8,128)(2,1)S(1)}, u32[]{:S(2)}, u32[]{:S(2)}) collective-permute-start(bf16[1,8,64,128]{3,2,1,0:T(8,128)(2,1)S(1)} %get-tuple-element.97.refs_2_), channel_id=1, source_target_pairs={{8,2},{10,4},{9,3},{11,5}} | collective-permute-start | bytes 393224 | tf_op jit(solution)/shard_map/ppermute | solution.py:649
  15.7 36.7 %collective-permute-start.15 = (bf16[1,8,64,128]{3,2,1,0:T(8,128)(2,1)S(1)}, bf16[1,8,64,128]{3,2,1,0:T(8,128)(2,1)S(1)}, u32[]{:S(2)}, u32[]{:S(2)}) collective-permute-start(bf16[1,8,64,128]{3,2,1,0:T(8,128)(2,1)S(1)} %get-tuple-element.97.refs_2_), channel_id=1, source_target_pairs={{8,0},{10,2},{12,4},{14,6},{9,1},{11,3},{13,5},{15,7}} | collective-permute-start | bytes 393224 | tf_op jit(solution)/shard_map/ppermute | solution.py:649
  49.6 2.8 %collective-permute-start.13 = (bf16[1,8,64,128]{3,2,1,0:T(8,128)(2,1)S(1)}, bf16[1,8,64,128]{3,2,1,0:T(8,128)(2,1)S(1)}, u32[]{:S(2)}, u32[]{:S(2)}) collective-permute-start(bf16[1,8,64,128]{3,2,1,0:T(8,128)(2,1)S(1)} %get-tuple-element.101), channel_id=1, source_target_pairs={{10,8},{8,10},{12,12},{14,14},{16,16},{20,18},{18,20},{22,22},{11,... | collective-permute-start | bytes 393224 | tf_op jit(solution)/shard_map/ppermute | solution.py:649
  50.3 2.1 %collective-permute-start.14 = (bf16[1,8,64,128]{3,2,1,0:T(8,128)(2,1)S(1)}, bf16[1,8,64,128]{3,2,1,0:T(8,128)(2,1)S(1)}, u32[]{:S(2)}, u32[]{:S(2)}) collective-permute-start(bf16[1,8,64,128]{3,2,1,0:T(8,128)(2,1)S(1)} %get-tuple-element.102), channel_id=1, source_target_pairs={{8,8},{10,10},{14,12},{12,14},{18,16},{22,18},{16,20},{20,22},{9,9... | collective-permute-start | bytes 393224 | tf_op jit(solution)/shard_map/ppermute | solution.py:649
  53.6 2.2 %collective-permute-start.19 = (bf16[4,192,128]{2,1,0:T(8,128)(2,1)S(1)}, bf16[4,192,128]{2,1,0:T(8,128)(2,1)S(1)}, u32[]{:S(2)}, u32[]{:S(2)}) collective-permute-start(bf16[4,192,128]{2,1,0:T(8,128)(2,1)S(1)} %shard_map.86), channel_id=1, source_target_pairs={{0,1},{1,0},{2,3},{3,2},{4,5},{5,4},{6,7},{7,6},{8,9},{9,8},{10,11... | collective-permute-start | bytes 589832 | tf_op jit(solution)/shard_map/ppermute | solution.py:611
  53.8 1.4 %collective-permute-start.18 = (bf16[2,1,64,128]{3,2,1,0:T(8,128)(2,1)S(1)}, bf16[2,1,64,128]{3,2,1,0:T(8,128)(2,1)S(1)}, u32[]{:S(2)}, u32[]{:S(2)}) collective-permute-start(bf16[2,1,64,128]{3,2,1,0:T(8,128)(2,1)S(1)} %get-tuple-element.114), channel_id=1, source_target_pairs={{0,1},{1,0},{2,3},{3,2},{4,5},{5,4},{6,7},{7,6},{8,9},{9,8},{10,11... | collective-permute-start | bytes 98312 | tf_op jit(solution)/shard_map/ppermute | solution.py:70
  55.9 7.9 %collective-permute-start.20 = (bf16[192,128]{1,0:T(8,128)(2,1)S(1)}, bf16[192,128]{1,0:T(8,128)(2,1)S(1)}, u32[]{:S(2)}, u32[]{:S(2)}) collective-permute-start(bf16[192,128]{1,0:T(8,128)(2,1)S(1)} %get-tuple-element.130), channel_id=1, source_target_pairs={{0,2},{2,0},{4,6},{6,4},{1,3},{3,1},{5,7},{7,5},{8,10},{10,8},{12,... | collective-permute-start | bytes 147464 | tf_op jit(solution)/shard_map/ppermute | solution.py:608
  60.7 6.7 %collective-permute-start.21 = (bf16[192,128]{1,0:T(8,128)(2,1)S(1)}, bf16[192,128]{1,0:T(8,128)(2,1)S(1)}, u32[]{:S(2)}, u32[]{:S(2)}) collective-permute-start(bf16[192,128]{1,0:T(8,128)(2,1)S(1)} %get-tuple-element.131), channel_id=1, source_target_pairs={{0,4},{2,6},{4,0},{6,2},{1,5},{3,7},{5,1},{7,3},{8,12},{10,14},{12... | collective-permute-start | bytes 147464 | tf_op jit(solution)/shard_map/ppermute | solution.py:608
  60.7 6.7 %collective-permute-start.22 = (bf16[192,128]{1,0:T(8,128)(2,1)S(1)}, bf16[192,128]{1,0:T(8,128)(2,1)S(1)}, u32[]{:S(2)}, u32[]{:S(2)}) collective-permute-start(bf16[192,128]{1,0:T(8,128)(2,1)S(1)} %get-tuple-element.132), channel_id=1, source_target_pairs={{0,6},{2,4},{4,2},{6,0},{1,7},{3,5},{5,3},{7,1},{8,14},{10,12},{12... | collective-permute-start | bytes 147464 | tf_op jit(solution)/shard_map/ppermute | solution.py:608
  67.4 6.3 %collective-permute-start.25 = (bf16[192,128]{1,0:T(8,128)(2,1)S(1)}, bf16[192,128]{1,0:T(8,128)(2,1)S(1)}, u32[]{:S(2)}, u32[]{:S(2)}) collective-permute-start(bf16[192,128]{1,0:T(8,128)(2,1)S(1)} %shard_map.89.refs_0_), channel_id=1, source_target_pairs={{0,6},{2,4},{4,2},{6,0},{1,7},{3,5},{5,3},{7,1},{8,14},{10,12},{12... | collective-permute-start | bytes 147464 | tf_op jit(solution)/shard_map/ppermute | solution.py:608
  69.2 5.8 %collective-permute-start.24 = (bf16[192,128]{1,0:T(8,128)(2,1)S(1)}, bf16[192,128]{1,0:T(8,128)(2,1)S(1)}, u32[]{:S(2)}, u32[]{:S(2)}) collective-permute-start(bf16[192,128]{1,0:T(8,128)(2,1)S(1)} %shard_map.89.refs_0_), channel_id=1, source_target_pairs={{0,4},{2,6},{4,0},{6,2},{1,5},{3,7},{5,1},{7,3},{8,12},{10,14},{12... | collective-permute-start | bytes 147464 | tf_op jit(solution)/shard_map/ppermute | solution.py:608
  70.3 4.7 %collective-permute-start.23 = (bf16[192,128]{1,0:T(8,128)(2,1)S(1)}, bf16[192,128]{1,0:T(8,128)(2,1)S(1)}, u32[]{:S(2)}, u32[]{:S(2)}) collective-permute-start(bf16[192,128]{1,0:T(8,128)(2,1)S(1)} %shard_map.89.refs_0_), channel_id=1, source_target_pairs={{0,2},{2,0},{4,6},{6,4},{1,3},{3,1},{5,7},{7,5},{8,10},{10,8},{12,... | collective-permute-start | bytes 147464 | tf_op jit(solution)/shard_map/ppermute | solution.py:608
  75.0 1.5 %collective-permute-start.26 = (bf16[4,192,128]{2,1,0:T(8,128)(2,1)S(1)}, bf16[4,192,128]{2,1,0:T(8,128)(2,1)S(1)}, u32[]{:S(2)}, u32[]{:S(2)}) collective-permute-start(bf16[4,192,128]{2,1,0:T(8,128)(2,1)S(1)} %shard_map.90.mine_ref), channel_id=1, source_target_pairs={{0,1},{1,0},{2,3},{3,2},{4,5},{5,4},{6,7},{7,6},{8,9},{9,8},{10,11... | collective-permute-start | bytes 589832 | tf_op jit(solution)/shard_map/ppermute | solution.py:619
  (7 other events, 8.1 us)

commit v7 on v6

--- a/solution.py
+++ b/solution.py
@@ -15,11 +15,12 @@
     return lax.dot_general(a, b, how, preferred_element_type=jnp.float32)
 
 
-def call(body, outs, args, flops, loose=False):
+def call(body, outs, args, flops, loose=False, aliases=None):
     moved = sum(a.size * a.dtype.itemsize for a in (*args, *outs))
     return pl.pallas_call(
         body,
         out_shape=outs,
+        input_output_aliases=aliases or {},
         in_specs=[pl.BlockSpec() if loose else pl.BlockSpec(memory_space=pltpu.VMEM) for _ in args],
         out_specs=[pl.BlockSpec(memory_space=pltpu.VMEM) for _ in outs],
         compiler_params=pltpu.CompilerParams(vmem_limit_bytes=VMEM_LIMIT),
@@ -82,6 +83,76 @@
         return [values]
     pairs = values.reshape((values.shape[0] // chains, chains) + values.shape[1:])
     return [pairs[:, at] for at in range(chains)]
+
+
+def put_picked(out_refs, picks, chain, put):
+    for ref, pick in zip(out_refs, picks):
+        if callable(pick):
+            wanted = pick() if chain == 0 else jnp.logical_not(pick())
+            pl.when(wanted)(lambda ref=ref: put(ref))
+        elif pick == chain:
+            put(ref)
+
+
+def split_branches(owner, grads_pre, edges, heres, taps_space, picks):
+    part = heres[0].shape
+    _, rows, cols, channels = part
+    count = len(heres)
+
+    def wide(sides, taps):
+        sums = mul(sides, taps, NT)
+        return (
+            moved_cols(sums[:, :channels], 1, cols)
+            + sums[:, channels : 2 * channels]
+            + moved_cols(sums[:, 2 * channels :], -1, cols)
+        )
+
+    def rounded(branch, here):
+        branch = branch.astype(jnp.bfloat16).astype(jnp.float32)
+        return (here.astype(jnp.float32) + branch).astype(jnp.bfloat16)
+
+    def inner(*refs):
+        @pl.when(lax.axis_index("section") == owner)
+        def _():
+            w_ref = refs[2 * count]
+            out_refs = refs[2 * count + 1 : -1]
+            taps = jnp.concatenate(
+                [jnp.concatenate([w_ref[2 - i, j] for i in range(3)], axis=1) for j in range(3)],
+                axis=0,
+            )
+            nothing = jnp.zeros((1, 1, cols, channels), jnp.bfloat16)
+            for chain in range(count):
+                sides = jnp.concatenate(moved_rows(refs[chain][...], nothing, nothing), axis=1)
+                branch = wide(sides, taps)
+                refs[-1][chain] = branch[(rows - 1) * cols :]
+                refs[-1][count + chain] = branch[:cols]
+                out = rounded(branch, flat(refs[count + chain][...])).reshape(part)
+                put_picked(
+                    out_refs, picks, chain, lambda ref, out=out: ref.__setitem__(..., out)
+                )
+
+    def outer(*refs):
+        @pl.when(lax.axis_index("section") == owner)
+        def _():
+            row = lax.axis_index("row")
+            at = (1 - row) * (rows - 1)
+            partial_ref, got_ref, *here_refs = refs[len(picks) : len(picks) + 2 + count]
+            w_ref = refs[len(picks) + 2 + count]
+            out_refs = refs[len(picks) + 3 + count :]
+            taps = jnp.concatenate([w_ref[2 * row, j] for j in range(3)], axis=0)
+            for chain in range(count):
+                branch = partial_ref[row * count + chain] + wide(got_ref[chain, 0], taps)
+                out = rounded(branch, here_refs[chain][0, at])
+                put_picked(
+                    out_refs, picks, chain, lambda ref, out=out: ref.__setitem__((0, at), out)
+                )
+
+    outs = [jax.ShapeDtypeStruct(part, jnp.bfloat16)] * len(picks)
+    rim = jax.ShapeDtypeStruct((2 * count, cols, channels), jnp.float32)
+    got = swap_edges(edges)
+    *begun, partial = call(inner, outs + [rim], [*grads_pre, *heres, taps_space], 0)
+    args = [*begun, partial, *got, *heres, taps_space]
+    return call(outer, outs, args, 0, aliases={k: k for k in range(len(picks))})
 
 
 def windows(cells, rows):
@@ -662,7 +733,7 @@
     def step(owner, triples, slopes, picks):
         pre, edges = temporal(owner, triples, slopes, taps_time)
         heres = [blocks[0] for blocks, _ in triples]
-        outs = branches(owner, pre, swap_edges(edges), heres, taps_space, picks)
+        outs = split_branches(owner, pre, edges, heres, taps_space, picks)
         return after(pre, *outs), outs
 
     x_own, slopes_own, actives_own = forward(block_input, x_got, taps_space, 2, (0, 3))

time: 77.8 us -> 76.9 us (0.988)
  waiting for transfers between devices: 44.7 us -> 43.8 us
    ppermute x14, waiting for transfers between devices: 33.8 us -> 32.9 us  [send(): return lax.ppermute(block, ('section', 'frame'), route)]
    pallas_call x25 -> x28, Pallas kernels: 4.69 us -> 4.72 us  [call(): pl.pallas_call(body, out_shape=outs, input_output_aliases=aliases or {},...]
where the time goes in v7:
time: 76.9 us; the launch traced here: 76.5 us
  waiting for transfers between devices  43.8 us (57%)
  starting transfers between devices  24.9 us (32%)
  Pallas kernels  4.72 us (6%)
  local copies, waits for them, and re-layouts  2.07 us (3%)
  between operations  1.04 us (1%)
    ppermute x14, waiting for transfers between devices, send(): return lax.ppermute(block, ('section', 'frame'), route)  32.9 us
    ppermute x6, starting transfers between devices, over_frame(): return lax.ppermute(block, 'frame', [(i, i ^ mask) for i in range(4)])  11.6 us
    ppermute x14, starting transfers between devices, send(): return lax.ppermute(block, ('section', 'frame'), route)  11.2 us
    ppermute x6, waiting for transfers between devices, over_frame(): return lax.ppermute(block, 'frame', [(i, i ^ mask) for i in range(4)])  6.66 us
    pallas_call x28, Pallas kernels, call(): pl.pallas_call(body, out_shape=outs, input_output_aliases=aliases or {},...  4.72 us
    ppermute x5, waiting for transfers between devices, swap_edges(): return [lax.ppermute(edges[0], 'row', [(0, 1), (1, 0)])]  2.81 us
    unnamed x8, local copies, waits for them, and re-layouts  2.07 us
    ppermute x5, starting transfers between devices, swap_edges(): return [lax.ppermute(edges[0], 'row', [(0, 1), (1, 0)])]  1.9 us
  transfers between devices with their start and end apart: 27, of which 10 were waited for; matrix products, arithmetic and copies ran while one was open for 0% of the time, Pallas kernels for 2%

profile of v7, /device:TPU:0, one launch (start us, length us, event | category | flops | bytes accessed | tf_op | source)
XLA Modules:
  0.0 76.5 jit_solution(2643222570275534085)
XLA Ops:
  0.6 1.0 %copy-done.2 = bf16[1,2,8,64,128]{4,3,2,1,0:T(8,128)(2,1)S(1)} copy-done((bf16[1,2,8,64,128]{4,3,2,1,0:T(8,128)(2,1)S(1)}, bf16[1,2,8,64,128]{4,3,2,1,0:T(8,128)(2,1)}, u32[]{:S(2)}) %copy-start.2) | copy-done | bytes 262168
  2.2 0.9 %copy-done.3 = bf16[2,8,64,128]{3,2,1,0:T(8,128)(2,1)S(1)} copy-done((bf16[2,8,64,128]{3,2,1,0:T(8,128)(2,1)S(1)}, bf16[2,8,64,128]{3,2,1,0:T(8,128)(2,1)}, u32[]{:S(2)}) %copy-start.3) | copy-done | bytes 262168
  3.2 0.8 shard_map.69
  7.5 0.9 %collective-permute-done.6.refs_5_ = bf16[2,1,64,128]{3,2,1,0:T(8,128)(2,1)S(1)} collective-permute-done((bf16[2,1,64,128]{3,2,1,0:T(8,128)(2,1)S(1)}, bf16[2,1,64,128]{3,2,1,0:T(8,128)(2,1)S(1)}, u32[]{:S(2)}, u32[]{:S(2)}) %collective-permute-start.6) | collective-permute-done | bytes 32800 | tf_op jit(solution)/shard_map/ppermute | solution.py:71
  10.9 0.9 %collective-permute-done.10.refs_3_ = bf16[2,1,64,128]{3,2,1,0:T(8,128)(2,1)S(1)} collective-permute-done((bf16[2,1,64,128]{3,2,1,0:T(8,128)(2,1)S(1)}, bf16[2,1,64,128]{3,2,1,0:T(8,128)(2,1)S(1)}, u32[]{:S(2)}, u32[]{:S(2)}) %collective-permute-start.10) | collective-permute-done | bytes 32800 | tf_op jit(solution)/shard_map/ppermute | solution.py:71
  11.8 1.3 %collective-permute-start.12 = (bf16[1,8,64,128]{3,2,1,0:T(8,128)(2,1)S(1)}, bf16[1,8,64,128]{3,2,1,0:T(8,128)(2,1)S(1)}, u32[]{:S(2)}, u32[]{:S(2)}) collective-permute-start(bf16[1,8,64,128]{3,2,1,0:T(8,128)(2,1)S(1)} %get-tuple-element.120.refs_3_), channel_id=1, source_target_pairs={{10,0},{12,6},{11,1},{13,7}} | collective-permute-start | bytes 393224 | tf_op jit(solution)/shard_map/ppermute | solution.py:720
  13.1 1.3 %collective-permute-start.11 = (bf16[1,8,64,128]{3,2,1,0:T(8,128)(2,1)S(1)}, bf16[1,8,64,128]{3,2,1,0:T(8,128)(2,1)S(1)}, u32[]{:S(2)}, u32[]{:S(2)}) collective-permute-start(bf16[1,8,64,128]{3,2,1,0:T(8,128)(2,1)S(1)} %get-tuple-element.120.refs_3_), channel_id=1, source_target_pairs={{8,0},{10,2},{12,4},{14,6},{9,1},{11,3},{13,5},{15,7}} | collective-permute-start | bytes 393224 | tf_op jit(solution)/shard_map/ppermute | solution.py:720
  15.7 1.3 %collective-permute-start.15 = (bf16[1,8,64,128]{3,2,1,0:T(8,128)(2,1)S(1)}, bf16[1,8,64,128]{3,2,1,0:T(8,128)(2,1)S(1)}, u32[]{:S(2)}, u32[]{:S(2)}) collective-permute-start(bf16[1,8,64,128]{3,2,1,0:T(8,128)(2,1)S(1)} %get-tuple-element.119.refs_2_), channel_id=1, source_target_pairs={{8,0},{10,2},{12,4},{14,6},{9,1},{11,3},{13,5},{15,7}} | collective-permute-start | bytes 393224 | tf_op jit(solution)/shard_map/ppermute | solution.py:720
  17.0 28.9 %collective-permute-done.12.refs_1_ = bf16[1,8,64,128]{3,2,1,0:T(8,128)(2,1)S(1)} collective-permute-done((bf16[1,8,64,128]{3,2,1,0:T(8,128)(2,1)S(1)}, bf16[1,8,64,128]{3,2,1,0:T(8,128)(2,1)S(1)}, u32[]{:S(2)}, u32[]{:S(2)}) %collective-permute-start.12) | collective-permute-done | bytes 131104 | tf_op jit(solution)/shard_map/ppermute | solution.py:720
  45.9 2.7 %collective-permute-done.11.refs_0_ = bf16[1,8,64,128]{3,2,1,0:T(8,128)(2,1)S(1)} collective-permute-done((bf16[1,8,64,128]{3,2,1,0:T(8,128)(2,1)S(1)}, bf16[1,8,64,128]{3,2,1,0:T(8,128)(2,1)S(1)}, u32[]{:S(2)}, u32[]{:S(2)}) %collective-permute-start.11) | collective-permute-done | bytes 131104 | tf_op jit(solution)/shard_map/ppermute | solution.py:720
  50.2 1.2 %collective-permute-done.15.refs_2_ = bf16[1,8,64,128]{3,2,1,0:T(8,128)(2,1)S(1)} collective-permute-done((bf16[1,8,64,128]{3,2,1,0:T(8,128)(2,1)S(1)}, bf16[1,8,64,128]{3,2,1,0:T(8,128)(2,1)S(1)}, u32[]{:S(2)}, u32[]{:S(2)}) %collective-permute-start.15) | collective-permute-done | bytes 131104 | tf_op jit(solution)/shard_map/ppermute | solution.py:720
  51.9 0.8 shard_map.88
  53.3 1.0 %collective-permute-done.18.refs_2_ = bf16[2,1,64,128]{3,2,1,0:T(8,128)(2,1)S(1)} collective-permute-done((bf16[2,1,64,128]{3,2,1,0:T(8,128)(2,1)S(1)}, bf16[2,1,64,128]{3,2,1,0:T(8,128)(2,1)S(1)}, u32[]{:S(2)}, u32[]{:S(2)}) %collective-permute-start.18) | collective-permute-done | bytes 32800 | tf_op jit(solution)/shard_map/ppermute | solution.py:71
  55.0 4.7 %collective-permute-start.20 = (bf16[192,128]{1,0:T(8,128)(2,1)S(1)}, bf16[192,128]{1,0:T(8,128)(2,1)S(1)}, u32[]{:S(2)}, u32[]{:S(2)}) collective-permute-start(bf16[192,128]{1,0:T(8,128)(2,1)S(1)} %get-tuple-element.152), channel_id=1, source_target_pairs={{0,2},{2,0},{4,6},{6,4},{1,3},{3,1},{5,7},{7,5},{8,10},{10,8},{12,... | collective-permute-start | bytes 147464 | tf_op jit(solution)/shard_map/ppermute | solution.py:679
  59.8 2.4 %collective-permute-start.22 = (bf16[192,128]{1,0:T(8,128)(2,1)S(1)}, bf16[192,128]{1,0:T(8,128)(2,1)S(1)}, u32[]{:S(2)}, u32[]{:S(2)}) collective-permute-start(bf16[192,128]{1,0:T(8,128)(2,1)S(1)} %get-tuple-element.154), channel_id=1, source_target_pairs={{0,6},{2,4},{4,2},{6,0},{1,7},{3,5},{5,3},{7,1},{8,14},{10,12},{12... | collective-permute-start | bytes 147464 | tf_op jit(solution)/shard_map/ppermute | solution.py:679
  62.2 0.7 shard_map.91
  62.9 3.5 %collective-permute-done.21.refs_2_ = bf16[192,128]{1,0:T(8,128)(2,1)S(1)} collective-permute-done((bf16[192,128]{1,0:T(8,128)(2,1)S(1)}, bf16[192,128]{1,0:T(8,128)(2,1)S(1)}, u32[]{:S(2)}, u32[]{:S(2)}) %collective-permute-start.21) | collective-permute-done | bytes 49184 | tf_op jit(solution)/shard_map/ppermute | solution.py:679
  66.5 1.8 %collective-permute-start.25 = (bf16[192,128]{1,0:T(8,128)(2,1)S(1)}, bf16[192,128]{1,0:T(8,128)(2,1)S(1)}, u32[]{:S(2)}, u32[]{:S(2)}) collective-permute-start(bf16[192,128]{1,0:T(8,128)(2,1)S(1)} %shard_map.92.refs_0_), channel_id=1, source_target_pairs={{0,6},{2,4},{4,2},{6,0},{1,7},{3,5},{5,3},{7,1},{8,14},{10,12},{12... | collective-permute-start | bytes 147464 | tf_op jit(solution)/shard_map/ppermute | solution.py:679
  68.3 1.1 %collective-permute-start.24 = (bf16[192,128]{1,0:T(8,128)(2,1)S(1)}, bf16[192,128]{1,0:T(8,128)(2,1)S(1)}, u32[]{:S(2)}, u32[]{:S(2)}) collective-permute-start(bf16[192,128]{1,0:T(8,128)(2,1)S(1)} %shard_map.92.refs_0_), channel_id=1, source_target_pairs={{0,4},{2,6},{4,0},{6,2},{1,5},{3,7},{5,1},{7,3},{8,12},{10,14},{12... | collective-permute-start | bytes 147464 | tf_op jit(solution)/shard_map/ppermute | solution.py:679
  69.4 1.5 %collective-permute-start.23 = (bf16[192,128]{1,0:T(8,128)(2,1)S(1)}, bf16[192,128]{1,0:T(8,128)(2,1)S(1)}, u32[]{:S(2)}, u32[]{:S(2)}) collective-permute-start(bf16[192,128]{1,0:T(8,128)(2,1)S(1)} %shard_map.92.refs_0_), channel_id=1, source_target_pairs={{0,2},{2,0},{4,6},{6,4},{1,3},{3,1},{5,7},{7,5},{8,10},{10,8},{12,... | collective-permute-start | bytes 147464 | tf_op jit(solution)/shard_map/ppermute | solution.py:679
  70.9 1.9 %collective-permute-done.25.refs_3_ = bf16[192,128]{1,0:T(8,128)(2,1)S(1)} collective-permute-done((bf16[192,128]{1,0:T(8,128)(2,1)S(1)}, bf16[192,128]{1,0:T(8,128)(2,1)S(1)}, u32[]{:S(2)}, u32[]{:S(2)}) %collective-permute-start.25) | collective-permute-done | bytes 49184 | tf_op jit(solution)/shard_map/ppermute | solution.py:679
  72.8 1.3 %collective-permute-done.24.refs_2_ = bf16[192,128]{1,0:T(8,128)(2,1)S(1)} collective-permute-done((bf16[192,128]{1,0:T(8,128)(2,1)S(1)}, bf16[192,128]{1,0:T(8,128)(2,1)S(1)}, u32[]{:S(2)}, u32[]{:S(2)}) %collective-permute-start.24) | collective-permute-done | bytes 49184 | tf_op jit(solution)/shard_map/ppermute | solution.py:679
  74.2 1.4 %collective-permute-done.26.other_ref = bf16[4,192,128]{2,1,0:T(8,128)(2,1)S(1)} collective-permute-done((bf16[4,192,128]{2,1,0:T(8,128)(2,1)S(1)}, bf16[4,192,128]{2,1,0:T(8,128)(2,1)S(1)}, u32[]{:S(2)}, u32[]{:S(2)}) %collective-permute-start.26) | collective-permute-done | bytes 196640 | tf_op jit(solution)/shard_map/ppermute | solution.py:690
  75.6 0.9 %shard_map.94 = (f32[6,192,128]{2,1,0:T(8,128)}, f32[2,192,128]{2,1,0:T(8,128)}) custom-call(bf16[4,192,128]{2,1,0:T(8,128)(2,1)S(1)} %shard_map.93.mine_ref, bf16[4,192,128]{2,1,0:T(8,128)(2,1)S(1)} %collective-permute-done.26.other_ref), custom_call_target="tpu_custom_call" | custom-call | flops 1 | bytes 1 | tf_op jit(solution)/shard_map/pallas_call | solution.py:20
  (66 shorter events, 11.2 us)
Async XLA Ops:
  1.7 1.5 %collective-permute-start = (bf16[2,1,64,128]{3,2,1,0:T(8,128)(2,1)S(1)}, bf16[2,1,64,128]{3,2,1,0:T(8,128)(2,1)S(1)}, u32[]{:S(2)}, u32[]{:S(2)}) collective-permute-start(bf16[2,1,64,128]{3,2,1,0:T(8,128)(2,1)S(1)} %get-tuple-element.86), channel_id=1, source_target_pairs={{0,1},{1,0},{2,3},{3,2},{4,5},{5,4},{6,7},{7,6},{8,9},{9,8},{10,11... | collective-permute-start | bytes 98312 | tf_op jit(solution)/shard_map/ppermute | solution.py:71
  4.1 1.6 %collective-permute-start.1 = (bf16[2,1,64,128]{3,2,1,0:T(8,128)(2,1)S(1)}, bf16[2,1,64,128]{3,2,1,0:T(8,128)(2,1)S(1)}, u32[]{:S(2)}, u32[]{:S(2)}) collective-permute-start(bf16[2,1,64,128]{3,2,1,0:T(8,128)(2,1)S(1)} %get-tuple-element.94), channel_id=1, source_target_pairs={{0,1},{1,0},{2,3},{3,2},{4,5},{5,4},{6,7},{7,6},{8,9},{9,8},{10,11... | collective-permute-start | bytes 98312 | tf_op jit(solution)/shard_map/ppermute | solution.py:71
  4.3 2.8 %collective-permute-start.4 = (bf16[1,10,64,128]{3,2,1,0:T(8,128)(2,1)S(1)}, bf16[1,10,64,128]{3,2,1,0:T(8,128)(2,1)S(1)}, u32[]{:S(2)}, u32[]{:S(2)}) collective-permute-start(bf16[1,10,64,128]{3,2,1,0:T(8,128)(2,1)S(1)} %get-tuple-element.97), channel_id=1, source_target_pairs={{8,10},{10,8},{12,12},{14,14},{16,16},{18,20},{20,18},{22,22},{9,1... | collective-permute-start | bytes 491528 | tf_op jit(solution)/shard_map/ppermute | solution.py:720
  5.0 2.1 %collective-permute-start.5 = (bf16[1,10,64,128]{3,2,1,0:T(8,128)(2,1)S(1)}, bf16[1,10,64,128]{3,2,1,0:T(8,128)(2,1)S(1)}, u32[]{:S(2)}, u32[]{:S(2)}) collective-permute-start(bf16[1,10,64,128]{3,2,1,0:T(8,128)(2,1)S(1)} %get-tuple-element.98), channel_id=1, source_target_pairs={{8,8},{10,10},{12,14},{14,12},{16,18},{18,22},{20,16},{22,20},{9,9... | collective-permute-start | bytes 491528 | tf_op jit(solution)/shard_map/ppermute | solution.py:720
  5.7 1.4 %collective-permute-start.2 = (bf16[1,8,64,128]{3,2,1,0:T(8,128)(2,1)S(1)}, bf16[1,8,64,128]{3,2,1,0:T(8,128)(2,1)S(1)}, u32[]{:S(2)}, u32[]{:S(2)}) collective-permute-start(bf16[1,8,64,128]{3,2,1,0:T(8,128)(2,1)S(1)} %get-tuple-element.95.refs_0_), channel_id=1, source_target_pairs={{24,16},{26,20},{28,18},{30,22},{25,17},{27,21},{29,19},{31,23}} | collective-permute-start | bytes 393224 | tf_op jit(solution)/shard_map/ppermute | solution.py:720
  7.1 1.3 %collective-permute-start.6 = (bf16[2,1,64,128]{3,2,1,0:T(8,128)(2,1)S(1)}, bf16[2,1,64,128]{3,2,1,0:T(8,128)(2,1)S(1)}, u32[]{:S(2)}, u32[]{:S(2)}) collective-permute-start(bf16[2,1,64,128]{3,2,1,0:T(8,128)(2,1)S(1)} %get-tuple-element.108), channel_id=1, source_target_pairs={{0,1},{1,0},{2,3},{3,2},{4,5},{5,4},{6,7},{7,6},{8,9},{9,8},{10,11... | collective-permute-start | bytes 98312 | tf_op jit(solution)/shard_map/ppermute | solution.py:71
  8.4 2.0 %collective-permute-start.9 = (bf16[1,8,64,128]{3,2,1,0:T(8,128)(2,1)S(1)}, bf16[1,8,64,128]{3,2,1,0:T(8,128)(2,1)S(1)}, u32[]{:S(2)}, u32[]{:S(2)}) collective-permute-start(bf16[1,8,64,128]{3,2,1,0:T(8,128)(2,1)S(1)} %get-tuple-element.112), channel_id=1, source_target_pairs={{16,8},{18,10},{20,12},{22,14},{17,9},{19,11},{21,13},{23,15}} | collective-permute-start | bytes 393224 | tf_op jit(solution)/shard_map/ppermute | solution.py:720
  9.1 1.4 %collective-permute-start.8 = (bf16[1,8,64,128]{3,2,1,0:T(8,128)(2,1)S(1)}, bf16[1,8,64,128]{3,2,1,0:T(8,128)(2,1)S(1)}, u32[]{:S(2)}, u32[]{:S(2)}) collective-permute-start(bf16[1,8,64,128]{3,2,1,0:T(8,128)(2,1)S(1)} %get-tuple-element.111), channel_id=1, source_target_pairs={{16,8},{18,10},{20,12},{22,14},{17,9},{19,11},{21,13},{23,15}} | collective-permute-start | bytes 393224 | tf_op jit(solution)/shard_map/ppermute | solution.py:720
  11.8 34.2 %collective-permute-start.12 = (bf16[1,8,64,128]{3,2,1,0:T(8,128)(2,1)S(1)}, bf16[1,8,64,128]{3,2,1,0:T(8,128)(2,1)S(1)}, u32[]{:S(2)}, u32[]{:S(2)}) collective-permute-start(bf16[1,8,64,128]{3,2,1,0:T(8,128)(2,1)S(1)} %get-tuple-element.120.refs_3_), channel_id=1, source_target_pairs={{10,0},{12,6},{11,1},{13,7}} | collective-permute-start | bytes 393224 | tf_op jit(solution)/shard_map/ppermute | solution.py:720
  13.1 35.6 %collective-permute-start.11 = (bf16[1,8,64,128]{3,2,1,0:T(8,128)(2,1)S(1)}, bf16[1,8,64,128]{3,2,1,0:T(8,128)(2,1)S(1)}, u32[]{:S(2)}, u32[]{:S(2)}) collective-permute-start(bf16[1,8,64,128]{3,2,1,0:T(8,128)(2,1)S(1)} %get-tuple-element.120.refs_3_), channel_id=1, source_target_pairs={{8,0},{10,2},{12,4},{14,6},{9,1},{11,3},{13,5},{15,7}} | collective-permute-start | bytes 393224 | tf_op jit(solution)/shard_map/ppermute | solution.py:720
  14.4 35.9 %collective-permute-start.17 = (bf16[1,8,64,128]{3,2,1,0:T(8,128)(2,1)S(1)}, bf16[1,8,64,128]{3,2,1,0:T(8,128)(2,1)S(1)}, u32[]{:S(2)}, u32[]{:S(2)}) collective-permute-start(bf16[1,8,64,128]{3,2,1,0:T(8,128)(2,1)S(1)} %get-tuple-element.119.refs_2_), channel_id=1, source_target_pairs={{12,2},{14,4},{13,3},{15,5}} | collective-permute-start | bytes 393224 | tf_op jit(solution)/shard_map/ppermute | solution.py:720
  15.0 35.2 %collective-permute-start.16 = (bf16[1,8,64,128]{3,2,1,0:T(8,128)(2,1)S(1)}, bf16[1,8,64,128]{3,2,1,0:T(8,128)(2,1)S(1)}, u32[]{:S(2)}, u32[]{:S(2)}) collective-permute-start(bf16[1,8,64,128]{3,2,1,0:T(8,128)(2,1)S(1)} %get-tuple-element.119.refs_2_), channel_id=1, source_target_pairs={{8,2},{10,4},{9,3},{11,5}} | collective-permute-start | bytes 393224 | tf_op jit(solution)/shard_map/ppermute | solution.py:720
  15.7 35.7 %collective-permute-start.15 = (bf16[1,8,64,128]{3,2,1,0:T(8,128)(2,1)S(1)}, bf16[1,8,64,128]{3,2,1,0:T(8,128)(2,1)S(1)}, u32[]{:S(2)}, u32[]{:S(2)}) collective-permute-start(bf16[1,8,64,128]{3,2,1,0:T(8,128)(2,1)S(1)} %get-tuple-element.119.refs_2_), channel_id=1, source_target_pairs={{8,0},{10,2},{12,4},{14,6},{9,1},{11,3},{13,5},{15,7}} | collective-permute-start | bytes 393224 | tf_op jit(solution)/shard_map/ppermute | solution.py:720
  48.7 2.8 %collective-permute-start.13 = (bf16[1,8,64,128]{3,2,1,0:T(8,128)(2,1)S(1)}, bf16[1,8,64,128]{3,2,1,0:T(8,128)(2,1)S(1)}, u32[]{:S(2)}, u32[]{:S(2)}) collective-permute-start(bf16[1,8,64,128]{3,2,1,0:T(8,128)(2,1)S(1)} %get-tuple-element.123), channel_id=1, source_target_pairs={{10,8},{8,10},{12,12},{14,14},{16,16},{20,18},{18,20},{22,22},{11,... | collective-permute-start | bytes 393224 | tf_op jit(solution)/shard_map/ppermute | solution.py:720
  49.4 2.1 %collective-permute-start.14 = (bf16[1,8,64,128]{3,2,1,0:T(8,128)(2,1)S(1)}, bf16[1,8,64,128]{3,2,1,0:T(8,128)(2,1)S(1)}, u32[]{:S(2)}, u32[]{:S(2)}) collective-permute-start(bf16[1,8,64,128]{3,2,1,0:T(8,128)(2,1)S(1)} %get-tuple-element.124), channel_id=1, source_target_pairs={{8,8},{10,10},{14,12},{12,14},{18,16},{22,18},{16,20},{20,22},{9,9... | collective-permute-start | bytes 393224 | tf_op jit(solution)/shard_map/ppermute | solution.py:720
  52.7 2.2 %collective-permute-start.19 = (bf16[4,192,128]{2,1,0:T(8,128)(2,1)S(1)}, bf16[4,192,128]{2,1,0:T(8,128)(2,1)S(1)}, u32[]{:S(2)}, u32[]{:S(2)}) collective-permute-start(bf16[4,192,128]{2,1,0:T(8,128)(2,1)S(1)} %shard_map.89), channel_id=1, source_target_pairs={{0,1},{1,0},{2,3},{3,2},{4,5},{5,4},{6,7},{7,6},{8,9},{9,8},{10,11... | collective-permute-start | bytes 589832 | tf_op jit(solution)/shard_map/ppermute | solution.py:682
  52.9 1.4 %collective-permute-start.18 = (bf16[2,1,64,128]{3,2,1,0:T(8,128)(2,1)S(1)}, bf16[2,1,64,128]{3,2,1,0:T(8,128)(2,1)S(1)}, u32[]{:S(2)}, u32[]{:S(2)}) collective-permute-start(bf16[2,1,64,128]{3,2,1,0:T(8,128)(2,1)S(1)} %get-tuple-element.136), channel_id=1, source_target_pairs={{0,1},{1,0},{2,3},{3,2},{4,5},{5,4},{6,7},{7,6},{8,9},{9,8},{10,11... | collective-permute-start | bytes 98312 | tf_op jit(solution)/shard_map/ppermute | solution.py:71
  55.0 7.9 %collective-permute-start.20 = (bf16[192,128]{1,0:T(8,128)(2,1)S(1)}, bf16[192,128]{1,0:T(8,128)(2,1)S(1)}, u32[]{:S(2)}, u32[]{:S(2)}) collective-permute-start(bf16[192,128]{1,0:T(8,128)(2,1)S(1)} %get-tuple-element.152), channel_id=1, source_target_pairs={{0,2},{2,0},{4,6},{6,4},{1,3},{3,1},{5,7},{7,5},{8,10},{10,8},{12,... | collective-permute-start | bytes 147464 | tf_op jit(solution)/shard_map/ppermute | solution.py:679
  59.8 6.7 %collective-permute-start.21 = (bf16[192,128]{1,0:T(8,128)(2,1)S(1)}, bf16[192,128]{1,0:T(8,128)(2,1)S(1)}, u32[]{:S(2)}, u32[]{:S(2)}) collective-permute-start(bf16[192,128]{1,0:T(8,128)(2,1)S(1)} %get-tuple-element.153), channel_id=1, source_target_pairs={{0,4},{2,6},{4,0},{6,2},{1,5},{3,7},{5,1},{7,3},{8,12},{10,14},{12... | collective-permute-start | bytes 147464 | tf_op jit(solution)/shard_map/ppermute | solution.py:679
  59.8 6.7 %collective-permute-start.22 = (bf16[192,128]{1,0:T(8,128)(2,1)S(1)}, bf16[192,128]{1,0:T(8,128)(2,1)S(1)}, u32[]{:S(2)}, u32[]{:S(2)}) collective-permute-start(bf16[192,128]{1,0:T(8,128)(2,1)S(1)} %get-tuple-element.154), channel_id=1, source_target_pairs={{0,6},{2,4},{4,2},{6,0},{1,7},{3,5},{5,3},{7,1},{8,14},{10,12},{12... | collective-permute-start | bytes 147464 | tf_op jit(solution)/shard_map/ppermute | solution.py:679
  66.5 6.3 %collective-permute-start.25 = (bf16[192,128]{1,0:T(8,128)(2,1)S(1)}, bf16[192,128]{1,0:T(8,128)(2,1)S(1)}, u32[]{:S(2)}, u32[]{:S(2)}) collective-permute-start(bf16[192,128]{1,0:T(8,128)(2,1)S(1)} %shard_map.92.refs_0_), channel_id=1, source_target_pairs={{0,6},{2,4},{4,2},{6,0},{1,7},{3,5},{5,3},{7,1},{8,14},{10,12},{12... | collective-permute-start | bytes 147464 | tf_op jit(solution)/shard_map/ppermute | solution.py:679
  68.3 5.8 %collective-permute-start.24 = (bf16[192,128]{1,0:T(8,128)(2,1)S(1)}, bf16[192,128]{1,0:T(8,128)(2,1)S(1)}, u32[]{:S(2)}, u32[]{:S(2)}) collective-permute-start(bf16[192,128]{1,0:T(8,128)(2,1)S(1)} %shard_map.92.refs_0_), channel_id=1, source_target_pairs={{0,4},{2,6},{4,0},{6,2},{1,5},{3,7},{5,1},{7,3},{8,12},{10,14},{12... | collective-permute-start | bytes 147464 | tf_op jit(solution)/shard_map/ppermute | solution.py:679
  69.4 4.7 %collective-permute-start.23 = (bf16[192,128]{1,0:T(8,128)(2,1)S(1)}, bf16[192,128]{1,0:T(8,128)(2,1)S(1)}, u32[]{:S(2)}, u32[]{:S(2)}) collective-permute-start(bf16[192,128]{1,0:T(8,128)(2,1)S(1)} %shard_map.92.refs_0_), channel_id=1, source_target_pairs={{0,2},{2,0},{4,6},{6,4},{1,3},{3,1},{5,7},{7,5},{8,10},{10,8},{12,... | collective-permute-start | bytes 147464 | tf_op jit(solution)/shard_map/ppermute | solution.py:679
  74.1 1.5 %collective-permute-start.26 = (bf16[4,192,128]{2,1,0:T(8,128)(2,1)S(1)}, bf16[4,192,128]{2,1,0:T(8,128)(2,1)S(1)}, u32[]{:S(2)}, u32[]{:S(2)}) collective-permute-start(bf16[4,192,128]{2,1,0:T(8,128)(2,1)S(1)} %shard_map.93.mine_ref), channel_id=1, source_target_pairs={{0,1},{1,0},{2,3},{3,2},{4,5},{5,4},{6,7},{7,6},{8,9},{9,8},{10,11... | collective-permute-start | bytes 589832 | tf_op jit(solution)/shard_map/ppermute | solution.py:690
  (7 other events, 8.1 us)

commit v8 on v7

--- a/solution.py
+++ b/solution.py
@@ -680,8 +680,7 @@
 
     swap = [(0, 1), (1, 0)]
     got = lax.ppermute(call(other_half, [half], [pieces], 0)[0], "row", swap)
-    got = after([got], *first_beside)
-    own, *parts = call(add_half, [wide] + [part] * 3, [pieces, *got], 0)
+    own, *parts = call(add_half, [wide] + [part] * 3, [pieces, got], 0)
     extra = then_beside(parts)
     came = [over_frame(block, mask) for mask, block in enumerate(parts, 1)]
     own = call(add_parts, [part], [own, *after(came, extra)], 0)[0]
@@ -800,7 +799,7 @@
         return finish(branches(0, pre, swap_edges(after(edges, parts)), heres, taps_space), parts)
 
     if dealt:
-        lasts = branches(0, pre, swap_edges(edges), heres, taps_space)
+        lasts = split_branches(0, pre, edges, heres, taps_space, [0, 1])
 
         def result(parts):
             return finish(after(lasts, *parts), parts)

time: 76.9 us -> 76.3 us (level)
    ppermute x6, waiting for transfers between devices: 6.66 us -> 5.13 us  [over_frame(): return lax.ppermute(block, 'frame', [(i, i ^ mask) for i in range(4)])]
    ppermute x1, waiting for transfers between devices: 0.01 us -> 1.38 us  [sum_kernels(): got = lax.ppermute(call(other_half, [half], [pieces], 0)[0], 'row', swap)]
    pallas_call x28 -> x29, Pallas kernels: 4.72 us -> 4.94 us  [call(): pl.pallas_call(body, out_shape=outs, input_output_aliases=aliases or {},...]
  transfers between devices with their start and end apart: 27 -> 27, of which waited for: 10 -> 11; matrix products, arithmetic and copies ran while one was open for 0% -> 0% of each run, Pallas kernels for 2% -> 2%
where the time goes in v8:
time: 76.3 us; the launch traced here: 75.7 us
  waiting for transfers between devices  43.2 us (57%)
  starting transfers between devices  24.5 us (32%)
  Pallas kernels  4.94 us (6%)
  local copies, waits for them, and re-layouts  2.07 us (3%)
  between operations  1.03 us (1%)
    ppermute x14, waiting for transfers between devices, send(): return lax.ppermute(block, ('section', 'frame'), route)  32.9 us
    ppermute x6, starting transfers between devices, over_frame(): return lax.ppermute(block, 'frame', [(i, i ^ mask) for i in range(4)])  11.6 us
    ppermute x14, starting transfers between devices, send(): return lax.ppermute(block, ('section', 'frame'), route)  11.2 us
    ppermute x6, waiting for transfers between devices, over_frame(): return lax.ppermute(block, 'frame', [(i, i ^ mask) for i in range(4)])  5.13 us
    pallas_call x29, Pallas kernels, call(): pl.pallas_call(body, out_shape=outs, input_output_aliases=aliases or {},...  4.94 us
    ppermute x5, waiting for transfers between devices, swap_edges(): return [lax.ppermute(edges[0], 'row', [(0, 1), (1, 0)])]  2.37 us
    unnamed x8, local copies, waits for them, and re-layouts  2.07 us
  transfers between devices with their start and end apart: 27, of which 11 were waited for; matrix products, arithmetic and copies ran while one was open for 0% of the time, Pallas kernels for 2%

profile of v8, /device:TPU:0, one launch (start us, length us, event | category | flops | bytes accessed | tf_op | source)
XLA Modules:
  0.0 75.7 jit_solution(5377108531071989364)
XLA Ops:
  0.6 1.0 %copy-done.2 = bf16[1,2,8,64,128]{4,3,2,1,0:T(8,128)(2,1)S(1)} copy-done((bf16[1,2,8,64,128]{4,3,2,1,0:T(8,128)(2,1)S(1)}, bf16[1,2,8,64,128]{4,3,2,1,0:T(8,128)(2,1)}, u32[]{:S(2)}) %copy-start.2) | copy-done | bytes 262168
  2.2 0.9 %copy-done.3 = bf16[2,8,64,128]{3,2,1,0:T(8,128)(2,1)S(1)} copy-done((bf16[2,8,64,128]{3,2,1,0:T(8,128)(2,1)S(1)}, bf16[2,8,64,128]{3,2,1,0:T(8,128)(2,1)}, u32[]{:S(2)}) %copy-start.3) | copy-done | bytes 262168
  3.2 0.8 shard_map.69
  7.5 0.9 %collective-permute-done.6.refs_5_ = bf16[2,1,64,128]{3,2,1,0:T(8,128)(2,1)S(1)} collective-permute-done((bf16[2,1,64,128]{3,2,1,0:T(8,128)(2,1)S(1)}, bf16[2,1,64,128]{3,2,1,0:T(8,128)(2,1)S(1)}, u32[]{:S(2)}, u32[]{:S(2)}) %collective-permute-start.6) | collective-permute-done | bytes 32800 | tf_op jit(solution)/shard_map/ppermute | solution.py:71
  10.9 0.9 %collective-permute-done.10.refs_3_ = bf16[2,1,64,128]{3,2,1,0:T(8,128)(2,1)S(1)} collective-permute-done((bf16[2,1,64,128]{3,2,1,0:T(8,128)(2,1)S(1)}, bf16[2,1,64,128]{3,2,1,0:T(8,128)(2,1)S(1)}, u32[]{:S(2)}, u32[]{:S(2)}) %collective-permute-start.10) | collective-permute-done | bytes 32800 | tf_op jit(solution)/shard_map/ppermute | solution.py:71
  11.8 1.3 %collective-permute-start.12 = (bf16[1,8,64,128]{3,2,1,0:T(8,128)(2,1)S(1)}, bf16[1,8,64,128]{3,2,1,0:T(8,128)(2,1)S(1)}, u32[]{:S(2)}, u32[]{:S(2)}) collective-permute-start(bf16[1,8,64,128]{3,2,1,0:T(8,128)(2,1)S(1)} %get-tuple-element.122.refs_3_), channel_id=1, source_target_pairs={{10,0},{12,6},{11,1},{13,7}} | collective-permute-start | bytes 393224 | tf_op jit(solution)/shard_map/ppermute | solution.py:719
  13.1 1.3 %collective-permute-start.11 = (bf16[1,8,64,128]{3,2,1,0:T(8,128)(2,1)S(1)}, bf16[1,8,64,128]{3,2,1,0:T(8,128)(2,1)S(1)}, u32[]{:S(2)}, u32[]{:S(2)}) collective-permute-start(bf16[1,8,64,128]{3,2,1,0:T(8,128)(2,1)S(1)} %get-tuple-element.122.refs_3_), channel_id=1, source_target_pairs={{8,0},{10,2},{12,4},{14,6},{9,1},{11,3},{13,5},{15,7}} | collective-permute-start | bytes 393224 | tf_op jit(solution)/shard_map/ppermute | solution.py:719
  15.7 1.3 %collective-permute-start.15 = (bf16[1,8,64,128]{3,2,1,0:T(8,128)(2,1)S(1)}, bf16[1,8,64,128]{3,2,1,0:T(8,128)(2,1)S(1)}, u32[]{:S(2)}, u32[]{:S(2)}) collective-permute-start(bf16[1,8,64,128]{3,2,1,0:T(8,128)(2,1)S(1)} %get-tuple-element.121.refs_2_), channel_id=1, source_target_pairs={{8,0},{10,2},{12,4},{14,6},{9,1},{11,3},{13,5},{15,7}} | collective-permute-start | bytes 393224 | tf_op jit(solution)/shard_map/ppermute | solution.py:719
  17.0 28.9 %collective-permute-done.12.refs_1_ = bf16[1,8,64,128]{3,2,1,0:T(8,128)(2,1)S(1)} collective-permute-done((bf16[1,8,64,128]{3,2,1,0:T(8,128)(2,1)S(1)}, bf16[1,8,64,128]{3,2,1,0:T(8,128)(2,1)S(1)}, u32[]{:S(2)}, u32[]{:S(2)}) %collective-permute-start.12) | collective-permute-done | bytes 131104 | tf_op jit(solution)/shard_map/ppermute | solution.py:719
  45.9 2.7 %collective-permute-done.11.refs_0_ = bf16[1,8,64,128]{3,2,1,0:T(8,128)(2,1)S(1)} collective-permute-done((bf16[1,8,64,128]{3,2,1,0:T(8,128)(2,1)S(1)}, bf16[1,8,64,128]{3,2,1,0:T(8,128)(2,1)S(1)}, u32[]{:S(2)}, u32[]{:S(2)}) %collective-permute-start.11) | collective-permute-done | bytes 131104 | tf_op jit(solution)/shard_map/ppermute | solution.py:719
  50.2 1.2 %collective-permute-done.15.refs_2_ = bf16[1,8,64,128]{3,2,1,0:T(8,128)(2,1)S(1)} collective-permute-done((bf16[1,8,64,128]{3,2,1,0:T(8,128)(2,1)S(1)}, bf16[1,8,64,128]{3,2,1,0:T(8,128)(2,1)S(1)}, u32[]{:S(2)}, u32[]{:S(2)}) %collective-permute-start.15) | collective-permute-done | bytes 131104 | tf_op jit(solution)/shard_map/ppermute | solution.py:719
  51.9 0.8 %shard_map.89 = f32[12,128,128]{2,1,0:T(8,128)S(1)} custom-call(bf16[2,10,64,128]{3,2,1,0:T(8,128)(2,1)S(1)} %get-tuple-element.144.refs_0_, bf16[1,8,64,128]{3,2,1,0:T(8,128)(2,1)S(1)} %get-tuple-element.136.refs_0_.refs_1_, bf16[1,8,64,128]{3,2,1,0:T(8,128)(2,1)S(1)} %get-tuple-element.137.refs_1_.refs_2_, ...), custom_call_target="tpu_custom_call" | custom-call | flops 1 | bytes 1 | tf_op jit(solution)/shard_map/pallas_call | solution.py:20
  52.9 1.4 %collective-permute-done.19.got_ref = bf16[4,192,128]{2,1,0:T(8,128)(2,1)S(1)} collective-permute-done((bf16[4,192,128]{2,1,0:T(8,128)(2,1)S(1)}, bf16[4,192,128]{2,1,0:T(8,128)(2,1)S(1)}, u32[]{:S(2)}, u32[]{:S(2)}) %collective-permute-start.19) | collective-permute-done | bytes 196640 | tf_op jit(solution)/shard_map/ppermute | solution.py:682
  54.3 4.7 %collective-permute-start.20 = (bf16[192,128]{1,0:T(8,128)(2,1)S(1)}, bf16[192,128]{1,0:T(8,128)(2,1)S(1)}, u32[]{:S(2)}, u32[]{:S(2)}) collective-permute-start(bf16[192,128]{1,0:T(8,128)(2,1)S(1)} %get-tuple-element.156), channel_id=1, source_target_pairs={{0,2},{2,0},{4,6},{6,4},{1,3},{3,1},{5,7},{7,5},{8,10},{10,8},{12,... | collective-permute-start | bytes 147464 | tf_op jit(solution)/shard_map/ppermute | solution.py:679
  59.0 2.4 %collective-permute-start.22 = (bf16[192,128]{1,0:T(8,128)(2,1)S(1)}, bf16[192,128]{1,0:T(8,128)(2,1)S(1)}, u32[]{:S(2)}, u32[]{:S(2)}) collective-permute-start(bf16[192,128]{1,0:T(8,128)(2,1)S(1)} %get-tuple-element.158), channel_id=1, source_target_pairs={{0,6},{2,4},{4,2},{6,0},{1,7},{3,5},{5,3},{7,1},{8,14},{10,12},{12... | collective-permute-start | bytes 147464 | tf_op jit(solution)/shard_map/ppermute | solution.py:679
  62.9 0.7 shard_map.92
  63.6 2.0 %collective-permute-done.21.refs_2_ = bf16[192,128]{1,0:T(8,128)(2,1)S(1)} collective-permute-done((bf16[192,128]{1,0:T(8,128)(2,1)S(1)}, bf16[192,128]{1,0:T(8,128)(2,1)S(1)}, u32[]{:S(2)}, u32[]{:S(2)}) %collective-permute-start.21) | collective-permute-done | bytes 49184 | tf_op jit(solution)/shard_map/ppermute | solution.py:679
  65.7 1.8 %collective-permute-start.25 = (bf16[192,128]{1,0:T(8,128)(2,1)S(1)}, bf16[192,128]{1,0:T(8,128)(2,1)S(1)}, u32[]{:S(2)}, u32[]{:S(2)}) collective-permute-start(bf16[192,128]{1,0:T(8,128)(2,1)S(1)} %shard_map.93.refs_0_), channel_id=1, source_target_pairs={{0,6},{2,4},{4,2},{6,0},{1,7},{3,5},{5,3},{7,1},{8,14},{10,12},{12... | collective-permute-start | bytes 147464 | tf_op jit(solution)/shard_map/ppermute | solution.py:679
  67.5 1.1 %collective-permute-start.24 = (bf16[192,128]{1,0:T(8,128)(2,1)S(1)}, bf16[192,128]{1,0:T(8,128)(2,1)S(1)}, u32[]{:S(2)}, u32[]{:S(2)}) collective-permute-start(bf16[192,128]{1,0:T(8,128)(2,1)S(1)} %shard_map.93.refs_0_), channel_id=1, source_target_pairs={{0,4},{2,6},{4,0},{6,2},{1,5},{3,7},{5,1},{7,3},{8,12},{10,14},{12... | collective-permute-start | bytes 147464 | tf_op jit(solution)/shard_map/ppermute | solution.py:679
  68.6 1.6 %collective-permute-start.23 = (bf16[192,128]{1,0:T(8,128)(2,1)S(1)}, bf16[192,128]{1,0:T(8,128)(2,1)S(1)}, u32[]{:S(2)}, u32[]{:S(2)}) collective-permute-start(bf16[192,128]{1,0:T(8,128)(2,1)S(1)} %shard_map.93.refs_0_), channel_id=1, source_target_pairs={{0,2},{2,0},{4,6},{6,4},{1,3},{3,1},{5,7},{7,5},{8,10},{10,8},{12,... | collective-permute-start | bytes 147464 | tf_op jit(solution)/shard_map/ppermute | solution.py:679
  70.2 1.8 %collective-permute-done.25.refs_3_ = bf16[192,128]{1,0:T(8,128)(2,1)S(1)} collective-permute-done((bf16[192,128]{1,0:T(8,128)(2,1)S(1)}, bf16[192,128]{1,0:T(8,128)(2,1)S(1)}, u32[]{:S(2)}, u32[]{:S(2)}) %collective-permute-start.25) | collective-permute-done | bytes 49184 | tf_op jit(solution)/shard_map/ppermute | solution.py:679
  72.0 1.3 %collective-permute-done.24.refs_2_ = bf16[192,128]{1,0:T(8,128)(2,1)S(1)} collective-permute-done((bf16[192,128]{1,0:T(8,128)(2,1)S(1)}, bf16[192,128]{1,0:T(8,128)(2,1)S(1)}, u32[]{:S(2)}, u32[]{:S(2)}) %collective-permute-start.24) | collective-permute-done | bytes 49184 | tf_op jit(solution)/shard_map/ppermute | solution.py:679
  73.3 1.4 %collective-permute-done.26.other_ref = bf16[4,192,128]{2,1,0:T(8,128)(2,1)S(1)} collective-permute-done((bf16[4,192,128]{2,1,0:T(8,128)(2,1)S(1)}, bf16[4,192,128]{2,1,0:T(8,128)(2,1)S(1)}, u32[]{:S(2)}, u32[]{:S(2)}) %collective-permute-start.26) | collective-permute-done | bytes 196640 | tf_op jit(solution)/shard_map/ppermute | solution.py:689
  74.8 0.9 %shard_map.95 = (f32[6,192,128]{2,1,0:T(8,128)}, f32[2,192,128]{2,1,0:T(8,128)}) custom-call(bf16[4,192,128]{2,1,0:T(8,128)(2,1)S(1)} %shard_map.94.mine_ref, bf16[4,192,128]{2,1,0:T(8,128)(2,1)S(1)} %collective-permute-done.26.other_ref), custom_call_target="tpu_custom_call" | custom-call | flops 1 | bytes 1 | tf_op jit(solution)/shard_map/pallas_call | solution.py:20
  (67 shorter events, 11.4 us)
Async XLA Ops:
  1.7 1.5 %collective-permute-start = (bf16[2,1,64,128]{3,2,1,0:T(8,128)(2,1)S(1)}, bf16[2,1,64,128]{3,2,1,0:T(8,128)(2,1)S(1)}, u32[]{:S(2)}, u32[]{:S(2)}) collective-permute-start(bf16[2,1,64,128]{3,2,1,0:T(8,128)(2,1)S(1)} %get-tuple-element.88), channel_id=1, source_target_pairs={{0,1},{1,0},{2,3},{3,2},{4,5},{5,4},{6,7},{7,6},{8,9},{9,8},{10,11... | collective-permute-start | bytes 98312 | tf_op jit(solution)/shard_map/ppermute | solution.py:71
  4.1 1.6 %collective-permute-start.1 = (bf16[2,1,64,128]{3,2,1,0:T(8,128)(2,1)S(1)}, bf16[2,1,64,128]{3,2,1,0:T(8,128)(2,1)S(1)}, u32[]{:S(2)}, u32[]{:S(2)}) collective-permute-start(bf16[2,1,64,128]{3,2,1,0:T(8,128)(2,1)S(1)} %get-tuple-element.96), channel_id=1, source_target_pairs={{0,1},{1,0},{2,3},{3,2},{4,5},{5,4},{6,7},{7,6},{8,9},{9,8},{10,11... | collective-permute-start | bytes 98312 | tf_op jit(solution)/shard_map/ppermute | solution.py:71
  4.3 2.8 %collective-permute-start.4 = (bf16[1,10,64,128]{3,2,1,0:T(8,128)(2,1)S(1)}, bf16[1,10,64,128]{3,2,1,0:T(8,128)(2,1)S(1)}, u32[]{:S(2)}, u32[]{:S(2)}) collective-permute-start(bf16[1,10,64,128]{3,2,1,0:T(8,128)(2,1)S(1)} %get-tuple-element.99), channel_id=1, source_target_pairs={{8,10},{10,8},{12,12},{14,14},{16,16},{18,20},{20,18},{22,22},{9,1... | collective-permute-start | bytes 491528 | tf_op jit(solution)/shard_map/ppermute | solution.py:719
  5.0 2.1 %collective-permute-start.5 = (bf16[1,10,64,128]{3,2,1,0:T(8,128)(2,1)S(1)}, bf16[1,10,64,128]{3,2,1,0:T(8,128)(2,1)S(1)}, u32[]{:S(2)}, u32[]{:S(2)}) collective-permute-start(bf16[1,10,64,128]{3,2,1,0:T(8,128)(2,1)S(1)} %get-tuple-element.100), channel_id=1, source_target_pairs={{8,8},{10,10},{12,14},{14,12},{16,18},{18,22},{20,16},{22,20},{9,9... | collective-permute-start | bytes 491528 | tf_op jit(solution)/shard_map/ppermute | solution.py:719
  5.7 1.4 %collective-permute-start.2 = (bf16[1,8,64,128]{3,2,1,0:T(8,128)(2,1)S(1)}, bf16[1,8,64,128]{3,2,1,0:T(8,128)(2,1)S(1)}, u32[]{:S(2)}, u32[]{:S(2)}) collective-permute-start(bf16[1,8,64,128]{3,2,1,0:T(8,128)(2,1)S(1)} %get-tuple-element.97.refs_0_), channel_id=1, source_target_pairs={{24,16},{26,20},{28,18},{30,22},{25,17},{27,21},{29,19},{31,23}} | collective-permute-start | bytes 393224 | tf_op jit(solution)/shard_map/ppermute | solution.py:719
  7.1 1.3 %collective-permute-start.6 = (bf16[2,1,64,128]{3,2,1,0:T(8,128)(2,1)S(1)}, bf16[2,1,64,128]{3,2,1,0:T(8,128)(2,1)S(1)}, u32[]{:S(2)}, u32[]{:S(2)}) collective-permute-start(bf16[2,1,64,128]{3,2,1,0:T(8,128)(2,1)S(1)} %get-tuple-element.110), channel_id=1, source_target_pairs={{0,1},{1,0},{2,3},{3,2},{4,5},{5,4},{6,7},{7,6},{8,9},{9,8},{10,11... | collective-permute-start | bytes 98312 | tf_op jit(solution)/shard_map/ppermute | solution.py:71
  8.4 2.0 %collective-permute-start.9 = (bf16[1,8,64,128]{3,2,1,0:T(8,128)(2,1)S(1)}, bf16[1,8,64,128]{3,2,1,0:T(8,128)(2,1)S(1)}, u32[]{:S(2)}, u32[]{:S(2)}) collective-permute-start(bf16[1,8,64,128]{3,2,1,0:T(8,128)(2,1)S(1)} %get-tuple-element.114), channel_id=1, source_target_pairs={{16,8},{18,10},{20,12},{22,14},{17,9},{19,11},{21,13},{23,15}} | collective-permute-start | bytes 393224 | tf_op jit(solution)/shard_map/ppermute | solution.py:719
  9.1 1.4 %collective-permute-start.8 = (bf16[1,8,64,128]{3,2,1,0:T(8,128)(2,1)S(1)}, bf16[1,8,64,128]{3,2,1,0:T(8,128)(2,1)S(1)}, u32[]{:S(2)}, u32[]{:S(2)}) collective-permute-start(bf16[1,8,64,128]{3,2,1,0:T(8,128)(2,1)S(1)} %get-tuple-element.113), channel_id=1, source_target_pairs={{16,8},{18,10},{20,12},{22,14},{17,9},{19,11},{21,13},{23,15}} | collective-permute-start | bytes 393224 | tf_op jit(solution)/shard_map/ppermute | solution.py:719
  10.5 1.3 %collective-permute-start.10 = (bf16[2,1,64,128]{3,2,1,0:T(8,128)(2,1)S(1)}, bf16[2,1,64,128]{3,2,1,0:T(8,128)(2,1)S(1)}, u32[]{:S(2)}, u32[]{:S(2)}) collective-permute-start(bf16[2,1,64,128]{3,2,1,0:T(8,128)(2,1)S(1)} %get-tuple-element.120), channel_id=1, source_target_pairs={{0,1},{1,0},{2,3},{3,2},{4,5},{5,4},{6,7},{7,6},{8,9},{9,8},{10,11... | collective-permute-start | bytes 98312 | tf_op jit(solution)/shard_map/ppermute | solution.py:71
  11.8 34.2 %collective-permute-start.12 = (bf16[1,8,64,128]{3,2,1,0:T(8,128)(2,1)S(1)}, bf16[1,8,64,128]{3,2,1,0:T(8,128)(2,1)S(1)}, u32[]{:S(2)}, u32[]{:S(2)}) collective-permute-start(bf16[1,8,64,128]{3,2,1,0:T(8,128)(2,1)S(1)} %get-tuple-element.122.refs_3_), channel_id=1, source_target_pairs={{10,0},{12,6},{11,1},{13,7}} | collective-permute-start | bytes 393224 | tf_op jit(solution)/shard_map/ppermute | solution.py:719
  13.1 35.6 %collective-permute-start.11 = (bf16[1,8,64,128]{3,2,1,0:T(8,128)(2,1)S(1)}, bf16[1,8,64,128]{3,2,1,0:T(8,128)(2,1)S(1)}, u32[]{:S(2)}, u32[]{:S(2)}) collective-permute-start(bf16[1,8,64,128]{3,2,1,0:T(8,128)(2,1)S(1)} %get-tuple-element.122.refs_3_), channel_id=1, source_target_pairs={{8,0},{10,2},{12,4},{14,6},{9,1},{11,3},{13,5},{15,7}} | collective-permute-start | bytes 393224 | tf_op jit(solution)/shard_map/ppermute | solution.py:719
  14.4 35.9 %collective-permute-start.17 = (bf16[1,8,64,128]{3,2,1,0:T(8,128)(2,1)S(1)}, bf16[1,8,64,128]{3,2,1,0:T(8,128)(2,1)S(1)}, u32[]{:S(2)}, u32[]{:S(2)}) collective-permute-start(bf16[1,8,64,128]{3,2,1,0:T(8,128)(2,1)S(1)} %get-tuple-element.121.refs_2_), channel_id=1, source_target_pairs={{12,2},{14,4},{13,3},{15,5}} | collective-permute-start | bytes 393224 | tf_op jit(solution)/shard_map/ppermute | solution.py:719
  15.0 35.2 %collective-permute-start.16 = (bf16[1,8,64,128]{3,2,1,0:T(8,128)(2,1)S(1)}, bf16[1,8,64,128]{3,2,1,0:T(8,128)(2,1)S(1)}, u32[]{:S(2)}, u32[]{:S(2)}) collective-permute-start(bf16[1,8,64,128]{3,2,1,0:T(8,128)(2,1)S(1)} %get-tuple-element.121.refs_2_), channel_id=1, source_target_pairs={{8,2},{10,4},{9,3},{11,5}} | collective-permute-start | bytes 393224 | tf_op jit(solution)/shard_map/ppermute | solution.py:719
  15.7 35.7 %collective-permute-start.15 = (bf16[1,8,64,128]{3,2,1,0:T(8,128)(2,1)S(1)}, bf16[1,8,64,128]{3,2,1,0:T(8,128)(2,1)S(1)}, u32[]{:S(2)}, u32[]{:S(2)}) collective-permute-start(bf16[1,8,64,128]{3,2,1,0:T(8,128)(2,1)S(1)} %get-tuple-element.121.refs_2_), channel_id=1, source_target_pairs={{8,0},{10,2},{12,4},{14,6},{9,1},{11,3},{13,5},{15,7}} | collective-permute-start | bytes 393224 | tf_op jit(solution)/shard_map/ppermute | solution.py:719
  48.7 2.8 %collective-permute-start.13 = (bf16[1,8,64,128]{3,2,1,0:T(8,128)(2,1)S(1)}, bf16[1,8,64,128]{3,2,1,0:T(8,128)(2,1)S(1)}, u32[]{:S(2)}, u32[]{:S(2)}) collective-permute-start(bf16[1,8,64,128]{3,2,1,0:T(8,128)(2,1)S(1)} %get-tuple-element.125), channel_id=1, source_target_pairs={{10,8},{8,10},{12,12},{14,14},{16,16},{20,18},{18,20},{22,22},{11,... | collective-permute-start | bytes 393224 | tf_op jit(solution)/shard_map/ppermute | solution.py:719
  49.4 2.1 %collective-permute-start.14 = (bf16[1,8,64,128]{3,2,1,0:T(8,128)(2,1)S(1)}, bf16[1,8,64,128]{3,2,1,0:T(8,128)(2,1)S(1)}, u32[]{:S(2)}, u32[]{:S(2)}) collective-permute-start(bf16[1,8,64,128]{3,2,1,0:T(8,128)(2,1)S(1)} %get-tuple-element.126), channel_id=1, source_target_pairs={{8,8},{10,10},{14,12},{12,14},{18,16},{22,18},{16,20},{20,22},{9,9... | collective-permute-start | bytes 393224 | tf_op jit(solution)/shard_map/ppermute | solution.py:719
  52.7 1.5 %collective-permute-start.19 = (bf16[4,192,128]{2,1,0:T(8,128)(2,1)S(1)}, bf16[4,192,128]{2,1,0:T(8,128)(2,1)S(1)}, u32[]{:S(2)}, u32[]{:S(2)}) collective-permute-start(bf16[4,192,128]{2,1,0:T(8,128)(2,1)S(1)} %shard_map.90), channel_id=1, source_target_pairs={{0,1},{1,0},{2,3},{3,2},{4,5},{5,4},{6,7},{7,6},{8,9},{9,8},{10,11... | collective-permute-start | bytes 589832 | tf_op jit(solution)/shard_map/ppermute | solution.py:682
  54.3 9.3 %collective-permute-start.20 = (bf16[192,128]{1,0:T(8,128)(2,1)S(1)}, bf16[192,128]{1,0:T(8,128)(2,1)S(1)}, u32[]{:S(2)}, u32[]{:S(2)}) collective-permute-start(bf16[192,128]{1,0:T(8,128)(2,1)S(1)} %get-tuple-element.156), channel_id=1, source_target_pairs={{0,2},{2,0},{4,6},{6,4},{1,3},{3,1},{5,7},{7,5},{8,10},{10,8},{12,... | collective-permute-start | bytes 147464 | tf_op jit(solution)/shard_map/ppermute | solution.py:679
  59.0 6.7 %collective-permute-start.21 = (bf16[192,128]{1,0:T(8,128)(2,1)S(1)}, bf16[192,128]{1,0:T(8,128)(2,1)S(1)}, u32[]{:S(2)}, u32[]{:S(2)}) collective-permute-start(bf16[192,128]{1,0:T(8,128)(2,1)S(1)} %get-tuple-element.157), channel_id=1, source_target_pairs={{0,4},{2,6},{4,0},{6,2},{1,5},{3,7},{5,1},{7,3},{8,12},{10,14},{12... | collective-permute-start | bytes 147464 | tf_op jit(solution)/shard_map/ppermute | solution.py:679
  59.0 6.7 %collective-permute-start.22 = (bf16[192,128]{1,0:T(8,128)(2,1)S(1)}, bf16[192,128]{1,0:T(8,128)(2,1)S(1)}, u32[]{:S(2)}, u32[]{:S(2)}) collective-permute-start(bf16[192,128]{1,0:T(8,128)(2,1)S(1)} %get-tuple-element.158), channel_id=1, source_target_pairs={{0,6},{2,4},{4,2},{6,0},{1,7},{3,5},{5,3},{7,1},{8,14},{10,12},{12... | collective-permute-start | bytes 147464 | tf_op jit(solution)/shard_map/ppermute | solution.py:679
  65.7 6.2 %collective-permute-start.25 = (bf16[192,128]{1,0:T(8,128)(2,1)S(1)}, bf16[192,128]{1,0:T(8,128)(2,1)S(1)}, u32[]{:S(2)}, u32[]{:S(2)}) collective-permute-start(bf16[192,128]{1,0:T(8,128)(2,1)S(1)} %shard_map.93.refs_0_), channel_id=1, source_target_pairs={{0,6},{2,4},{4,2},{6,0},{1,7},{3,5},{5,3},{7,1},{8,14},{10,12},{12... | collective-permute-start | bytes 147464 | tf_op jit(solution)/shard_map/ppermute | solution.py:679
  67.5 5.7 %collective-permute-start.24 = (bf16[192,128]{1,0:T(8,128)(2,1)S(1)}, bf16[192,128]{1,0:T(8,128)(2,1)S(1)}, u32[]{:S(2)}, u32[]{:S(2)}) collective-permute-start(bf16[192,128]{1,0:T(8,128)(2,1)S(1)} %shard_map.93.refs_0_), channel_id=1, source_target_pairs={{0,4},{2,6},{4,0},{6,2},{1,5},{3,7},{5,1},{7,3},{8,12},{10,14},{12... | collective-permute-start | bytes 147464 | tf_op jit(solution)/shard_map/ppermute | solution.py:679
  68.6 4.6 %collective-permute-start.23 = (bf16[192,128]{1,0:T(8,128)(2,1)S(1)}, bf16[192,128]{1,0:T(8,128)(2,1)S(1)}, u32[]{:S(2)}, u32[]{:S(2)}) collective-permute-start(bf16[192,128]{1,0:T(8,128)(2,1)S(1)} %shard_map.93.refs_0_), channel_id=1, source_target_pairs={{0,2},{2,0},{4,6},{6,4},{1,3},{3,1},{5,7},{7,5},{8,10},{10,8},{12,... | collective-permute-start | bytes 147464 | tf_op jit(solution)/shard_map/ppermute | solution.py:679
  73.3 1.5 %collective-permute-start.26 = (bf16[4,192,128]{2,1,0:T(8,128)(2,1)S(1)}, bf16[4,192,128]{2,1,0:T(8,128)(2,1)S(1)}, u32[]{:S(2)}, u32[]{:S(2)}) collective-permute-start(bf16[4,192,128]{2,1,0:T(8,128)(2,1)S(1)} %shard_map.94.mine_ref), channel_id=1, source_target_pairs={{0,1},{1,0},{2,3},{3,2},{4,5},{5,4},{6,7},{7,6},{8,9},{9,8},{10,11... | collective-permute-start | bytes 589832 | tf_op jit(solution)/shard_map/ppermute | solution.py:689
  (7 other events, 8.0 us)

commit v9 on v8

--- a/solution.py
+++ b/solution.py
@@ -414,7 +414,7 @@
 
 
 def line_up(pieces):
-    table = ((None, 0, 1, 2), (0, 3, 2, 4), (3, 2, 4, 0), (2, 1, 0, None))
+    table = ((None, 0, 3, 2), (0, 1, 2, 3), (1, 2, 3, 0), (2, 1, 0, None))
 
     def body(*refs):
         for place, order in enumerate(table):
@@ -759,19 +759,19 @@
     grads = kernel_grads(2, x_moved, pre, actives, ready, grads)
 
     ready = [([cross, other, end], low), ([end, cross], low)]
-    pre, (middles, ends) = step(1, ready, slopes, [0, 1])
+    pre, outs = step(1, ready, slopes, [0, 1, lambda: place() < 2, lambda: place() >= 2])
+    middles, ends, ups, downs = outs
     results += [middles, ends]
     pieces = [
         send(ends, (1, 0, stay)),
-        send(ends, (1, 0, [(1, 0), (2, 3)])),
+        send(ups, (1, 0, [(0, 1), (1, 2), (2, 3)])),
         send(middles, (1, 0, stay)),
-        send(middles, (1, 0, [(0, 1), (1, 2)])),
-        send(middles, (1, 0, [(2, 1), (3, 2)])),
+        send(downs, (1, 0, [(1, 0), (2, 1), (3, 2)])),
     ]
     grads = kernel_grads(1, x_moved, pre, actives, ready, grads)
     returned = [
         send(block, *((s, s, back(deal[s][k])) for s in (1, 2)))
-        for k, block in enumerate(after(to_return(results), *pieces[:2]))
+        for k, block in enumerate(after(to_return(results), pieces[1], pieces[3]))
     ]
     before, one, two, later = line_up(after(pieces, *returned))
     ready = [([one, two, before], None), ([two, later, one], None)]

time: 76.3 us -> 75.9 us (level)
  starting transfers between devices: 24.5 us -> 22.1 us
  waiting for transfers between devices: 43.2 us -> 45.4 us
    ppermute x14 -> x13, waiting for transfers between devices: 32.9 us -> 35.2 us  [send(): return lax.ppermute(block, ('section', 'frame'), route)]
    ppermute x6, starting transfers between devices: 11.6 us -> 9.9 us  [over_frame(): return lax.ppermute(block, 'frame', [(i, i ^ mask) for i in range(4)])]
    ppermute x14 -> x13, starting transfers between devices: 11.2 us -> 10.5 us  [send(): return lax.ppermute(block, ('section', 'frame'), route)]
  transfers between devices with their start and end apart: 27 -> 26, of which waited for: 11 -> 11; matrix products, arithmetic and copies ran while one was open for 0% -> 0% of each run, Pallas kernels for 2% -> 2%
where the time goes in v9:
time: 75.9 us; the launch traced here: 75.5 us
  waiting for transfers between devices  45.4 us (60%)
  starting transfers between devices  22.1 us (29%)
  Pallas kernels  4.94 us (7%)
  local copies, waits for them, and re-layouts  2.07 us (3%)
  between operations  1.01 us (1%)
    ppermute x13, waiting for transfers between devices, send(): return lax.ppermute(block, ('section', 'frame'), route)  35.2 us
    ppermute x13, starting transfers between devices, send(): return lax.ppermute(block, ('section', 'frame'), route)  10.5 us
    ppermute x6, starting transfers between devices, over_frame(): return lax.ppermute(block, 'frame', [(i, i ^ mask) for i in range(4)])  9.9 us
    ppermute x6, waiting for transfers between devices, over_frame(): return lax.ppermute(block, 'frame', [(i, i ^ mask) for i in range(4)])  5.1 us
    pallas_call x29, Pallas kernels, call(): pl.pallas_call(body, out_shape=outs, input_output_aliases=aliases or {},...  4.94 us
    ppermute x5, waiting for transfers between devices, swap_edges(): return [lax.ppermute(edges[0], 'row', [(0, 1), (1, 0)])]  2.37 us
    unnamed x8, local copies, waits for them, and re-layouts  2.07 us
  transfers between devices with their start and end apart: 26, of which 11 were waited for; matrix products, arithmetic and copies ran while one was open for 0% of the time, Pallas kernels for 2%

profile of v9, /device:TPU:0, one launch (start us, length us, event | category | flops | bytes accessed | tf_op | source)
XLA Modules:
  0.0 75.5 jit_solution(4670560843561308247)
XLA Ops:
  0.6 1.0 %copy-done.2 = bf16[1,2,8,64,128]{4,3,2,1,0:T(8,128)(2,1)S(1)} copy-done((bf16[1,2,8,64,128]{4,3,2,1,0:T(8,128)(2,1)S(1)}, bf16[1,2,8,64,128]{4,3,2,1,0:T(8,128)(2,1)}, u32[]{:S(2)}) %copy-start.2) | copy-done | bytes 262168
  2.2 0.9 %copy-done.3 = bf16[2,8,64,128]{3,2,1,0:T(8,128)(2,1)S(1)} copy-done((bf16[2,8,64,128]{3,2,1,0:T(8,128)(2,1)S(1)}, bf16[2,8,64,128]{3,2,1,0:T(8,128)(2,1)}, u32[]{:S(2)}) %copy-start.3) | copy-done | bytes 262168
  3.2 0.8 %shard_map.69 = (bf16[2,10,64,128]{3,2,1,0:T(8,128)(2,1)S(1)}, f32[1,8,64,128]{3,2,1,0:T(8,128)S(1)}, f32[1,8,64,128]{3,2,1,0:T(8,128)S(1)}, bf16[1,8,64,128]{3,...) custom-call(bf16[2,8,64,128]{3,2,1,0:T(8,128)(2,1)S(1)} %get-tuple-element.90.refs_0_, ...), custom_call_target="tpu_custom_call" | custom-call | flops 1 | bytes 1 | tf_op jit(solution)/shard_map/pallas_call | solution.py:20
  7.5 0.9 %collective-permute-done.6.refs_5_ = bf16[2,1,64,128]{3,2,1,0:T(8,128)(2,1)S(1)} collective-permute-done((bf16[2,1,64,128]{3,2,1,0:T(8,128)(2,1)S(1)}, bf16[2,1,64,128]{3,2,1,0:T(8,128)(2,1)S(1)}, u32[]{:S(2)}, u32[]{:S(2)}) %collective-permute-start.6) | collective-permute-done | bytes 32800 | tf_op jit(solution)/shard_map/ppermute | solution.py:71
  10.9 0.9 %collective-permute-done.10.refs_5_ = bf16[2,1,64,128]{3,2,1,0:T(8,128)(2,1)S(1)} collective-permute-done((bf16[2,1,64,128]{3,2,1,0:T(8,128)(2,1)S(1)}, bf16[2,1,64,128]{3,2,1,0:T(8,128)(2,1)S(1)}, u32[]{:S(2)}, u32[]{:S(2)}) %collective-permute-start.10) | collective-permute-done | bytes 32800 | tf_op jit(solution)/shard_map/ppermute | solution.py:71
  12.4 1.3 %collective-permute-start.12 = (bf16[1,8,64,128]{3,2,1,0:T(8,128)(2,1)S(1)}, bf16[1,8,64,128]{3,2,1,0:T(8,128)(2,1)S(1)}, u32[]{:S(2)}, u32[]{:S(2)}) collective-permute-start(bf16[1,8,64,128]{3,2,1,0:T(8,128)(2,1)S(1)} %get-tuple-element.131), channel_id=1, source_target_pairs={{10,0},{12,2},{14,4},{11,1},{13,3},{15,5}} | collective-permute-start | bytes 393224 | tf_op jit(solution)/shard_map/ppermute | solution.py:719
  13.7 1.3 %collective-permute-start.16 = (bf16[1,8,64,128]{3,2,1,0:T(8,128)(2,1)S(1)}, bf16[1,8,64,128]{3,2,1,0:T(8,128)(2,1)S(1)}, u32[]{:S(2)}, u32[]{:S(2)}) collective-permute-start(bf16[1,8,64,128]{3,2,1,0:T(8,128)(2,1)S(1)} %get-tuple-element.126.refs_2_), channel_id=1, source_target_pairs={{8,0},{10,2},{12,4},{14,6},{9,1},{11,3},{13,5},{15,7}} | collective-permute-start | bytes 393224 | tf_op jit(solution)/shard_map/ppermute | solution.py:719
  15.0 1.3 %collective-permute-start.15 = (bf16[1,8,64,128]{3,2,1,0:T(8,128)(2,1)S(1)}, bf16[1,8,64,128]{3,2,1,0:T(8,128)(2,1)S(1)}, u32[]{:S(2)}, u32[]{:S(2)}) collective-permute-start(bf16[1,8,64,128]{3,2,1,0:T(8,128)(2,1)S(1)} %get-tuple-element.127.refs_3_), channel_id=1, source_target_pairs={{8,0},{10,2},{12,4},{14,6},{9,1},{11,3},{13,5},{15,7}} | collective-permute-start | bytes 393224 | tf_op jit(solution)/shard_map/ppermute | solution.py:719
  16.4 31.1 %collective-permute-done.12.refs_3_ = bf16[1,8,64,128]{3,2,1,0:T(8,128)(2,1)S(1)} collective-permute-done((bf16[1,8,64,128]{3,2,1,0:T(8,128)(2,1)S(1)}, bf16[1,8,64,128]{3,2,1,0:T(8,128)(2,1)S(1)}, u32[]{:S(2)}, u32[]{:S(2)}) %collective-permute-start.12) | collective-permute-done | bytes 131104 | tf_op jit(solution)/shard_map/ppermute | solution.py:719
  49.0 1.2 %collective-permute-done.16.refs_2_ = bf16[1,8,64,128]{3,2,1,0:T(8,128)(2,1)S(1)} collective-permute-done((bf16[1,8,64,128]{3,2,1,0:T(8,128)(2,1)S(1)}, bf16[1,8,64,128]{3,2,1,0:T(8,128)(2,1)S(1)}, u32[]{:S(2)}, u32[]{:S(2)}) %collective-permute-start.16) | collective-permute-done | bytes 131104 | tf_op jit(solution)/shard_map/ppermute | solution.py:719
  50.3 2.8 %collective-permute-done.15.refs_0_ = bf16[1,8,64,128]{3,2,1,0:T(8,128)(2,1)S(1)} collective-permute-done((bf16[1,8,64,128]{3,2,1,0:T(8,128)(2,1)S(1)}, bf16[1,8,64,128]{3,2,1,0:T(8,128)(2,1)S(1)}, u32[]{:S(2)}, u32[]{:S(2)}) %collective-permute-start.15) | collective-permute-done | bytes 131104 | tf_op jit(solution)/shard_map/ppermute | solution.py:719
  53.5 0.8 %shard_map.89 = f32[12,128,128]{2,1,0:T(8,128)S(1)} custom-call(bf16[2,10,64,128]{3,2,1,0:T(8,128)(2,1)S(1)} %get-tuple-element.150.refs_0_, bf16[1,8,64,128]{3,2,1,0:T(8,128)(2,1)S(1)} %get-tuple-element.142.refs_0_.refs_1_, bf16[1,8,64,128]{3,2,1,0:T(8,128)(2,1)S(1)} %get-tuple-element.143.refs_1_.refs_2_, ...), custom_call_target="tpu_custom_call" | custom-call | flops 1 | bytes 1 | tf_op jit(solution)/shard_map/pallas_call | solution.py:20
  54.5 1.4 %collective-permute-done.18.got_ref = bf16[4,192,128]{2,1,0:T(8,128)(2,1)S(1)} collective-permute-done((bf16[4,192,128]{2,1,0:T(8,128)(2,1)S(1)}, bf16[4,192,128]{2,1,0:T(8,128)(2,1)S(1)}, u32[]{:S(2)}, u32[]{:S(2)}) %collective-permute-start.18) | collective-permute-done | bytes 196640 | tf_op jit(solution)/shard_map/ppermute | solution.py:682
  55.9 3.0 %collective-permute-start.19 = (bf16[192,128]{1,0:T(8,128)(2,1)S(1)}, bf16[192,128]{1,0:T(8,128)(2,1)S(1)}, u32[]{:S(2)}, u32[]{:S(2)}) collective-permute-start(bf16[192,128]{1,0:T(8,128)(2,1)S(1)} %get-tuple-element.162), channel_id=1, source_target_pairs={{0,2},{2,0},{4,6},{6,4},{1,3},{3,1},{5,7},{7,5},{8,10},{10,8},{12,... | collective-permute-start | bytes 147464 | tf_op jit(solution)/shard_map/ppermute | solution.py:679
  59.0 2.4 %collective-permute-start.21 = (bf16[192,128]{1,0:T(8,128)(2,1)S(1)}, bf16[192,128]{1,0:T(8,128)(2,1)S(1)}, u32[]{:S(2)}, u32[]{:S(2)}) collective-permute-start(bf16[192,128]{1,0:T(8,128)(2,1)S(1)} %get-tuple-element.164), channel_id=1, source_target_pairs={{0,6},{2,4},{4,2},{6,0},{1,7},{3,5},{5,3},{7,1},{8,14},{10,12},{12... | collective-permute-start | bytes 147464 | tf_op jit(solution)/shard_map/ppermute | solution.py:679
  62.7 0.7 shard_map.92
  63.5 2.2 %collective-permute-done.20.refs_2_ = bf16[192,128]{1,0:T(8,128)(2,1)S(1)} collective-permute-done((bf16[192,128]{1,0:T(8,128)(2,1)S(1)}, bf16[192,128]{1,0:T(8,128)(2,1)S(1)}, u32[]{:S(2)}, u32[]{:S(2)}) %collective-permute-start.20) | collective-permute-done | bytes 49184 | tf_op jit(solution)/shard_map/ppermute | solution.py:679
  65.7 1.8 %collective-permute-start.24 = (bf16[192,128]{1,0:T(8,128)(2,1)S(1)}, bf16[192,128]{1,0:T(8,128)(2,1)S(1)}, u32[]{:S(2)}, u32[]{:S(2)}) collective-permute-start(bf16[192,128]{1,0:T(8,128)(2,1)S(1)} %shard_map.93.refs_0_), channel_id=1, source_target_pairs={{0,6},{2,4},{4,2},{6,0},{1,7},{3,5},{5,3},{7,1},{8,14},{10,12},{12... | collective-permute-start | bytes 147464 | tf_op jit(solution)/shard_map/ppermute | solution.py:679
  67.5 1.0 %collective-permute-start.23 = (bf16[192,128]{1,0:T(8,128)(2,1)S(1)}, bf16[192,128]{1,0:T(8,128)(2,1)S(1)}, u32[]{:S(2)}, u32[]{:S(2)}) collective-permute-start(bf16[192,128]{1,0:T(8,128)(2,1)S(1)} %shard_map.93.refs_0_), channel_id=1, source_target_pairs={{0,4},{2,6},{4,0},{6,2},{1,5},{3,7},{5,1},{7,3},{8,12},{10,14},{12... | collective-permute-start | bytes 147464 | tf_op jit(solution)/shard_map/ppermute | solution.py:679
  68.5 1.7 %collective-permute-start.22 = (bf16[192,128]{1,0:T(8,128)(2,1)S(1)}, bf16[192,128]{1,0:T(8,128)(2,1)S(1)}, u32[]{:S(2)}, u32[]{:S(2)}) collective-permute-start(bf16[192,128]{1,0:T(8,128)(2,1)S(1)} %shard_map.93.refs_0_), channel_id=1, source_target_pairs={{0,2},{2,0},{4,6},{6,4},{1,3},{3,1},{5,7},{7,5},{8,10},{10,8},{12,... | collective-permute-start | bytes 147464 | tf_op jit(solution)/shard_map/ppermute | solution.py:679
  70.2 1.6 %collective-permute-done.24.refs_3_ = bf16[192,128]{1,0:T(8,128)(2,1)S(1)} collective-permute-done((bf16[192,128]{1,0:T(8,128)(2,1)S(1)}, bf16[192,128]{1,0:T(8,128)(2,1)S(1)}, u32[]{:S(2)}, u32[]{:S(2)}) %collective-permute-start.24) | collective-permute-done | bytes 49184 | tf_op jit(solution)/shard_map/ppermute | solution.py:679
  71.8 1.3 %collective-permute-done.23.refs_2_ = bf16[192,128]{1,0:T(8,128)(2,1)S(1)} collective-permute-done((bf16[192,128]{1,0:T(8,128)(2,1)S(1)}, bf16[192,128]{1,0:T(8,128)(2,1)S(1)}, u32[]{:S(2)}, u32[]{:S(2)}) %collective-permute-start.23) | collective-permute-done | bytes 49184 | tf_op jit(solution)/shard_map/ppermute | solution.py:679
  73.2 1.4 %collective-permute-done.25.other_ref = bf16[4,192,128]{2,1,0:T(8,128)(2,1)S(1)} collective-permute-done((bf16[4,192,128]{2,1,0:T(8,128)(2,1)S(1)}, bf16[4,192,128]{2,1,0:T(8,128)(2,1)S(1)}, u32[]{:S(2)}, u32[]{:S(2)}) %collective-permute-start.25) | collective-permute-done | bytes 196640 | tf_op jit(solution)/shard_map/ppermute | solution.py:689
  74.6 0.9 %shard_map.95 = (f32[6,192,128]{2,1,0:T(8,128)}, f32[2,192,128]{2,1,0:T(8,128)}) custom-call(bf16[4,192,128]{2,1,0:T(8,128)(2,1)S(1)} %shard_map.94.mine_ref, bf16[4,192,128]{2,1,0:T(8,128)(2,1)S(1)} %collective-permute-done.25.other_ref), custom_call_target="tpu_custom_call" | custom-call | flops 1 | bytes 1 | tf_op jit(solution)/shard_map/pallas_call | solution.py:20
  (65 shorter events, 10.9 us)
Async XLA Ops:
  1.7 1.5 %collective-permute-start = (bf16[2,1,64,128]{3,2,1,0:T(8,128)(2,1)S(1)}, bf16[2,1,64,128]{3,2,1,0:T(8,128)(2,1)S(1)}, u32[]{:S(2)}, u32[]{:S(2)}) collective-permute-start(bf16[2,1,64,128]{3,2,1,0:T(8,128)(2,1)S(1)} %get-tuple-element.91), channel_id=1, source_target_pairs={{0,1},{1,0},{2,3},{3,2},{4,5},{5,4},{6,7},{7,6},{8,9},{9,8},{10,11... | collective-permute-start | bytes 98312 | tf_op jit(solution)/shard_map/ppermute | solution.py:71
  4.1 1.6 %collective-permute-start.1 = (bf16[2,1,64,128]{3,2,1,0:T(8,128)(2,1)S(1)}, bf16[2,1,64,128]{3,2,1,0:T(8,128)(2,1)S(1)}, u32[]{:S(2)}, u32[]{:S(2)}) collective-permute-start(bf16[2,1,64,128]{3,2,1,0:T(8,128)(2,1)S(1)} %get-tuple-element.99), channel_id=1, source_target_pairs={{0,1},{1,0},{2,3},{3,2},{4,5},{5,4},{6,7},{7,6},{8,9},{9,8},{10,11... | collective-permute-start | bytes 98312 | tf_op jit(solution)/shard_map/ppermute | solution.py:71
  4.3 2.8 %collective-permute-start.4 = (bf16[1,10,64,128]{3,2,1,0:T(8,128)(2,1)S(1)}, bf16[1,10,64,128]{3,2,1,0:T(8,128)(2,1)S(1)}, u32[]{:S(2)}, u32[]{:S(2)}) collective-permute-start(bf16[1,10,64,128]{3,2,1,0:T(8,128)(2,1)S(1)} %get-tuple-element.102), channel_id=1, source_target_pairs={{8,10},{10,8},{12,12},{14,14},{16,16},{18,20},{20,18},{22,22},{9,1... | collective-permute-start | bytes 491528 | tf_op jit(solution)/shard_map/ppermute | solution.py:719
  5.0 2.1 %collective-permute-start.5 = (bf16[1,10,64,128]{3,2,1,0:T(8,128)(2,1)S(1)}, bf16[1,10,64,128]{3,2,1,0:T(8,128)(2,1)S(1)}, u32[]{:S(2)}, u32[]{:S(2)}) collective-permute-start(bf16[1,10,64,128]{3,2,1,0:T(8,128)(2,1)S(1)} %get-tuple-element.103), channel_id=1, source_target_pairs={{8,8},{10,10},{12,14},{14,12},{16,18},{18,22},{20,16},{22,20},{9,9... | collective-permute-start | bytes 491528 | tf_op jit(solution)/shard_map/ppermute | solution.py:719
  5.7 1.4 %collective-permute-start.2 = (bf16[1,8,64,128]{3,2,1,0:T(8,128)(2,1)S(1)}, bf16[1,8,64,128]{3,2,1,0:T(8,128)(2,1)S(1)}, u32[]{:S(2)}, u32[]{:S(2)}) collective-permute-start(bf16[1,8,64,128]{3,2,1,0:T(8,128)(2,1)S(1)} %get-tuple-element.100.refs_0_), channel_id=1, source_target_pairs={{24,16},{26,20},{28,18},{30,22},{25,17},{27,21},{29,19},{31,23}} | collective-permute-start | bytes 393224 | tf_op jit(solution)/shard_map/ppermute | solution.py:719
  7.1 1.3 %collective-permute-start.6 = (bf16[2,1,64,128]{3,2,1,0:T(8,128)(2,1)S(1)}, bf16[2,1,64,128]{3,2,1,0:T(8,128)(2,1)S(1)}, u32[]{:S(2)}, u32[]{:S(2)}) collective-permute-start(bf16[2,1,64,128]{3,2,1,0:T(8,128)(2,1)S(1)} %get-tuple-element.113), channel_id=1, source_target_pairs={{0,1},{1,0},{2,3},{3,2},{4,5},{5,4},{6,7},{7,6},{8,9},{9,8},{10,11... | collective-permute-start | bytes 98312 | tf_op jit(solution)/shard_map/ppermute | solution.py:71
  8.4 2.0 %collective-permute-start.9 = (bf16[1,8,64,128]{3,2,1,0:T(8,128)(2,1)S(1)}, bf16[1,8,64,128]{3,2,1,0:T(8,128)(2,1)S(1)}, u32[]{:S(2)}, u32[]{:S(2)}) collective-permute-start(bf16[1,8,64,128]{3,2,1,0:T(8,128)(2,1)S(1)} %get-tuple-element.117), channel_id=1, source_target_pairs={{16,8},{18,10},{20,12},{22,14},{17,9},{19,11},{21,13},{23,15}} | collective-permute-start | bytes 393224 | tf_op jit(solution)/shard_map/ppermute | solution.py:719
  9.1 1.4 %collective-permute-start.8 = (bf16[1,8,64,128]{3,2,1,0:T(8,128)(2,1)S(1)}, bf16[1,8,64,128]{3,2,1,0:T(8,128)(2,1)S(1)}, u32[]{:S(2)}, u32[]{:S(2)}) collective-permute-start(bf16[1,8,64,128]{3,2,1,0:T(8,128)(2,1)S(1)} %get-tuple-element.116), channel_id=1, source_target_pairs={{16,8},{18,10},{20,12},{22,14},{17,9},{19,11},{21,13},{23,15}} | collective-permute-start | bytes 393224 | tf_op jit(solution)/shard_map/ppermute | solution.py:719
  10.5 1.3 %collective-permute-start.10 = (bf16[2,1,64,128]{3,2,1,0:T(8,128)(2,1)S(1)}, bf16[2,1,64,128]{3,2,1,0:T(8,128)(2,1)S(1)}, u32[]{:S(2)}, u32[]{:S(2)}) collective-permute-start(bf16[2,1,64,128]{3,2,1,0:T(8,128)(2,1)S(1)} %get-tuple-element.125), channel_id=1, source_target_pairs={{0,1},{1,0},{2,3},{3,2},{4,5},{5,4},{6,7},{7,6},{8,9},{9,8},{10,11... | collective-permute-start | bytes 98312 | tf_op jit(solution)/shard_map/ppermute | solution.py:71
  11.8 4.6 %collective-permute-start.11 = (bf16[1,8,64,128]{3,2,1,0:T(8,128)(2,1)S(1)}, bf16[1,8,64,128]{3,2,1,0:T(8,128)(2,1)S(1)}, u32[]{:S(2)}, u32[]{:S(2)}) collective-permute-start(bf16[1,8,64,128]{3,2,1,0:T(8,128)(2,1)S(1)} %get-tuple-element.130), channel_id=1, source_target_pairs={{8,2},{10,4},{12,6},{9,3},{11,5},{13,7}} | collective-permute-start | bytes 393224 | tf_op jit(solution)/shard_map/ppermute | solution.py:719
  12.4 35.1 %collective-permute-start.12 = (bf16[1,8,64,128]{3,2,1,0:T(8,128)(2,1)S(1)}, bf16[1,8,64,128]{3,2,1,0:T(8,128)(2,1)S(1)}, u32[]{:S(2)}, u32[]{:S(2)}) collective-permute-start(bf16[1,8,64,128]{3,2,1,0:T(8,128)(2,1)S(1)} %get-tuple-element.131), channel_id=1, source_target_pairs={{10,0},{12,2},{14,4},{11,1},{13,3},{15,5}} | collective-permute-start | bytes 393224 | tf_op jit(solution)/shard_map/ppermute | solution.py:719
  13.7 36.5 %collective-permute-start.16 = (bf16[1,8,64,128]{3,2,1,0:T(8,128)(2,1)S(1)}, bf16[1,8,64,128]{3,2,1,0:T(8,128)(2,1)S(1)}, u32[]{:S(2)}, u32[]{:S(2)}) collective-permute-start(bf16[1,8,64,128]{3,2,1,0:T(8,128)(2,1)S(1)} %get-tuple-element.126.refs_2_), channel_id=1, source_target_pairs={{8,0},{10,2},{12,4},{14,6},{9,1},{11,3},{13,5},{15,7}} | collective-permute-start | bytes 393224 | tf_op jit(solution)/shard_map/ppermute | solution.py:719
  15.0 38.0 %collective-permute-start.15 = (bf16[1,8,64,128]{3,2,1,0:T(8,128)(2,1)S(1)}, bf16[1,8,64,128]{3,2,1,0:T(8,128)(2,1)S(1)}, u32[]{:S(2)}, u32[]{:S(2)}) collective-permute-start(bf16[1,8,64,128]{3,2,1,0:T(8,128)(2,1)S(1)} %get-tuple-element.127.refs_3_), channel_id=1, source_target_pairs={{8,0},{10,2},{12,4},{14,6},{9,1},{11,3},{13,5},{15,7}} | collective-permute-start | bytes 393224 | tf_op jit(solution)/shard_map/ppermute | solution.py:719
  47.5 5.5 %collective-permute-start.13 = (bf16[1,8,64,128]{3,2,1,0:T(8,128)(2,1)S(1)}, bf16[1,8,64,128]{3,2,1,0:T(8,128)(2,1)S(1)}, u32[]{:S(2)}, u32[]{:S(2)}) collective-permute-start(bf16[1,8,64,128]{3,2,1,0:T(8,128)(2,1)S(1)} %get-tuple-element.132), channel_id=1, source_target_pairs={{10,8},{8,10},{12,12},{14,14},{16,16},{20,18},{18,20},{22,22},{11,... | collective-permute-start | bytes 393224 | tf_op jit(solution)/shard_map/ppermute | solution.py:719
  48.2 4.9 %collective-permute-start.14 = (bf16[1,8,64,128]{3,2,1,0:T(8,128)(2,1)S(1)}, bf16[1,8,64,128]{3,2,1,0:T(8,128)(2,1)S(1)}, u32[]{:S(2)}, u32[]{:S(2)}) collective-permute-start(bf16[1,8,64,128]{3,2,1,0:T(8,128)(2,1)S(1)} %get-tuple-element.133), channel_id=1, source_target_pairs={{8,8},{10,10},{14,12},{12,14},{18,16},{22,18},{16,20},{20,22},{9,9... | collective-permute-start | bytes 393224 | tf_op jit(solution)/shard_map/ppermute | solution.py:719
  54.3 1.5 %collective-permute-start.18 = (bf16[4,192,128]{2,1,0:T(8,128)(2,1)S(1)}, bf16[4,192,128]{2,1,0:T(8,128)(2,1)S(1)}, u32[]{:S(2)}, u32[]{:S(2)}) collective-permute-start(bf16[4,192,128]{2,1,0:T(8,128)(2,1)S(1)} %shard_map.90), channel_id=1, source_target_pairs={{0,1},{1,0},{2,3},{3,2},{4,5},{5,4},{6,7},{7,6},{8,9},{9,8},{10,11... | collective-permute-start | bytes 589832 | tf_op jit(solution)/shard_map/ppermute | solution.py:682
  55.9 7.6 %collective-permute-start.19 = (bf16[192,128]{1,0:T(8,128)(2,1)S(1)}, bf16[192,128]{1,0:T(8,128)(2,1)S(1)}, u32[]{:S(2)}, u32[]{:S(2)}) collective-permute-start(bf16[192,128]{1,0:T(8,128)(2,1)S(1)} %get-tuple-element.162), channel_id=1, source_target_pairs={{0,2},{2,0},{4,6},{6,4},{1,3},{3,1},{5,7},{7,5},{8,10},{10,8},{12,... | collective-permute-start | bytes 147464 | tf_op jit(solution)/shard_map/ppermute | solution.py:679
  58.9 6.8 %collective-permute-start.20 = (bf16[192,128]{1,0:T(8,128)(2,1)S(1)}, bf16[192,128]{1,0:T(8,128)(2,1)S(1)}, u32[]{:S(2)}, u32[]{:S(2)}) collective-permute-start(bf16[192,128]{1,0:T(8,128)(2,1)S(1)} %get-tuple-element.163), channel_id=1, source_target_pairs={{0,4},{2,6},{4,0},{6,2},{1,5},{3,7},{5,1},{7,3},{8,12},{10,14},{12... | collective-permute-start | bytes 147464 | tf_op jit(solution)/shard_map/ppermute | solution.py:679
  59.0 6.7 %collective-permute-start.21 = (bf16[192,128]{1,0:T(8,128)(2,1)S(1)}, bf16[192,128]{1,0:T(8,128)(2,1)S(1)}, u32[]{:S(2)}, u32[]{:S(2)}) collective-permute-start(bf16[192,128]{1,0:T(8,128)(2,1)S(1)} %get-tuple-element.164), channel_id=1, source_target_pairs={{0,6},{2,4},{4,2},{6,0},{1,7},{3,5},{5,3},{7,1},{8,14},{10,12},{12... | collective-permute-start | bytes 147464 | tf_op jit(solution)/shard_map/ppermute | solution.py:679
  61.3 1.2 %collective-permute-start.17 = (bf16[2,1,64,128]{3,2,1,0:T(8,128)(2,1)S(1)}, bf16[2,1,64,128]{3,2,1,0:T(8,128)(2,1)S(1)}, u32[]{:S(2)}, u32[]{:S(2)}) collective-permute-start(bf16[2,1,64,128]{3,2,1,0:T(8,128)(2,1)S(1)} %get-tuple-element.147), channel_id=1, source_target_pairs={{0,1},{1,0},{2,3},{3,2},{4,5},{5,4},{6,7},{7,6},{8,9},{9,8},{10,11... | collective-permute-start | bytes 98312 | tf_op jit(solution)/shard_map/ppermute | solution.py:71
  65.7 6.1 %collective-permute-start.24 = (bf16[192,128]{1,0:T(8,128)(2,1)S(1)}, bf16[192,128]{1,0:T(8,128)(2,1)S(1)}, u32[]{:S(2)}, u32[]{:S(2)}) collective-permute-start(bf16[192,128]{1,0:T(8,128)(2,1)S(1)} %shard_map.93.refs_0_), channel_id=1, source_target_pairs={{0,6},{2,4},{4,2},{6,0},{1,7},{3,5},{5,3},{7,1},{8,14},{10,12},{12... | collective-permute-start | bytes 147464 | tf_op jit(solution)/shard_map/ppermute | solution.py:679
  67.5 5.6 %collective-permute-start.23 = (bf16[192,128]{1,0:T(8,128)(2,1)S(1)}, bf16[192,128]{1,0:T(8,128)(2,1)S(1)}, u32[]{:S(2)}, u32[]{:S(2)}) collective-permute-start(bf16[192,128]{1,0:T(8,128)(2,1)S(1)} %shard_map.93.refs_0_), channel_id=1, source_target_pairs={{0,4},{2,6},{4,0},{6,2},{1,5},{3,7},{5,1},{7,3},{8,12},{10,14},{12... | collective-permute-start | bytes 147464 | tf_op jit(solution)/shard_map/ppermute | solution.py:679
  68.5 4.6 %collective-permute-start.22 = (bf16[192,128]{1,0:T(8,128)(2,1)S(1)}, bf16[192,128]{1,0:T(8,128)(2,1)S(1)}, u32[]{:S(2)}, u32[]{:S(2)}) collective-permute-start(bf16[192,128]{1,0:T(8,128)(2,1)S(1)} %shard_map.93.refs_0_), channel_id=1, source_target_pairs={{0,2},{2,0},{4,6},{6,4},{1,3},{3,1},{5,7},{7,5},{8,10},{10,8},{12,... | collective-permute-start | bytes 147464 | tf_op jit(solution)/shard_map/ppermute | solution.py:679
  73.1 1.5 %collective-permute-start.25 = (bf16[4,192,128]{2,1,0:T(8,128)(2,1)S(1)}, bf16[4,192,128]{2,1,0:T(8,128)(2,1)S(1)}, u32[]{:S(2)}, u32[]{:S(2)}) collective-permute-start(bf16[4,192,128]{2,1,0:T(8,128)(2,1)S(1)} %shard_map.94.mine_ref), channel_id=1, source_target_pairs={{0,1},{1,0},{2,3},{3,2},{4,5},{5,4},{6,7},{7,6},{8,9},{9,8},{10,11... | collective-permute-start | bytes 589832 | tf_op jit(solution)/shard_map/ppermute | solution.py:689
  (6 other events, 6.8 us)

commit v10 on v9

--- a/solution.py
+++ b/solution.py
@@ -303,13 +303,14 @@
     return call(body, outs, args, 18 * sum(h.size for h in heres) * channels)
 
 
-def kernel_grads(owner, x_rows, grads_pre, actives, triples, before):
+def kernel_grads(owner, x_rows, grads_pre, actives, triples, before, halve=False):
     _, rows, cols, channels = x_rows.shape
     rows -= 2
     chains = len(actives)
 
     def body(*refs):
         section = lax.axis_index("section")
+        refs, half_refs = (refs[:-1], refs[-1:]) if halve else (refs, ())
         out_ref = refs[-1]
 
         if before is not None:
@@ -353,12 +354,19 @@
             for k in range(3):
                 out_ref[9 + k] = time[k]
 
+        for ref in half_refs:
+            start = (1 - lax.axis_index("row")) * 6
+            ref[...] = out_ref[pl.ds(start, 6)].astype(jnp.bfloat16)
+
     args = [x_rows, *grads_pre, *actives]
     args += [block for blocks, _ in triples for block in blocks]
     if before is not None:
         args.append(before)
     outs = [jax.ShapeDtypeStruct((12, channels, channels), jnp.float32)]
-    return call(body, outs, args, 24 * x_rows.size * channels)[0]
+    if halve:
+        outs.append(jax.ShapeDtypeStruct((6, channels, channels), jnp.bfloat16))
+    outs = call(body, outs, args, 24 * x_rows.size * channels)
+    return outs if halve else outs[0]
 
 
 def place_first(section):
@@ -641,17 +649,14 @@
     return grads, (pre, edges, [blocks[0] for blocks, _ in ready]), finish
 
 
-def sum_kernels(grads, first_beside, then_beside):
+def sum_kernels(grads, other, first_beside, then_beside):
     channels = grads.shape[-1]
     eighth = 12 * channels // 8
     pieces = grads.reshape(8, eighth, channels)
+    other = other.reshape(4, eighth, channels)
     half = jax.ShapeDtypeStruct((4, eighth, channels), jnp.bfloat16)
     part = jax.ShapeDtypeStruct((eighth, channels), jnp.bfloat16)
     wide = jax.ShapeDtypeStruct((eighth, channels), jnp.float32)
-
-    def other_half(pieces_ref, out_ref):
-        start = (1 - lax.axis_index("row")) * 4
-        out_ref[...] = pieces_ref[pl.ds(start, 4)].astype(jnp.bfloat16)
 
     def add_half(pieces_ref, got_ref, *out_refs):
         start = lax.axis_index("row") * 4
@@ -679,7 +684,7 @@
         return lax.ppermute(block, "frame", [(i, i ^ mask) for i in range(4)])
 
     swap = [(0, 1), (1, 0)]
-    got = lax.ppermute(call(other_half, [half], [pieces], 0)[0], "row", swap)
+    got = lax.ppermute(other, "row", swap)
     own, *parts = call(add_half, [wide] + [part] * 3, [pieces, got], 0)
     extra = then_beside(parts)
     came = [over_frame(block, mask) for mask, block in enumerate(parts, 1)]
@@ -776,7 +781,7 @@
     before, one, two, later = line_up(after(pieces, *returned))
     ready = [([one, two, before], None), ([two, later, one], None)]
     pre, edges = temporal(0, ready, slopes_own, taps_time)
-    grads = kernel_grads(0, x_own, pre, actives_own, ready, grads)
+    grads = kernel_grads(0, x_own, pre, actives_own, ready, grads, True)
 
     def finish(lasts, parts):
         return own_result(tops, returned, lasts)
@@ -804,7 +809,7 @@
         def result(parts):
             return finish(after(lasts, *parts), parts)
 
-        space, time, own = sum_kernels(grads, lasts, result)
+        space, time, own = sum_kernels(*grads, lasts, result)
         return (
             own[None],
             space.reshape((1, 3, 3, channels, channels)),

time: 75.9 us -> 75.9 us (level)
    pallas_call x29 -> x28, Pallas kernels: 4.94 us -> 4.94 us  [call(): pl.pallas_call(body, out_shape=outs, input_output_aliases=aliases or {},...]
where the time goes in v10:
time: 75.9 us; the launch traced here: 75.5 us
  waiting for transfers between devices  45.4 us (60%)
  starting transfers between devices  22.1 us (29%)
  Pallas kernels  4.94 us (7%)
  local copies, waits for them, and re-layouts  2.07 us (3%)
  between operations  1.01 us (1%)
    ppermute x13, waiting for transfers between devices, send(): return lax.ppermute(block, ('section', 'frame'), route)  35.2 us
    ppermute x13, starting transfers between devices, send(): return lax.ppermute(block, ('section', 'frame'), route)  10.5 us
    ppermute x6, starting transfers between devices, over_frame(): return lax.ppermute(block, 'frame', [(i, i ^ mask) for i in range(4)])  9.9 us
    ppermute x6, waiting for transfers between devices, over_frame(): return lax.ppermute(block, 'frame', [(i, i ^ mask) for i in range(4)])  5.1 us
    pallas_call x28, Pallas kernels, call(): pl.pallas_call(body, out_shape=outs, input_output_aliases=aliases or {},...  4.94 us
    ppermute x5, waiting for transfers between devices, swap_edges(): return [lax.ppermute(edges[0], 'row', [(0, 1), (1, 0)])]  2.37 us
    unnamed x8, local copies, waits for them, and re-layouts  2.07 us
  transfers between devices with their start and end apart: 26, of which 11 were waited for; matrix products, arithmetic and copies ran while one was open for 0% of the time, Pallas kernels for 2%

profile of v10, /device:TPU:0, one launch (start us, length us, event | category | flops | bytes accessed | tf_op | source)
XLA Modules:
  0.0 75.5 jit_solution(15670491662096168205)
XLA Ops:
  0.6 1.0 %copy-done.2 = bf16[1,2,8,64,128]{4,3,2,1,0:T(8,128)(2,1)S(1)} copy-done((bf16[1,2,8,64,128]{4,3,2,1,0:T(8,128)(2,1)S(1)}, bf16[1,2,8,64,128]{4,3,2,1,0:T(8,128)(2,1)}, u32[]{:S(2)}) %copy-start.2) | copy-done | bytes 262168
  2.2 0.9 %copy-done.3 = bf16[2,8,64,128]{3,2,1,0:T(8,128)(2,1)S(1)} copy-done((bf16[2,8,64,128]{3,2,1,0:T(8,128)(2,1)S(1)}, bf16[2,8,64,128]{3,2,1,0:T(8,128)(2,1)}, u32[]{:S(2)}) %copy-start.3) | copy-done | bytes 262168
  3.2 0.8 %shard_map.69 = (bf16[2,10,64,128]{3,2,1,0:T(8,128)(2,1)S(1)}, f32[1,8,64,128]{3,2,1,0:T(8,128)S(1)}, f32[1,8,64,128]{3,2,1,0:T(8,128)S(1)}, bf16[1,8,64,128]{3,...) custom-call(bf16[2,8,64,128]{3,2,1,0:T(8,128)(2,1)S(1)} %get-tuple-element.92.refs_0_, ...), custom_call_target="tpu_custom_call" | custom-call | flops 1 | bytes 1 | tf_op jit(solution)/shard_map/pallas_call | solution.py:20
  7.5 0.9 %collective-permute-done.6.refs_5_ = bf16[2,1,64,128]{3,2,1,0:T(8,128)(2,1)S(1)} collective-permute-done((bf16[2,1,64,128]{3,2,1,0:T(8,128)(2,1)S(1)}, bf16[2,1,64,128]{3,2,1,0:T(8,128)(2,1)S(1)}, u32[]{:S(2)}, u32[]{:S(2)}) %collective-permute-start.6) | collective-permute-done | bytes 32800 | tf_op jit(solution)/shard_map/ppermute | solution.py:71
  10.9 0.9 %collective-permute-done.10.refs_5_ = bf16[2,1,64,128]{3,2,1,0:T(8,128)(2,1)S(1)} collective-permute-done((bf16[2,1,64,128]{3,2,1,0:T(8,128)(2,1)S(1)}, bf16[2,1,64,128]{3,2,1,0:T(8,128)(2,1)S(1)}, u32[]{:S(2)}, u32[]{:S(2)}) %collective-permute-start.10) | collective-permute-done | bytes 32800 | tf_op jit(solution)/shard_map/ppermute | solution.py:71
  12.4 1.3 %collective-permute-start.12 = (bf16[1,8,64,128]{3,2,1,0:T(8,128)(2,1)S(1)}, bf16[1,8,64,128]{3,2,1,0:T(8,128)(2,1)S(1)}, u32[]{:S(2)}, u32[]{:S(2)}) collective-permute-start(bf16[1,8,64,128]{3,2,1,0:T(8,128)(2,1)S(1)} %get-tuple-element.133), channel_id=1, source_target_pairs={{10,0},{12,2},{14,4},{11,1},{13,3},{15,5}} | collective-permute-start | bytes 393224 | tf_op jit(solution)/shard_map/ppermute | solution.py:724
  13.7 1.3 %collective-permute-start.16 = (bf16[1,8,64,128]{3,2,1,0:T(8,128)(2,1)S(1)}, bf16[1,8,64,128]{3,2,1,0:T(8,128)(2,1)S(1)}, u32[]{:S(2)}, u32[]{:S(2)}) collective-permute-start(bf16[1,8,64,128]{3,2,1,0:T(8,128)(2,1)S(1)} %get-tuple-element.128.refs_2_), channel_id=1, source_target_pairs={{8,0},{10,2},{12,4},{14,6},{9,1},{11,3},{13,5},{15,7}} | collective-permute-start | bytes 393224 | tf_op jit(solution)/shard_map/ppermute | solution.py:724
  15.0 1.3 %collective-permute-start.15 = (bf16[1,8,64,128]{3,2,1,0:T(8,128)(2,1)S(1)}, bf16[1,8,64,128]{3,2,1,0:T(8,128)(2,1)S(1)}, u32[]{:S(2)}, u32[]{:S(2)}) collective-permute-start(bf16[1,8,64,128]{3,2,1,0:T(8,128)(2,1)S(1)} %get-tuple-element.129.refs_3_), channel_id=1, source_target_pairs={{8,0},{10,2},{12,4},{14,6},{9,1},{11,3},{13,5},{15,7}} | collective-permute-start | bytes 393224 | tf_op jit(solution)/shard_map/ppermute | solution.py:724
  16.4 31.1 %collective-permute-done.12.refs_3_ = bf16[1,8,64,128]{3,2,1,0:T(8,128)(2,1)S(1)} collective-permute-done((bf16[1,8,64,128]{3,2,1,0:T(8,128)(2,1)S(1)}, bf16[1,8,64,128]{3,2,1,0:T(8,128)(2,1)S(1)}, u32[]{:S(2)}, u32[]{:S(2)}) %collective-permute-start.12) | collective-permute-done | bytes 131104 | tf_op jit(solution)/shard_map/ppermute | solution.py:724
  49.0 1.2 %collective-permute-done.16.refs_2_ = bf16[1,8,64,128]{3,2,1,0:T(8,128)(2,1)S(1)} collective-permute-done((bf16[1,8,64,128]{3,2,1,0:T(8,128)(2,1)S(1)}, bf16[1,8,64,128]{3,2,1,0:T(8,128)(2,1)S(1)}, u32[]{:S(2)}, u32[]{:S(2)}) %collective-permute-start.16) | collective-permute-done | bytes 131104 | tf_op jit(solution)/shard_map/ppermute | solution.py:724
  50.3 2.8 %collective-permute-done.15.refs_0_ = bf16[1,8,64,128]{3,2,1,0:T(8,128)(2,1)S(1)} collective-permute-done((bf16[1,8,64,128]{3,2,1,0:T(8,128)(2,1)S(1)}, bf16[1,8,64,128]{3,2,1,0:T(8,128)(2,1)S(1)}, u32[]{:S(2)}, u32[]{:S(2)}) %collective-permute-start.15) | collective-permute-done | bytes 131104 | tf_op jit(solution)/shard_map/ppermute | solution.py:724
  53.5 0.8 %shard_map.89 = (f32[12,128,128]{2,1,0:T(8,128)S(1)}, bf16[6,128,128]{2,1,0:T(8,128)(2,1)S(1)}) custom-call(bf16[2,10,64,128]{3,2,1,0:T(8,128)(2,1)S(1)} %get-tuple-element.152.refs_0_, bf16[1,8,64,128]{3,2,1,0:T(8,128)(2,1)S(1)} %get-tuple-element.144.refs_0_.refs_1_, bf16[1,8,64,128]{3,2,1,0:T(8,128)(2,1)S(1)} %get-tuple-element.145.refs_1_.refs_2_, ...), custom_call_target="tpu_custom_call" | custom-call | flops 1 | bytes 1 | tf_op jit(solution)/shard_map/pallas_call | solution.py:20
  54.4 1.4 %collective-permute-done.18.got_ref = bf16[4,192,128]{2,1,0:T(8,128)(2,1)S(1)} collective-permute-done((bf16[4,192,128]{2,1,0:T(8,128)(2,1)S(1)}, bf16[4,192,128]{2,1,0:T(8,128)(2,1)S(1)}, u32[]{:S(2)}, u32[]{:S(2)}) %collective-permute-start.18) | collective-permute-done | bytes 196640 | tf_op jit(solution)/shard_map/ppermute | solution.py:687
  55.9 3.0 %collective-permute-start.19 = (bf16[192,128]{1,0:T(8,128)(2,1)S(1)}, bf16[192,128]{1,0:T(8,128)(2,1)S(1)}, u32[]{:S(2)}, u32[]{:S(2)}) collective-permute-start(bf16[192,128]{1,0:T(8,128)(2,1)S(1)} %get-tuple-element.166), channel_id=1, source_target_pairs={{0,2},{2,0},{4,6},{6,4},{1,3},{3,1},{5,7},{7,5},{8,10},{10,8},{12,... | collective-permute-start | bytes 147464 | tf_op jit(solution)/shard_map/ppermute | solution.py:684
  58.9 2.4 %collective-permute-start.21 = (bf16[192,128]{1,0:T(8,128)(2,1)S(1)}, bf16[192,128]{1,0:T(8,128)(2,1)S(1)}, u32[]{:S(2)}, u32[]{:S(2)}) collective-permute-start(bf16[192,128]{1,0:T(8,128)(2,1)S(1)} %get-tuple-element.168), channel_id=1, source_target_pairs={{0,6},{2,4},{4,2},{6,0},{1,7},{3,5},{5,3},{7,1},{8,14},{10,12},{12... | collective-permute-start | bytes 147464 | tf_op jit(solution)/shard_map/ppermute | solution.py:684
  62.7 0.7 shard_map.91
  63.5 2.2 %collective-permute-done.20.refs_2_ = bf16[192,128]{1,0:T(8,128)(2,1)S(1)} collective-permute-done((bf16[192,128]{1,0:T(8,128)(2,1)S(1)}, bf16[192,128]{1,0:T(8,128)(2,1)S(1)}, u32[]{:S(2)}, u32[]{:S(2)}) %collective-permute-start.20) | collective-permute-done | bytes 49184 | tf_op jit(solution)/shard_map/ppermute | solution.py:684
  65.7 1.8 %collective-permute-start.24 = (bf16[192,128]{1,0:T(8,128)(2,1)S(1)}, bf16[192,128]{1,0:T(8,128)(2,1)S(1)}, u32[]{:S(2)}, u32[]{:S(2)}) collective-permute-start(bf16[192,128]{1,0:T(8,128)(2,1)S(1)} %shard_map.92.refs_0_), channel_id=1, source_target_pairs={{0,6},{2,4},{4,2},{6,0},{1,7},{3,5},{5,3},{7,1},{8,14},{10,12},{12... | collective-permute-start | bytes 147464 | tf_op jit(solution)/shard_map/ppermute | solution.py:684
  67.4 1.0 %collective-permute-start.23 = (bf16[192,128]{1,0:T(8,128)(2,1)S(1)}, bf16[192,128]{1,0:T(8,128)(2,1)S(1)}, u32[]{:S(2)}, u32[]{:S(2)}) collective-permute-start(bf16[192,128]{1,0:T(8,128)(2,1)S(1)} %shard_map.92.refs_0_), channel_id=1, source_target_pairs={{0,4},{2,6},{4,0},{6,2},{1,5},{3,7},{5,1},{7,3},{8,12},{10,14},{12... | collective-permute-start | bytes 147464 | tf_op jit(solution)/shard_map/ppermute | solution.py:684
  68.4 1.7 %collective-permute-start.22 = (bf16[192,128]{1,0:T(8,128)(2,1)S(1)}, bf16[192,128]{1,0:T(8,128)(2,1)S(1)}, u32[]{:S(2)}, u32[]{:S(2)}) collective-permute-start(bf16[192,128]{1,0:T(8,128)(2,1)S(1)} %shard_map.92.refs_0_), channel_id=1, source_target_pairs={{0,2},{2,0},{4,6},{6,4},{1,3},{3,1},{5,7},{7,5},{8,10},{10,8},{12,... | collective-permute-start | bytes 147464 | tf_op jit(solution)/shard_map/ppermute | solution.py:684
  70.1 1.6 %collective-permute-done.24.refs_3_ = bf16[192,128]{1,0:T(8,128)(2,1)S(1)} collective-permute-done((bf16[192,128]{1,0:T(8,128)(2,1)S(1)}, bf16[192,128]{1,0:T(8,128)(2,1)S(1)}, u32[]{:S(2)}, u32[]{:S(2)}) %collective-permute-start.24) | collective-permute-done | bytes 49184 | tf_op jit(solution)/shard_map/ppermute | solution.py:684
  71.7 1.3 %collective-permute-done.23.refs_2_ = bf16[192,128]{1,0:T(8,128)(2,1)S(1)} collective-permute-done((bf16[192,128]{1,0:T(8,128)(2,1)S(1)}, bf16[192,128]{1,0:T(8,128)(2,1)S(1)}, u32[]{:S(2)}, u32[]{:S(2)}) %collective-permute-start.23) | collective-permute-done | bytes 49184 | tf_op jit(solution)/shard_map/ppermute | solution.py:684
  73.2 1.4 %collective-permute-done.25.other_ref = bf16[4,192,128]{2,1,0:T(8,128)(2,1)S(1)} collective-permute-done((bf16[4,192,128]{2,1,0:T(8,128)(2,1)S(1)}, bf16[4,192,128]{2,1,0:T(8,128)(2,1)S(1)}, u32[]{:S(2)}, u32[]{:S(2)}) %collective-permute-start.25) | collective-permute-done | bytes 196640 | tf_op jit(solution)/shard_map/ppermute | solution.py:694
  74.6 0.9 %shard_map.94 = (f32[6,192,128]{2,1,0:T(8,128)}, f32[2,192,128]{2,1,0:T(8,128)}) custom-call(bf16[4,192,128]{2,1,0:T(8,128)(2,1)S(1)} %shard_map.93.mine_ref, bf16[4,192,128]{2,1,0:T(8,128)(2,1)S(1)} %collective-permute-done.25.other_ref), custom_call_target="tpu_custom_call" | custom-call | flops 1 | bytes 1 | tf_op jit(solution)/shard_map/pallas_call | solution.py:20
  (64 shorter events, 10.8 us)
Async XLA Ops:
  1.7 1.5 %collective-permute-start = (bf16[2,1,64,128]{3,2,1,0:T(8,128)(2,1)S(1)}, bf16[2,1,64,128]{3,2,1,0:T(8,128)(2,1)S(1)}, u32[]{:S(2)}, u32[]{:S(2)}) collective-permute-start(bf16[2,1,64,128]{3,2,1,0:T(8,128)(2,1)S(1)} %get-tuple-element.93), channel_id=1, source_target_pairs={{0,1},{1,0},{2,3},{3,2},{4,5},{5,4},{6,7},{7,6},{8,9},{9,8},{10,11... | collective-permute-start | bytes 98312 | tf_op jit(solution)/shard_map/ppermute | solution.py:71
  4.1 1.6 %collective-permute-start.1 = (bf16[2,1,64,128]{3,2,1,0:T(8,128)(2,1)S(1)}, bf16[2,1,64,128]{3,2,1,0:T(8,128)(2,1)S(1)}, u32[]{:S(2)}, u32[]{:S(2)}) collective-permute-start(bf16[2,1,64,128]{3,2,1,0:T(8,128)(2,1)S(1)} %get-tuple-element.101), channel_id=1, source_target_pairs={{0,1},{1,0},{2,3},{3,2},{4,5},{5,4},{6,7},{7,6},{8,9},{9,8},{10,11... | collective-permute-start | bytes 98312 | tf_op jit(solution)/shard_map/ppermute | solution.py:71
  4.3 2.8 %collective-permute-start.4 = (bf16[1,10,64,128]{3,2,1,0:T(8,128)(2,1)S(1)}, bf16[1,10,64,128]{3,2,1,0:T(8,128)(2,1)S(1)}, u32[]{:S(2)}, u32[]{:S(2)}) collective-permute-start(bf16[1,10,64,128]{3,2,1,0:T(8,128)(2,1)S(1)} %get-tuple-element.104), channel_id=1, source_target_pairs={{8,10},{10,8},{12,12},{14,14},{16,16},{18,20},{20,18},{22,22},{9,1... | collective-permute-start | bytes 491528 | tf_op jit(solution)/shard_map/ppermute | solution.py:724
  5.0 2.1 %collective-permute-start.5 = (bf16[1,10,64,128]{3,2,1,0:T(8,128)(2,1)S(1)}, bf16[1,10,64,128]{3,2,1,0:T(8,128)(2,1)S(1)}, u32[]{:S(2)}, u32[]{:S(2)}) collective-permute-start(bf16[1,10,64,128]{3,2,1,0:T(8,128)(2,1)S(1)} %get-tuple-element.105), channel_id=1, source_target_pairs={{8,8},{10,10},{12,14},{14,12},{16,18},{18,22},{20,16},{22,20},{9,9... | collective-permute-start | bytes 491528 | tf_op jit(solution)/shard_map/ppermute | solution.py:724
  5.7 1.4 %collective-permute-start.2 = (bf16[1,8,64,128]{3,2,1,0:T(8,128)(2,1)S(1)}, bf16[1,8,64,128]{3,2,1,0:T(8,128)(2,1)S(1)}, u32[]{:S(2)}, u32[]{:S(2)}) collective-permute-start(bf16[1,8,64,128]{3,2,1,0:T(8,128)(2,1)S(1)} %get-tuple-element.102.refs_0_), channel_id=1, source_target_pairs={{24,16},{26,20},{28,18},{30,22},{25,17},{27,21},{29,19},{31,23}} | collective-permute-start | bytes 393224 | tf_op jit(solution)/shard_map/ppermute | solution.py:724
  7.1 1.3 %collective-permute-start.6 = (bf16[2,1,64,128]{3,2,1,0:T(8,128)(2,1)S(1)}, bf16[2,1,64,128]{3,2,1,0:T(8,128)(2,1)S(1)}, u32[]{:S(2)}, u32[]{:S(2)}) collective-permute-start(bf16[2,1,64,128]{3,2,1,0:T(8,128)(2,1)S(1)} %get-tuple-element.115), channel_id=1, source_target_pairs={{0,1},{1,0},{2,3},{3,2},{4,5},{5,4},{6,7},{7,6},{8,9},{9,8},{10,11... | collective-permute-start | bytes 98312 | tf_op jit(solution)/shard_map/ppermute | solution.py:71
  8.4 2.0 %collective-permute-start.9 = (bf16[1,8,64,128]{3,2,1,0:T(8,128)(2,1)S(1)}, bf16[1,8,64,128]{3,2,1,0:T(8,128)(2,1)S(1)}, u32[]{:S(2)}, u32[]{:S(2)}) collective-permute-start(bf16[1,8,64,128]{3,2,1,0:T(8,128)(2,1)S(1)} %get-tuple-element.119), channel_id=1, source_target_pairs={{16,8},{18,10},{20,12},{22,14},{17,9},{19,11},{21,13},{23,15}} | collective-permute-start | bytes 393224 | tf_op jit(solution)/shard_map/ppermute | solution.py:724
  9.1 1.4 %collective-permute-start.8 = (bf16[1,8,64,128]{3,2,1,0:T(8,128)(2,1)S(1)}, bf16[1,8,64,128]{3,2,1,0:T(8,128)(2,1)S(1)}, u32[]{:S(2)}, u32[]{:S(2)}) collective-permute-start(bf16[1,8,64,128]{3,2,1,0:T(8,128)(2,1)S(1)} %get-tuple-element.118), channel_id=1, source_target_pairs={{16,8},{18,10},{20,12},{22,14},{17,9},{19,11},{21,13},{23,15}} | collective-permute-start | bytes 393224 | tf_op jit(solution)/shard_map/ppermute | solution.py:724
  10.5 1.3 %collective-permute-start.10 = (bf16[2,1,64,128]{3,2,1,0:T(8,128)(2,1)S(1)}, bf16[2,1,64,128]{3,2,1,0:T(8,128)(2,1)S(1)}, u32[]{:S(2)}, u32[]{:S(2)}) collective-permute-start(bf16[2,1,64,128]{3,2,1,0:T(8,128)(2,1)S(1)} %get-tuple-element.127), channel_id=1, source_target_pairs={{0,1},{1,0},{2,3},{3,2},{4,5},{5,4},{6,7},{7,6},{8,9},{9,8},{10,11... | collective-permute-start | bytes 98312 | tf_op jit(solution)/shard_map/ppermute | solution.py:71
  11.8 4.6 %collective-permute-start.11 = (bf16[1,8,64,128]{3,2,1,0:T(8,128)(2,1)S(1)}, bf16[1,8,64,128]{3,2,1,0:T(8,128)(2,1)S(1)}, u32[]{:S(2)}, u32[]{:S(2)}) collective-permute-start(bf16[1,8,64,128]{3,2,1,0:T(8,128)(2,1)S(1)} %get-tuple-element.132), channel_id=1, source_target_pairs={{8,2},{10,4},{12,6},{9,3},{11,5},{13,7}} | collective-permute-start | bytes 393224 | tf_op jit(solution)/shard_map/ppermute | solution.py:724
  12.4 35.1 %collective-permute-start.12 = (bf16[1,8,64,128]{3,2,1,0:T(8,128)(2,1)S(1)}, bf16[1,8,64,128]{3,2,1,0:T(8,128)(2,1)S(1)}, u32[]{:S(2)}, u32[]{:S(2)}) collective-permute-start(bf16[1,8,64,128]{3,2,1,0:T(8,128)(2,1)S(1)} %get-tuple-element.133), channel_id=1, source_target_pairs={{10,0},{12,2},{14,4},{11,1},{13,3},{15,5}} | collective-permute-start | bytes 393224 | tf_op jit(solution)/shard_map/ppermute | solution.py:724
  13.7 36.5 %collective-permute-start.16 = (bf16[1,8,64,128]{3,2,1,0:T(8,128)(2,1)S(1)}, bf16[1,8,64,128]{3,2,1,0:T(8,128)(2,1)S(1)}, u32[]{:S(2)}, u32[]{:S(2)}) collective-permute-start(bf16[1,8,64,128]{3,2,1,0:T(8,128)(2,1)S(1)} %get-tuple-element.128.refs_2_), channel_id=1, source_target_pairs={{8,0},{10,2},{12,4},{14,6},{9,1},{11,3},{13,5},{15,7}} | collective-permute-start | bytes 393224 | tf_op jit(solution)/shard_map/ppermute | solution.py:724
  15.0 38.0 %collective-permute-start.15 = (bf16[1,8,64,128]{3,2,1,0:T(8,128)(2,1)S(1)}, bf16[1,8,64,128]{3,2,1,0:T(8,128)(2,1)S(1)}, u32[]{:S(2)}, u32[]{:S(2)}) collective-permute-start(bf16[1,8,64,128]{3,2,1,0:T(8,128)(2,1)S(1)} %get-tuple-element.129.refs_3_), channel_id=1, source_target_pairs={{8,0},{10,2},{12,4},{14,6},{9,1},{11,3},{13,5},{15,7}} | collective-permute-start | bytes 393224 | tf_op jit(solution)/shard_map/ppermute | solution.py:724
  47.5 5.5 %collective-permute-start.13 = (bf16[1,8,64,128]{3,2,1,0:T(8,128)(2,1)S(1)}, bf16[1,8,64,128]{3,2,1,0:T(8,128)(2,1)S(1)}, u32[]{:S(2)}, u32[]{:S(2)}) collective-permute-start(bf16[1,8,64,128]{3,2,1,0:T(8,128)(2,1)S(1)} %get-tuple-element.134), channel_id=1, source_target_pairs={{10,8},{8,10},{12,12},{14,14},{16,16},{20,18},{18,20},{22,22},{11,... | collective-permute-start | bytes 393224 | tf_op jit(solution)/shard_map/ppermute | solution.py:724
  48.2 4.9 %collective-permute-start.14 = (bf16[1,8,64,128]{3,2,1,0:T(8,128)(2,1)S(1)}, bf16[1,8,64,128]{3,2,1,0:T(8,128)(2,1)S(1)}, u32[]{:S(2)}, u32[]{:S(2)}) collective-permute-start(bf16[1,8,64,128]{3,2,1,0:T(8,128)(2,1)S(1)} %get-tuple-element.135), channel_id=1, source_target_pairs={{8,8},{10,10},{14,12},{12,14},{18,16},{22,18},{16,20},{20,22},{9,9... | collective-permute-start | bytes 393224 | tf_op jit(solution)/shard_map/ppermute | solution.py:724
  54.3 1.5 %collective-permute-start.18 = (bf16[4,192,128]{2,1,0:T(8,128)(2,1)S(1)}, bf16[4,192,128]{2,1,0:T(8,128)(2,1)S(1)}, u32[]{:S(2)}, u32[]{:S(2)}) collective-permute-start(bf16[4,192,128]{2,1,0:T(8,128)(2,1)S(1)} %bitcast.24), channel_id=1, source_target_pairs={{0,1},{1,0},{2,3},{3,2},{4,5},{5,4},{6,7},{7,6},{8,9},{9,8},{10,11... | collective-permute-start | bytes 589832 | tf_op jit(solution)/shard_map/ppermute | solution.py:687
  55.9 7.6 %collective-permute-start.19 = (bf16[192,128]{1,0:T(8,128)(2,1)S(1)}, bf16[192,128]{1,0:T(8,128)(2,1)S(1)}, u32[]{:S(2)}, u32[]{:S(2)}) collective-permute-start(bf16[192,128]{1,0:T(8,128)(2,1)S(1)} %get-tuple-element.166), channel_id=1, source_target_pairs={{0,2},{2,0},{4,6},{6,4},{1,3},{3,1},{5,7},{7,5},{8,10},{10,8},{12,... | collective-permute-start | bytes 147464 | tf_op jit(solution)/shard_map/ppermute | solution.py:684
  58.9 6.8 %collective-permute-start.20 = (bf16[192,128]{1,0:T(8,128)(2,1)S(1)}, bf16[192,128]{1,0:T(8,128)(2,1)S(1)}, u32[]{:S(2)}, u32[]{:S(2)}) collective-permute-start(bf16[192,128]{1,0:T(8,128)(2,1)S(1)} %get-tuple-element.167), channel_id=1, source_target_pairs={{0,4},{2,6},{4,0},{6,2},{1,5},{3,7},{5,1},{7,3},{8,12},{10,14},{12... | collective-permute-start | bytes 147464 | tf_op jit(solution)/shard_map/ppermute | solution.py:684
  58.9 6.7 %collective-permute-start.21 = (bf16[192,128]{1,0:T(8,128)(2,1)S(1)}, bf16[192,128]{1,0:T(8,128)(2,1)S(1)}, u32[]{:S(2)}, u32[]{:S(2)}) collective-permute-start(bf16[192,128]{1,0:T(8,128)(2,1)S(1)} %get-tuple-element.168), channel_id=1, source_target_pairs={{0,6},{2,4},{4,2},{6,0},{1,7},{3,5},{5,3},{7,1},{8,14},{10,12},{12... | collective-permute-start | bytes 147464 | tf_op jit(solution)/shard_map/ppermute | solution.py:684
  61.3 1.2 %collective-permute-start.17 = (bf16[2,1,64,128]{3,2,1,0:T(8,128)(2,1)S(1)}, bf16[2,1,64,128]{3,2,1,0:T(8,128)(2,1)S(1)}, u32[]{:S(2)}, u32[]{:S(2)}) collective-permute-start(bf16[2,1,64,128]{3,2,1,0:T(8,128)(2,1)S(1)} %get-tuple-element.149), channel_id=1, source_target_pairs={{0,1},{1,0},{2,3},{3,2},{4,5},{5,4},{6,7},{7,6},{8,9},{9,8},{10,11... | collective-permute-start | bytes 98312 | tf_op jit(solution)/shard_map/ppermute | solution.py:71
  65.7 6.1 %collective-permute-start.24 = (bf16[192,128]{1,0:T(8,128)(2,1)S(1)}, bf16[192,128]{1,0:T(8,128)(2,1)S(1)}, u32[]{:S(2)}, u32[]{:S(2)}) collective-permute-start(bf16[192,128]{1,0:T(8,128)(2,1)S(1)} %shard_map.92.refs_0_), channel_id=1, source_target_pairs={{0,6},{2,4},{4,2},{6,0},{1,7},{3,5},{5,3},{7,1},{8,14},{10,12},{12... | collective-permute-start | bytes 147464 | tf_op jit(solution)/shard_map/ppermute | solution.py:684
  67.4 5.6 %collective-permute-start.23 = (bf16[192,128]{1,0:T(8,128)(2,1)S(1)}, bf16[192,128]{1,0:T(8,128)(2,1)S(1)}, u32[]{:S(2)}, u32[]{:S(2)}) collective-permute-start(bf16[192,128]{1,0:T(8,128)(2,1)S(1)} %shard_map.92.refs_0_), channel_id=1, source_target_pairs={{0,4},{2,6},{4,0},{6,2},{1,5},{3,7},{5,1},{7,3},{8,12},{10,14},{12... | collective-permute-start | bytes 147464 | tf_op jit(solution)/shard_map/ppermute | solution.py:684
  68.4 4.6 %collective-permute-start.22 = (bf16[192,128]{1,0:T(8,128)(2,1)S(1)}, bf16[192,128]{1,0:T(8,128)(2,1)S(1)}, u32[]{:S(2)}, u32[]{:S(2)}) collective-permute-start(bf16[192,128]{1,0:T(8,128)(2,1)S(1)} %shard_map.92.refs_0_), channel_id=1, source_target_pairs={{0,2},{2,0},{4,6},{6,4},{1,3},{3,1},{5,7},{7,5},{8,10},{10,8},{12,... | collective-permute-start | bytes 147464 | tf_op jit(solution)/shard_map/ppermute | solution.py:684
  73.1 1.5 %collective-permute-start.25 = (bf16[4,192,128]{2,1,0:T(8,128)(2,1)S(1)}, bf16[4,192,128]{2,1,0:T(8,128)(2,1)S(1)}, u32[]{:S(2)}, u32[]{:S(2)}) collective-permute-start(bf16[4,192,128]{2,1,0:T(8,128)(2,1)S(1)} %shard_map.93.mine_ref), channel_id=1, source_target_pairs={{0,1},{1,0},{2,3},{3,2},{4,5},{5,4},{6,7},{7,6},{8,9},{9,8},{10,11... | collective-permute-start | bytes 589832 | tf_op jit(solution)/shard_map/ppermute | solution.py:694
  (6 other events, 6.8 us)
